TPU v7x, 256 devices: a whole 4x4x8 slice. The times are simulated.
256 devices in a mesh: shot: 8 (over y_lo, x), mp: 32 (over z, y_hi, core).
Axes of the slice: x: 4, y: 4 (y_hi: 2, y_lo: 2; y = y_hi * 2 + y_lo), z: 8, core: 2. Of those that a mesh axis runs over, the one named last changes fastest.
Arguments:
- courant: float32 [2, 512, 64, 256], P(None, 'mp'), may hold values from 0.05 to 0.2
- aperture_first: int32 [8], P('shot'), may hold values from 0 to 32
- source_pos: int32 [8, 3], P('shot'), may hold values from 0 to 511, as said below
- wavelet: float32 [8, 4], P('shot'), may hold values from -6 to 6
- receiver_pos: int32 [8, 32, 3], P('shot'), may hold values from 0 to 511, as said below
- residual: float32 [8, 4, 32], P('shot'), may hold values from -6 to 6
- step_count: int32 [8], P('shot'), may hold values from 2 to 4
- forward_prev: float32 [8, 512, 64, 256], P('shot', 'mp'), may hold values from -1 to 1
- forward_now: float32 [8, 512, 64, 256], P('shot', 'mp'), may hold values from -1 to 1
- adjoint_prev: float32 [8, 512, 64, 256], P('shot', 'mp'), may hold values from -1 to 1
- adjoint_now: float32 [8, 512, 64, 256], P('shot', 'mp'), may hold values from -1 to 1
Outputs:
- gradient: float32 [2, 512, 64, 256], P(None, 'mp', 'shot')
Inputs may be any that keep to these rules, and one draw needn't show every extreme that they name: `source_pos`: each component lies inside the aperture grid: first in 0..511, second in 0..63, third in 0..255. `receiver_pos`: each component lies inside the aperture grid (first in 0..511, second in 0..63, third in 0..255), within 12 cells of the shot's source along every dimension. The aperture covers model tiles aperture_first .. aperture_first + 31.
All inputs are finite; a program needn't handle non-finite values.
Results may differ from a plain program's by a relative error of at most 0.0003.
Values sent between devices are 32-bit elements; how exact they have to be, the bound alone decides.
No kernel may reach another device: no remote copies, remote signals or barrier semaphores. Data moves between devices by JAX's collectives and lax.ppermute only.
A program may use at most 128 MiB of HBM per device.

v0:
```python
import jax
import jax.numpy as jnp
from jax import lax
from jax.sharding import PartitionSpec as P

COEF = (-205.0 / 72.0, 1.6, -0.2, 8.0 / 315.0, -1.0 / 560.0)


def extended(value, sides, width):
    for axis, dim in sides:
        size, length = (lax.axis_size(axis), value.shape[dim])
        up = [(i, (i + 1) % size) for i in range(size - 1)]
        down = [(j, i) for i, j in up]
        last = lax.slice_in_dim(value, length - width, length, axis=dim)
        leading = lax.slice_in_dim(value, 0, width, axis=dim)
        before = lax.ppermute(last, axis, up)
        after = lax.ppermute(leading, axis, down)
        value = jnp.concatenate([before, value, after], axis=dim)
    return value


def passed_along(value, axis, steps):
    count = lax.axis_size(axis)
    pairs = [(source, (source + steps) % count) for source in range(count)]
    return lax.ppermute(value, axis, pairs)


def laplace_core(padded, width):
    ys = padded.shape[2]
    zs = padded.shape[3]
    centre = padded[:, 4 : 4 + width]
    side = jnp.pad(centre, ((0, 0), (0, 0), (4, 4), (4, 4)))
    total = 3.0 * COEF[0] * centre
    for k in range(1, 5):
        total = total + COEF[k] * (
            padded[:, 4 + k : 4 + k + width] + padded[:, 4 - k : 4 - k + width]
        )
        total = total + COEF[k] * (
            side[:, :, 4 + k : 4 + k + ys, 4 : 4 + zs] + side[:, :, 4 - k : 4 - k + ys, 4 : 4 + zs]
        )
        total = total + COEF[k] * (
            side[:, :, 4 : 4 + ys, 4 + k : 4 + k + zs] + side[:, :, 4 : 4 + ys, 4 - k : 4 - k + zs]
        )
    return total


def laplace(field):
    width = field.shape[1]
    padded = extended(field, (("mp", 1),), 4)
    return laplace_core(padded, width)


def body(
    courant,
    aperture_first,
    source_pos,
    wavelet,
    receiver_pos,
    residual,
    step_count,
    forward_prev,
    forward_now,
    adjoint_prev,
    adjoint_now,
):
    tile_x = courant.shape[1]
    ny_cells = courant.shape[2]
    nz_cells = courant.shape[3]
    mp_size = lax.axis_size("mp")
    bit_count = mp_size.bit_length() - 1
    me_index = lax.axis_index("mp")
    first = aperture_first[0]
    owned = jnp.where(me_index < first, courant[1], courant[0])
    for bit in range(bit_count):
        moved = passed_along(owned, "mp", mp_size - (1 << bit))
        owned = jnp.where((first >> bit) % 2 == 1, moved, owned)
    steps = wavelet.shape[1]
    margin = 0
    u_prev, u_now = (forward_prev, forward_now)
    w_prev, w_now = (adjoint_prev, adjoint_now)
    width = tile_x + 2 * margin
    x_base = me_index * tile_x - margin
    x_cells = jnp.arange(width, dtype=jnp.int32) + x_base
    y_cells = jnp.arange(ny_cells, dtype=jnp.int32)
    z_cells = jnp.arange(nz_cells, dtype=jnp.int32)
    src_x = (x_cells[None, :] == source_pos[:, 0:1]).astype(jnp.float32)
    src_y = (y_cells[None, :] == source_pos[:, 1:2]).astype(jnp.float32)
    src_z = (z_cells[None, :] == source_pos[:, 2:3]).astype(jnp.float32)
    src_field = src_x[:, :, None, None] * (src_y[:, :, None] * src_z[:, None, :])[:, None, :, :]
    rec_x = (x_cells[None, None, :] == receiver_pos[:, :, 0:1]).astype(jnp.float32)
    rec_y = (y_cells[None, None, :] == receiver_pos[:, :, 1:2]).astype(jnp.float32)
    rec_z = (z_cells[None, None, :] == receiver_pos[:, :, 2:3]).astype(jnp.float32)
    rec_plane = rec_y[:, :, :, None] * rec_z[:, :, None, :]
    stored = []
    for n in range(steps):
        drive = laplace(u_now) + wavelet[:, n][:, None, None, None] * src_field
        u_next = 2.0 * u_now - u_prev + owned[None] * drive
        active = (n < step_count)[:, None, None, None]
        stored.append(jnp.where(active, drive, 0.0))
        u_prev, u_now = (jnp.where(active, u_now, u_prev), jnp.where(active, u_next, u_now))
    image = jnp.zeros((width, ny_cells, nz_cells), jnp.float32)
    for k in range(steps):
        n = steps - 1 - k
        weighted = rec_x * residual[:, n, :][:, :, None]
        inject = jnp.einsum("srx,sryz->sxyz", weighted, rec_plane, precision=lax.Precision.HIGHEST)
        w_next = 2.0 * w_now - w_prev + owned[None] * (laplace(w_now) + inject)
        active = (n < step_count)[:, None, None, None]
        image = image + jnp.sum(jnp.where(active, w_next * stored[n], 0.0), axis=0)
        w_prev, w_now = (jnp.where(active, w_now, w_prev), jnp.where(active, w_next, w_now))
    returned = image
    for bit in range(bit_count):
        moved = passed_along(returned, "mp", 1 << bit)
        returned = jnp.where((first >> bit) % 2 == 1, moved, returned)
    blank = jnp.zeros_like(returned)
    both_rows = jnp.where(
        me_index < first, jnp.stack([blank, returned]), jnp.stack([returned, blank])
    )
    return lax.psum_scatter(both_rows, "shot", scatter_dimension=2, tiled=True)


def solution(mesh):
    return jax.shard_map(
        body,
        mesh=mesh,
        in_specs=(
            P(None, "mp", None, None),
            P("shot"),
            P("shot", None),
            P("shot", None),
            P("shot", None, None),
            P("shot", None, None),
            P("shot"),
            P("shot", "mp", None, None),
            P("shot", "mp", None, None),
            P("shot", "mp", None, None),
            P("shot", "mp", None, None),
        ),
        out_specs=P(None, "mp", "shot", None),
        check_vma=False,
    )
```

profile of v0, /device:TPU:1, one launch (start us, length us, event | category | flops | bytes accessed | tf_op | source)
XLA Modules:
  0.0 554.7 jit_solution(5776535224956411188)
XLA Ops:
  13.3 13.6 %collective-permute-done = f32[16,64,256]{2,0,1:T(8,128)S(1)} collective-permute-done((f32[16,64,256]{2,0,1:T(8,128)S(1)}, f32[16,64,256]{2,0,1:T(8,128)S(1)}, u32[]{:S(2)}, u32[]{:S(2)}) %collective-permute-start) | collective-permute-done | bytes 1048608 | tf_op jit(solution)/shard_map/ppermute | solution.py:25
  27.1 10.2 %collective-permute-start.1 = (f32[16,64,256]{2,0,1:T(8,128)S(1)}, f32[16,64,256]{2,0,1:T(8,128)S(1)}, u32[]{:S(2)}, u32[]{:S(2)}) collective-permute-start(f32[16,64,256]{2,0,1:T(8,128)S(1)} %broadcast_select_fusion.5), channel_id=1, source_target_pairs={{0,30},{1,31},{2,0},{3,1},{4,2},{5,3},{6,4},{7,5},{8,6},{9,7},{10,... | collective-permute-start | bytes 3145736 | tf_op jit(solution)/shard_map/ppermute | solution.py:25
  37.3 18.6 %collective-permute-done.1 = f32[16,64,256]{2,0,1:T(8,128)S(1)} collective-permute-done((f32[16,64,256]{2,0,1:T(8,128)S(1)}, f32[16,64,256]{2,0,1:T(8,128)S(1)}, u32[]{:S(2)}, u32[]{:S(2)}) %collective-permute-start.1) | collective-permute-done | bytes 1048608 | tf_op jit(solution)/shard_map/ppermute | solution.py:25
  75.3 8.8 %collective-permute-done.2 = f32[16,64,256]{2,0,1:T(8,128)} collective-permute-done((f32[16,64,256]{2,0,1:T(8,128)}, f32[16,64,256]{2,0,1:T(8,128)}, u32[]{:S(2)}, u32[]{:S(2)}) %collective-permute-start.2) | collective-permute-done | bytes 1048608 | tf_op jit(solution)/shard_map/ppermute | solution.py:25
  98.4 21.1 %collective-permute-done.3 = f32[16,64,256]{2,0,1:T(8,128)} collective-permute-done((f32[16,64,256]{2,0,1:T(8,128)}, f32[16,64,256]{2,0,1:T(8,128)}, u32[]{:S(2)}, u32[]{:S(2)}) %collective-permute-start.3) | collective-permute-done | bytes 1048608 | tf_op jit(solution)/shard_map/ppermute | solution.py:25
  127.9 44.8 %collective-permute-done.4 = f32[16,64,256]{2,0,1:T(8,128)} collective-permute-done((f32[16,64,256]{2,0,1:T(8,128)}, f32[16,64,256]{2,0,1:T(8,128)}, u32[]{:S(2)}, u32[]{:S(2)}) %collective-permute-start.4) | collective-permute-done | bytes 1048608 | tf_op jit(solution)/shard_map/ppermute | solution.py:25
  172.8 15.7 %fusion.409 = (f32[1,16,64,256]{3,1,2,0:T(8,128)S(1)}, f32[1,16,64,256]{3,1,2,0:T(8,128)S(1)}, f32[16,64,256]{2,0,1:T(8,128)S(1)}) fusion(f32[1,16,64,256]{3,2,1,0:T(8,128)S(1)} %copy-done.1, pred[]{:T(512)} %bitcast.12, f32[1,16,64,256]{3,2,1,0:T(8,128)S(1)} %copy-done, f32[64,256]{1,0:T(8,128)S(1)} %broadcast_multiply_fusion, ...), kind=kLoop, calls=%fused_computation.604 | loop fusion | flops 13107200 | bytes 12910662 | tf_op jit(solution)/shard_map/jit(_where)/select_n | solution.py:100
  192.2 14.7 %collective-permute-start.10 = (f32[1,4,64,256]{3,1,2,0:T(4,128)S(1)}, f32[1,4,64,256]{3,1,2,0:T(4,128)S(1)}, u32[]{:S(2)}, u32[]{:S(2)}) collective-permute-start(f32[1,4,64,256]{3,1,2,0:T(4,128)S(1)} %get-tuple-element.21), channel_id=1, source_target_pairs={{0,1},{1,2},{2,3},{3,4},{4,5},{5,6},{6,7},{7,8},{8,9},{9,10},{10,1... | collective-permute-start | bytes 786440 | tf_op jit(solution)/shard_map/ppermute | solution.py:16
  207.0 9.8 %broadcast_select_fusion.3 = (f32[1,16,64,256]{3,1,2,0:T(8,128)S(1)}, f32[1,16,64,256]{3,1,2,0:T(8,128)}) fusion(pred[]{:T(512)} %bitcast.1, f32[1,16,64,256]{3,2,1,0:T(8,128)S(1)} %copy-done.5, f32[32,256]{1,0:T(8,128)S(1)} %fusion.423, f32[32,64]{0,1:T(8,128)S(1)} %fusion.422, f32[32]{0:T(128)S(1)} %copy-done.19, s32[32]{0:T(128)S(1)} %get-tuple-element.39, ...), kind=kOutput, calls=%fused_computation.624 | convolution fusion | flops 113509376 | bytes 10789185 | tf_op jit(solution)/shard_map/srx,sryz->sxyz/dot_general | solution.py:105
  218.9 5.1 collective-permute-start.16
  224.8 7.7 %fusion.411 = (f32[1,16,64,256]{3,1,2,0:T(8,128)S(1)}, f32[1,16,64,256]{3,1,2,0:T(8,128)S(1)}) fusion(f32[16,64,256]{2,0,1:T(8,128)S(1)} %get-tuple-element.11, pred[]{:T(512)} %bitcast.11, f32[1,16,64,256]{3,2,1,0:T(8,128)S(1)} %copy-done.1, pred[]{:T(512)} %bitcast.12, f32[1,16,64,256]{3,1,2,0:T(8,128)S(1)} %get-tuple-element.10, ...), kind=kLoop, calls=%fused_computation.606 | loop fusion | flops 15466496 | bytes 7929926 | tf_op jit(solution)/shard_map/jit(_where)/select_n | solution.py:100
  234.5 5.1 collective-permute-start.12
  239.7 6.3 %broadcast_select_fusion.1 = (f32[1,16,64,256]{3,1,2,0:T(8,128)S(1)}, f32[1,16,64,256]{3,1,2,0:T(8,128)}) fusion(f32[1,16,64,256]{3,1,2,0:T(8,128)S(1)} %copy-done.10, pred[]{:T(512)} %bitcast.10, f32[32,256]{1,0:T(8,128)S(1)} %fusion.423, f32[32,64]{0,1:T(8,128)S(1)} %fusion.422, f32[32]{0:T(128)S(1)} %copy-done.18, s32[32]{0:T(128)S(1)} %get-tuple-element.39, ...), kind=kOutput, calls=%fused_computation.622 | convolution fusion | flops 114557952 | bytes 5808449 | tf_op jit(solution)/shard_map/srx,sryz->sxyz/dot_general | solution.py:105
  248.9 5.1 collective-permute-start.18
  254.8 7.6 %fusion.413 = (f32[1,16,64,256]{3,1,2,0:T(8,128)S(1)}, f32[1,16,64,256]{3,1,2,0:T(8,128)S(1)}) fusion(f32[16,64,256]{2,0,1:T(8,128)S(1)} %get-tuple-element.11, f32[1,16,64,256]{3,1,2,0:T(8,128)S(1)} %get-tuple-element.8, pred[]{:T(512)} %bitcast.11, pred[]{:T(512)} %bitcast.10, f32[1,16,64,256]{3,2,1,0:T(8,128)S(1)} %copy-done.1, pred[]{:T(512)} %bitcast.12, ...), kind=kLoop, calls=%fused_computation.608 | loop fusion | flops 17039360 | bytes 8978503 | tf_op jit(solution)/shard_map/jit(_where)/select_n | solution.py:100
  269.6 17.4 %broadcast_select_fusion = (f32[1,16,64,256]{3,1,2,0:T(8,128)S(1)}, f32[1,16,64,256]{3,1,2,0:T(8,128)}) fusion(f32[1,16,64,256]{3,1,2,0:T(8,128)} %copy-done.12, pred[]{:T(512)} %bitcast.11, f32[32,256]{1,0:T(8,128)S(1)} %fusion.423, f32[32,64]{0,1:T(8,128)S(1)} %fusion.422, f32[32]{0:T(128)S(1)} %get-tuple-element.38, s32[32]{0:T(128)S(1)} %get-tuple-element.39, ...), kind=kOutput, calls=%fused_computation.621 | convolution fusion | flops 114820096 | bytes 6857026 | tf_op jit(solution)/shard_map/srx,sryz->sxyz/dot_general | solution.py:105
  301.0 11.8 %fusion.38 = f32[16,64,256]{2,0,1:T(8,128)S(1)} fusion(f32[1,16,64,256]{3,1,2,0:T(8,128)S(1)} %get-tuple-element.53, f32[1,16,64,256]{3,1,2,0:T(8,128)} %get-tuple-element.50, f32[1,16,64,256]{3,1,2,0:T(8,128)S(1)} %get-tuple-element.5, f32[1,4,64,256]{3,1,2,0:T(4,128)} %copy-done.22, f32[1,4,64,256]{3,1,2,0:T(4,128)} %copy-done.21, ...), kind=kOutput, calls=%fused_computation.235 | convolution fusion | flops 131335168 | bytes 14786952 | tf_op jit(solution)/shard_map/srx,sryz->sxyz/dot_general | solution.py:105
  317.1 11.7 %collective-permute-done.21 = f32[16,64,256]{2,0,1:T(8,128)S(1)} collective-permute-done((f32[16,64,256]{2,0,1:T(8,128)S(1)}, f32[16,64,256]{2,0,1:T(8,128)S(1)}, u32[]{:S(2)}, u32[]{:S(2)}) %collective-permute-start.21) | collective-permute-done | bytes 1048608 | tf_op jit(solution)/shard_map/ppermute | solution.py:25
  331.8 22.5 %collective-permute-done.22 = f32[16,64,256]{2,0,1:T(8,128)S(1)} collective-permute-done((f32[16,64,256]{2,0,1:T(8,128)S(1)}, f32[16,64,256]{2,0,1:T(8,128)S(1)}, u32[]{:S(2)}, u32[]{:S(2)}) %collective-permute-start.22) | collective-permute-done | bytes 1048608 | tf_op jit(solution)/shard_map/ppermute | solution.py:25
  354.6 21.9 %collective-permute-done.23 = f32[16,64,256]{2,0,1:T(8,128)S(1)} collective-permute-done((f32[16,64,256]{2,0,1:T(8,128)S(1)}, f32[16,64,256]{2,0,1:T(8,128)S(1)}, u32[]{:S(2)}, u32[]{:S(2)}) %collective-permute-start.23) | collective-permute-done | bytes 1048608 | tf_op jit(solution)/shard_map/ppermute | solution.py:25
  376.8 12.3 %collective-permute-start.24 = (f32[16,64,256]{2,0,1:T(8,128)S(1)}, f32[16,64,256]{2,0,1:T(8,128)S(1)}, u32[]{:S(2)}, u32[]{:S(2)}) collective-permute-start(f32[16,64,256]{2,0,1:T(8,128)S(1)} %broadcast_select_fusion.8), channel_id=1, source_target_pairs={{0,8},{1,9},{2,10},{3,11},{4,12},{5,13},{6,14},{7,15},{8,16},{9,17... | collective-permute-start | bytes 3145736 | tf_op jit(solution)/shard_map/ppermute | solution.py:25
  389.1 42.5 %collective-permute-done.24 = f32[16,64,256]{2,0,1:T(8,128)S(1)} collective-permute-done((f32[16,64,256]{2,0,1:T(8,128)S(1)}, f32[16,64,256]{2,0,1:T(8,128)S(1)}, u32[]{:S(2)}, u32[]{:S(2)}) %collective-permute-start.24) | collective-permute-done | bytes 1048608 | tf_op jit(solution)/shard_map/ppermute | solution.py:25
  431.9 27.9 %collective-permute-done.25 = f32[16,64,256]{2,0,1:T(8,128)S(1)} collective-permute-done((f32[16,64,256]{2,0,1:T(8,128)S(1)}, f32[16,64,256]{2,0,1:T(8,128)S(1)}, u32[]{:S(2)}, u32[]{:S(2)}) %collective-permute-start.25) | collective-permute-done | bytes 1048608 | tf_op jit(solution)/shard_map/ppermute | solution.py:25
  463.2 84.7 %reduce-scatter.5.cloned.1.call-done = f32[8,8192]{1,0:T(8,128)} async-done(((f32[64,8192]{1,0:T(8,128)}), f32[8,8192]{1,0:T(8,128)}) %reduce-scatter.5.cloned.1.call-update) | async-done | bytes 262160
  (125 shorter events, 92.2 us)
Async XLA Ops:
  6.5 541.3 %reduce-scatter.5.cloned.1.call-start = ((), (), s32[]{:S(2)}) async-start(), calls=%async_computation.1 | async-start | bytes 2359296
  10.1 16.9 %collective-permute-start = (f32[16,64,256]{2,0,1:T(8,128)S(1)}, f32[16,64,256]{2,0,1:T(8,128)S(1)}, u32[]{:S(2)}, u32[]{:S(2)}) collective-permute-start(f32[16,64,256]{2,0,1:T(8,128)S(1)} %fusion.407), channel_id=1, source_target_pairs={{0,31},{1,0},{2,1},{3,2},{4,3},{5,4},{6,5},{7,6},{8,7},{9,8},{10,9... | collective-permute-start | bytes 3145736 | tf_op jit(solution)/shard_map/ppermute | solution.py:25
  27.1 28.8 %collective-permute-start.1 = (f32[16,64,256]{2,0,1:T(8,128)S(1)}, f32[16,64,256]{2,0,1:T(8,128)S(1)}, u32[]{:S(2)}, u32[]{:S(2)}) collective-permute-start(f32[16,64,256]{2,0,1:T(8,128)S(1)} %broadcast_select_fusion.5), channel_id=1, source_target_pairs={{0,30},{1,31},{2,0},{3,1},{4,2},{5,3},{6,4},{7,5},{8,6},{9,7},{10,... | collective-permute-start | bytes 3145736 | tf_op jit(solution)/shard_map/ppermute | solution.py:25
  57.1 27.0 %collective-permute-start.2 = (f32[16,64,256]{2,0,1:T(8,128)}, f32[16,64,256]{2,0,1:T(8,128)}, u32[]{:S(2)}, u32[]{:S(2)}) collective-permute-start(f32[16,64,256]{2,0,1:T(8,128)} %broadcast_select_fusion.7), channel_id=1, source_target_pairs={{0,28},{1,29},{2,30},{3,31},{4,0},{5,1},{6,2},{7,3},{8,4},{9,5},{1... | collective-permute-start | bytes 3145736 | tf_op jit(solution)/shard_map/ppermute | solution.py:25
  63.5 63.5 %collective-permute-start.7 = (f32[1,4,64,256]{3,1,2,0:T(4,128)}, f32[1,4,64,256]{3,1,2,0:T(4,128)S(1)}, u32[]{:S(2)}, u32[]{:S(2)}) collective-permute-start(f32[1,4,64,256]{3,1,2,0:T(4,128)} %get-tuple-element.29), channel_id=1, source_target_pairs={{1,0},{2,1},{3,2},{4,3},{5,4},{6,5},{7,6},{8,7},{9,8},{10,9},{11,1... | collective-permute-start | bytes 786440 | tf_op jit(solution)/shard_map/ppermute | solution.py:17
  65.4 62.5 %collective-permute-start.8 = (f32[1,4,64,256]{3,1,2,0:T(4,128)}, f32[1,4,64,256]{3,1,2,0:T(4,128)S(1)}, u32[]{:S(2)}, u32[]{:S(2)}) collective-permute-start(f32[1,4,64,256]{3,1,2,0:T(4,128)} %get-tuple-element.30), channel_id=1, source_target_pairs={{0,1},{1,2},{2,3},{3,4},{4,5},{5,6},{6,7},{7,8},{8,9},{9,10},{10,1... | collective-permute-start | bytes 786440 | tf_op jit(solution)/shard_map/ppermute | solution.py:16
  86.5 33.0 %collective-permute-start.3 = (f32[16,64,256]{2,0,1:T(8,128)}, f32[16,64,256]{2,0,1:T(8,128)}, u32[]{:S(2)}, u32[]{:S(2)}) collective-permute-start(f32[16,64,256]{2,0,1:T(8,128)} %broadcast_select_fusion.9), channel_id=1, source_target_pairs={{0,24},{1,25},{2,26},{3,27},{4,28},{5,29},{6,30},{7,31},{8,0},{9,1... | collective-permute-start | bytes 3145736 | tf_op jit(solution)/shard_map/ppermute | solution.py:25
  89.6 37.5 %collective-permute-start.5 = (f32[1,4,64,256]{3,1,2,0:T(4,128)}, f32[1,4,64,256]{3,1,2,0:T(4,128)S(1)}, u32[]{:S(2)}, u32[]{:S(2)}) collective-permute-start(f32[1,4,64,256]{3,1,2,0:T(4,128)} %get-tuple-element.33), channel_id=1, source_target_pairs={{1,0},{2,1},{3,2},{4,3},{5,4},{6,5},{7,6},{8,7},{9,8},{10,9},{11,1... | collective-permute-start | bytes 786440 | tf_op jit(solution)/shard_map/ppermute | solution.py:17
  93.0 114.0 %collective-permute-start.6 = (f32[1,4,64,256]{3,1,2,0:T(4,128)}, f32[1,4,64,256]{3,1,2,0:T(4,128)}, u32[]{:S(2)}, u32[]{:S(2)}) collective-permute-start(f32[1,4,64,256]{3,1,2,0:T(4,128)} %get-tuple-element.34), channel_id=1, source_target_pairs={{0,1},{1,2},{2,3},{3,4},{4,5},{5,6},{6,7},{7,8},{8,9},{9,10},{10,1... | collective-permute-start | bytes 786440 | tf_op jit(solution)/shard_map/ppermute | solution.py:16
  121.9 50.8 %collective-permute-start.4 = (f32[16,64,256]{2,0,1:T(8,128)}, f32[16,64,256]{2,0,1:T(8,128)}, u32[]{:S(2)}, u32[]{:S(2)}) collective-permute-start(f32[16,64,256]{2,0,1:T(8,128)} %broadcast_select_fusion.11), channel_id=1, source_target_pairs={{0,16},{1,17},{2,18},{3,19},{4,20},{5,21},{6,22},{7,23},{8,24},{9,... | collective-permute-start | bytes 3145736 | tf_op jit(solution)/shard_map/ppermute | solution.py:25
  188.6 35.4 %collective-permute-start.9 = (f32[1,4,64,256]{3,1,2,0:T(4,128)S(1)}, f32[1,4,64,256]{3,1,2,0:T(4,128)S(1)}, u32[]{:S(2)}, u32[]{:S(2)}) collective-permute-start(f32[1,4,64,256]{3,1,2,0:T(4,128)S(1)} %get-tuple-element.20), channel_id=1, source_target_pairs={{1,0},{2,1},{3,2},{4,3},{5,4},{6,5},{7,6},{8,7},{9,8},{10,9},{11,1... | collective-permute-start | bytes 786440 | tf_op jit(solution)/shard_map/ppermute | solution.py:17
  192.2 31.8 %collective-permute-start.10 = (f32[1,4,64,256]{3,1,2,0:T(4,128)S(1)}, f32[1,4,64,256]{3,1,2,0:T(4,128)S(1)}, u32[]{:S(2)}, u32[]{:S(2)}) collective-permute-start(f32[1,4,64,256]{3,1,2,0:T(4,128)S(1)} %get-tuple-element.21), channel_id=1, source_target_pairs={{0,1},{1,2},{2,3},{3,4},{4,5},{5,6},{6,7},{7,8},{8,9},{9,10},{10,1... | collective-permute-start | bytes 786440 | tf_op jit(solution)/shard_map/ppermute | solution.py:16
  216.9 22.7 %collective-permute-start.15 = (f32[1,4,64,256]{3,1,2,0:T(4,128)S(1)}, f32[1,4,64,256]{3,1,2,0:T(4,128)S(1)}, u32[]{:S(2)}, u32[]{:S(2)}) collective-permute-start(f32[1,4,64,256]{3,1,2,0:T(4,128)S(1)} %get-tuple-element.27), channel_id=1, source_target_pairs={{1,0},{2,1},{3,2},{4,3},{5,4},{6,5},{7,6},{8,7},{9,8},{10,9},{11,1... | collective-permute-start | bytes 786440 | tf_op jit(solution)/shard_map/ppermute | solution.py:17
  218.9 20.8 %collective-permute-start.16 = (f32[1,4,64,256]{3,1,2,0:T(4,128)S(1)}, f32[1,4,64,256]{3,1,2,0:T(4,128)}, u32[]{:S(2)}, u32[]{:S(2)}) collective-permute-start(f32[1,4,64,256]{3,1,2,0:T(4,128)S(1)} %get-tuple-element.28), channel_id=1, source_target_pairs={{0,1},{1,2},{2,3},{3,4},{4,5},{5,6},{6,7},{7,8},{8,9},{9,10},{10,1... | collective-permute-start | bytes 786440 | tf_op jit(solution)/shard_map/ppermute | solution.py:16
  232.6 21.5 %collective-permute-start.11 = (f32[1,4,64,256]{3,1,2,0:T(4,128)S(1)}, f32[1,4,64,256]{3,1,2,0:T(4,128)S(1)}, u32[]{:S(2)}, u32[]{:S(2)}) collective-permute-start(f32[1,4,64,256]{3,1,2,0:T(4,128)S(1)} %get-tuple-element.18), channel_id=1, source_target_pairs={{1,0},{2,1},{3,2},{4,3},{5,4},{6,5},{7,6},{8,7},{9,8},{10,9},{11,1... | collective-permute-start | bytes 786440 | tf_op jit(solution)/shard_map/ppermute | solution.py:17
  234.5 19.6 %collective-permute-start.12 = (f32[1,4,64,256]{3,1,2,0:T(4,128)S(1)}, f32[1,4,64,256]{3,1,2,0:T(4,128)S(1)}, u32[]{:S(2)}, u32[]{:S(2)}) collective-permute-start(f32[1,4,64,256]{3,1,2,0:T(4,128)S(1)} %get-tuple-element.19), channel_id=1, source_target_pairs={{0,1},{1,2},{2,3},{3,4},{4,5},{5,6},{6,7},{7,8},{8,9},{9,10},{10,1... | collective-permute-start | bytes 786440 | tf_op jit(solution)/shard_map/ppermute | solution.py:16
  247.0 22.6 %collective-permute-start.17 = (f32[1,4,64,256]{3,1,2,0:T(4,128)}, f32[1,4,64,256]{3,1,2,0:T(4,128)}, u32[]{:S(2)}, u32[]{:S(2)}) collective-permute-start(f32[1,4,64,256]{3,1,2,0:T(4,128)} %get-tuple-element.22), channel_id=1, source_target_pairs={{1,0},{2,1},{3,2},{4,3},{5,4},{6,5},{7,6},{8,7},{9,8},{10,9},{11,1... | collective-permute-start | bytes 786440 | tf_op jit(solution)/shard_map/ppermute | solution.py:17
  248.9 20.7 %collective-permute-start.18 = (f32[1,4,64,256]{3,1,2,0:T(4,128)}, f32[1,4,64,256]{3,1,2,0:T(4,128)}, u32[]{:S(2)}, u32[]{:S(2)}) collective-permute-start(f32[1,4,64,256]{3,1,2,0:T(4,128)} %get-tuple-element.23), channel_id=1, source_target_pairs={{0,1},{1,2},{2,3},{3,4},{4,5},{5,6},{6,7},{7,8},{8,9},{9,10},{10,1... | collective-permute-start | bytes 786440 | tf_op jit(solution)/shard_map/ppermute | solution.py:16
  262.5 31.7 %collective-permute-start.13 = (f32[1,4,64,256]{3,1,2,0:T(4,128)S(1)}, f32[1,4,64,256]{3,1,2,0:T(4,128)S(1)}, u32[]{:S(2)}, u32[]{:S(2)}) collective-permute-start(f32[1,4,64,256]{3,1,2,0:T(4,128)S(1)} %get-tuple-element.14), channel_id=1, source_target_pairs={{1,0},{2,1},{3,2},{4,3},{5,4},{6,5},{7,6},{8,7},{9,8},{10,9},{11,1... | collective-permute-start | bytes 786440 | tf_op jit(solution)/shard_map/ppermute | solution.py:17
  264.4 29.8 %collective-permute-start.14 = (f32[1,4,64,256]{3,1,2,0:T(4,128)S(1)}, f32[1,4,64,256]{3,1,2,0:T(4,128)S(1)}, u32[]{:S(2)}, u32[]{:S(2)}) collective-permute-start(f32[1,4,64,256]{3,1,2,0:T(4,128)S(1)} %get-tuple-element.15), channel_id=1, source_target_pairs={{0,1},{1,2},{2,3},{3,4},{4,5},{5,6},{6,7},{7,8},{8,9},{9,10},{10,1... | collective-permute-start | bytes 786440 | tf_op jit(solution)/shard_map/ppermute | solution.py:16
  329.1 25.3 %collective-permute-start.22 = (f32[16,64,256]{2,0,1:T(8,128)S(1)}, f32[16,64,256]{2,0,1:T(8,128)S(1)}, u32[]{:S(2)}, u32[]{:S(2)}) collective-permute-start(f32[16,64,256]{2,0,1:T(8,128)S(1)} %broadcast_select_fusion.4), channel_id=1, source_target_pairs={{0,2},{1,3},{2,4},{3,5},{4,6},{5,7},{6,8},{7,9},{8,10},{9,11},{10,... | collective-permute-start | bytes 3145736 | tf_op jit(solution)/shard_map/ppermute | solution.py:25
  354.6 22.0 %collective-permute-start.23 = (f32[16,64,256]{2,0,1:T(8,128)S(1)}, f32[16,64,256]{2,0,1:T(8,128)S(1)}, u32[]{:S(2)}, u32[]{:S(2)}) collective-permute-start(f32[16,64,256]{2,0,1:T(8,128)S(1)} %broadcast_select_fusion.6), channel_id=1, source_target_pairs={{0,4},{1,5},{2,6},{3,7},{4,8},{5,9},{6,10},{7,11},{8,12},{9,13},{1... | collective-permute-start | bytes 3145736 | tf_op jit(solution)/shard_map/ppermute | solution.py:25
  376.8 54.8 %collective-permute-start.24 = (f32[16,64,256]{2,0,1:T(8,128)S(1)}, f32[16,64,256]{2,0,1:T(8,128)S(1)}, u32[]{:S(2)}, u32[]{:S(2)}) collective-permute-start(f32[16,64,256]{2,0,1:T(8,128)S(1)} %broadcast_select_fusion.8), channel_id=1, source_target_pairs={{0,8},{1,9},{2,10},{3,11},{4,12},{5,13},{6,14},{7,15},{8,16},{9,17... | collective-permute-start | bytes 3145736 | tf_op jit(solution)/shard_map/ppermute | solution.py:25
  431.8 28.0 %collective-permute-start.25 = (f32[16,64,256]{2,0,1:T(8,128)S(1)}, f32[16,64,256]{2,0,1:T(8,128)S(1)}, u32[]{:S(2)}, u32[]{:S(2)}) collective-permute-start(f32[16,64,256]{2,0,1:T(8,128)S(1)} %broadcast_select_fusion.10), channel_id=1, source_target_pairs={{0,16},{1,17},{2,18},{3,19},{4,20},{5,21},{6,22},{7,23},{8,24},{9,... | collective-permute-start | bytes 3145736 | tf_op jit(solution)/shard_map/ppermute | solution.py:25
  (28 other events, 516.6 us)
Sparse Core Ops, SparseCore 0:
  463.3 84.5 reduce-scatter.4
where the time goes:
time: 560 us; the launch traced here: 555 us
  waiting for transfers between devices  324 us (58%)
  starting transfers between devices  109 us (19%)
  other arithmetic  46.2 us (8%)
  matrix products  45.3 us (8%)
  between operations  15.4 us (3%)
  local copies, waits for them, and re-layouts  14.2 us (3%)
    ppermute x10, waiting for transfers between devices, passed_along(): return lax.ppermute(value, axis, pairs)  233 us
    unnamed x2, waiting for transfers between devices  84.7 us
    ppermute x8, starting transfers between devices, extended(): before = lax.ppermute(last, axis, up)  49.2 us
    dot_general x4, matrix products, body(): jnp.einsum('srx,sryz->sxyz', weighted, rec_plane, precision=lax.Precision...  45.3 us
    ppermute x10, starting transfers between devices, passed_along(): return lax.ppermute(value, axis, pairs)  41.5 us
    select_n x3, other arithmetic, body(): jnp.where(active, u_next, u_now)  31 us
    ppermute x8, starting transfers between devices, extended(): after = lax.ppermute(leading, axis, down)  18.6 us
  transfers between devices with their start and end apart: 27, of which 13 were waited for; matrix products, arithmetic and copies ran while one was open for 15% of the time, Pallas kernels for 0%

commit v1 on v0

v1 whole, which is shorter than its diff:
```python
import jax
import jax.numpy as jnp
from jax import lax
from jax.sharding import Mesh, PartitionSpec as P

COEF = (-205.0 / 72.0, 1.6, -0.2, 8.0 / 315.0, -1.0 / 560.0)
QUAD = 4
MP = ("zz", "quad")
PLANE = ("shot", "quad")


def shifted(value, axes, steps, wrap=False):
    count = lax.axis_size(axes)
    pairs = [(i, (i + steps) % count) for i in range(count) if wrap or 0 <= i + steps < count]
    return lax.ppermute(value, axes, pairs)


def all_first(first):
    shots = lax.axis_size("shot")
    me = lax.axis_index("shot")
    known = jnp.where(jnp.arange(shots, dtype=jnp.int32) == me, first, 0)
    step = 1
    while step < shots:
        known = known + lax.ppermute(known, "shot", [(i, i ^ step) for i in range(shots)])
        step *= 2
    return known


def quad_exchange(parts, axis):
    return lax.all_to_all(parts, "quad", split_axis=axis, concat_axis=axis, tiled=True)


def fetch_model(courant, firsts):
    rows, tile_x, ny, nz = courant.shape
    shots = lax.axis_size("shot")
    zs = lax.axis_size("zz")
    slab = ny // shots
    planes = tile_x // QUAD
    me_shot = lax.axis_index("shot")
    me_z = lax.axis_index("zz")
    mine = lax.dynamic_slice_in_dim(courant, me_shot * slab, slab, 2)
    block = quad_exchange(mine, 1).reshape(rows, QUAD, planes, slab, nz)
    line = [block[0]]
    for j in range(1, zs):
        line.append(shifted(jnp.where(me_z >= j, block[0], block[1]), "zz", -j, wrap=True))
    line.append(block[1])
    line = jnp.concatenate(line, axis=0)
    sent = [lax.dynamic_slice_in_dim(line, firsts[s], QUAD, 0) for s in range(shots)]
    sent = jnp.concatenate(sent, axis=0)
    got = lax.all_to_all(sent, PLANE, split_axis=0, concat_axis=0, tiled=True)
    got = got.reshape(shots, QUAD * planes, slab, nz)
    return got.transpose(1, 0, 2, 3).reshape(tile_x, ny, nz)


def return_image(image, firsts):
    tile_x, ny, nz = image.shape
    shots = lax.axis_size("shot")
    zs = lax.axis_size("zz")
    slab = ny // shots
    planes = tile_x // QUAD
    me_z = lax.axis_index("zz")
    sent = image.reshape(QUAD, planes, shots, slab, nz).transpose(2, 0, 1, 3, 4)
    sent = sent.reshape(shots * QUAD, planes, slab, nz)
    got = lax.all_to_all(sent, PLANE, split_axis=0, concat_axis=0, tiled=True)
    got = got.reshape(shots, QUAD, planes, slab, nz)
    line = jnp.zeros(((zs + 1) * QUAD, planes, slab, nz), jnp.float32)
    for s in range(shots):
        old = lax.dynamic_slice_in_dim(line, firsts[s], QUAD, 0)
        line = lax.dynamic_update_slice_in_dim(line, old + got[s], firsts[s], 0)
    line = line.reshape(zs + 1, QUAD, planes, slab, nz)
    low, high = line[0], line[zs]
    for j in range(1, zs):
        came = shifted(line[j], "zz", j, wrap=True)
        low = low + jnp.where(me_z >= j, came, 0.0)
        high = high + jnp.where(me_z >= j, 0.0, came)
    both = jnp.stack([low, high]).reshape(2, tile_x, slab, nz)
    return quad_exchange(both, 1)


def laplace_core(padded, width):
    ys = padded.shape[1]
    zs = padded.shape[2]
    centre = padded[4 : 4 + width]
    side = jnp.pad(centre, ((0, 0), (4, 4), (4, 4)))
    total = 3.0 * COEF[0] * centre
    for k in range(1, 5):
        total = total + COEF[k] * (padded[4 + k : 4 + k + width] + padded[4 - k : 4 - k + width])
        total = total + COEF[k] * (
            side[:, 4 + k : 4 + k + ys, 4 : 4 + zs] + side[:, 4 - k : 4 - k + ys, 4 : 4 + zs]
        )
        total = total + COEF[k] * (
            side[:, 4 : 4 + ys, 4 + k : 4 + k + zs] + side[:, 4 : 4 + ys, 4 - k : 4 - k + zs]
        )
    return total


def body(
    courant,
    aperture_first,
    source_pos,
    wavelet,
    receiver_pos,
    residual,
    step_count,
    forward_prev,
    forward_now,
    adjoint_prev,
    adjoint_now,
):
    tile_x = courant.shape[1]
    ny_cells = courant.shape[2]
    nz_cells = courant.shape[3]
    me_index = lax.axis_index(MP)
    firsts = all_first(aperture_first[0])
    owned = fetch_model(courant, firsts)
    steps = wavelet.shape[1]
    count = step_count[0]
    u_prev, u_now = (forward_prev[0], forward_now[0])
    w_prev, w_now = (adjoint_prev[0], adjoint_now[0])
    x_cells = jnp.arange(tile_x, dtype=jnp.int32) + me_index * tile_x
    y_cells = jnp.arange(ny_cells, dtype=jnp.int32)
    z_cells = jnp.arange(nz_cells, dtype=jnp.int32)
    src_x = (x_cells == source_pos[0, 0]).astype(jnp.float32)
    src_y = (y_cells == source_pos[0, 1]).astype(jnp.float32)
    src_z = (z_cells == source_pos[0, 2]).astype(jnp.float32)
    src_field = src_x[:, None, None] * (src_y[:, None] * src_z[None, :])[None]
    rec = receiver_pos[0]
    rec_x = (x_cells[None, :] == rec[:, 0:1]).astype(jnp.float32)
    rec_y = (y_cells[None, :] == rec[:, 1:2]).astype(jnp.float32)
    rec_z = (z_cells[None, :] == rec[:, 2:3]).astype(jnp.float32)
    rec_plane = rec_y[:, :, None] * rec_z[:, None, :]
    drives = []
    image = jnp.zeros((tile_x, ny_cells, nz_cells), jnp.float32)
    adjoint = []
    for n in range(steps):
        k = steps - 1 - n
        before = shifted(jnp.concatenate([u_now[-4:], w_now[-4:]]), MP, 1)
        after = shifted(jnp.concatenate([u_now[:4], w_now[:4]]), MP, -1)
        lap_u = laplace_core(jnp.concatenate([before[:4], u_now, after[:4]]), tile_x)
        lap_w = laplace_core(jnp.concatenate([before[4:], w_now, after[4:]]), tile_x)
        drive = lap_u + wavelet[0, n] * src_field
        u_next = 2.0 * u_now - u_prev + owned * drive
        drives.append(jnp.where(n < count, drive, 0.0))
        u_prev, u_now = jnp.where(n < count, u_now, u_prev), jnp.where(n < count, u_next, u_now)
        weighted = rec_x * residual[0, k][:, None]
        inject = jnp.einsum("rx,ryz->xyz", weighted, rec_plane, precision=lax.Precision.HIGHEST)
        w_next = 2.0 * w_now - w_prev + owned * (lap_w + inject)
        adjoint.append(w_next)
        w_prev, w_now = jnp.where(k < count, w_now, w_prev), jnp.where(k < count, w_next, w_now)
    for k in range(steps):
        n = steps - 1 - k
        image = image + jnp.where(n < count, adjoint[k] * drives[n], 0.0)
    return return_image(image, firsts)


def solution(mesh):
    shots, mp = mesh.devices.shape
    fine = Mesh(mesh.devices.reshape(shots, mp // QUAD, QUAD), ("shot", "zz", "quad"))
    return jax.shard_map(
        body,
        mesh=fine,
        in_specs=(
            P(None, MP, None, None),
            P("shot"),
            P("shot", None),
            P("shot", None),
            P("shot", None, None),
            P("shot", None, None),
            P("shot"),
            P("shot", MP, None, None),
            P("shot", MP, None, None),
            P("shot", MP, None, None),
            P("shot", MP, None, None),
        ),
        out_specs=P(None, MP, "shot", None),
        check_vma=False,
    )
```

time: 560 us -> 329 us (0.59)
  waiting for transfers between devices: 324 us -> 61.7 us
  blocking collectives: 0 us -> 34.4 us
  local copies, waits for them, and re-layouts: 14.2 us -> 40.9 us
  starting transfers between devices: 109 us -> 86.8 us
  other arithmetic: 46.2 us -> 30.1 us
  matrix products: 45.3 us -> 57 us
    ppermute x26 -> x25, waiting for transfers between devices: 240 us -> 50.2 us  [the longest x22 48.1 us: shifted(): return lax.ppermute(value, axes, pairs)]
    unnamed x2 -> x0, waiting for transfers between devices: 84.7 us -> none
    ppermute x26 -> x25, starting transfers between devices: 109 us -> 70.3 us  [the longest x22 66.7 us: shifted(): return lax.ppermute(value, axes, pairs)]
    all_to_all x0 -> x2, blocking collectives: none -> 34.4 us  [the longest x1 24 us: return_image(): got = lax.all_to_all(sent, PLANE, split_axis=0, concat_axis=0, tiled=True)]
    select_n x14 -> x5, other arithmetic: 43.6 us -> 22.9 us  [the longest x3 21.9 us: body(): jnp.where(n < count, u_next, u_now)]
    all_to_all x0 -> x2, starting transfers between devices: none -> 16.5 us  [the longest x1 9.97 us: fetch_model(): got = lax.all_to_all(sent, PLANE, split_axis=0, concat_axis=0, tiled=True)]
    unnamed x53 -> x62, local copies, waits for them, and re-layouts: 6.53 us -> 20.5 us
    dot_general x4, matrix products: 45.3 us -> 57 us  [body(): jnp.einsum('rx,ryz->xyz', weighted, rec_plane, precision=lax.Precision.HI...]
  transfers between devices with their start and end apart: 27 -> 27, of which waited for: 13 -> 15; matrix products, arithmetic and copies ran while one was open for 15% -> 11% of each run, Pallas kernels for 0% -> 0%
where the time goes in v1:
time: 329 us; the launch traced here: 328 us
  starting transfers between devices  86.8 us (26%)
  waiting for transfers between devices  61.7 us (19%)
  matrix products  57 us (17%)
  local copies, waits for them, and re-layouts  40.9 us (12%)
  blocking collectives  34.4 us (10%)
  other arithmetic  30.1 us (9%)
  between operations  17.2 us (5%)
    ppermute x22, starting transfers between devices, shifted(): return lax.ppermute(value, axes, pairs)  66.7 us
    dot_general x4, matrix products, body(): jnp.einsum('rx,ryz->xyz', weighted, rec_plane, precision=lax.Precision.HI...  57 us
    ppermute x22, waiting for transfers between devices, shifted(): return lax.ppermute(value, axes, pairs)  48.1 us
    all_to_all x1, blocking collectives, return_image(): got = lax.all_to_all(sent, PLANE, split_axis=0, concat_axis=0, tiled=True)  24 us
    select_n x3, other arithmetic, body(): jnp.where(n < count, u_next, u_now)  21.9 us
    unnamed x62, local copies, waits for them, and re-layouts  20.5 us
    all_to_all x1, waiting for transfers between devices, fetch_model(): got = lax.all_to_all(sent, PLANE, split_axis=0, concat_axis=0, tiled=True)  11.5 us
    all_to_all x1, blocking collectives, quad_exchange(): lax.all_to_all(parts, 'quad', split_axis=axis, concat_axis=axis, tiled=True)  10.4 us
  transfers between devices with their start and end apart: 27, of which 15 were waited for; matrix products, arithmetic and copies ran while one was open for 11% of the time, Pallas kernels for 0%

profile of v1, /device:TPU:1, one launch (start us, length us, event | category | flops | bytes accessed | tf_op | source)
XLA Modules:
  0.0 328.1 jit_solution(13304427652702177527)
XLA Ops:
  2.3 6.6 %all-to-all-start = ((f32[2,16,8,256]{3,2,0,1:T(8,128)}), f32[2,16,8,256]{3,2,0,1:T(8,128)S(1)}, u32[]{:S(2)}, u32[]{:S(2)}) async-start(f32[2,16,8,256]{3,2,0,1:T(8,128)} %copy.45), calls=%async_computation | async-start | bytes 524288 | tf_op jit(solution)/shard_map/all_to_all | solution.py:30
  16.0 5.0 %collective-permute-start.11 = (f32[8,64,256]{2,0,1:T(8,128)}, f32[8,64,256]{2,0,1:T(8,128)}, u32[]{:S(2)}, u32[]{:S(2)}) collective-permute-start(f32[8,64,256]{2,0,1:T(8,128)} %pad_maximum_fusion.17), channel_id=1, source_target_pairs={{0,1},{1,2},{2,3},{3,4},{4,5},{5,6},{6,7},{7,8},{8,9},{9,10},{10,1... | collective-permute-start | bytes 1572872 | tf_op jit(solution)/shard_map/ppermute | solution.py:15
  30.1 5.6 %collective-permute-start = (f32[4,4,8,256]{3,2,1,0:T(8,128)}, f32[4,4,8,256]{3,2,1,0:T(8,128)S(1)}, u32[]{:S(2)}, u32[]{:S(2)}) collective-permute-start(f32[4,4,8,256]{3,2,1,0:T(8,128)} %get-tuple-element.64), channel_id=1, source_target_pairs={{0,28},{4,0},{8,4},{12,8},{16,12},{20,16},{24,20},{28,24},{1,29},{... | collective-permute-start | bytes 393224 | tf_op jit(solution)/shard_map/ppermute | solution.py:15
  67.7 5.3 %collective-permute-start.6 = (f32[4,4,8,256]{3,2,1,0:T(8,128)}, f32[4,4,8,256]{3,2,1,0:T(8,128)S(1)}, u32[]{:S(2)}, u32[]{:S(2)}) collective-permute-start(f32[4,4,8,256]{3,2,1,0:T(8,128)} %get-tuple-element.58), channel_id=1, source_target_pairs={{0,4},{4,8},{8,12},{12,16},{16,20},{20,24},{24,28},{28,0},{1,5},{5... | collective-permute-start | bytes 393224 | tf_op jit(solution)/shard_map/ppermute | solution.py:15
  74.3 6.8 %collective-permute-done.5 = f32[4,4,8,256]{3,2,1,0:T(8,128)S(1)} collective-permute-done((f32[4,4,8,256]{3,2,1,0:T(8,128)}, f32[4,4,8,256]{3,2,1,0:T(8,128)S(1)}, u32[]{:S(2)}, u32[]{:S(2)}) %collective-permute-start.5) | collective-permute-done | bytes 131104 | tf_op jit(solution)/shard_map/ppermute | solution.py:15
  97.3 10.0 %all-to-all-start.1 = ((f32[32,4,8,256]{3,2,1,0:T(8,128)}), f32[32,4,8,256]{3,2,1,0:T(8,128)}, u32[]{:S(2)}, u32[]{:S(2)}) async-start(f32[32,4,8,256]{3,2,1,0:T(8,128)} %dynamic-slice_dynamic-update-slice_fusion), calls=%async_computation.1 | async-start | bytes 2097152 | tf_op jit(solution)/shard_map/all_to_all | solution.py:50
  112.9 11.5 %all-to-all-done.1 = f32[32,4,8,256]{3,2,1,0:T(8,128)} async-done(((f32[32,4,8,256]{3,2,1,0:T(8,128)}), f32[32,4,8,256]{3,2,1,0:T(8,128)}, u32[]{:S(2)}, u32[]{:S(2)}) %all-to-all-start.1) | async-done | bytes 1048608 | tf_op jit(solution)/shard_map/all_to_all | solution.py:50
  126.3 7.3 %fusion.399 = (f32[16,64,256]{2,0,1:T(8,128)S(1)}, f32[16,64,256]{2,0,1:T(8,128)S(1)}) fusion(f32[16,8,8,256]{3,0,2,1:T(8,128)S(1)} %copy.33, f32[1,16,64,256]{3,2,1,0:T(8,128)S(1)} %copy-done.2, pred[]{:T(512)} %bitcast.28, f32[1,16,64,256]{3,2,1,0:T(8,128)S(1)} %copy-done.1, f32[64,256]{1,0:T(8,128)S(1)} %broadcast_multiply_fusion, ...), kind=kLoop, calls=%fused_computation.615 | loop fusion | flops 13893632 | bytes 6881349 | tf_op jit(solution)/shard_map/jit(_where)/select_n | solution.py:144
  134.4 8.3 %bitcast_select_fusion.1 = (f32[16,64,256]{2,0,1:T(8,128)}, f32[16,64,256]{2,0,1:T(8,128)}, f32[16,64,256]{2,0,1:T(8,128)}) fusion(f32[1,16,64,256]{3,2,1,0:T(8,128)} %param.20, pred[]{:T(512)} %bitcast, f32[1,16,64,256]{3,2,1,0:T(8,128)S(1)} %copy-done.9, f32[16,64,256]{2,0,1:T(8,128)S(1)} %bitcast.136, f32[32,256]{1,0:T(8,128)S(1)} %copy-done.15, ...), kind=kOutput, calls=%fused_computation.623 | convolution fusion | flops 114820096 | bytes 7905601 | tf_op jit(solution)/shard_map/rx,ryz->xyz/dot_general | solution.py:146
  146.6 4.7 %collective-permute-start.13 = (f32[8,64,256]{2,0,1:T(8,128)S(1)}, f32[8,64,256]{2,0,1:T(8,128)S(1)}, u32[]{:S(2)}, u32[]{:S(2)}) collective-permute-start(f32[8,64,256]{2,0,1:T(8,128)S(1)} %pad_maximum_fusion.19), channel_id=1, source_target_pairs={{0,1},{1,2},{2,3},{3,4},{4,5},{5,6},{6,7},{7,8},{8,9},{9,10},{10,1... | collective-permute-start | bytes 1572872 | tf_op jit(solution)/shard_map/ppermute | solution.py:15
  151.4 4.8 %collective-permute-done.12 = f32[8,64,256]{2,0,1:T(8,128)S(1)} collective-permute-done((f32[8,64,256]{2,0,1:T(8,128)S(1)}, f32[8,64,256]{2,0,1:T(8,128)S(1)}, u32[]{:S(2)}, u32[]{:S(2)}) %collective-permute-start.12) | collective-permute-done | bytes 524320 | tf_op jit(solution)/shard_map/ppermute | solution.py:15
  160.4 6.2 %fusion.401 = (f32[16,64,256]{2,0,1:T(8,128)S(1)}, f32[16,64,256]{2,0,1:T(8,128)S(1)}) fusion(f32[16,8,8,256]{3,0,2,1:T(8,128)S(1)} %copy.33, pred[]{:T(512)} %bitcast.27, f32[1,16,64,256]{3,2,1,0:T(8,128)S(1)} %copy-done.2, pred[]{:T(512)} %bitcast.28, f32[1,16,64,256]{3,2,1,0:T(8,128)S(1)} %copy-done.1, f32[16,64,256]{2,0,1:T(8,128)S(1)} %get-tuple-element.10, ...), kind=kLoop, calls=%fused_computation.620 | loop fusion | flops 15466496 | bytes 7929926 | tf_op jit(solution)/shard_map/jit(_where)/select_n | solution.py:144
  166.7 6.6 %broadcast_select_fusion.2 = (f32[16,64,256]{2,0,1:T(8,128)}, f32[16,64,256]{2,0,1:T(8,128)}) fusion(f32[16,64,256]{2,0,1:T(8,128)S(1)} %copy-done.11, pred[]{:T(512)} %bitcast.26, f32[16,64,256]{2,0,1:T(8,128)S(1)} %bitcast.137, f32[32,256]{1,0:T(8,128)S(1)} %copy-done.15, f32[32,64]{0,1:T(8,128)S(1)} %copy-done.14, f32[32]{0:T(128)S(1)} %get-tuple-element.69, ...), kind=kOutput, calls=%fused_computation.644 | convolution fusion | flops 114557952 | bytes 5808449 | tf_op jit(solution)/shard_map/rx,ryz->xyz/dot_general | solution.py:146
  176.7 6.1 %collective-permute-start.15 = (f32[8,64,256]{2,0,1:T(8,128)S(1)}, f32[8,64,256]{2,0,1:T(8,128)S(1)}, u32[]{:S(2)}, u32[]{:S(2)}) collective-permute-start(f32[8,64,256]{2,0,1:T(8,128)S(1)} %pad_maximum_fusion.21), channel_id=1, source_target_pairs={{0,1},{1,2},{2,3},{3,4},{4,5},{5,6},{6,7},{7,8},{8,9},{9,10},{10,1... | collective-permute-start | bytes 1572872 | tf_op jit(solution)/shard_map/ppermute | solution.py:15
  182.9 4.6 %collective-permute-done.14 = f32[8,64,256]{2,0,1:T(8,128)S(1)} collective-permute-done((f32[8,64,256]{2,0,1:T(8,128)S(1)}, f32[8,64,256]{2,0,1:T(8,128)S(1)}, u32[]{:S(2)}, u32[]{:S(2)}) %collective-permute-start.14) | collective-permute-done | bytes 524320 | tf_op jit(solution)/shard_map/ppermute | solution.py:15
  190.6 8.4 %fusion.403 = (f32[16,64,256]{2,0,1:T(8,128)S(1)}, f32[16,64,256]{2,0,1:T(8,128)}) fusion(f32[16,8,8,256]{3,0,2,1:T(8,128)S(1)} %copy.33, f32[16,64,256]{2,0,1:T(8,128)S(1)} %get-tuple-element.8, pred[]{:T(512)} %bitcast.27, pred[]{:T(512)} %bitcast.26, f32[1,16,64,256]{3,2,1,0:T(8,128)S(1)} %copy-done.2, pred[]{:T(512)} %bitcast.28, ...), kind=kLoop, calls=%fused_computation.622 | loop fusion | flops 17039360 | bytes 8978503 | tf_op jit(solution)/shard_map/jit(_where)/select_n | solution.py:144
  199.2 18.0 %broadcast_select_fusion = (f32[16,64,256]{2,0,1:T(8,128)S(1)}, f32[16,64,256]{2,0,1:T(8,128)}) fusion(f32[16,64,256]{2,0,1:T(8,128)} %get-tuple-element.91, pred[]{:T(512)} %bitcast.27, f32[16,64,256]{2,0,1:T(8,128)S(1)} %bitcast.138, f32[32,256]{1,0:T(8,128)S(1)} %copy-done.15, f32[32,64]{0,1:T(8,128)S(1)} %copy-done.14, f32[32]{0:T(128)S(1)} %get-tuple-element.71, ...), kind=kOutput, calls=%fused_computation.642 | convolution fusion | flops 114820096 | bytes 6857026 | tf_op jit(solution)/shard_map/rx,ryz->xyz/dot_general | solution.py:146
  220.4 6.0 %collective-permute-start.17 = (f32[8,64,256]{2,0,1:T(8,128)S(1)}, f32[8,64,256]{2,0,1:T(8,128)S(1)}, u32[]{:S(2)}, u32[]{:S(2)}) collective-permute-start(f32[8,64,256]{2,0,1:T(8,128)S(1)} %pad_maximum_fusion.23), channel_id=1, source_target_pairs={{0,1},{1,2},{2,3},{3,4},{4,5},{5,6},{6,7},{7,8},{8,9},{9,10},{10,1... | collective-permute-start | bytes 1572872 | tf_op jit(solution)/shard_map/ppermute | solution.py:15
  226.4 4.7 %collective-permute-done.16 = f32[8,64,256]{2,0,1:T(8,128)S(1)} collective-permute-done((f32[8,64,256]{2,0,1:T(8,128)S(1)}, f32[8,64,256]{2,0,1:T(8,128)S(1)}, u32[]{:S(2)}, u32[]{:S(2)}) %collective-permute-start.16) | collective-permute-done | bytes 524320 | tf_op jit(solution)/shard_map/ppermute | solution.py:15
  233.5 24.1 %fusion.32 = f32[16,64,256]{2,0,1:T(8,128)} fusion(f32[16,64,256]{2,0,1:T(8,128)S(1)} %bitcast.139, f32[16,64,256]{2,0,1:T(8,128)} %copy-done.13, f32[16,64,256]{2,0,1:T(8,128)} %get-tuple-element.90, f32[16,64,256]{2,0,1:T(8,128)S(1)} %get-tuple-element.5, f32[4,64,256]{2,0,1:T(4,128)S(1)} %get-tuple-element.45, f32[4,64,256]{2,0,1:T(4,128)S(1)} %get-tuple-element.43, ...), kind=kOutput, calls=%fused_computation.244 | convolution fusion | flops 131335168 | bytes 14786952 | tf_op jit(solution)/shard_map/rx,ryz->xyz/dot_general | solution.py:146
  259.8 24.0 %all_to_all.20 = f32[32,4,8,256]{3,2,1,0:T(8,128)S(1)} all-to-all(f32[32,4,8,256]{3,2,1,0:T(8,128)S(1)} %bitcast.141), channel_id=1, replica_groups=mesh['shot'=8,'zz'=8,'quad'=4] {'shot','quad'}, dimensions={0} | all-to-all | bytes 2097152 | tf_op jit(solution)/shard_map/all_to_all | solution.py:64
  304.8 5.3 %collective-permute-done.21 = f32[4,4,8,256]{3,2,1,0:T(8,128)S(1)} collective-permute-done((f32[4,4,8,256]{3,2,1,0:T(8,128)S(1)}, f32[4,4,8,256]{3,2,1,0:T(8,128)S(1)}, u32[]{:S(2)}, u32[]{:S(2)}) %collective-permute-start.21) | collective-permute-done | bytes 131104 | tf_op jit(solution)/shard_map/ppermute | solution.py:15
  310.2 6.2 %collective-permute-done.23 = f32[4,4,8,256]{3,2,1,0:T(8,128)S(1)} collective-permute-done((f32[4,4,8,256]{3,2,1,0:T(8,128)S(1)}, f32[4,4,8,256]{3,2,1,0:T(8,128)S(1)}, u32[]{:S(2)}, u32[]{:S(2)}) %collective-permute-start.23) | collective-permute-done | bytes 131104 | tf_op jit(solution)/shard_map/ppermute | solution.py:15
  317.0 10.4 %all_to_all.21 = f32[2,16,8,256]{3,2,0,1:T(8,128)S(1)} all-to-all(f32[2,16,8,256]{3,2,0,1:T(8,128)S(1)} %pad_maximum_fusion.24), channel_id=1, replica_groups=mesh['shot'=8,'zz'=8,'quad'=4] {'quad'}, dimensions={1} | all-to-all | bytes 524288 | tf_op jit(solution)/shard_map/all_to_all | solution.py:30
  (161 shorter events, 104.3 us)
Async XLA Ops:
  2.3 26.7 %all-to-all-start = ((f32[2,16,8,256]{3,2,0,1:T(8,128)}), f32[2,16,8,256]{3,2,0,1:T(8,128)S(1)}, u32[]{:S(2)}, u32[]{:S(2)}) async-start(f32[2,16,8,256]{3,2,0,1:T(8,128)} %copy.45), calls=%async_computation | async-start | bytes 524288 | tf_op jit(solution)/shard_map/all_to_all | solution.py:30
  9.7 16.3 %collective-permute-start.7 = (s32[8]{0:T(128)S(1)}, s32[8]{0:T(128)S(1)}, u32[]{:S(2)}, u32[]{:S(2)}) collective-permute-start(s32[8]{0:T(128)S(1)} %compare_select_fusion.4), channel_id=1, source_target_pairs={{0,32},{32,0},{64,96},{96,64},{128,160},{160,128},{192,224},{224,1... | collective-permute-start | bytes 104 | tf_op jit(solution)/shard_map/ppermute | solution.py:24
  12.9 95.8 %collective-permute-start.10 = (f32[8,64,256]{2,0,1:T(8,128)}, f32[8,64,256]{2,0,1:T(8,128)}, u32[]{:S(2)}, u32[]{:S(2)}) collective-permute-start(f32[8,64,256]{2,0,1:T(8,128)} %pad_maximum_fusion.16), channel_id=1, source_target_pairs={{1,0},{2,1},{3,2},{4,3},{5,4},{6,5},{7,6},{8,7},{9,8},{10,9},{11,1... | collective-permute-start | bytes 1572872 | tf_op jit(solution)/shard_map/ppermute | solution.py:15
  16.0 94.8 %collective-permute-start.11 = (f32[8,64,256]{2,0,1:T(8,128)}, f32[8,64,256]{2,0,1:T(8,128)}, u32[]{:S(2)}, u32[]{:S(2)}) collective-permute-start(f32[8,64,256]{2,0,1:T(8,128)} %pad_maximum_fusion.17), channel_id=1, source_target_pairs={{0,1},{1,2},{2,3},{3,4},{4,5},{5,6},{6,7},{7,8},{8,9},{9,10},{10,1... | collective-permute-start | bytes 1572872 | tf_op jit(solution)/shard_map/ppermute | solution.py:15
  30.1 26.2 %collective-permute-start = (f32[4,4,8,256]{3,2,1,0:T(8,128)}, f32[4,4,8,256]{3,2,1,0:T(8,128)S(1)}, u32[]{:S(2)}, u32[]{:S(2)}) collective-permute-start(f32[4,4,8,256]{3,2,1,0:T(8,128)} %get-tuple-element.64), channel_id=1, source_target_pairs={{0,28},{4,0},{8,4},{12,8},{16,12},{20,16},{24,20},{28,24},{1,29},{... | collective-permute-start | bytes 393224 | tf_op jit(solution)/shard_map/ppermute | solution.py:15
  38.2 23.0 %collective-permute-start.1 = (f32[4,4,8,256]{3,2,1,0:T(8,128)}, f32[4,4,8,256]{3,2,1,0:T(8,128)S(1)}, u32[]{:S(2)}, u32[]{:S(2)}) collective-permute-start(f32[4,4,8,256]{3,2,1,0:T(8,128)} %get-tuple-element.63), channel_id=1, source_target_pairs={{0,24},{4,28},{8,0},{12,4},{16,8},{20,12},{24,16},{28,20},{1,25},{... | collective-permute-start | bytes 393224 | tf_op jit(solution)/shard_map/ppermute | solution.py:15
  56.3 11.3 %collective-permute-start.3 = (f32[4,4,8,256]{3,2,1,0:T(8,128)}, f32[4,4,8,256]{3,2,1,0:T(8,128)S(1)}, u32[]{:S(2)}, u32[]{:S(2)}) collective-permute-start(f32[4,4,8,256]{3,2,1,0:T(8,128)} %get-tuple-element.61), channel_id=1, source_target_pairs={{0,16},{4,20},{8,24},{12,28},{16,0},{20,4},{24,8},{28,12},{1,17},{... | collective-permute-start | bytes 393224 | tf_op jit(solution)/shard_map/ppermute | solution.py:15
  61.2 12.4 %collective-permute-start.4 = (f32[4,4,8,256]{3,2,1,0:T(8,128)}, f32[4,4,8,256]{3,2,1,0:T(8,128)S(1)}, u32[]{:S(2)}, u32[]{:S(2)}) collective-permute-start(f32[4,4,8,256]{3,2,1,0:T(8,128)} %get-tuple-element.60), channel_id=1, source_target_pairs={{0,12},{4,16},{8,20},{12,24},{16,28},{20,0},{24,4},{28,8},{1,13},{... | collective-permute-start | bytes 393224 | tf_op jit(solution)/shard_map/ppermute | solution.py:15
  61.9 19.2 %collective-permute-start.5 = (f32[4,4,8,256]{3,2,1,0:T(8,128)}, f32[4,4,8,256]{3,2,1,0:T(8,128)S(1)}, u32[]{:S(2)}, u32[]{:S(2)}) collective-permute-start(f32[4,4,8,256]{3,2,1,0:T(8,128)} %get-tuple-element.59), channel_id=1, source_target_pairs={{0,8},{4,12},{8,16},{12,20},{16,24},{20,28},{24,0},{28,4},{1,9},{5... | collective-permute-start | bytes 393224 | tf_op jit(solution)/shard_map/ppermute | solution.py:15
  67.7 15.7 %collective-permute-start.6 = (f32[4,4,8,256]{3,2,1,0:T(8,128)}, f32[4,4,8,256]{3,2,1,0:T(8,128)S(1)}, u32[]{:S(2)}, u32[]{:S(2)}) collective-permute-start(f32[4,4,8,256]{3,2,1,0:T(8,128)} %get-tuple-element.58), channel_id=1, source_target_pairs={{0,4},{4,8},{8,12},{12,16},{16,20},{20,24},{24,28},{28,0},{1,5},{5... | collective-permute-start | bytes 393224 | tf_op jit(solution)/shard_map/ppermute | solution.py:15
  97.3 27.1 %all-to-all-start.1 = ((f32[32,4,8,256]{3,2,1,0:T(8,128)}), f32[32,4,8,256]{3,2,1,0:T(8,128)}, u32[]{:S(2)}, u32[]{:S(2)}) async-start(f32[32,4,8,256]{3,2,1,0:T(8,128)} %dynamic-slice_dynamic-update-slice_fusion), calls=%async_computation.1 | async-start | bytes 2097152 | tf_op jit(solution)/shard_map/all_to_all | solution.py:50
  144.2 12.0 %collective-permute-start.12 = (f32[8,64,256]{2,0,1:T(8,128)S(1)}, f32[8,64,256]{2,0,1:T(8,128)S(1)}, u32[]{:S(2)}, u32[]{:S(2)}) collective-permute-start(f32[8,64,256]{2,0,1:T(8,128)S(1)} %pad_maximum_fusion.18), channel_id=1, source_target_pairs={{1,0},{2,1},{3,2},{4,3},{5,4},{6,5},{7,6},{8,7},{9,8},{10,9},{11,1... | collective-permute-start | bytes 1572872 | tf_op jit(solution)/shard_map/ppermute | solution.py:15
  146.6 13.0 %collective-permute-start.13 = (f32[8,64,256]{2,0,1:T(8,128)S(1)}, f32[8,64,256]{2,0,1:T(8,128)S(1)}, u32[]{:S(2)}, u32[]{:S(2)}) collective-permute-start(f32[8,64,256]{2,0,1:T(8,128)S(1)} %pad_maximum_fusion.19), channel_id=1, source_target_pairs={{0,1},{1,2},{2,3},{3,4},{4,5},{5,6},{6,7},{7,8},{8,9},{9,10},{10,1... | collective-permute-start | bytes 1572872 | tf_op jit(solution)/shard_map/ppermute | solution.py:15
  174.7 12.8 %collective-permute-start.14 = (f32[8,64,256]{2,0,1:T(8,128)S(1)}, f32[8,64,256]{2,0,1:T(8,128)S(1)}, u32[]{:S(2)}, u32[]{:S(2)}) collective-permute-start(f32[8,64,256]{2,0,1:T(8,128)S(1)} %pad_maximum_fusion.20), channel_id=1, source_target_pairs={{1,0},{2,1},{3,2},{4,3},{5,4},{6,5},{7,6},{8,7},{9,8},{10,9},{11,1... | collective-permute-start | bytes 1572872 | tf_op jit(solution)/shard_map/ppermute | solution.py:15
  176.7 13.0 %collective-permute-start.15 = (f32[8,64,256]{2,0,1:T(8,128)S(1)}, f32[8,64,256]{2,0,1:T(8,128)S(1)}, u32[]{:S(2)}, u32[]{:S(2)}) collective-permute-start(f32[8,64,256]{2,0,1:T(8,128)S(1)} %pad_maximum_fusion.21), channel_id=1, source_target_pairs={{0,1},{1,2},{2,3},{3,4},{4,5},{5,6},{6,7},{7,8},{8,9},{9,10},{10,1... | collective-permute-start | bytes 1572872 | tf_op jit(solution)/shard_map/ppermute | solution.py:15
  218.3 12.8 %collective-permute-start.16 = (f32[8,64,256]{2,0,1:T(8,128)S(1)}, f32[8,64,256]{2,0,1:T(8,128)S(1)}, u32[]{:S(2)}, u32[]{:S(2)}) collective-permute-start(f32[8,64,256]{2,0,1:T(8,128)S(1)} %pad_maximum_fusion.22), channel_id=1, source_target_pairs={{1,0},{2,1},{3,2},{4,3},{5,4},{6,5},{7,6},{8,7},{9,8},{10,9},{11,1... | collective-permute-start | bytes 1572872 | tf_op jit(solution)/shard_map/ppermute | solution.py:15
  220.4 13.0 %collective-permute-start.17 = (f32[8,64,256]{2,0,1:T(8,128)S(1)}, f32[8,64,256]{2,0,1:T(8,128)S(1)}, u32[]{:S(2)}, u32[]{:S(2)}) collective-permute-start(f32[8,64,256]{2,0,1:T(8,128)S(1)} %pad_maximum_fusion.23), channel_id=1, source_target_pairs={{0,1},{1,2},{2,3},{3,4},{4,5},{5,6},{6,7},{7,8},{8,9},{9,10},{10,1... | collective-permute-start | bytes 1572872 | tf_op jit(solution)/shard_map/ppermute | solution.py:15
  284.3 11.8 %collective-permute-start.18 = (f32[4,4,8,256]{3,2,1,0:T(8,128)S(1)}, f32[4,4,8,256]{3,2,1,0:T(8,128)S(1)}, u32[]{:S(2)}, u32[]{:S(2)}) collective-permute-start(f32[4,4,8,256]{3,2,1,0:T(8,128)S(1)} %get-tuple-element.13), channel_id=1, source_target_pairs={{0,4},{4,8},{8,12},{12,16},{16,20},{20,24},{24,28},{28,0},{1,5},{5... | collective-permute-start | bytes 393224 | tf_op jit(solution)/shard_map/ppermute | solution.py:15
  287.5 10.5 %collective-permute-start.19 = (f32[4,4,8,256]{3,2,1,0:T(8,128)S(1)}, f32[4,4,8,256]{3,2,1,0:T(8,128)S(1)}, u32[]{:S(2)}, u32[]{:S(2)}) collective-permute-start(f32[4,4,8,256]{3,2,1,0:T(8,128)S(1)} %get-tuple-element.19), channel_id=1, source_target_pairs={{0,8},{4,12},{8,16},{12,20},{16,24},{20,28},{24,0},{28,4},{1,9},{5... | collective-permute-start | bytes 393224 | tf_op jit(solution)/shard_map/ppermute | solution.py:15
  288.3 16.5 %collective-permute-start.20 = (f32[4,4,8,256]{3,2,1,0:T(8,128)S(1)}, f32[4,4,8,256]{3,2,1,0:T(8,128)S(1)}, u32[]{:S(2)}, u32[]{:S(2)}) collective-permute-start(f32[4,4,8,256]{3,2,1,0:T(8,128)S(1)} %get-tuple-element.18), channel_id=1, source_target_pairs={{0,12},{4,16},{8,20},{12,24},{16,28},{20,0},{24,4},{28,8},{1,13},{... | collective-permute-start | bytes 393224 | tf_op jit(solution)/shard_map/ppermute | solution.py:15
  290.7 19.5 %collective-permute-start.21 = (f32[4,4,8,256]{3,2,1,0:T(8,128)S(1)}, f32[4,4,8,256]{3,2,1,0:T(8,128)S(1)}, u32[]{:S(2)}, u32[]{:S(2)}) collective-permute-start(f32[4,4,8,256]{3,2,1,0:T(8,128)S(1)} %get-tuple-element.17), channel_id=1, source_target_pairs={{0,16},{4,20},{8,24},{12,28},{16,0},{20,4},{24,8},{28,12},{1,17},{... | collective-permute-start | bytes 393224 | tf_op jit(solution)/shard_map/ppermute | solution.py:15
  293.6 16.5 %collective-permute-start.22 = (f32[4,4,8,256]{3,2,1,0:T(8,128)S(1)}, f32[4,4,8,256]{3,2,1,0:T(8,128)S(1)}, u32[]{:S(2)}, u32[]{:S(2)}) collective-permute-start(f32[4,4,8,256]{3,2,1,0:T(8,128)S(1)} %get-tuple-element.16), channel_id=1, source_target_pairs={{0,20},{4,24},{8,28},{12,0},{16,4},{20,8},{24,12},{28,16},{1,21},{... | collective-permute-start | bytes 393224 | tf_op jit(solution)/shard_map/ppermute | solution.py:15
  296.1 20.3 %collective-permute-start.23 = (f32[4,4,8,256]{3,2,1,0:T(8,128)S(1)}, f32[4,4,8,256]{3,2,1,0:T(8,128)S(1)}, u32[]{:S(2)}, u32[]{:S(2)}) collective-permute-start(f32[4,4,8,256]{3,2,1,0:T(8,128)S(1)} %get-tuple-element.15), channel_id=1, source_target_pairs={{0,24},{4,28},{8,0},{12,4},{16,8},{20,12},{24,16},{28,20},{1,25},{... | collective-permute-start | bytes 393224 | tf_op jit(solution)/shard_map/ppermute | solution.py:15
  298.0 18.8 %collective-permute-start.24 = (f32[4,4,8,256]{3,2,1,0:T(8,128)S(1)}, f32[4,4,8,256]{3,2,1,0:T(8,128)S(1)}, u32[]{:S(2)}, u32[]{:S(2)}) collective-permute-start(f32[4,4,8,256]{3,2,1,0:T(8,128)S(1)} %get-tuple-element.14), channel_id=1, source_target_pairs={{0,28},{4,0},{8,4},{12,8},{16,12},{20,16},{24,20},{28,24},{1,29},{... | collective-permute-start | bytes 393224 | tf_op jit(solution)/shard_map/ppermute | solution.py:15
  (25 other events, 165.8 us)

commit v2 on v1

v2 whole, which is shorter than its diff:
```python
import functools

import jax
import jax.numpy as jnp
from jax import lax
from jax.experimental import pallas as pl
from jax.experimental.pallas import tpu as pltpu
from jax.sharding import Mesh, PartitionSpec as P

COEF = (-205.0 / 72.0, 1.6, -0.2, 8.0 / 315.0, -1.0 / 560.0)
QUAD = 4
MP = ("zz", "quad")
PLANE = ("shot", "quad")
LANES = 128
SUB = 8
REACH = 4
COUNT, BASE, SOURCE, RECEIVERS = 0, 1, 2, 5
VMEM_LIMIT = 24 << 20


def shifted(value, axes, steps):
    count = lax.axis_size(axes)
    pairs = [(i, i + steps) for i in range(count) if 0 <= i + steps < count]
    return lax.ppermute(value, axes, pairs)


def all_first(first):
    shots = lax.axis_size("shot")
    me = lax.axis_index("shot")
    known = jnp.where(jnp.arange(shots, dtype=jnp.int32) == me, first, 0)
    step = 1
    while step < shots:
        known = known + lax.ppermute(known, "shot", [(i, i ^ step) for i in range(shots)])
        step *= 2
    return known


def f32(*shape):
    return jax.ShapeDtypeStruct(shape, jnp.float32)


def local_kernel(body, name, scalars, arrays, outs, scratch=()):
    vmem = pl.BlockSpec(memory_space=pltpu.VMEM)
    smem = pl.BlockSpec(memory_space=pltpu.SMEM)
    return pl.pallas_call(
        body,
        out_shape=outs,
        in_specs=[smem] * len(scalars) + [vmem] * len(arrays),
        out_specs=[vmem] * len(outs),
        scratch_shapes=list(scratch),
        compiler_params=pltpu.CompilerParams(vmem_limit_bytes=VMEM_LIMIT),
        name=name,
    )(*scalars, *arrays)


def band_matrix(nz):
    rows = lax.broadcasted_iota(jnp.int32, (nz, nz), 0)
    cols = lax.broadcasted_iota(jnp.int32, (nz, nz), 1)
    apart = jnp.abs(rows - cols)
    band = jnp.where(apart == 0, 3.0 * COEF[0], 0.0)
    for k in range(1, REACH + 1):
        band = jnp.where(apart == k, COEF[k], band)
    return band


def prepare(field, padded, along_z):
    xs, ys, nz = field.shape
    along_z[...] = jnp.dot(
        field[...].reshape(xs * ys, nz),
        band_matrix(nz),
        precision=lax.Precision.HIGHEST,
        preferred_element_type=jnp.float32,
    ).reshape(xs, ys, nz)
    edge = jnp.zeros((xs, SUB, LANES), jnp.float32)
    for h in range(nz // LANES):
        padded[h, :, 0:SUB, :] = edge
        padded[h, :, SUB + ys : SUB + ys + SUB, :] = edge
        padded[h, :, SUB : SUB + ys, :] = field[:, :, h * LANES : (h + 1) * LANES]


def add_point(target, x, y, z, amount):
    xs, _, nz = target.shape

    @pl.when((x >= 0) & (x < xs))
    def _():
        cells = lax.broadcasted_iota(jnp.int32, (1, 1, nz), 2)
        place = (pl.ds(x, 1), pl.ds(y, 1), slice(None))
        target[place] = target[place] + jnp.where(cells == z, amount, 0.0)


def add_source(target, ints, floats, n):
    x = ints[SOURCE] - ints[BASE]
    add_point(target, x, ints[SOURCE + 1], ints[SOURCE + 2], floats[n])


def add_receivers(target, ints, floats, steps, receivers, n):
    def one(j, carry):
        at = RECEIVERS + 3 * j
        amount = floats[steps + n * receivers + j]
        add_point(target, ints[at] - ints[BASE], ints[at + 1], ints[at + 2], amount)
        return carry

    lax.fori_loop(0, receivers, one, 0)


def laplacian(padded, along_z, before, after, plane, y0, h):
    xs = along_z.shape[0]
    rows = pl.ds(y0, SUB)
    lanes = slice(h * LANES, (h + 1) * LANES)
    column = [before[plane + j, rows, lanes] for j in range(REACH)]
    column += [padded[h, x, pl.ds(y0 + SUB, SUB), :] for x in range(xs)]
    column += [after[plane + j, rows, lanes] for j in range(REACH)]
    for x in range(xs):
        total = along_z[x, rows, lanes]
        for k in range(1, REACH + 1):
            pair = column[x + REACH + k] + column[x + REACH - k]
            pair = pair + (
                padded[h, x, pl.ds(y0 + SUB + k, SUB), :]
                + padded[h, x, pl.ds(y0 + SUB - k, SUB), :]
            )
            total = total + COEF[k] * pair
        yield x, column[x + REACH], total


def each_block(field, work):
    _, ys, nz = field.shape

    def step(i, carry):
        y0 = pl.multiple_of(i * SUB, SUB)
        for h in range(nz // LANES):
            work(i, y0, h, slice(h * LANES, (h + 1) * LANES))
        return carry

    lax.fori_loop(0, ys // SUB, step, 0)


def switch_on(ints, n):
    return jnp.where(ints[COUNT] > n, 1.0, 0.0).astype(jnp.float32)


def first_kernel(dims, ints, floats, u, w, before, after, d, e, pad_u, pad_w):
    steps, receivers = dims
    prepare(u, pad_u, d)
    prepare(w, pad_w, e)
    add_source(d, ints, floats, 0)
    add_receivers(e, ints, floats, steps, receivers, steps - 1)
    live = switch_on(ints, 0)

    def work(i, y0, h, lanes):
        rows = pl.ds(y0, SUB)
        for x, _, total in laplacian(pad_u, d, before, after, 0, y0, h):
            d[x, rows, lanes] = live * total
        for x, _, total in laplacian(pad_w, e, before, after, REACH, y0, h):
            e[x, rows, lanes] = total

    each_block(u, work)


def send_planes(low, high, plane, x, xs, rows, lanes, value):
    if x < REACH:
        low[plane + x, rows, lanes] = value
    if x >= xs - REACH:
        high[plane + x - (xs - REACH), rows, lanes] = value


def advance_kernel(dims, ints, u, ub, d, w, wb, e, p, u1, vu1, w1, vw1, low, high):
    steps, _ = dims
    xs = u.shape[0]
    live = switch_on(ints, steps - 1)

    def work(i, y0, h, lanes):
        rows = pl.ds(y0, SUB)
        for x in range(xs):
            speed = p[i, x, :, lanes]
            now = u[x, rows, lanes]
            gain = (now - ub[x, rows, lanes]) + speed * d[x, rows, lanes]
            vu1[x, rows, lanes] = gain
            now = now + gain
            u1[x, rows, lanes] = now
            send_planes(low, high, 0, x, xs, rows, lanes, now)
            now = w[x, rows, lanes]
            gain = (now - wb[x, rows, lanes]) + (live * speed) * e[x, rows, lanes]
            vw1[x, rows, lanes] = gain
            now = now + live * gain
            w1[x, rows, lanes] = now
            send_planes(low, high, REACH, x, xs, rows, lanes, now)

    each_block(u, work)


def round_kernel(dims, n, ints, floats, u, vu, w, vw, p, before, after, *rest):
    steps, receivers = dims
    last = n == steps - 1
    image_round = n == steps - 2
    if last:
        partial, d_first, w_first, image, pad_u, pad_w, z_u, z_w = rest
    elif image_round:
        d_before, d_out, u1, vu1, w1, vw1, low, high, pad_u, pad_w, z_u, z_w = rest
    else:
        d_out, u1, vu1, w1, vw1, low, high, pad_u, pad_w, z_u, z_w = rest
    xs = u.shape[0]
    back = steps - 1 - n
    prepare(u, pad_u, z_u)
    prepare(w, pad_w, z_w)
    add_source(z_u, ints, floats, n)
    add_receivers(z_w, ints, floats, steps, receivers, back)
    live = switch_on(ints, n)
    live_back = switch_on(ints, back)

    def work(i, y0, h, lanes):
        rows = pl.ds(y0, SUB)
        for x, now, total in laplacian(pad_u, z_u, before, after, 0, y0, h):
            drive = live * total
            if last:
                image[i, x, :, lanes] = partial[x, rows, lanes] + w_first[x, rows, lanes] * drive
                continue
            if image_round:
                d_out[x, rows, lanes] = drive * w[x, rows, lanes]
            else:
                d_out[x, rows, lanes] = drive
            gain = vu[x, rows, lanes] + p[i, x, :, lanes] * drive
            vu1[x, rows, lanes] = gain
            now = now + gain
            u1[x, rows, lanes] = now
            send_planes(low, high, 0, x, xs, rows, lanes, now)
        for x, now, total in laplacian(pad_w, z_w, before, after, REACH, y0, h):
            gain = vw[x, rows, lanes] + (live_back * p[i, x, :, lanes]) * total
            now = now + live_back * gain
            if last:
                image[i, x, :, lanes] = image[i, x, :, lanes] + now * d_first[x, rows, lanes]
                continue
            if image_round:
                d_out[x, rows, lanes] = d_out[x, rows, lanes] + now * d_before[x, rows, lanes]
            vw1[x, rows, lanes] = gain
            w1[x, rows, lanes] = now
            send_planes(low, high, REACH, x, xs, rows, lanes, now)

    each_block(u, work)


def gather_kernel(zs, firsts, line, extra, sent):
    me_z = firsts[sent.shape[0] // QUAD]

    def one(slot, carry):
        tile = firsts[slot // QUAD] + slot % QUAD
        place = ((me_z + tile // QUAD) % zs) * QUAD + tile % QUAD

        @pl.when(tile < zs * QUAD)
        def _():
            sent[slot] = line[place]

        @pl.when(tile >= zs * QUAD)
        def _():
            sent[slot] = extra[tile % QUAD]

        return carry

    lax.fori_loop(0, sent.shape[0], one, 0)


def scatter_kernel(zs, firsts, got, line, extra):
    me_z = firsts[got.shape[0] // QUAD]
    line[...] = jnp.zeros_like(line)
    extra[...] = jnp.zeros_like(extra)

    def one(slot, carry):
        tile = firsts[slot // QUAD] + slot % QUAD
        place = ((me_z + tile // QUAD) % zs) * QUAD + tile % QUAD

        @pl.when(tile < zs * QUAD)
        def _():
            line[place] = line[place] + got[slot]

        @pl.when(tile >= zs * QUAD)
        def _():
            extra[tile % QUAD] = extra[tile % QUAD] + got[slot]

        return carry

    lax.fori_loop(0, got.shape[0], one, 0)


def finish_kernel(zs, where, came, extra, out):
    planes = came.shape[1]
    me_z = where[0]
    for q in range(QUAD):
        low = came[q]
        high = extra[q]
        for z in range(1, zs):
            value = came[z * QUAD + q]
            low = low + jnp.where(z <= me_z, value, 0.0)
            high = high + jnp.where(z <= me_z, 0.0, value)
        out[0, q * planes : (q + 1) * planes] = low
        out[1, q * planes : (q + 1) * planes] = high


def exchange(parts, axes):
    return lax.all_to_all(parts, axes, split_axis=0, concat_axis=0, tiled=True)


def fetch_model(courant, table):
    _, tile_x, ny, nz = courant.shape
    shots = lax.axis_size("shot")
    zs = lax.axis_size("zz")
    slab = ny // shots
    planes = tile_x // QUAD
    me_z = lax.axis_index("zz")
    mine = lax.dynamic_slice_in_dim(courant, lax.axis_index("shot") * slab, slab, 2)
    near = (jnp.arange(zs) <= me_z)[:, None, None, None]
    parts = jnp.where(near, mine[0][None], mine[1][None])
    line = exchange(parts.reshape(zs * QUAD, planes, slab, nz), MP)
    extra = exchange(mine[1].reshape(QUAD, planes, slab, nz), "quad")
    (sent,) = local_kernel(
        functools.partial(gather_kernel, zs),
        "gather",
        [table],
        [line, extra],
        [f32(shots * QUAD, planes, slab, nz)],
    )
    return exchange(sent, PLANE).reshape(shots, tile_x, slab, nz)


def return_image(image, table, here):
    shots, tile_x, slab, nz = image.shape
    zs = lax.axis_size("zz")
    planes = tile_x // QUAD
    got = exchange(image.reshape(shots * QUAD, planes, slab, nz), PLANE)
    line, extra = local_kernel(
        functools.partial(scatter_kernel, zs),
        "scatter",
        [table],
        [got],
        [f32(zs * QUAD, planes, slab, nz), f32(QUAD, planes, slab, nz)],
    )
    came = exchange(line, MP)
    came_extra = exchange(extra, "quad")
    (out,) = local_kernel(
        functools.partial(finish_kernel, zs),
        "finish",
        [here],
        [came, came_extra],
        [f32(2, tile_x, slab, nz)],
    )
    return out


def body(
    courant,
    aperture_first,
    source_pos,
    wavelet,
    receiver_pos,
    residual,
    step_count,
    forward_prev,
    forward_now,
    adjoint_prev,
    adjoint_now,
):
    tile_x, ny, nz = forward_now.shape[1:]
    steps = wavelet.shape[1]
    receivers = receiver_pos.shape[1]
    dims = (steps, receivers)
    here = lax.axis_index("zz").reshape(1).astype(jnp.int32)
    table = jnp.concatenate([all_first(aperture_first[0]), here])
    base = (lax.axis_index(MP) * tile_x).reshape(1).astype(jnp.int32)
    ints = jnp.concatenate([step_count, base, source_pos[0], receiver_pos[0].reshape(-1)])
    floats = jnp.concatenate([wavelet[0], residual[0].reshape(-1)])
    u, w = forward_now[0], adjoint_now[0]
    low = jnp.concatenate([u[:REACH], w[:REACH]])
    high = jnp.concatenate([u[tile_x - REACH :], w[tile_x - REACH :]])
    before, after = shifted(high, MP, 1), shifted(low, MP, -1)
    field = f32(tile_x, ny, nz)
    edge = f32(2 * REACH, ny, nz)
    padded = pltpu.VMEM((nz // LANES, tile_x, ny + 2 * SUB, LANES), jnp.float32)
    work = pltpu.VMEM((tile_x, ny, nz), jnp.float32)
    drive, push = local_kernel(
        functools.partial(first_kernel, dims),
        "first",
        [ints, floats],
        [u, w, before, after],
        [field, field],
        [padded, padded],
    )
    owned = fetch_model(courant, table)
    d_first = drive
    u, vu, w, vw, low, high = local_kernel(
        functools.partial(advance_kernel, dims),
        "advance",
        [ints],
        [u, forward_prev[0], drive, w, adjoint_prev[0], push, owned],
        [field, field, field, field, edge, edge],
    )
    w_first = w
    d_before = None
    for n in range(1, steps):
        before, after = shifted(high, MP, 1), shifted(low, MP, -1)
        arrays = [u, vu, w, vw, owned, before, after]
        if n == steps - 1:
            (image,) = local_kernel(
                functools.partial(round_kernel, dims, n),
                "last",
                [ints, floats],
                arrays + [d_before, d_first, w_first],
                [f32(ny // SUB, tile_x, SUB, nz)],
                [padded, padded, work, work],
            )
            break
        if n == steps - 2:
            arrays = arrays + [d_before]
        d_before, u, vu, w, vw, low, high = local_kernel(
            functools.partial(round_kernel, dims, n),
            "round",
            [ints, floats],
            arrays,
            [field, field, field, field, field, edge, edge],
            [padded, padded, work, work],
        )
    return return_image(image, table, here)


def solution(mesh):
    shots, mp = mesh.devices.shape
    fine = Mesh(mesh.devices.reshape(shots, mp // QUAD, QUAD), ("shot", "zz", "quad"))
    return jax.shard_map(
        body,
        mesh=fine,
        in_specs=(
            P(None, MP, None, None),
            P("shot"),
            P("shot", None),
            P("shot", None),
            P("shot", None, None),
            P("shot", None, None),
            P("shot"),
            P("shot", MP, None, None),
            P("shot", MP, None, None),
            P("shot", MP, None, None),
            P("shot", MP, None, None),
        ),
        out_specs=P(None, MP, "shot", None),
        check_vma=False,
    )
```

time: 329 us -> 237 us (0.72)
  matrix products: 57 us -> 0 us
  local copies, waits for them, and re-layouts: 40.9 us -> 11.1 us
  blocking collectives: 34.4 us -> 64 us
  starting transfers between devices: 86.8 us -> 57.3 us
  Pallas kernels: 0 us -> 27.8 us
  other arithmetic: 30.1 us -> 3.06 us
  between operations: 17.2 us -> 1.56 us
  waiting for transfers between devices: 61.7 us -> 70.9 us
    dot_general x4 -> x0, matrix products: 57 us -> none  [body(): jnp.einsum('rx,ryz->xyz', weighted, rec_plane, precision=lax.Precision.HI...]
    ppermute x22 -> x8, starting transfers between devices: 66.7 us -> 29 us  [shifted(): return lax.ppermute(value, axes, pairs)]
    all_to_all x2 -> x3, blocking collectives: 34.4 us -> 64 us  [exchange(): return lax.all_to_all(parts, axes, split_axis=0, concat_axis=0, tiled=True)]
    pallas_call x0 -> x8, Pallas kernels: none -> 27.8 us  [local_kernel(): pl.pallas_call(body, out_shape=outs, in_specs=[smem] * len(scalars) + [vm...]
    select_n x4 -> x1, other arithmetic: 22.9 us -> 1.14 us  [fetch_model(): parts = jnp.where(near, mine[0][None], mine[1][None])]
    unnamed x62 -> x29, local copies, waits for them, and re-layouts: 20.5 us -> 7.94 us
    slice x20 -> x2, local copies, waits for them, and re-layouts: 12.9 us -> 1.74 us  [the longest x1 1.64 us: fetch_model(): parts = jnp.where(near, mine[0][None], mine[1][None])]
    all_to_all x2 -> x3, waiting for transfers between devices: 11.5 us -> 20.6 us  [exchange(): return lax.all_to_all(parts, axes, split_axis=0, concat_axis=0, tiled=True)]
  transfers between devices with their start and end apart: 27 -> 14, of which waited for: 15 -> 12; matrix products, arithmetic and copies ran while one was open for 11% -> 2% of each run, Pallas kernels for 0% -> 2%
where the time goes in v2:
time: 237 us; the launch traced here: 236 us
  waiting for transfers between devices  70.9 us (30%)
  blocking collectives  64 us (27%)
  starting transfers between devices  57.3 us (24%)
  Pallas kernels  27.8 us (12%)
  local copies, waits for them, and re-layouts  11.1 us (5%)
  other arithmetic  3.06 us (1%)
    all_to_all x3, blocking collectives, exchange(): return lax.all_to_all(parts, axes, split_axis=0, concat_axis=0, tiled=True)  64 us
    ppermute x8, waiting for transfers between devices, shifted(): return lax.ppermute(value, axes, pairs)  45.3 us
    ppermute x8, starting transfers between devices, shifted(): return lax.ppermute(value, axes, pairs)  29 us
    pallas_call x8, Pallas kernels, local_kernel(): pl.pallas_call(body, out_shape=outs, in_specs=[smem] * len(scalars) + [vm...  27.8 us
    all_to_all x3, starting transfers between devices, exchange(): return lax.all_to_all(parts, axes, split_axis=0, concat_axis=0, tiled=True)  23.9 us
    all_to_all x3, waiting for transfers between devices, exchange(): return lax.all_to_all(parts, axes, split_axis=0, concat_axis=0, tiled=True)  20.6 us
    unnamed x29, local copies, waits for them, and re-layouts  7.94 us
    ppermute x3, waiting for transfers between devices, all_first(): lax.ppermute(known, 'shot', [(i, i ^ step) for i in range(shots)])  5 us
  transfers between devices with their start and end apart: 14, of which 12 were waited for; matrix products, arithmetic and copies ran while one was open for 2% of the time, Pallas kernels for 2%

profile of v2, /device:TPU:1, one launch (start us, length us, event | category | flops | bytes accessed | tf_op | source)
XLA Modules:
  0.0 235.8 jit_solution(13897312018442483122)
XLA Ops:
  1.6 6.5 %all-to-all-start.1 = ((f32[4,4,8,256]{3,2,1,0:T(8,128)}), f32[4,4,8,256]{3,2,1,0:T(8,128)S(1)}, u32[]{:S(2)}, u32[]{:S(2)}) async-start(f32[4,4,8,256]{3,2,1,0:T(8,128)} %bitcast.17), calls=%async_computation.1 | async-start | bytes 262144 | tf_op jit(solution)/shard_map/all_to_all | solution.py:298
  10.5 2.7 %all-to-all-done.1.extra = f32[4,4,8,256]{3,2,1,0:T(8,128)S(1)} async-done(((f32[4,4,8,256]{3,2,1,0:T(8,128)}), f32[4,4,8,256]{3,2,1,0:T(8,128)S(1)}, u32[]{:S(2)}, u32[]{:S(2)}) %all-to-all-start.1) | async-done | bytes 131104 | tf_op jit(solution)/shard_map/all_to_all | solution.py:298
  13.2 9.1 %all-to-all-start = ((f32[32,4,8,256]{3,2,1,0:T(8,128)}), f32[32,4,8,256]{3,2,1,0:T(8,128)S(1)}, u32[]{:S(2)}, u32[]{:S(2)}) async-start(f32[32,4,8,256]{3,2,1,0:T(8,128)} %broadcast_select_fusion), calls=%async_computation | async-start | bytes 2097152 | tf_op jit(solution)/shard_map/all_to_all | solution.py:298
  25.5 2.7 %collective-permute-start.1 = (s32[8]{0:T(128)S(1)}, s32[8]{0:T(128)S(1)}, u32[]{:S(2)}, u32[]{:S(2)}) collective-permute-start(s32[8]{0:T(128)S(1)} %fusion), channel_id=1, source_target_pairs={{0,64},{32,96},{64,0},{96,32},{128,192},{160,224},{192,128},{224,1... | collective-permute-start | bytes 104 | tf_op jit(solution)/shard_map/ppermute | solution.py:33
  30.1 2.3 collective-permute-done.2
  32.5 17.9 %all-to-all-done.line = f32[32,4,8,256]{3,2,1,0:T(8,128)S(1)} async-done(((f32[32,4,8,256]{3,2,1,0:T(8,128)}), f32[32,4,8,256]{3,2,1,0:T(8,128)S(1)}, u32[]{:S(2)}, u32[]{:S(2)}) %all-to-all-start) | async-done | bytes 1048608 | tf_op jit(solution)/shard_map/all_to_all | solution.py:298
  53.1 8.3 %all-to-all-start.2 = ((f32[32,4,8,256]{3,2,1,0:T(8,128)}), f32[32,4,8,256]{3,2,1,0:T(8,128)S(1)}, u32[]{:S(2)}, u32[]{:S(2)}) async-start(f32[32,4,8,256]{3,2,1,0:T(8,128)} %copy-done.2), calls=%async_computation.2 | async-start | bytes 2097152 | tf_op jit(solution)/shard_map/all_to_all | solution.py:298
  62.3 5.0 %collective-permute-start.3 = (f32[8,64,256]{2,1,0:T(8,128)}, f32[8,64,256]{2,1,0:T(8,128)}, u32[]{:S(2)}, u32[]{:S(2)}) collective-permute-start(f32[8,64,256]{2,1,0:T(8,128)} %pad_maximum_fusion), channel_id=1, source_target_pairs={{0,1},{1,2},{2,3},{3,4},{4,5},{5,6},{6,7},{7,8},{8,9},{9,10},{10,1... | collective-permute-start | bytes 1572872 | tf_op jit(solution)/shard_map/ppermute | solution.py:24
  71.2 15.3 %collective-permute-done.3.before = f32[8,64,256]{2,1,0:T(8,128)} collective-permute-done((f32[8,64,256]{2,1,0:T(8,128)}, f32[8,64,256]{2,1,0:T(8,128)}, u32[]{:S(2)}, u32[]{:S(2)}) %collective-permute-start.3) | collective-permute-done | bytes 524320 | tf_op jit(solution)/shard_map/ppermute | solution.py:24
  86.5 5.4 %first.1 = (f32[16,64,256]{2,1,0:T(8,128)S(1)}, f32[16,64,256]{2,1,0:T(8,128)S(1)}) custom-call(s32[101]{0:T(128)S(1)} %pad_add_fusion.1.ints, f32[132]{0:T(256)S(1)} %pad_maximum_fusion.2.floats, f32[16,64,256]{2,1,0:T(8,128)S(1)} %bitcast.32, f32[16,64,256]{2,1,0:T(8,128)S(1)} %bitcast.34, f32[8,64,256]{2,1,0:T(8,128)} %collective-permute-done.3.before, ...), custom_call_target="tpu_custom_call" | custom-call | tf_op jit(solution)/shard_map/first/pallas_call | solution.py:45
  100.3 5.9 %collective-permute-start.5 = (f32[8,64,256]{2,1,0:T(8,128)S(1)}, f32[8,64,256]{2,1,0:T(8,128)S(1)}, u32[]{:S(2)}, u32[]{:S(2)}) collective-permute-start(f32[8,64,256]{2,1,0:T(8,128)S(1)} %get-tuple-element.35), channel_id=1, source_target_pairs={{0,1},{1,2},{2,3},{3,4},{4,5},{5,6},{6,7},{7,8},{8,9},{9,10},{10,1... | collective-permute-start | bytes 1572872 | tf_op jit(solution)/shard_map/ppermute | solution.py:24
  106.2 1.9 collective-permute-start.6
  108.2 9.8 %collective-permute-done.5.before = f32[8,64,256]{2,1,0:T(8,128)S(1)} collective-permute-done((f32[8,64,256]{2,1,0:T(8,128)S(1)}, f32[8,64,256]{2,1,0:T(8,128)S(1)}, u32[]{:S(2)}, u32[]{:S(2)}) %collective-permute-start.5) | collective-permute-done | bytes 524320 | tf_op jit(solution)/shard_map/ppermute | solution.py:24
  118.2 5.3 %round.2 = (f32[16,64,256]{2,1,0:T(8,128)S(1)}, f32[16,64,256]{2,1,0:T(8,128)S(1)}, f32[16,64,256]{2,1,0:T(8,128)S(1)}, f32[16,64,256]{2,1,0:T(8,128)S(1)}, f32[...) custom-call(s32[101]{0:T(128)S(1)} %pad_add_fusion.1.ints, ...), custom_call_target="tpu_custom_call" | custom-call | tf_op jit(solution)/shard_map/round/pallas_call | solution.py:45
  123.6 5.6 %collective-permute-start.7 = (f32[8,64,256]{2,1,0:T(8,128)S(1)}, f32[8,64,256]{2,1,0:T(8,128)S(1)}, u32[]{:S(2)}, u32[]{:S(2)}) collective-permute-start(f32[8,64,256]{2,1,0:T(8,128)S(1)} %get-tuple-element.41), channel_id=1, source_target_pairs={{0,1},{1,2},{2,3},{3,4},{4,5},{5,6},{6,7},{7,8},{8,9},{9,10},{10,1... | collective-permute-start | bytes 1572872 | tf_op jit(solution)/shard_map/ppermute | solution.py:24
  131.1 8.8 %collective-permute-done.7.before = f32[8,64,256]{2,1,0:T(8,128)S(1)} collective-permute-done((f32[8,64,256]{2,1,0:T(8,128)S(1)}, f32[8,64,256]{2,1,0:T(8,128)S(1)}, u32[]{:S(2)}, u32[]{:S(2)}) %collective-permute-start.7) | collective-permute-done | bytes 524320 | tf_op jit(solution)/shard_map/ppermute | solution.py:24
  141.2 5.7 %round.3 = (f32[16,64,256]{2,1,0:T(8,128)S(1)}, f32[16,64,256]{2,1,0:T(8,128)S(1)}, f32[16,64,256]{2,1,0:T(8,128)S(1)}, f32[16,64,256]{2,1,0:T(8,128)S(1)}, f32[...) custom-call(s32[101]{0:T(128)S(1)} %pad_add_fusion.1.ints, ...), custom_call_target="tpu_custom_call" | custom-call | tf_op jit(solution)/shard_map/round/pallas_call | solution.py:45
  146.9 4.7 %collective-permute-start.9 = (f32[8,64,256]{2,1,0:T(8,128)S(1)}, f32[8,64,256]{2,1,0:T(8,128)S(1)}, u32[]{:S(2)}, u32[]{:S(2)}) collective-permute-start(f32[8,64,256]{2,1,0:T(8,128)S(1)} %get-tuple-element.48), channel_id=1, source_target_pairs={{0,1},{1,2},{2,3},{3,4},{4,5},{5,6},{6,7},{7,8},{8,9},{9,10},{10,1... | collective-permute-start | bytes 1572872 | tf_op jit(solution)/shard_map/ppermute | solution.py:24
  151.5 2.1 collective-permute-start.10
  153.7 9.6 %collective-permute-done.9.before = f32[8,64,256]{2,1,0:T(8,128)S(1)} collective-permute-done((f32[8,64,256]{2,1,0:T(8,128)S(1)}, f32[8,64,256]{2,1,0:T(8,128)S(1)}, u32[]{:S(2)}, u32[]{:S(2)}) %collective-permute-start.9) | collective-permute-done | bytes 524320 | tf_op jit(solution)/shard_map/ppermute | solution.py:24
  163.6 5.5 %last.1 = f32[8,16,8,256]{3,2,1,0:T(8,128)S(1)} custom-call(s32[101]{0:T(128)S(1)} %pad_add_fusion.1.ints, f32[132]{0:T(256)S(1)} %pad_maximum_fusion.2.floats, f32[16,64,256]{2,1,0:T(8,128)S(1)} %get-tuple-element.44.u, f32[16,64,256]{2,1,0:T(8,128)S(1)} %get-tuple-element.45.vu, f32[16,64,256]{2,1,0:T(8,128)S(1)} %get-tuple-element.46.w, ...), custom_call_target="tpu_custom_call" | custom-call | tf_op jit(solution)/shard_map/last/pallas_call | solution.py:45
  169.1 24.1 %all_to_all.30.got = f32[32,4,8,256]{3,2,1,0:T(8,128)S(1)} all-to-all(f32[32,4,8,256]{3,2,1,0:T(8,128)S(1)} %bitcast.36), channel_id=1, replica_groups=mesh['shot'=8,'zz'=8,'quad'=4] {'shot','quad'}, dimensions={0} | all-to-all | bytes 2097152 | tf_op jit(solution)/shard_map/all_to_all | solution.py:298
  195.0 8.2 %all_to_all.31.extra = f32[4,4,8,256]{3,2,1,0:T(8,128)S(1)} all-to-all(f32[4,4,8,256]{3,2,1,0:T(8,128)S(1)} %get-tuple-element.52), channel_id=1, replica_groups=mesh['shot'=8,'zz'=8,'quad'=4] {'quad'}, dimensions={0} | all-to-all | bytes 262144 | tf_op jit(solution)/shard_map/all_to_all | solution.py:298
  203.2 31.7 %all_to_all.32.came = f32[32,4,8,256]{3,2,1,0:T(8,128)S(1)} all-to-all(f32[32,4,8,256]{3,2,1,0:T(8,128)S(1)} %get-tuple-element.51), channel_id=1, replica_groups=mesh['shot'=8,'zz'=8,'quad'=4] {'zz','quad'}, dimensions={0} | all-to-all | bytes 2097152 | tf_op jit(solution)/shard_map/all_to_all | solution.py:298
  (63 shorter events, 30.0 us)
Async XLA Ops:
  1.6 11.6 %all-to-all-start.1 = ((f32[4,4,8,256]{3,2,1,0:T(8,128)}), f32[4,4,8,256]{3,2,1,0:T(8,128)S(1)}, u32[]{:S(2)}, u32[]{:S(2)}) async-start(f32[4,4,8,256]{3,2,1,0:T(8,128)} %bitcast.17), calls=%async_computation.1 | async-start | bytes 262144 | tf_op jit(solution)/shard_map/all_to_all | solution.py:298
  13.2 37.2 %all-to-all-start = ((f32[32,4,8,256]{3,2,1,0:T(8,128)}), f32[32,4,8,256]{3,2,1,0:T(8,128)S(1)}, u32[]{:S(2)}, u32[]{:S(2)}) async-start(f32[32,4,8,256]{3,2,1,0:T(8,128)} %broadcast_select_fusion), calls=%async_computation | async-start | bytes 2097152 | tf_op jit(solution)/shard_map/all_to_all | solution.py:298
  23.0 2.5 %collective-permute-start = (s32[8]{0:T(128)S(1)}, s32[8]{0:T(128)S(1)}, u32[]{:S(2)}, u32[]{:S(2)}) collective-permute-start(s32[8]{0:T(128)S(1)} %compare_select_fusion), channel_id=1, source_target_pairs={{0,32},{32,0},{64,96},{96,64},{128,160},{160,128},{192,224},{224,1... | collective-permute-start | bytes 104 | tf_op jit(solution)/shard_map/ppermute | solution.py:33
  25.5 4.2 %collective-permute-start.1 = (s32[8]{0:T(128)S(1)}, s32[8]{0:T(128)S(1)}, u32[]{:S(2)}, u32[]{:S(2)}) collective-permute-start(s32[8]{0:T(128)S(1)} %fusion), channel_id=1, source_target_pairs={{0,64},{32,96},{64,0},{96,32},{128,192},{160,224},{192,128},{224,1... | collective-permute-start | bytes 104 | tf_op jit(solution)/shard_map/ppermute | solution.py:33
  29.7 2.7 %collective-permute-start.2 = (s32[8]{0:T(128)S(1)}, s32[8]{0:T(128)S(1)}, u32[]{:S(2)}, u32[]{:S(2)}) collective-permute-start(s32[8]{0:T(128)S(1)} %fusion.1), channel_id=1, source_target_pairs={{0,128},{32,160},{64,192},{96,224},{128,0},{160,32},{192,64},{224,... | collective-permute-start | bytes 104 | tf_op jit(solution)/shard_map/ppermute | solution.py:33
  32.5 28.8 %copy-start = (f32[1,16,64,256]{3,2,1,0:T(8,128)S(1)}, f32[1,16,64,256]{3,2,1,0:T(8,128)}, u32[]{:S(2)}) copy-start(f32[1,16,64,256]{3,2,1,0:T(8,128)} %param.19) | copy-start | bytes 3145732
  32.5 28.8 %copy-start.1 = (f32[1,16,64,256]{3,2,1,0:T(8,128)S(1)}, f32[1,16,64,256]{3,2,1,0:T(8,128)}, u32[]{:S(2)}) copy-start(f32[1,16,64,256]{3,2,1,0:T(8,128)} %param.21) | copy-start | bytes 3145732
  53.1 40.8 %all-to-all-start.2 = ((f32[32,4,8,256]{3,2,1,0:T(8,128)}), f32[32,4,8,256]{3,2,1,0:T(8,128)S(1)}, u32[]{:S(2)}, u32[]{:S(2)}) async-start(f32[32,4,8,256]{3,2,1,0:T(8,128)} %copy-done.2), calls=%async_computation.2 | async-start | bytes 2097152 | tf_op jit(solution)/shard_map/all_to_all | solution.py:298
  61.4 9.4 %copy-start.10 = (f32[1,4,32]{2,1,0:T(4,128)S(1)}, f32[1,4,32]{2,1,0:T(4,128)}, u32[]{:S(2)}) copy-start(f32[1,4,32]{2,1,0:T(4,128)} %param.16) | copy-start | bytes 1540
  61.4 9.5 %copy-start.11 = (s32[1,32,3]{1,0,2:T(1,128)S(1)}, s32[1,32,3]{1,0,2:T(1,128)}, u32[]{:S(2)}) copy-start(s32[1,32,3]{1,0,2:T(1,128)} %param.15) | copy-start | bytes 1156
  61.4 9.7 %copy-start.12 = (s32[1,3]{1,0:T(1,128)S(1)}, s32[1,3]{1,0:T(1,128)}, u32[]{:S(2)}) copy-start(s32[1,3]{1,0:T(1,128)} %param.13) | copy-start | bytes 40
  61.4 9.8 %copy-start.13 = (f32[1,4]{1,0:T(1,128)S(1)}, f32[1,4]{1,0:T(1,128)}, u32[]{:S(2)}) copy-start(f32[1,4]{1,0:T(1,128)} %param.14) | copy-start | bytes 52
  62.3 24.2 %collective-permute-start.3 = (f32[8,64,256]{2,1,0:T(8,128)}, f32[8,64,256]{2,1,0:T(8,128)}, u32[]{:S(2)}, u32[]{:S(2)}) collective-permute-start(f32[8,64,256]{2,1,0:T(8,128)} %pad_maximum_fusion), channel_id=1, source_target_pairs={{0,1},{1,2},{2,3},{3,4},{4,5},{5,6},{6,7},{7,8},{8,9},{9,10},{10,1... | collective-permute-start | bytes 1572872 | tf_op jit(solution)/shard_map/ppermute | solution.py:24
  68.2 18.3 %collective-permute-start.4 = (f32[8,64,256]{2,1,0:T(8,128)}, f32[8,64,256]{2,1,0:T(8,128)}, u32[]{:S(2)}, u32[]{:S(2)}) collective-permute-start(f32[8,64,256]{2,1,0:T(8,128)} %pad_maximum_fusion.1), channel_id=1, source_target_pairs={{1,0},{2,1},{3,2},{4,3},{5,4},{6,5},{7,6},{8,7},{9,8},{10,9},{11,1... | collective-permute-start | bytes 1572872 | tf_op jit(solution)/shard_map/ppermute | solution.py:24
  93.9 1.2 copy-start.4
  95.1 1.2 copy-start.6
  97.6 1.2 copy-start.9
  100.3 17.6 %collective-permute-start.5 = (f32[8,64,256]{2,1,0:T(8,128)S(1)}, f32[8,64,256]{2,1,0:T(8,128)S(1)}, u32[]{:S(2)}, u32[]{:S(2)}) collective-permute-start(f32[8,64,256]{2,1,0:T(8,128)S(1)} %get-tuple-element.35), channel_id=1, source_target_pairs={{0,1},{1,2},{2,3},{3,4},{4,5},{5,6},{6,7},{7,8},{8,9},{9,10},{10,1... | collective-permute-start | bytes 1572872 | tf_op jit(solution)/shard_map/ppermute | solution.py:24
  106.2 12.0 %collective-permute-start.6 = (f32[8,64,256]{2,1,0:T(8,128)S(1)}, f32[8,64,256]{2,1,0:T(8,128)S(1)}, u32[]{:S(2)}, u32[]{:S(2)}) collective-permute-start(f32[8,64,256]{2,1,0:T(8,128)S(1)} %get-tuple-element.36), channel_id=1, source_target_pairs={{1,0},{2,1},{3,2},{4,3},{5,4},{6,5},{7,6},{8,7},{9,8},{10,9},{11,1... | collective-permute-start | bytes 1572872 | tf_op jit(solution)/shard_map/ppermute | solution.py:24
  123.6 16.4 %collective-permute-start.7 = (f32[8,64,256]{2,1,0:T(8,128)S(1)}, f32[8,64,256]{2,1,0:T(8,128)S(1)}, u32[]{:S(2)}, u32[]{:S(2)}) collective-permute-start(f32[8,64,256]{2,1,0:T(8,128)S(1)} %get-tuple-element.41), channel_id=1, source_target_pairs={{0,1},{1,2},{2,3},{3,4},{4,5},{5,6},{6,7},{7,8},{8,9},{9,10},{10,1... | collective-permute-start | bytes 1572872 | tf_op jit(solution)/shard_map/ppermute | solution.py:24
  129.2 12.0 %collective-permute-start.8 = (f32[8,64,256]{2,1,0:T(8,128)S(1)}, f32[8,64,256]{2,1,0:T(8,128)S(1)}, u32[]{:S(2)}, u32[]{:S(2)}) collective-permute-start(f32[8,64,256]{2,1,0:T(8,128)S(1)} %get-tuple-element.42), channel_id=1, source_target_pairs={{1,0},{2,1},{3,2},{4,3},{5,4},{6,5},{7,6},{8,7},{9,8},{10,9},{11,1... | collective-permute-start | bytes 1572872 | tf_op jit(solution)/shard_map/ppermute | solution.py:24
  141.2 22.4 %copy-start.5 = (f32[16,64,256]{2,1,0:T(8,128)S(1)}, f32[16,64,256]{2,1,0:T(8,128)}, u32[]{:S(2)}) copy-start(f32[16,64,256]{2,1,0:T(8,128)} %copy-done.3) | copy-start | bytes 3145732
  146.9 16.4 %collective-permute-start.9 = (f32[8,64,256]{2,1,0:T(8,128)S(1)}, f32[8,64,256]{2,1,0:T(8,128)S(1)}, u32[]{:S(2)}, u32[]{:S(2)}) collective-permute-start(f32[8,64,256]{2,1,0:T(8,128)S(1)} %get-tuple-element.48), channel_id=1, source_target_pairs={{0,1},{1,2},{2,3},{3,4},{4,5},{5,6},{6,7},{7,8},{8,9},{9,10},{10,1... | collective-permute-start | bytes 1572872 | tf_op jit(solution)/shard_map/ppermute | solution.py:24
  151.5 12.0 %collective-permute-start.10 = (f32[8,64,256]{2,1,0:T(8,128)S(1)}, f32[8,64,256]{2,1,0:T(8,128)S(1)}, u32[]{:S(2)}, u32[]{:S(2)}) collective-permute-start(f32[8,64,256]{2,1,0:T(8,128)S(1)} %get-tuple-element.49), channel_id=1, source_target_pairs={{1,0},{2,1},{3,2},{4,3},{5,4},{6,5},{7,6},{8,7},{9,8},{10,9},{11,1... | collective-permute-start | bytes 1572872 | tf_op jit(solution)/shard_map/ppermute | solution.py:24
  (4 other events, 4.2 us)

commit v3 on v2

v3 whole, which is shorter than its diff:
```python
import functools

import jax
import jax.numpy as jnp
from jax import lax
from jax.experimental import pallas as pl
from jax.experimental.pallas import tpu as pltpu
from jax.sharding import Mesh, PartitionSpec as P

COEF = (-205.0 / 72.0, 1.6, -0.2, 8.0 / 315.0, -1.0 / 560.0)
QUAD = 4
MP = ("zz", "quad")
PLANE = ("shot", "quad")
LANES = 128
SUB = 8
REACH = 4
COUNT, BASE, SOURCE, RECEIVERS = 0, 1, 2, 5
VMEM_LIMIT = 16 << 20


def shifted(value, axes, steps):
    count = lax.axis_size(axes)
    pairs = [(i, i + steps) for i in range(count) if 0 <= i + steps < count]
    return lax.ppermute(value, axes, pairs)


def all_first(first):
    shots = lax.axis_size("shot")
    me = lax.axis_index("shot")
    known = jnp.where(jnp.arange(shots, dtype=jnp.int32) == me, first, 0)
    step = 1
    while step < shots:
        known = known + lax.ppermute(known, "shot", [(i, i ^ step) for i in range(shots)])
        step *= 2
    return known


def f32(*shape):
    return jax.ShapeDtypeStruct(shape, jnp.float32)


def local_kernel(body, name, scalars, arrays, outs, scratch=()):
    vmem = pl.BlockSpec(memory_space=pltpu.VMEM)
    smem = pl.BlockSpec(memory_space=pltpu.SMEM)
    return pl.pallas_call(
        body,
        out_shape=outs,
        in_specs=[smem] * len(scalars) + [vmem] * len(arrays),
        out_specs=[vmem] * len(outs),
        scratch_shapes=list(scratch),
        compiler_params=pltpu.CompilerParams(vmem_limit_bytes=VMEM_LIMIT),
        name=name,
    )(*scalars, *arrays)


def in_hbm(value):
    return pltpu.with_memory_space_constraint(value, pltpu.HBM)


def band_matrix(nz):
    rows = lax.broadcasted_iota(jnp.int32, (nz, nz), 0)
    cols = lax.broadcasted_iota(jnp.int32, (nz, nz), 1)
    apart = jnp.abs(rows - cols)
    band = jnp.where(apart == 0, 3.0 * COEF[0], 0.0)
    for k in range(1, REACH + 1):
        band = jnp.where(apart == k, COEF[k], band)
    return band


def prepare(field, padded, along_z):
    xs, ys, nz = field.shape
    along_z[...] = jnp.dot(
        field[...].reshape(xs * ys, nz),
        band_matrix(nz),
        precision=lax.Precision.HIGHEST,
        preferred_element_type=jnp.float32,
    ).reshape(xs, ys, nz)
    edge = jnp.zeros((xs, SUB, LANES), jnp.float32)
    for h in range(nz // LANES):
        padded[h, :, 0:SUB, :] = edge
        padded[h, :, SUB + ys : SUB + ys + SUB, :] = edge
        padded[h, :, SUB : SUB + ys, :] = field[:, :, h * LANES : (h + 1) * LANES]


def add_point(target, x, y, z, amount):
    xs, _, nz = target.shape

    @pl.when((x >= 0) & (x < xs))
    def _():
        cells = lax.broadcasted_iota(jnp.int32, (1, 1, nz), 2)
        place = (pl.ds(x, 1), pl.ds(y, 1), slice(None))
        target[place] = target[place] + jnp.where(cells == z, amount, 0.0)


def add_source(target, ints, floats, n):
    x = ints[SOURCE] - ints[BASE]
    add_point(target, x, ints[SOURCE + 1], ints[SOURCE + 2], floats[n])


def add_receivers(target, ints, floats, steps, receivers, n):
    def one(j, carry):
        at = RECEIVERS + 3 * j
        amount = floats[steps + n * receivers + j]
        add_point(target, ints[at] - ints[BASE], ints[at + 1], ints[at + 2], amount)
        return carry

    lax.fori_loop(0, receivers, one, 0)


def laplacian(padded, along_z, before, after, y0, h):
    xs = along_z.shape[0]
    rows = pl.ds(y0, SUB)
    lanes = slice(h * LANES, (h + 1) * LANES)
    column = [before[j, rows, lanes] for j in range(REACH)]
    column += [padded[h, x, pl.ds(y0 + SUB, SUB), :] for x in range(xs)]
    column += [after[j, rows, lanes] for j in range(REACH)]
    for x in range(xs):
        total = along_z[x, rows, lanes]
        for k in range(1, REACH + 1):
            pair = column[x + REACH + k] + column[x + REACH - k]
            pair = pair + (
                padded[h, x, pl.ds(y0 + SUB + k, SUB), :]
                + padded[h, x, pl.ds(y0 + SUB - k, SUB), :]
            )
            total = total + COEF[k] * pair
        yield x, column[x + REACH], total


def each_block(field, work):
    _, ys, nz = field.shape

    def step(i, carry):
        y0 = pl.multiple_of(i * SUB, SUB)
        for h in range(nz // LANES):
            work(i, y0, h, slice(h * LANES, (h + 1) * LANES))
        return carry

    lax.fori_loop(0, ys // SUB, step, 0)


def switch_on(ints, n):
    return jnp.where(ints[COUNT] > n, 1.0, 0.0).astype(jnp.float32)


def first_kernel(steps, receivers, kind, ints, floats, field, before, after, out, pad):
    prepare(field, pad, out)
    if kind == "forward":
        add_source(out, ints, floats, 0)
        live = switch_on(ints, 0)
    else:
        add_receivers(out, ints, floats, steps, receivers, steps - 1)
        live = switch_on(ints, steps - 1)

    def work(i, y0, h, lanes):
        rows = pl.ds(y0, SUB)
        for x, _, total in laplacian(pad, out, before, after, y0, h):
            out[x, rows, lanes] = live * total

    each_block(field, work)


def send_planes(low, high, x, xs, rows, lanes, value):
    if x < REACH:
        low[x, rows, lanes] = value
    if x >= xs - REACH:
        high[x - (xs - REACH), rows, lanes] = value


def advance_kernel(n, ints, now, back, drive, speed, new, gain, low, high):
    xs = now.shape[0]
    live = switch_on(ints, n)

    def work(i, y0, h, lanes):
        rows = pl.ds(y0, SUB)
        for x in range(xs):
            here = now[x, rows, lanes]
            more = (here - back[x, rows, lanes]) + speed[i, x, :, lanes] * drive[x, rows, lanes]
            gain[x, rows, lanes] = more
            here = here + live * more
            new[x, rows, lanes] = here
            send_planes(low, high, x, xs, rows, lanes, here)

    each_block(now, work)


def forward_kernel(n, last, ints, floats, u, vu, p, before, after, drive, *rest):
    if last:
        pad, along = rest
    else:
        new, gain, low, high, pad, along = rest
    xs = u.shape[0]
    prepare(u, pad, along)
    add_source(along, ints, floats, n)
    live = switch_on(ints, n)

    def work(i, y0, h, lanes):
        rows = pl.ds(y0, SUB)
        for x, here, total in laplacian(pad, along, before, after, y0, h):
            total = live * total
            drive[x, rows, lanes] = total
            if last:
                continue
            more = vu[x, rows, lanes] + p[i, x, :, lanes] * total
            gain[x, rows, lanes] = more
            here = here + more
            new[x, rows, lanes] = here
            send_planes(low, high, x, xs, rows, lanes, here)

    each_block(u, work)


def adjoint_kernel(steps, receivers, n, last, ints, floats, w, vw, p, before, after, *rest):
    if last:
        partial, drive, image, pad, along = rest
    else:
        new, gain, low, high, pad, along = rest
    xs = w.shape[0]
    prepare(w, pad, along)
    add_receivers(along, ints, floats, steps, receivers, n)
    live = switch_on(ints, n)

    def work(i, y0, h, lanes):
        rows = pl.ds(y0, SUB)
        for x, here, total in laplacian(pad, along, before, after, y0, h):
            more = vw[x, rows, lanes] + (live * p[i, x, :, lanes]) * total
            here = here + live * more
            if last:
                image[i, x, :, lanes] = partial[x, rows, lanes] + here * drive[x, rows, lanes]
                continue
            gain[x, rows, lanes] = more
            new[x, rows, lanes] = here
            send_planes(low, high, x, xs, rows, lanes, here)

    each_block(w, work)


def products_kernel(pairs, *refs):
    out = refs[-1]

    def work(i, y0, h, lanes):
        rows = pl.ds(y0, SUB)
        for x in range(out.shape[0]):
            total = refs[0][x, rows, lanes] * refs[1][x, rows, lanes]
            for j in range(1, pairs):
                total = total + refs[2 * j][x, rows, lanes] * refs[2 * j + 1][x, rows, lanes]
            out[x, rows, lanes] = total

    each_block(out, work)


def split_kernel(spot, courant, parts, *rest):
    extras, sems = rest[:QUAD], rest[QUAD]
    zs = parts.shape[0]
    _, planes, slab, _ = extras[0].shape
    me_shot, me_z, me_q = spot[0], spot[1], spot[2]
    rows = pl.ds(pl.multiple_of(me_shot * slab, SUB), slab)
    copies = []
    for z in range(zs):
        row = jnp.where(z <= me_z, 0, 1)
        copies.append(
            pltpu.make_async_copy(courant.at[row, :, rows, :], parts.at[z], sems.at[z])
        )
    for r in range(QUAD):
        to = ((me_q + r) % QUAD) * planes
        copies.append(
            pltpu.make_async_copy(
                courant.at[1, pl.ds(to, planes), rows, :], extras[r].at[0], sems.at[zs + r]
            )
        )
    for copy in copies:
        copy.start()
    for copy in copies:
        copy.wait()


def gather_kernel(zs, table, spot, line, *rest):
    extras, sent, sems = rest[:QUAD], rest[QUAD], rest[QUAD + 1]
    slots = sent.shape[0]
    me_z, me_q = spot[1], spot[2]
    for slot in range(slots):
        tile = table[slot // QUAD] + slot % QUAD
        place = ((me_z + tile // QUAD) % zs) * QUAD + tile % QUAD
        turn = (me_q + QUAD - tile % QUAD) % QUAD
        near = tile < zs * QUAD

        @pl.when(near)
        def _():
            pltpu.make_async_copy(line.at[place], sent.at[slot], sems.at[slot]).start()

        for r in range(QUAD):

            @pl.when(jnp.logical_not(near) & (turn == r))
            def _():
                pltpu.make_async_copy(extras[r].at[0], sent.at[slot], sems.at[slot]).start()

    for slot in range(slots):
        pltpu.make_async_copy(line.at[0], sent.at[slot], sems.at[slot]).wait()


def scatter_kernel(zs, table, spot, got, line, *rest):
    extras, held = rest[:QUAD], rest[QUAD]
    me_z, me_q = spot[1], spot[2]
    line[...] = jnp.zeros_like(line)
    held[...] = jnp.zeros_like(held)

    def one(slot, carry):
        tile = table[slot // QUAD] + slot % QUAD
        place = ((me_z + tile // QUAD) % zs) * QUAD + tile % QUAD
        turn = (tile % QUAD + QUAD - me_q) % QUAD

        @pl.when(tile < zs * QUAD)
        def _():
            line[place] = line[place] + got[slot]

        @pl.when(tile >= zs * QUAD)
        def _():
            held[turn] = held[turn] + got[slot]

        return carry

    lax.fori_loop(0, got.shape[0], one, 0)
    for r in range(QUAD):
        extras[r][0] = held[r]


def finish_kernel(zs, spot, came, *rest):
    extras, out = rest[:QUAD], rest[QUAD]
    planes = came.shape[1]
    me_z, me_q = spot[1], spot[2]
    for r in range(QUAD):
        q = (me_q + QUAD - r) % QUAD
        low = came[q]
        high = extras[r][0]
        for z in range(1, zs):
            value = came[z * QUAD + q]
            low = low + jnp.where(z <= me_z, value, 0.0)
            high = high + jnp.where(z <= me_z, 0.0, value)
        out[0, pl.ds(q * planes, planes)] = low
        out[1, pl.ds(q * planes, planes)] = high


def exchange(parts, axes):
    return lax.all_to_all(parts, axes, split_axis=0, concat_axis=0, tiled=True)


def quad_turn(extras):
    turned = [extras[0]]
    for r in range(1, QUAD):
        pairs = [(q, (q + r) % QUAD) for q in range(QUAD)]
        turned.append(lax.ppermute(extras[r], "quad", pairs))
    return turned


def model_line(courant, spot):
    _, tile_x, ny, nz = courant.shape
    zs = lax.axis_size("zz")
    slab = ny // lax.axis_size("shot")
    planes = tile_x // QUAD
    hbm = pl.BlockSpec(memory_space=pltpu.HBM)
    parts, *extras = pl.pallas_call(
        split_kernel,
        out_shape=[f32(zs, tile_x, slab, nz)] + [f32(1, planes, slab, nz)] * QUAD,
        in_specs=[pl.BlockSpec(memory_space=pltpu.SMEM), hbm],
        out_specs=[hbm] * (1 + QUAD),
        scratch_shapes=[pltpu.SemaphoreType.DMA((zs + QUAD,))],
        compiler_params=pltpu.CompilerParams(vmem_limit_bytes=1 << 20),
        name="split",
    )(spot, in_hbm(courant))
    line = exchange(parts.reshape(zs * QUAD, planes, slab, nz), MP)
    return line, quad_turn(extras)


def model_parts(line, extras, table, spot):
    slots = lax.axis_size("shot") * QUAD
    smem = pl.BlockSpec(memory_space=pltpu.SMEM)
    anywhere = pl.BlockSpec(memory_space=pl.ANY)
    return pl.pallas_call(
        functools.partial(gather_kernel, lax.axis_size("zz")),
        out_shape=f32(slots, *line.shape[1:]),
        in_specs=[smem, smem] + [anywhere] * (1 + QUAD),
        out_specs=pl.BlockSpec(memory_space=pltpu.HBM),
        scratch_shapes=[pltpu.SemaphoreType.DMA((slots,))],
        compiler_params=pltpu.CompilerParams(vmem_limit_bytes=1 << 20),
        name="gather",
    )(table, spot, line, *extras)


def return_image(image, table, spot):
    shots, tile_x, slab, nz = image.shape
    zs = lax.axis_size("zz")
    planes = tile_x // QUAD
    got = exchange(image.reshape(shots * QUAD, planes, slab, nz), PLANE)
    line, *extras = local_kernel(
        functools.partial(scatter_kernel, zs),
        "scatter",
        [table, spot],
        [got],
        [f32(zs * QUAD, planes, slab, nz)] + [f32(1, planes, slab, nz)] * QUAD,
        [pltpu.VMEM((QUAD, planes, slab, nz), jnp.float32)],
    )
    extras = quad_turn(extras)
    came = exchange(line, MP)
    (out,) = local_kernel(
        functools.partial(finish_kernel, zs),
        "finish",
        [spot],
        [came, *extras],
        [f32(2, tile_x, slab, nz)],
    )
    return out


def advance(n, name, ints, now, back, drive, speed):
    tile_x, ny, nz = now.shape
    rows = 2 * SUB
    block = pl.BlockSpec((tile_x, rows, nz), lambda i: (0, i, 0))
    side = pl.BlockSpec((REACH, rows, nz), lambda i: (0, i, 0))
    return pl.pallas_call(
        functools.partial(advance_kernel, n),
        grid=(ny // rows,),
        out_shape=[f32(tile_x, ny, nz)] * 2 + [f32(REACH, ny, nz)] * 2,
        in_specs=[
            pl.BlockSpec(memory_space=pltpu.SMEM),
            block,
            block,
            block,
            pl.BlockSpec((2, tile_x, SUB, nz), lambda i: (i, 0, 0, 0)),
        ],
        out_specs=[block, block, side, side],
        compiler_params=pltpu.CompilerParams(vmem_limit_bytes=VMEM_LIMIT),
        name=name,
    )(ints, in_hbm(now), in_hbm(back), in_hbm(drive), speed)


def halos(low, high):
    return shifted(high, MP, 1), shifted(low, MP, -1)


def body(
    courant,
    aperture_first,
    source_pos,
    wavelet,
    receiver_pos,
    residual,
    step_count,
    forward_prev,
    forward_now,
    adjoint_prev,
    adjoint_now,
):
    tile_x, ny, nz = forward_now.shape[1:]
    steps = wavelet.shape[1]
    receivers = receiver_pos.shape[1]
    spot = [lax.axis_index(name) for name in ("shot", "zz", "quad")]
    spot = jnp.stack(spot).astype(jnp.int32)
    line, extras = model_line(courant, spot)
    table = all_first(aperture_first[0])
    base = (lax.axis_index(MP) * tile_x).reshape(1).astype(jnp.int32)
    ints = jnp.concatenate([step_count, base, source_pos[0], receiver_pos[0].reshape(-1)])
    floats = jnp.concatenate([wavelet[0], residual[0].reshape(-1)])
    u, w = forward_now[0], adjoint_now[0]
    field = f32(tile_x, ny, nz)
    edge = f32(REACH, ny, nz)
    padded = pltpu.VMEM((nz // LANES, tile_x, ny + 2 * SUB, LANES), jnp.float32)
    along = pltpu.VMEM((tile_x, ny, nz), jnp.float32)
    scalars = [ints, floats]
    u_sides = halos(u[:REACH], u[tile_x - REACH :])
    w_sides = halos(w[:REACH], w[tile_x - REACH :])
    drives = []
    (drive,) = local_kernel(
        functools.partial(first_kernel, steps, receivers, "forward"),
        "first_forward",
        scalars,
        [u, *u_sides],
        [field],
        [padded],
    )
    (push,) = local_kernel(
        functools.partial(first_kernel, steps, receivers, "adjoint"),
        "first_adjoint",
        scalars,
        [w, *w_sides],
        [field],
        [padded],
    )
    sent = model_parts(line, extras, table, spot)
    sent, drive, push = lax.optimization_barrier((sent, drive, push))
    owned = exchange(sent, PLANE).reshape(-1, tile_x, SUB, nz)
    drives.append(drive)
    u, vu, low, high = advance(0, "advance_forward", ints, u, forward_prev[0], drive, owned)
    u_sides = halos(low, high)
    w, vw, low, high = advance(steps - 1, "advance_adjoint", ints, w, adjoint_prev[0], push, owned)
    w_sides = halos(low, high)
    backs = [w]
    for n in range(1, steps):
        last = n == steps - 1
        drive, *moved = local_kernel(
            functools.partial(forward_kernel, n, last),
            "forward",
            scalars,
            [u, vu, owned, *u_sides],
            [field] if last else [field, field, field, edge, edge],
            [padded, along],
        )
        drives.append(drive)
        if not last:
            u, vu, low, high = moved
            u_sides = halos(low, high)
        extra_in = []
        if last:
            pairs = []
            for k in range(steps - 1):
                pairs += [backs[k], drives[steps - 1 - k]]
            (partial,) = local_kernel(
                functools.partial(products_kernel, steps - 1), "products", [], pairs, [field]
            )
            extra_in = [partial, drives[0]]
        moved = local_kernel(
            functools.partial(adjoint_kernel, steps, receivers, steps - 1 - n, last),
            "adjoint",
            scalars,
            [w, vw, owned, *w_sides, *extra_in],
            [f32(ny // SUB, tile_x, SUB, nz)] if last else [field, field, edge, edge],
            [padded, along],
        )
        if not last:
            w, vw, low, high = moved
            w_sides = halos(low, high)
            backs.append(w)
    return return_image(moved[0], table, spot)


def solution(mesh):
    shots, mp = mesh.devices.shape
    fine = Mesh(mesh.devices.reshape(shots, mp // QUAD, QUAD), ("shot", "zz", "quad"))
    return jax.shard_map(
        body,
        mesh=fine,
        in_specs=(
            P(None, MP, None, None),
            P("shot"),
            P("shot", None),
            P("shot", None),
            P("shot", None, None),
            P("shot", None, None),
            P("shot"),
            P("shot", MP, None, None),
            P("shot", MP, None, None),
            P("shot", MP, None, None),
            P("shot", MP, None, None),
        ),
        out_specs=P(None, MP, "shot", None),
        check_vma=False,
    )
```

time: 237 us -> 236 us (level)
  starting transfers between devices: 57.3 us -> 99.3 us
  waiting for transfers between devices: 70.9 us -> 33.5 us
  Pallas kernels: 27.8 us -> 42.4 us
  blocking collectives: 64 us -> 51.8 us
  local copies, waits for them, and re-layouts: 11.1 us -> 5.57 us
    ppermute x8 -> x16, waiting for transfers between devices: 45.3 us -> 4.95 us  [shifted(): return lax.ppermute(value, axes, pairs)]
    ppermute x8 -> x16, starting transfers between devices: 29 us -> 58.4 us  [shifted(): return lax.ppermute(value, axes, pairs)]
    pallas_call x0 -> x4, Pallas kernels: none -> 13.2 us  [the longest x2 5.88 us: advance(): pl.pallas_call(functools.partial(advance_kernel, n), grid=(ny // rows,),...]
    all_to_all x3 -> x2, blocking collectives: 64 us -> 51.8 us  [exchange(): return lax.all_to_all(parts, axes, split_axis=0, concat_axis=0, tiled=True)]
    ppermute x0 -> x6, starting transfers between devices: none -> 9.01 us  [quad_turn(): turned.append(lax.ppermute(extras[r], 'quad', pairs))]
    ppermute x0 -> x6, waiting for transfers between devices: none -> 4.76 us  [quad_turn(): turned.append(lax.ppermute(extras[r], 'quad', pairs))]
    unnamed x29 -> x21, local copies, waits for them, and re-layouts: 7.94 us -> 3.68 us
    all_to_all x3 -> x2, starting transfers between devices: 23.9 us -> 27.7 us  [exchange(): return lax.all_to_all(parts, axes, split_axis=0, concat_axis=0, tiled=True)]
  transfers between devices with their start and end apart: 14 -> 27, of which waited for: 12 -> 8; matrix products, arithmetic and copies ran while one was open for 2% -> 1% of each run, Pallas kernels for 2% -> 10%
where the time goes in v3:
time: 236 us; the launch traced here: 235 us
  starting transfers between devices  99.3 us (42%)
  blocking collectives  51.8 us (22%)
  Pallas kernels  42.4 us (18%)
  waiting for transfers between devices  33.5 us (14%)
  local copies, waits for them, and re-layouts  5.57 us (2%)
    ppermute x16, starting transfers between devices, shifted(): return lax.ppermute(value, axes, pairs)  58.4 us
    all_to_all x2, blocking collectives, exchange(): return lax.all_to_all(parts, axes, split_axis=0, concat_axis=0, tiled=True)  51.8 us
    pallas_call x11, Pallas kernels, local_kernel(): pl.pallas_call(body, out_shape=outs, in_specs=[smem] * len(scalars) + [vm...  29.2 us
    all_to_all x2, starting transfers between devices, exchange(): return lax.all_to_all(parts, axes, split_axis=0, concat_axis=0, tiled=True)  27.7 us
    all_to_all x2, waiting for transfers between devices, exchange(): return lax.all_to_all(parts, axes, split_axis=0, concat_axis=0, tiled=True)  19.6 us
    ppermute x6, starting transfers between devices, quad_turn(): turned.append(lax.ppermute(extras[r], 'quad', pairs))  9.01 us
    pallas_call x2, Pallas kernels, advance(): pl.pallas_call(functools.partial(advance_kernel, n), grid=(ny // rows,),...  5.88 us
    ppermute x16, waiting for transfers between devices, shifted(): return lax.ppermute(value, axes, pairs)  4.95 us
  transfers between devices with their start and end apart: 27, of which 8 were waited for; matrix products, arithmetic and copies ran while one was open for 1% of the time, Pallas kernels for 10%

profile of v3, /device:TPU:1, one launch (start us, length us, event | category | flops | bytes accessed | tf_op | source)
XLA Modules:
  0.0 235.1 jit_solution(15684676831089560852)
XLA Ops:
  0.1 3.8 %split.1 = (f32[8,16,8,256]{3,2,1,0:T(8,128)S(1)}, f32[1,4,8,256]{3,2,1,0:T(8,128)S(1)}, f32[1,4,8,256]{3,2,1,0:T(8,128)}, f32[1,4,8,256]{3,2,1,0:T(8,128)}, f32[1,4,8,256]{3,2,1,0:T(8,128)S(1)}) custom-call(s32[3]{0:T(128)S(1)} %pad_add_fusion.spot, f32[2,16,64,256]{3,2,1,0:T(8,128)} %courant.1), custom_call_target="tpu_custom_call" | custom-call | tf_op jit(solution)/shard_map/split/pallas_call | solution.py:360
  5.5 12.9 %all-to-all-start = ((f32[32,4,8,256]{3,2,1,0:T(8,128)}), f32[32,4,8,256]{3,2,1,0:T(8,128)S(1)}, u32[]{:S(2)}, u32[]{:S(2)}) async-start(f32[32,4,8,256]{3,2,1,0:T(8,128)} %bitcast.38), calls=%async_computation | async-start | bytes 2097152 | tf_op jit(solution)/shard_map/all_to_all | solution.py:343
  21.2 5.3 %collective-permute-start.6 = (f32[4,64,256]{2,1,0:T(8,128)}, f32[4,64,256]{2,1,0:T(8,128)S(1)}, u32[]{:S(2)}, u32[]{:S(2)}) collective-permute-start(f32[4,64,256]{2,1,0:T(8,128)} %get-tuple-element.86), channel_id=1, source_target_pairs={{0,1},{1,2},{2,3},{3,4},{4,5},{5,6},{6,7},{7,8},{8,9},{9,10},{10,1... | collective-permute-start | bytes 786440 | tf_op jit(solution)/shard_map/ppermute | solution.py:24
  29.3 5.1 %collective-permute-start.8 = (f32[4,64,256]{2,1,0:T(8,128)}, f32[4,64,256]{2,1,0:T(8,128)}, u32[]{:S(2)}, u32[]{:S(2)}) collective-permute-start(f32[4,64,256]{2,1,0:T(8,128)} %get-tuple-element.84), channel_id=1, source_target_pairs={{0,1},{1,2},{2,3},{3,4},{4,5},{5,6},{6,7},{7,8},{8,9},{9,10},{10,1... | collective-permute-start | bytes 786440 | tf_op jit(solution)/shard_map/ppermute | solution.py:24
  44.5 4.9 %collective-permute-start.3 = (f32[1,4,8,256]{3,2,1,0:T(8,128)}, f32[1,4,8,256]{3,2,1,0:T(8,128)S(1)}, u32[]{:S(2)}, u32[]{:S(2)}) collective-permute-start(f32[1,4,8,256]{3,2,1,0:T(8,128)} %get-tuple-element.46), channel_id=1, source_target_pairs={{0,1},{1,2},{2,3},{3,0},{4,5},{5,6},{6,7},{7,4},{8,9},{9,10},{10,1... | collective-permute-start | bytes 98312 | tf_op jit(solution)/shard_map/ppermute | solution.py:350
  54.4 3.5 %first_adjoint.1.drive = f32[16,64,256]{2,1,0:T(8,128)S(1)} custom-call(s32[101]{0:T(128)S(1)} %pad_add_fusion.1.ints, f32[132]{0:T(256)S(1)} %pad_maximum_fusion.floats, f32[16,64,256]{2,1,0:T(8,128)S(1)} %bitcast.36, f32[4,64,256]{2,1,0:T(8,128)} %collective-permute-done.8.before, f32[4,64,256]{2,1,0:T(8,128)} %collective-permute-done.9.after), custom_call_target="tpu_custom_call" | custom-call | tf_op jit(solution)/shard_map/first_adjoint/pallas_call | solution.py:45
  58.9 3.5 %gather.1 = f32[32,4,8,256]{3,2,1,0:T(8,128)S(1)} custom-call(s32[8]{0:T(128)S(1)} %add.14.table, s32[3]{0:T(128)S(1)} %pad_add_fusion.spot, f32[32,4,8,256]{3,2,1,0:T(8,128)S(1)} %all-to-all-done.line, f32[1,4,8,256]{3,2,1,0:T(8,128)S(1)} %get-tuple-element.45.rest_0_, f32[1,4,8,256]{3,2,1,0:T(8,128)S(1)} %collective-permute-done.3.rest_1_, ...), custom_call_target="tpu_custom_call" | custom-call | tf_op jit(solution)/shard_map/gather/pallas_call | solution.py:377
  62.4 24.2 %all_to_all.20 = f32[32,4,8,256]{3,2,1,0:T(8,128)S(1)} all-to-all(f32[32,4,8,256]{3,2,1,0:T(8,128)S(1)} %gather.1), channel_id=1, replica_groups=mesh['shot'=8,'zz'=8,'quad'=4] {'shot','quad'}, dimensions={0} | all-to-all | bytes 2097152 | tf_op jit(solution)/shard_map/all_to_all | solution.py:343
  89.5 3.6 %collective-permute-start.16 = (f32[4,64,256]{2,1,0:T(8,128)S(1)}, f32[4,64,256]{2,1,0:T(8,128)S(1)}, u32[]{:S(2)}, u32[]{:S(2)}) collective-permute-start(f32[4,64,256]{2,1,0:T(8,128)S(1)} %get-tuple-element.66), channel_id=1, source_target_pairs={{0,1},{1,2},{2,3},{3,4},{4,5},{5,6},{6,7},{7,8},{8,9},{9,10},{10,1... | collective-permute-start | bytes 786440 | tf_op jit(solution)/shard_map/ppermute | solution.py:24
  95.0 3.0 %advance_adjoint.1 = (f32[16,64,256]{2,1,0:T(8,128)S(1)}, f32[16,64,256]{2,1,0:T(8,128)S(1)}, f32[4,64,256]{2,1,0:T(8,128)S(1)}, f32[4,64,256]{2,1,0:T(8,128)S(1)}) custom-call(s32[101]{0:T(128)S(1)} %pad_add_fusion.1.ints, f32[16,64,256]{2,1,0:T(8,128)} %bitcast.35, f32[16,64,256]{2,1,0:T(8,128)} %bitcast.40, f32[16,64,256]{2,1,0:T(8,128)} %copy-done.4, ...), custom_call_target="tpu_custom_call" | custom-call | tf_op jit(solution)/shard_map/advance_adjoint/pallas_call | solution.py:418
  98.0 5.1 %collective-permute-start.10 = (f32[4,64,256]{2,1,0:T(8,128)S(1)}, f32[4,64,256]{2,1,0:T(8,128)S(1)}, u32[]{:S(2)}, u32[]{:S(2)}) collective-permute-start(f32[4,64,256]{2,1,0:T(8,128)S(1)} %get-tuple-element.53), channel_id=1, source_target_pairs={{0,1},{1,2},{2,3},{3,4},{4,5},{5,6},{6,7},{7,8},{8,9},{9,10},{10,1... | collective-permute-start | bytes 786440 | tf_op jit(solution)/shard_map/ppermute | solution.py:24
  107.8 5.5 %collective-permute-start.18 = (f32[4,64,256]{2,1,0:T(8,128)S(1)}, f32[4,64,256]{2,1,0:T(8,128)S(1)}, u32[]{:S(2)}, u32[]{:S(2)}) collective-permute-start(f32[4,64,256]{2,1,0:T(8,128)S(1)} %get-tuple-element.70), channel_id=1, source_target_pairs={{0,1},{1,2},{2,3},{3,4},{4,5},{5,6},{6,7},{7,8},{8,9},{9,10},{10,1... | collective-permute-start | bytes 786440 | tf_op jit(solution)/shard_map/ppermute | solution.py:24
  115.5 3.3 %adjoint.3 = (f32[16,64,256]{2,1,0:T(8,128)S(1)}, f32[16,64,256]{2,1,0:T(8,128)S(1)}, f32[4,64,256]{2,1,0:T(8,128)S(1)}, f32[4,64,256]{2,1,0:T(8,128)S(1)}) custom-call(s32[101]{0:T(128)S(1)} %pad_add_fusion.1.ints, f32[132]{0:T(256)S(1)} %pad_maximum_fusion.floats, f32[16,64,256]{2,1,0:T(8,128)S(1)} %get-tuple-element.51.w.refs_0_, ...), custom_call_target="tpu_custom_call" | custom-call | tf_op jit(solution)/shard_map/adjoint/pallas_call | solution.py:45
  118.8 6.0 %collective-permute-start.12 = (f32[4,64,256]{2,1,0:T(8,128)S(1)}, f32[4,64,256]{2,1,0:T(8,128)S(1)}, u32[]{:S(2)}, u32[]{:S(2)}) collective-permute-start(f32[4,64,256]{2,1,0:T(8,128)S(1)} %get-tuple-element.57), channel_id=1, source_target_pairs={{0,1},{1,2},{2,3},{3,4},{4,5},{5,6},{6,7},{7,8},{8,9},{9,10},{10,1... | collective-permute-start | bytes 786440 | tf_op jit(solution)/shard_map/ppermute | solution.py:24
  129.5 6.0 %collective-permute-start.20 = (f32[4,64,256]{2,1,0:T(8,128)S(1)}, f32[4,64,256]{2,1,0:T(8,128)S(1)}, u32[]{:S(2)}, u32[]{:S(2)}) collective-permute-start(f32[4,64,256]{2,1,0:T(8,128)S(1)} %get-tuple-element.74), channel_id=1, source_target_pairs={{0,1},{1,2},{2,3},{3,4},{4,5},{5,6},{6,7},{7,8},{8,9},{9,10},{10,1... | collective-permute-start | bytes 786440 | tf_op jit(solution)/shard_map/ppermute | solution.py:24
  137.5 3.3 %adjoint.4 = (f32[16,64,256]{2,1,0:T(8,128)S(1)}, f32[16,64,256]{2,1,0:T(8,128)S(1)}, f32[4,64,256]{2,1,0:T(8,128)S(1)}, f32[4,64,256]{2,1,0:T(8,128)S(1)}) custom-call(s32[101]{0:T(128)S(1)} %pad_add_fusion.1.ints, f32[132]{0:T(256)S(1)} %pad_maximum_fusion.floats, f32[16,64,256]{2,1,0:T(8,128)S(1)} %get-tuple-element.55.w.refs_2_, ...), custom_call_target="tpu_custom_call" | custom-call | tf_op jit(solution)/shard_map/adjoint/pallas_call | solution.py:45
  140.8 6.0 %collective-permute-start.14 = (f32[4,64,256]{2,1,0:T(8,128)S(1)}, f32[4,64,256]{2,1,0:T(8,128)S(1)}, u32[]{:S(2)}, u32[]{:S(2)}) collective-permute-start(f32[4,64,256]{2,1,0:T(8,128)S(1)} %get-tuple-element.61), channel_id=1, source_target_pairs={{0,1},{1,2},{2,3},{3,4},{4,5},{5,6},{6,7},{7,8},{8,9},{9,10},{10,1... | collective-permute-start | bytes 786440 | tf_op jit(solution)/shard_map/ppermute | solution.py:24
  152.9 4.0 %collective-permute-done.15.after = f32[4,64,256]{2,1,0:T(8,128)S(1)} collective-permute-done((f32[4,64,256]{2,1,0:T(8,128)S(1)}, f32[4,64,256]{2,1,0:T(8,128)S(1)}, u32[]{:S(2)}, u32[]{:S(2)}) %collective-permute-start.15) | collective-permute-done | bytes 262176 | tf_op jit(solution)/shard_map/ppermute | solution.py:24
  156.9 3.5 %adjoint.5 = f32[8,16,8,256]{3,2,1,0:T(8,128)S(1)} custom-call(s32[101]{0:T(128)S(1)} %pad_add_fusion.1.ints, f32[132]{0:T(256)S(1)} %pad_maximum_fusion.floats, f32[16,64,256]{2,1,0:T(8,128)S(1)} %get-tuple-element.59.refs_4_.w, f32[16,64,256]{2,1,0:T(8,128)S(1)} %get-tuple-element.60.vw, f32[8,16,8,256]{3,2,1,0:T(8,128)S(1)} %bitcast.32, ...), custom_call_target="tpu_custom_call" | custom-call | tf_op jit(solution)/shard_map/adjoint/pallas_call | solution.py:45
  160.4 27.6 %all_to_all.21.got = f32[32,4,8,256]{3,2,1,0:T(8,128)S(1)} all-to-all(f32[32,4,8,256]{3,2,1,0:T(8,128)S(1)} %bitcast.37), channel_id=1, replica_groups=mesh['shot'=8,'zz'=8,'quad'=4] {'shot','quad'}, dimensions={0} | all-to-all | bytes 2097152 | tf_op jit(solution)/shard_map/all_to_all | solution.py:343
  190.8 14.8 %all-to-all-start.3 = ((f32[32,4,8,256]{3,2,1,0:T(8,128)}), f32[32,4,8,256]{3,2,1,0:T(8,128)S(1)}, u32[]{:S(2)}, u32[]{:S(2)}) async-start(f32[32,4,8,256]{3,2,1,0:T(8,128)} %get-tuple-element.78), calls=%async_computation.3 | async-start | bytes 2097152 | tf_op jit(solution)/shard_map/all_to_all | solution.py:343
  205.7 3.2 %collective-permute-start.22 = (f32[1,4,8,256]{3,2,1,0:T(8,128)S(1)}, f32[1,4,8,256]{3,2,1,0:T(8,128)S(1)}, u32[]{:S(2)}, u32[]{:S(2)}) collective-permute-start(f32[1,4,8,256]{3,2,1,0:T(8,128)S(1)} %get-tuple-element.80), channel_id=1, source_target_pairs={{0,1},{1,2},{2,3},{3,0},{4,5},{5,6},{6,7},{7,4},{8,9},{9,10},{10,1... | collective-permute-start | bytes 98312 | tf_op jit(solution)/shard_map/ppermute | solution.py:350
  209.9 3.5 %collective-permute-done.23.rest_2_ = f32[1,4,8,256]{3,2,1,0:T(8,128)S(1)} collective-permute-done((f32[1,4,8,256]{3,2,1,0:T(8,128)S(1)}, f32[1,4,8,256]{3,2,1,0:T(8,128)S(1)}, u32[]{:S(2)}, u32[]{:S(2)}) %collective-permute-start.23) | collective-permute-done | bytes 32800 | tf_op jit(solution)/shard_map/ppermute | solution.py:350
  214.1 19.6 %all-to-all-done.3.came = f32[32,4,8,256]{3,2,1,0:T(8,128)S(1)} async-done(((f32[32,4,8,256]{3,2,1,0:T(8,128)}), f32[32,4,8,256]{3,2,1,0:T(8,128)S(1)}, u32[]{:S(2)}, u32[]{:S(2)}) %all-to-all-start.3) | async-done | bytes 1048608 | tf_op jit(solution)/shard_map/all_to_all | solution.py:343
  (79 shorter events, 52.1 us)
Async XLA Ops:
  5.5 53.4 %all-to-all-start = ((f32[32,4,8,256]{3,2,1,0:T(8,128)}), f32[32,4,8,256]{3,2,1,0:T(8,128)S(1)}, u32[]{:S(2)}, u32[]{:S(2)}) async-start(f32[32,4,8,256]{3,2,1,0:T(8,128)} %bitcast.38), calls=%async_computation | async-start | bytes 2097152 | tf_op jit(solution)/shard_map/all_to_all | solution.py:343
  19.0 18.4 %collective-permute-start = (s32[8]{0:T(128)S(1)}, s32[8]{0:T(128)S(1)}, u32[]{:S(2)}, u32[]{:S(2)}) collective-permute-start(s32[8]{0:T(128)S(1)} %compare_select_fusion), channel_id=1, source_target_pairs={{0,32},{32,0},{64,96},{96,64},{128,160},{160,128},{192,224},{224,1... | collective-permute-start | bytes 104 | tf_op jit(solution)/shard_map/ppermute | solution.py:33
  21.2 28.2 %collective-permute-start.6 = (f32[4,64,256]{2,1,0:T(8,128)}, f32[4,64,256]{2,1,0:T(8,128)S(1)}, u32[]{:S(2)}, u32[]{:S(2)}) collective-permute-start(f32[4,64,256]{2,1,0:T(8,128)} %get-tuple-element.86), channel_id=1, source_target_pairs={{0,1},{1,2},{2,3},{3,4},{4,5},{5,6},{6,7},{7,8},{8,9},{9,10},{10,1... | collective-permute-start | bytes 786440 | tf_op jit(solution)/shard_map/ppermute | solution.py:24
  26.5 22.9 %collective-permute-start.7 = (f32[4,64,256]{2,1,0:T(8,128)}, f32[4,64,256]{2,1,0:T(8,128)}, u32[]{:S(2)}, u32[]{:S(2)}) collective-permute-start(f32[4,64,256]{2,1,0:T(8,128)} %get-tuple-element.85), channel_id=1, source_target_pairs={{1,0},{2,1},{3,2},{4,3},{5,4},{6,5},{7,6},{8,7},{9,8},{10,9},{11,1... | collective-permute-start | bytes 786440 | tf_op jit(solution)/shard_map/ppermute | solution.py:24
  29.3 25.1 %collective-permute-start.8 = (f32[4,64,256]{2,1,0:T(8,128)}, f32[4,64,256]{2,1,0:T(8,128)}, u32[]{:S(2)}, u32[]{:S(2)}) collective-permute-start(f32[4,64,256]{2,1,0:T(8,128)} %get-tuple-element.84), channel_id=1, source_target_pairs={{0,1},{1,2},{2,3},{3,4},{4,5},{5,6},{6,7},{7,8},{8,9},{9,10},{10,1... | collective-permute-start | bytes 786440 | tf_op jit(solution)/shard_map/ppermute | solution.py:24
  34.4 20.0 %collective-permute-start.9 = (f32[4,64,256]{2,1,0:T(8,128)}, f32[4,64,256]{2,1,0:T(8,128)}, u32[]{:S(2)}, u32[]{:S(2)}) collective-permute-start(f32[4,64,256]{2,1,0:T(8,128)} %get-tuple-element.83), channel_id=1, source_target_pairs={{1,0},{2,1},{3,2},{4,3},{5,4},{6,5},{7,6},{8,7},{9,8},{10,9},{11,1... | collective-permute-start | bytes 786440 | tf_op jit(solution)/shard_map/ppermute | solution.py:24
  44.5 14.4 %collective-permute-start.3 = (f32[1,4,8,256]{3,2,1,0:T(8,128)}, f32[1,4,8,256]{3,2,1,0:T(8,128)S(1)}, u32[]{:S(2)}, u32[]{:S(2)}) collective-permute-start(f32[1,4,8,256]{3,2,1,0:T(8,128)} %get-tuple-element.46), channel_id=1, source_target_pairs={{0,1},{1,2},{2,3},{3,0},{4,5},{5,6},{6,7},{7,4},{8,9},{9,10},{10,1... | collective-permute-start | bytes 98312 | tf_op jit(solution)/shard_map/ppermute | solution.py:350
  49.4 9.5 %collective-permute-start.4 = (f32[1,4,8,256]{3,2,1,0:T(8,128)}, f32[1,4,8,256]{3,2,1,0:T(8,128)S(1)}, u32[]{:S(2)}, u32[]{:S(2)}) collective-permute-start(f32[1,4,8,256]{3,2,1,0:T(8,128)} %get-tuple-element.47), channel_id=1, source_target_pairs={{0,2},{1,3},{2,0},{3,1},{4,6},{5,7},{6,4},{7,5},{8,10},{9,11},{10,... | collective-permute-start | bytes 98312 | tf_op jit(solution)/shard_map/ppermute | solution.py:350
  49.4 9.5 %collective-permute-start.5 = (f32[1,4,8,256]{3,2,1,0:T(8,128)}, f32[1,4,8,256]{3,2,1,0:T(8,128)S(1)}, u32[]{:S(2)}, u32[]{:S(2)}) collective-permute-start(f32[1,4,8,256]{3,2,1,0:T(8,128)} %copy-done.6), channel_id=1, source_target_pairs={{0,3},{1,0},{2,1},{3,2},{4,7},{5,4},{6,5},{7,6},{8,11},{9,8},{10,9... | collective-permute-start | bytes 98312 | tf_op jit(solution)/shard_map/ppermute | solution.py:350
  89.5 15.6 %collective-permute-start.16 = (f32[4,64,256]{2,1,0:T(8,128)S(1)}, f32[4,64,256]{2,1,0:T(8,128)S(1)}, u32[]{:S(2)}, u32[]{:S(2)}) collective-permute-start(f32[4,64,256]{2,1,0:T(8,128)S(1)} %get-tuple-element.66), channel_id=1, source_target_pairs={{0,1},{1,2},{2,3},{3,4},{4,5},{5,6},{6,7},{7,8},{8,9},{9,10},{10,1... | collective-permute-start | bytes 786440 | tf_op jit(solution)/shard_map/ppermute | solution.py:24
  93.1 12.0 %collective-permute-start.17 = (f32[4,64,256]{2,1,0:T(8,128)S(1)}, f32[4,64,256]{2,1,0:T(8,128)S(1)}, u32[]{:S(2)}, u32[]{:S(2)}) collective-permute-start(f32[4,64,256]{2,1,0:T(8,128)S(1)} %get-tuple-element.67), channel_id=1, source_target_pairs={{1,0},{2,1},{3,2},{4,3},{5,4},{6,5},{7,6},{8,7},{9,8},{10,9},{11,1... | collective-permute-start | bytes 786440 | tf_op jit(solution)/shard_map/ppermute | solution.py:24
  98.0 17.5 %collective-permute-start.10 = (f32[4,64,256]{2,1,0:T(8,128)S(1)}, f32[4,64,256]{2,1,0:T(8,128)S(1)}, u32[]{:S(2)}, u32[]{:S(2)}) collective-permute-start(f32[4,64,256]{2,1,0:T(8,128)S(1)} %get-tuple-element.53), channel_id=1, source_target_pairs={{0,1},{1,2},{2,3},{3,4},{4,5},{5,6},{6,7},{7,8},{8,9},{9,10},{10,1... | collective-permute-start | bytes 786440 | tf_op jit(solution)/shard_map/ppermute | solution.py:24
  103.2 12.3 %collective-permute-start.11 = (f32[4,64,256]{2,1,0:T(8,128)S(1)}, f32[4,64,256]{2,1,0:T(8,128)S(1)}, u32[]{:S(2)}, u32[]{:S(2)}) collective-permute-start(f32[4,64,256]{2,1,0:T(8,128)S(1)} %get-tuple-element.54), channel_id=1, source_target_pairs={{1,0},{2,1},{3,2},{4,3},{5,4},{6,5},{7,6},{8,7},{9,8},{10,9},{11,1... | collective-permute-start | bytes 786440 | tf_op jit(solution)/shard_map/ppermute | solution.py:24
  107.8 18.9 %collective-permute-start.18 = (f32[4,64,256]{2,1,0:T(8,128)S(1)}, f32[4,64,256]{2,1,0:T(8,128)S(1)}, u32[]{:S(2)}, u32[]{:S(2)}) collective-permute-start(f32[4,64,256]{2,1,0:T(8,128)S(1)} %get-tuple-element.70), channel_id=1, source_target_pairs={{0,1},{1,2},{2,3},{3,4},{4,5},{5,6},{6,7},{7,8},{8,9},{9,10},{10,1... | collective-permute-start | bytes 786440 | tf_op jit(solution)/shard_map/ppermute | solution.py:24
  113.4 13.4 %collective-permute-start.19 = (f32[4,64,256]{2,1,0:T(8,128)S(1)}, f32[4,64,256]{2,1,0:T(8,128)S(1)}, u32[]{:S(2)}, u32[]{:S(2)}) collective-permute-start(f32[4,64,256]{2,1,0:T(8,128)S(1)} %get-tuple-element.71), channel_id=1, source_target_pairs={{1,0},{2,1},{3,2},{4,3},{5,4},{6,5},{7,6},{8,7},{9,8},{10,9},{11,1... | collective-permute-start | bytes 786440 | tf_op jit(solution)/shard_map/ppermute | solution.py:24
  118.8 18.7 %collective-permute-start.12 = (f32[4,64,256]{2,1,0:T(8,128)S(1)}, f32[4,64,256]{2,1,0:T(8,128)S(1)}, u32[]{:S(2)}, u32[]{:S(2)}) collective-permute-start(f32[4,64,256]{2,1,0:T(8,128)S(1)} %get-tuple-element.57), channel_id=1, source_target_pairs={{0,1},{1,2},{2,3},{3,4},{4,5},{5,6},{6,7},{7,8},{8,9},{9,10},{10,1... | collective-permute-start | bytes 786440 | tf_op jit(solution)/shard_map/ppermute | solution.py:24
  124.8 12.7 %collective-permute-start.13 = (f32[4,64,256]{2,1,0:T(8,128)S(1)}, f32[4,64,256]{2,1,0:T(8,128)S(1)}, u32[]{:S(2)}, u32[]{:S(2)}) collective-permute-start(f32[4,64,256]{2,1,0:T(8,128)S(1)} %get-tuple-element.58), channel_id=1, source_target_pairs={{1,0},{2,1},{3,2},{4,3},{5,4},{6,5},{7,6},{8,7},{9,8},{10,9},{11,1... | collective-permute-start | bytes 786440 | tf_op jit(solution)/shard_map/ppermute | solution.py:24
  129.5 19.3 %collective-permute-start.20 = (f32[4,64,256]{2,1,0:T(8,128)S(1)}, f32[4,64,256]{2,1,0:T(8,128)S(1)}, u32[]{:S(2)}, u32[]{:S(2)}) collective-permute-start(f32[4,64,256]{2,1,0:T(8,128)S(1)} %get-tuple-element.74), channel_id=1, source_target_pairs={{0,1},{1,2},{2,3},{3,4},{4,5},{5,6},{6,7},{7,8},{8,9},{9,10},{10,1... | collective-permute-start | bytes 786440 | tf_op jit(solution)/shard_map/ppermute | solution.py:24
  135.6 13.2 %collective-permute-start.21 = (f32[4,64,256]{2,1,0:T(8,128)S(1)}, f32[4,64,256]{2,1,0:T(8,128)S(1)}, u32[]{:S(2)}, u32[]{:S(2)}) collective-permute-start(f32[4,64,256]{2,1,0:T(8,128)S(1)} %get-tuple-element.75), channel_id=1, source_target_pairs={{1,0},{2,1},{3,2},{4,3},{5,4},{6,5},{7,6},{8,7},{9,8},{10,9},{11,1... | collective-permute-start | bytes 786440 | tf_op jit(solution)/shard_map/ppermute | solution.py:24
  140.8 12.2 %collective-permute-start.14 = (f32[4,64,256]{2,1,0:T(8,128)S(1)}, f32[4,64,256]{2,1,0:T(8,128)S(1)}, u32[]{:S(2)}, u32[]{:S(2)}) collective-permute-start(f32[4,64,256]{2,1,0:T(8,128)S(1)} %get-tuple-element.61), channel_id=1, source_target_pairs={{0,1},{1,2},{2,3},{3,4},{4,5},{5,6},{6,7},{7,8},{8,9},{9,10},{10,1... | collective-permute-start | bytes 786440 | tf_op jit(solution)/shard_map/ppermute | solution.py:24
  146.8 10.1 %collective-permute-start.15 = (f32[4,64,256]{2,1,0:T(8,128)S(1)}, f32[4,64,256]{2,1,0:T(8,128)S(1)}, u32[]{:S(2)}, u32[]{:S(2)}) collective-permute-start(f32[4,64,256]{2,1,0:T(8,128)S(1)} %get-tuple-element.62), channel_id=1, source_target_pairs={{1,0},{2,1},{3,2},{4,3},{5,4},{6,5},{7,6},{8,7},{9,8},{10,9},{11,1... | collective-permute-start | bytes 786440 | tf_op jit(solution)/shard_map/ppermute | solution.py:24
  190.8 42.9 %all-to-all-start.3 = ((f32[32,4,8,256]{3,2,1,0:T(8,128)}), f32[32,4,8,256]{3,2,1,0:T(8,128)S(1)}, u32[]{:S(2)}, u32[]{:S(2)}) async-start(f32[32,4,8,256]{3,2,1,0:T(8,128)} %get-tuple-element.78), calls=%async_computation.3 | async-start | bytes 2097152 | tf_op jit(solution)/shard_map/all_to_all | solution.py:343
  208.9 4.6 %collective-permute-start.23 = (f32[1,4,8,256]{3,2,1,0:T(8,128)S(1)}, f32[1,4,8,256]{3,2,1,0:T(8,128)S(1)}, u32[]{:S(2)}, u32[]{:S(2)}) collective-permute-start(f32[1,4,8,256]{3,2,1,0:T(8,128)S(1)} %get-tuple-element.81), channel_id=1, source_target_pairs={{0,2},{1,3},{2,0},{3,1},{4,6},{5,7},{6,4},{7,5},{8,10},{9,11},{10,... | collective-permute-start | bytes 98312 | tf_op jit(solution)/shard_map/ppermute | solution.py:350
  208.9 5.3 %collective-permute-start.24 = (f32[1,4,8,256]{3,2,1,0:T(8,128)S(1)}, f32[1,4,8,256]{3,2,1,0:T(8,128)S(1)}, u32[]{:S(2)}, u32[]{:S(2)}) collective-permute-start(f32[1,4,8,256]{3,2,1,0:T(8,128)S(1)} %get-tuple-element.82), channel_id=1, source_target_pairs={{0,3},{1,0},{2,1},{3,2},{4,7},{5,4},{6,5},{7,6},{8,11},{9,8},{10,9... | collective-permute-start | bytes 98312 | tf_op jit(solution)/shard_map/ppermute | solution.py:350
  (13 other events, 158.3 us)

commit v4 on v3

v4 whole, which is shorter than its diff:
```python
import functools

import jax
import jax.numpy as jnp
from jax import lax
from jax.experimental import pallas as pl
from jax.experimental.pallas import tpu as pltpu
from jax.sharding import Mesh, PartitionSpec as P

COEF = (-205.0 / 72.0, 1.6, -0.2, 8.0 / 315.0, -1.0 / 560.0)
QUAD = 4
MP = ("zz", "quad")
PLANE = ("shot", "quad")
LANES = 128
SUB = 8
REACH = 4
COUNT, BASE, EVEN, SOURCE, RECEIVERS = 0, 1, 2, 3, 6
NEAR = 12
VMEM_LIMIT = 16 << 20


def all_first(first):
    return lax.all_gather(first, "shot", tiled=True)


def f32(*shape):
    return jax.ShapeDtypeStruct(shape, jnp.float32)


def local_kernel(body, name, scalars, arrays, outs, scratch=()):
    vmem = pl.BlockSpec(memory_space=pltpu.VMEM)
    smem = pl.BlockSpec(memory_space=pltpu.SMEM)
    return pl.pallas_call(
        body,
        out_shape=outs,
        in_specs=[smem] * len(scalars) + [vmem] * len(arrays),
        out_specs=[vmem] * len(outs),
        scratch_shapes=list(scratch),
        compiler_params=pltpu.CompilerParams(vmem_limit_bytes=VMEM_LIMIT),
        name=name,
    )(*scalars, *arrays)


def in_hbm(value):
    return pltpu.with_memory_space_constraint(value, pltpu.HBM)


def band_matrix(nz):
    rows = lax.broadcasted_iota(jnp.int32, (nz, nz), 0)
    cols = lax.broadcasted_iota(jnp.int32, (nz, nz), 1)
    apart = jnp.abs(rows - cols)
    band = jnp.where(apart == 0, 3.0 * COEF[0], 0.0)
    for k in range(1, REACH + 1):
        band = jnp.where(apart == k, COEF[k], band)
    return band


def prepare(field, padded, along_z):
    xs, ys, nz = field.shape
    along_z[...] = jnp.dot(
        field[...].reshape(xs * ys, nz),
        band_matrix(nz),
        precision=lax.Precision.HIGHEST,
        preferred_element_type=jnp.float32,
    ).reshape(xs, ys, nz)
    edge = jnp.zeros((xs, SUB, LANES), jnp.float32)
    for h in range(nz // LANES):
        padded[h, :, 0:SUB, :] = edge
        padded[h, :, SUB + ys : SUB + ys + SUB, :] = edge
        padded[h, :, SUB : SUB + ys, :] = field[:, :, h * LANES : (h + 1) * LANES]


def add_point(target, x, y, z, amount):
    xs, _, nz = target.shape

    @pl.when((x >= 0) & (x < xs))
    def _():
        cells = lax.broadcasted_iota(jnp.int32, (1, 1, nz), 2)
        place = (pl.ds(x, 1), pl.ds(y, 1), slice(None))
        target[place] = target[place] + jnp.where(cells == z, amount, 0.0)


def add_source(target, ints, floats, n):
    x = ints[SOURCE] - ints[BASE]
    add_point(target, x, ints[SOURCE + 1], ints[SOURCE + 2], floats[n])


def add_receivers(target, ints, floats, steps, receivers, n):
    xs = target.shape[0]
    away = ints[SOURCE] - ints[BASE]

    @pl.when((away + NEAR >= 0) & (away - NEAR < xs))
    def _():
        def one(j, carry):
            at = RECEIVERS + 3 * j
            amount = floats[steps + n * receivers + j]
            add_point(target, ints[at] - ints[BASE], ints[at + 1], ints[at + 2], amount)
            return carry

        lax.fori_loop(0, receivers, one, 0)


def laplacian(padded, along_z, even, inner, outer, y0, h, plane=0):
    xs = along_z.shape[0]
    rows = pl.ds(y0, SUB)
    lanes = slice(h * LANES, (h + 1) * LANES)
    near = [inner[plane + j, rows, lanes] for j in range(REACH)]
    far = [outer[plane + j, rows, lanes] for j in range(REACH)]
    column = [jnp.where(even, far[j], near[j]) for j in range(REACH)]
    column += [padded[h, x, pl.ds(y0 + SUB, SUB), :] for x in range(xs)]
    column += [jnp.where(even, near[j], far[j]) for j in range(REACH)]
    for x in range(xs):
        total = along_z[x, rows, lanes]
        for k in range(1, REACH + 1):
            pair = column[x + REACH + k] + column[x + REACH - k]
            pair = pair + (
                padded[h, x, pl.ds(y0 + SUB + k, SUB), :]
                + padded[h, x, pl.ds(y0 + SUB - k, SUB), :]
            )
            total = total + COEF[k] * pair
        yield x, column[x + REACH], total


def each_block(field, work):
    _, ys, nz = field.shape

    def step(i, carry):
        y0 = pl.multiple_of(i * SUB, SUB)
        for h in range(nz // LANES):
            work(i, y0, h, slice(h * LANES, (h + 1) * LANES))
        return carry

    lax.fori_loop(0, ys // SUB, step, 0)


def switch_on(ints, n):
    return jnp.where(ints[COUNT] > n, 1.0, 0.0).astype(jnp.float32)


def first_kernel(steps, receivers, ints, floats, u, w, inner, outer, d, e, pad_u, pad_w):
    prepare(u, pad_u, d)
    prepare(w, pad_w, e)
    add_source(d, ints, floats, 0)
    add_receivers(e, ints, floats, steps, receivers, steps - 1)
    live_u = switch_on(ints, 0)
    live_w = switch_on(ints, steps - 1)
    even = ints[EVEN] == 1

    def work(i, y0, h, lanes):
        rows = pl.ds(y0, SUB)
        for x, _, total in laplacian(pad_u, d, even, inner, outer, y0, h):
            d[x, rows, lanes] = live_u * total
        for x, _, total in laplacian(pad_w, e, even, inner, outer, y0, h, REACH):
            e[x, rows, lanes] = live_w * total

    each_block(u, work)


def edge_out(even, field, inner, outer):
    xs = field.shape[0]

    @pl.when(even)
    def _():
        inner[...] = field[xs - REACH :]
        outer[...] = field[:REACH]

    @pl.when(jnp.logical_not(even))
    def _():
        inner[...] = field[:REACH]
        outer[...] = field[xs - REACH :]


def edges_kernel(n, ints, now, back, drive, speed, inner, outer, held, sems):
    xs, ys, nz = now.shape
    live = switch_on(ints, n)
    even = ints[EVEN] == 1
    starts = (0, xs - REACH)
    copies = []
    for k, source in enumerate((now, back, drive)):
        for side, x0 in enumerate(starts):
            copies.append(
                pltpu.make_async_copy(
                    source.at[pl.ds(x0, REACH)], held.at[k, side], sems.at[k, side]
                )
            )
    for copy in copies:
        copy.start()
    for copy in copies:
        copy.wait()

    def step(i, carry):
        rows = pl.ds(pl.multiple_of(i * SUB, SUB), SUB)
        for side, x0 in enumerate(starts):
            for j in range(REACH):
                here = held[0, side, j, rows, :]
                more = (here - held[1, side, j, rows, :]) + speed[i, x0 + j] * held[2, side, j, rows, :]
                held[0, side, j, rows, :] = here + live * more
        return carry

    lax.fori_loop(0, ys // SUB, step, 0)

    @pl.when(even)
    def _():
        inner[...] = held[0, 1]
        outer[...] = held[0, 0]

    @pl.when(jnp.logical_not(even))
    def _():
        inner[...] = held[0, 0]
        outer[...] = held[0, 1]


def advance_kernel(n, ints, now, back, drive, speed, new, gain):
    live = switch_on(ints, n)

    def work(i, y0, h, lanes):
        rows = pl.ds(y0, SUB)
        for x in range(now.shape[0]):
            here = now[x, rows, lanes]
            more = (here - back[x, rows, lanes]) + speed[i, x, :, lanes] * drive[x, rows, lanes]
            gain[x, rows, lanes] = more
            new[x, rows, lanes] = here + live * more

    each_block(now, work)


def forward_kernel(n, last, ints, floats, u, vu, p, near, far, drive, *rest):
    if last:
        pad, along = rest
    else:
        new, gain, inner, outer, pad, along = rest
    prepare(u, pad, along)
    add_source(along, ints, floats, n)
    live = switch_on(ints, n)
    even = ints[EVEN] == 1

    def work(i, y0, h, lanes):
        rows = pl.ds(y0, SUB)
        for x, here, total in laplacian(pad, along, even, near, far, y0, h):
            total = live * total
            drive[x, rows, lanes] = total
            if last:
                continue
            more = vu[x, rows, lanes] + p[i, x, :, lanes] * total
            gain[x, rows, lanes] = more
            new[x, rows, lanes] = here + more

    each_block(u, work)
    if not last:
        edge_out(even, new, inner, outer)


def adjoint_kernel(steps, receivers, n, last, ints, floats, w, vw, p, near, far, *rest):
    if last:
        partial, drive, image, pad, along = rest
    else:
        new, gain, inner, outer, pad, along = rest
    prepare(w, pad, along)
    add_receivers(along, ints, floats, steps, receivers, n)
    live = switch_on(ints, n)
    even = ints[EVEN] == 1

    def work(i, y0, h, lanes):
        rows = pl.ds(y0, SUB)
        for x, here, total in laplacian(pad, along, even, near, far, y0, h):
            more = vw[x, rows, lanes] + (live * p[i, x, :, lanes]) * total
            here = here + live * more
            if last:
                image[i, x, :, lanes] = partial[x, rows, lanes] + here * drive[x, rows, lanes]
                continue
            gain[x, rows, lanes] = more
            new[x, rows, lanes] = here

    each_block(w, work)
    if not last:
        edge_out(even, new, inner, outer)


def products_kernel(pairs, *refs):
    out = refs[-1]

    def work(i, y0, h, lanes):
        rows = pl.ds(y0, SUB)
        for x in range(out.shape[0]):
            total = refs[0][x, rows, lanes] * refs[1][x, rows, lanes]
            for j in range(1, pairs):
                total = total + refs[2 * j][x, rows, lanes] * refs[2 * j + 1][x, rows, lanes]
            out[x, rows, lanes] = total

    each_block(out, work)


def split_kernel(spot, courant, parts, swap, keep, slab_in, sems):
    zs = parts.shape[0]
    _, tile_x, slab, _ = slab_in.shape
    planes = tile_x // QUAD
    me_shot, me_z, me_q = spot[0], spot[1], spot[2]
    rows = pl.ds(pl.multiple_of(me_shot * slab, SUB), slab)
    load = pltpu.make_async_copy(courant.at[:, :, rows, :], slab_in, sems.at[zs])
    load.start()
    load.wait()
    copies = []
    for z in range(zs):
        row = jnp.where(z <= me_z, 0, 1)
        copies.append(pltpu.make_async_copy(slab_in.at[row], parts.at[z], sems.at[z]))
    for copy in copies:
        copy.start()
    for k, turn in enumerate((0, 2)):
        keep[k] = slab_in[1, pl.ds((me_q ^ turn) * planes, planes)]
        swap[k] = slab_in[1, pl.ds((me_q ^ turn ^ 1) * planes, planes)]
    for copy in copies:
        copy.wait()


def relay_kernel(keep, swapped, out):
    out[0] = keep[1]
    out[1] = swapped[1]


def gather_kernel(zs, table, spot, line, keep, swapped, far, sent, held, sems):
    shots = sent.shape[0] // QUAD
    me_z, me_q = spot[1], spot[2]
    copies = []
    for s in range(shots):

        def one(j, carry):
            tile = table[s] + j
            place = ((me_z + tile // QUAD) % zs) * QUAD + tile % QUAD
            turn = me_q ^ (tile % QUAD)

            @pl.when(tile < zs * QUAD)
            def _():
                held[s, j] = line[place]

            @pl.when(tile >= zs * QUAD)
            def _():
                near = jnp.where(turn == 0, keep[0], swapped[0])
                other = jnp.where(turn == 2, far[0], far[1])
                held[s, j] = jnp.where(turn < 2, near, other)

            return carry

        lax.fori_loop(0, QUAD, one, 0)
        copy = pltpu.make_async_copy(held.at[s], sent.at[pl.ds(s * QUAD, QUAD)], sems.at[s])
        copy.start()
        copies.append(copy)
    for copy in copies:
        copy.wait()


def scatter_kernel(zs, table, spot, got, line, keep, swap, held, sems):
    me_z, me_q = spot[1], spot[2]
    planes = held.shape[1]
    held[...] = jnp.zeros_like(held)
    keep[...] = jnp.zeros_like(keep)
    swap[...] = jnp.zeros_like(swap)

    def one(slot, carry):
        tile = table[slot // QUAD] + slot % QUAD
        place = ((me_z + tile // QUAD) % zs) * QUAD + tile % QUAD
        turn = me_q ^ (tile % QUAD)

        @pl.when(tile < zs * QUAD)
        def _():
            held[place] = held[place] + got[slot]

        @pl.when((tile >= zs * QUAD) & (turn % 2 == 0))
        def _():
            keep[turn // 2] = keep[turn // 2] + got[slot]

        @pl.when((tile >= zs * QUAD) & (turn % 2 == 1))
        def _():
            swap[turn // 2] = swap[turn // 2] + got[slot]

        return carry

    lax.fori_loop(0, got.shape[0], one, 0)
    copy = pltpu.make_async_copy(held, line, sems.at[0])
    copy.start()
    copy.wait()


def finish_kernel(zs, spot, came, keep, swapped, far, out):
    planes = came.shape[1]
    me_z, me_q = spot[1], spot[2]
    extras = (keep[0], swapped[0], far[0], far[1])
    for turn in range(QUAD):
        q = me_q ^ turn
        low = came[q]
        high = extras[turn]
        for z in range(1, zs):
            value = came[z * QUAD + q]
            low = low + jnp.where(z <= me_z, value, 0.0)
            high = high + jnp.where(z <= me_z, 0.0, value)
        out[0, pl.ds(q * planes, planes)] = low
        out[1, pl.ds(q * planes, planes)] = high


def exchange(parts, axes):
    return lax.all_to_all(parts, axes, split_axis=0, concat_axis=0, tiled=True)


def swap_quads(value, turn):
    return lax.ppermute(value, "quad", [(q, q ^ turn) for q in range(QUAD)])


def quad_relay(keep, swap):
    swapped = swap_quads(swap, 1)
    (far,) = local_kernel(relay_kernel, "relay", [], [keep, swapped], [f32(*keep.shape)])
    return keep, swapped, swap_quads(far, 2)


def model_line(courant, spot):
    rows, tile_x, ny, nz = courant.shape
    zs = lax.axis_size("zz")
    slab = ny // lax.axis_size("shot")
    planes = tile_x // QUAD
    hbm = pl.BlockSpec(memory_space=pltpu.HBM)
    vmem = pl.BlockSpec(memory_space=pltpu.VMEM)
    parts, swap, keep = pl.pallas_call(
        split_kernel,
        out_shape=[f32(zs, tile_x, slab, nz)] + [f32(2, planes, slab, nz)] * 2,
        in_specs=[pl.BlockSpec(memory_space=pltpu.SMEM), hbm],
        out_specs=[hbm, vmem, vmem],
        scratch_shapes=[
            pltpu.VMEM((rows, tile_x, slab, nz), jnp.float32),
            pltpu.SemaphoreType.DMA((zs + 1,)),
        ],
        compiler_params=pltpu.CompilerParams(vmem_limit_bytes=VMEM_LIMIT),
        name="split",
    )(spot, in_hbm(courant))
    line = exchange(parts.reshape(zs * QUAD, planes, slab, nz), MP)
    return line, quad_relay(keep, swap)


def model_parts(line, extras, table, spot):
    shots = lax.axis_size("shot")
    smem = pl.BlockSpec(memory_space=pltpu.SMEM)
    vmem = pl.BlockSpec(memory_space=pltpu.VMEM)
    shape = line.shape[1:]
    return pl.pallas_call(
        functools.partial(gather_kernel, lax.axis_size("zz")),
        out_shape=f32(shots * QUAD, *shape),
        in_specs=[smem, smem] + [vmem] * 4,
        out_specs=pl.BlockSpec(memory_space=pltpu.HBM),
        scratch_shapes=[
            pltpu.VMEM((shots, QUAD, *shape), jnp.float32),
            pltpu.SemaphoreType.DMA((shots,)),
        ],
        compiler_params=pltpu.CompilerParams(vmem_limit_bytes=VMEM_LIMIT),
        name="gather",
    )(table, spot, line, *extras)


def return_image(image, table, spot):
    shots, tile_x, slab, nz = image.shape
    zs = lax.axis_size("zz")
    planes = tile_x // QUAD
    got = exchange(image.reshape(shots * QUAD, planes, slab, nz), PLANE)
    smem = pl.BlockSpec(memory_space=pltpu.SMEM)
    vmem = pl.BlockSpec(memory_space=pltpu.VMEM)
    line, keep, swap = pl.pallas_call(
        functools.partial(scatter_kernel, zs),
        out_shape=[f32(zs * QUAD, planes, slab, nz)] + [f32(2, planes, slab, nz)] * 2,
        in_specs=[smem, smem, vmem],
        out_specs=[pl.BlockSpec(memory_space=pltpu.HBM), vmem, vmem],
        scratch_shapes=[
            pltpu.VMEM((zs * QUAD, planes, slab, nz), jnp.float32),
            pltpu.SemaphoreType.DMA((1,)),
        ],
        compiler_params=pltpu.CompilerParams(vmem_limit_bytes=VMEM_LIMIT),
        name="scatter",
    )(table, spot, got)
    came = exchange(line, MP)
    extras = quad_relay(keep, swap)
    (out,) = local_kernel(
        functools.partial(finish_kernel, zs),
        "finish",
        [spot],
        [came, *extras],
        [f32(2, tile_x, slab, nz)],
    )
    return out


def edges(n, name, ints, now, back, drive, speed):
    _, ny, nz = now.shape
    hbm = pl.BlockSpec(memory_space=pltpu.HBM)
    vmem = pl.BlockSpec(memory_space=pltpu.VMEM)
    return pl.pallas_call(
        functools.partial(edges_kernel, n),
        out_shape=[f32(REACH, ny, nz)] * 2,
        in_specs=[pl.BlockSpec(memory_space=pltpu.SMEM), hbm, hbm, hbm, vmem],
        out_specs=[vmem, vmem],
        scratch_shapes=[
            pltpu.VMEM((3, 2, REACH, ny, nz), jnp.float32),
            pltpu.SemaphoreType.DMA((3, 2)),
        ],
        compiler_params=pltpu.CompilerParams(vmem_limit_bytes=VMEM_LIMIT),
        name=name,
    )(ints, in_hbm(now), in_hbm(back), in_hbm(drive), speed)


def advance(n, name, ints, now, back, drive, speed):
    tile_x, ny, nz = now.shape
    rows = 2 * SUB
    block = pl.BlockSpec((tile_x, rows, nz), lambda i: (0, i, 0))
    return pl.pallas_call(
        functools.partial(advance_kernel, n),
        grid=(ny // rows,),
        out_shape=[f32(tile_x, ny, nz)] * 2,
        in_specs=[
            pl.BlockSpec(memory_space=pltpu.SMEM),
            block,
            block,
            block,
            pl.BlockSpec((2, tile_x, SUB, nz), lambda i: (i, 0, 0, 0)),
        ],
        out_specs=[block, block],
        compiler_params=pltpu.CompilerParams(vmem_limit_bytes=VMEM_LIMIT),
        name=name,
    )(ints, in_hbm(now), in_hbm(back), in_hbm(drive), speed)


def halos(inner, outer):
    count = lax.axis_size(MP)
    across = [(i, i + 1) for i in range(1, count - 1, 2)]
    return (
        lax.ppermute(inner, MP, [(i, i ^ 1) for i in range(count)]),
        lax.ppermute(outer, MP, across + [(j, i) for i, j in across]),
    )


def body(
    courant,
    aperture_first,
    source_pos,
    wavelet,
    receiver_pos,
    residual,
    step_count,
    forward_prev,
    forward_now,
    adjoint_prev,
    adjoint_now,
):
    tile_x, ny, nz = forward_now.shape[1:]
    steps = wavelet.shape[1]
    receivers = receiver_pos.shape[1]
    spot = [lax.axis_index(name) for name in ("shot", "zz", "quad")]
    spot = jnp.stack(spot).astype(jnp.int32)
    line, extras = model_line(courant, spot)
    table = all_first(aperture_first)
    me_index = lax.axis_index(MP)
    even = me_index % 2 == 0
    base = (me_index * tile_x).reshape(1).astype(jnp.int32)
    ints = jnp.concatenate(
        [
            step_count,
            base,
            even.reshape(1).astype(jnp.int32),
            source_pos[0],
            receiver_pos[0].reshape(-1),
        ]
    )
    floats = jnp.concatenate([wavelet[0], residual[0].reshape(-1)])
    u, w = forward_now[0], adjoint_now[0]
    field = f32(tile_x, ny, nz)
    edge = f32(REACH, ny, nz)
    padded = pltpu.VMEM((nz // LANES, tile_x, ny + 2 * SUB, LANES), jnp.float32)
    along = pltpu.VMEM((tile_x, ny, nz), jnp.float32)
    scalars = [ints, floats]
    low = jnp.concatenate([u[:REACH], w[:REACH]])
    high = jnp.concatenate([u[tile_x - REACH :], w[tile_x - REACH :]])
    sides = halos(jnp.where(even, high, low), jnp.where(even, low, high))
    drives = []
    drive, push = local_kernel(
        functools.partial(first_kernel, steps, receivers),
        "first",
        scalars,
        [u, w, *sides],
        [field, field],
        [padded, padded],
    )
    sent = model_parts(line, extras, table, spot)
    sent, drive, push = lax.optimization_barrier((sent, drive, push))
    owned = exchange(sent, PLANE).reshape(-1, tile_x, SUB, nz)
    drives.append(drive)
    before_u = (0, ints, u, forward_prev[0], drive, owned)
    before_w = (steps - 1, ints, w, adjoint_prev[0], push, owned)
    u_sides = halos(*edges(before_u[0], "edges_forward", *before_u[1:]))
    w_sides = halos(*edges(before_w[0], "edges_adjoint", *before_w[1:]))
    u, vu = advance(before_u[0], "advance_forward", *before_u[1:])
    w, vw = advance(before_w[0], "advance_adjoint", *before_w[1:])
    backs = [w]
    for n in range(1, steps):
        last = n == steps - 1
        drive, *moved = local_kernel(
            functools.partial(forward_kernel, n, last),
            "forward",
            scalars,
            [u, vu, owned, *u_sides],
            [field] if last else [field, field, field, edge, edge],
            [padded, along],
        )
        drives.append(drive)
        if not last:
            u, vu, inner, outer = moved
            u_sides = halos(inner, outer)
        extra_in = []
        if last:
            pairs = []
            for k in range(steps - 1):
                pairs += [backs[k], drives[steps - 1 - k]]
            (partial,) = local_kernel(
                functools.partial(products_kernel, steps - 1), "products", [], pairs, [field]
            )
            extra_in = [partial, drives[0]]
        moved = local_kernel(
            functools.partial(adjoint_kernel, steps, receivers, steps - 1 - n, last),
            "adjoint",
            scalars,
            [w, vw, owned, *w_sides, *extra_in],
            [f32(ny // SUB, tile_x, SUB, nz)] if last else [field, field, edge, edge],
            [padded, along],
        )
        if not last:
            w, vw, inner, outer = moved
            w_sides = halos(inner, outer)
            backs.append(w)
    return return_image(moved[0], table, spot)


def solution(mesh):
    shots, mp = mesh.devices.shape
    fine = Mesh(mesh.devices.reshape(shots, mp // QUAD, QUAD), ("shot", "zz", "quad"))
    return jax.shard_map(
        body,
        mesh=fine,
        in_specs=(
            P(None, MP, None, None),
            P("shot"),
            P("shot", None),
            P("shot", None),
            P("shot", None, None),
            P("shot", None, None),
            P("shot"),
            P("shot", MP, None, None),
            P("shot", MP, None, None),
            P("shot", MP, None, None),
            P("shot", MP, None, None),
        ),
        out_specs=P(None, MP, "shot", None),
        check_vma=False,
    )
```

time: 236 us -> 204 us (0.86)
  starting transfers between devices: 99.3 us -> 58.5 us
  blocking collectives: 51.8 us -> 66.4 us
  waiting for transfers between devices: 33.5 us -> 27.7 us
    ppermute x25 -> x18, starting transfers between devices: 71.6 us -> 37.7 us  [the longest x7 31.2 us: halos(): lax.ppermute(outer, MP, across + [(j, i) for i, j in across])]
    unnamed x0 -> x1, blocking collectives: none -> 9.42 us
    ppermute x25 -> x18, waiting for transfers between devices: 13.9 us -> 5.97 us  [the longest x4 3.12 us: swap_quads(): return lax.ppermute(value, 'quad', [(q, q ^ turn) for q in range(QUAD)])]
    pallas_call x0 -> x3, Pallas kernels: none -> 7.46 us  [the longest x2 4.29 us: edges(): pl.pallas_call(functools.partial(edges_kernel, n), out_shape=[f32(REACH,...]
    all_to_all x2, starting transfers between devices: 27.7 us -> 20.8 us  [exchange(): return lax.all_to_all(parts, axes, split_axis=0, concat_axis=0, tiled=True)]
    pallas_call x11, Pallas kernels: 29.2 us -> 23.7 us  [local_kernel(): pl.pallas_call(body, out_shape=outs, in_specs=[smem] * len(scalars) + [vm...]
    all_to_all x2, blocking collectives: 51.8 us -> 57 us  [exchange(): return lax.all_to_all(parts, axes, split_axis=0, concat_axis=0, tiled=True)]
  transfers between devices with their start and end apart: 27 -> 20, of which waited for: 8 -> 4; matrix products, arithmetic and copies ran while one was open for 1% -> 1% of each run, Pallas kernels for 10% -> 13%
where the time goes in v4:
time: 204 us; the launch traced here: 203 us
  blocking collectives  66.4 us (33%)
  starting transfers between devices  58.5 us (29%)
  Pallas kernels  42.9 us (21%)
  waiting for transfers between devices  27.7 us (14%)
  local copies, waits for them, and re-layouts  4.77 us (2%)
    all_to_all x2, blocking collectives, exchange(): return lax.all_to_all(parts, axes, split_axis=0, concat_axis=0, tiled=True)  57 us
    ppermute x7, starting transfers between devices, halos(): lax.ppermute(outer, MP, across + [(j, i) for i, j in across])  31.2 us
    pallas_call x11, Pallas kernels, local_kernel(): pl.pallas_call(body, out_shape=outs, in_specs=[smem] * len(scalars) + [vm...  23.7 us
    all_to_all x2, waiting for transfers between devices, exchange(): return lax.all_to_all(parts, axes, split_axis=0, concat_axis=0, tiled=True)  21.8 us
    all_to_all x2, starting transfers between devices, exchange(): return lax.all_to_all(parts, axes, split_axis=0, concat_axis=0, tiled=True)  20.8 us
    unnamed x1, blocking collectives  9.42 us
    pallas_call x2, Pallas kernels, advance(): pl.pallas_call(functools.partial(advance_kernel, n), grid=(ny // rows,),...  5.84 us
    ppermute x4, starting transfers between devices, swap_quads(): return lax.ppermute(value, 'quad', [(q, q ^ turn) for q in range(QUAD)])  5.35 us
  transfers between devices with their start and end apart: 20, of which 4 were waited for; matrix products, arithmetic and copies ran while one was open for 1% of the time, Pallas kernels for 13%

profile of v4, /device:TPU:1, one launch (start us, length us, event | category | flops | bytes accessed | tf_op | source)
XLA Modules:
  0.0 203.3 jit_solution(11852092810095640478)
XLA Ops:
  0.1 3.0 %split.1 = (f32[8,16,8,256]{3,2,1,0:T(8,128)S(1)}, f32[2,4,8,256]{3,2,1,0:T(8,128)S(1)}, f32[2,4,8,256]{3,2,1,0:T(8,128)S(1)}) custom-call(s32[3]{0:T(128)S(1)} %pad_add_fusion.spot, f32[2,16,64,256]{3,2,1,0:T(8,128)} %courant.1), custom_call_target="tpu_custom_call" | custom-call | tf_op jit(solution)/shard_map/split/pallas_call | solution.py:420
  4.1 12.7 %all-to-all-start = ((f32[32,4,8,256]{3,2,1,0:T(8,128)}), f32[32,4,8,256]{3,2,1,0:T(8,128)S(1)}, u32[]{:S(2)}, u32[]{:S(2)}) async-start(f32[32,4,8,256]{3,2,1,0:T(8,128)} %bitcast.40), calls=%async_computation | async-start | bytes 2097152 | tf_op jit(solution)/shard_map/all_to_all | solution.py:400
  18.4 4.9 %collective-permute-start.3 = (f32[8,64,256]{2,1,0:T(8,128)}, f32[8,64,256]{2,1,0:T(8,128)}, u32[]{:S(2)}, u32[]{:S(2)}) collective-permute-start(f32[8,64,256]{2,1,0:T(8,128)} %get-tuple-element.79), channel_id=1, source_target_pairs={{1,2},{3,4},{5,6},{7,8},{9,10},{11,12},{13,14},{15,16},{17,18},{19... | collective-permute-start | bytes 1572872 | tf_op jit(solution)/shard_map/ppermute | solution.py:530
  25.4 9.4 %all-reduce.table = s32[8]{0:T(128)S(1)} all-reduce(s32[8]{0:T(128)S(1)} %dynamic-update-slice), channel_id=1, replica_groups=mesh['shot'=8,'zz'=8,'quad'=4] {'shot'}, use_global_device_ids=true, to_apply=%add | all-reduce | flops 8 | bytes 64
  38.0 4.9 %first.1 = (f32[16,64,256]{2,1,0:T(8,128)S(1)}, f32[16,64,256]{2,1,0:T(8,128)S(1)}) custom-call(s32[102]{0:T(128)S(1)} %concatenate.12.ints, f32[132]{0:T(256)S(1)} %pad_maximum_fusion.2.floats, f32[16,64,256]{2,1,0:T(8,128)S(1)} %bitcast.35, f32[16,64,256]{2,1,0:T(8,128)S(1)} %bitcast.38, f32[8,64,256]{2,1,0:T(8,128)} %collective-permute-done.2.inner, ...), custom_call_target="tpu_custom_call" | custom-call | tf_op jit(solution)/shard_map/first/pallas_call | solution.py:33
  44.9 2.9 %gather.1 = f32[32,4,8,256]{3,2,1,0:T(8,128)S(1)} custom-call(s32[8]{0:T(128)S(1)} %all-reduce.table, s32[3]{0:T(128)S(1)} %pad_add_fusion.spot, f32[32,4,8,256]{3,2,1,0:T(8,128)S(1)} %all-to-all-done.line, f32[2,4,8,256]{3,2,1,0:T(8,128)S(1)} %get-tuple-element.43.keep, f32[2,4,8,256]{3,2,1,0:T(8,128)S(1)} %collective-permute-done.swapped, ...), custom_call_target="tpu_custom_call" | custom-call | tf_op jit(solution)/shard_map/gather/pallas_call | solution.py:441
  47.9 33.4 %all_to_all.20 = f32[32,4,8,256]{3,2,1,0:T(8,128)S(1)} all-to-all(f32[32,4,8,256]{3,2,1,0:T(8,128)S(1)} %gather.1), channel_id=1, replica_groups=mesh['shot'=8,'zz'=8,'quad'=4] {'shot','quad'}, dimensions={0} | all-to-all | bytes 2097152 | tf_op jit(solution)/shard_map/all_to_all | solution.py:400
  83.9 3.2 %collective-permute-start.11 = (f32[4,64,256]{2,1,0:T(8,128)S(1)}, f32[4,64,256]{2,1,0:T(8,128)S(1)}, u32[]{:S(2)}, u32[]{:S(2)}) collective-permute-start(f32[4,64,256]{2,1,0:T(8,128)S(1)} %get-tuple-element.65), channel_id=1, source_target_pairs={{1,2},{3,4},{5,6},{7,8},{9,10},{11,12},{13,14},{15,16},{17,18},{19... | collective-permute-start | bytes 786440 | tf_op jit(solution)/shard_map/ppermute | solution.py:530
  89.3 4.9 %collective-permute-start.5 = (f32[4,64,256]{2,1,0:T(8,128)S(1)}, f32[4,64,256]{2,1,0:T(8,128)S(1)}, u32[]{:S(2)}, u32[]{:S(2)}) collective-permute-start(f32[4,64,256]{2,1,0:T(8,128)S(1)} %get-tuple-element.52), channel_id=1, source_target_pairs={{1,2},{3,4},{5,6},{7,8},{9,10},{11,12},{13,14},{15,16},{17,18},{19... | collective-permute-start | bytes 786440 | tf_op jit(solution)/shard_map/ppermute | solution.py:530
  94.2 2.9 %advance_forward.1 = (f32[16,64,256]{2,1,0:T(8,128)S(1)}, f32[16,64,256]{2,1,0:T(8,128)S(1)}) custom-call(s32[102]{0:T(128)S(1)} %concatenate.12.ints, f32[16,64,256]{2,1,0:T(8,128)} %bitcast.34, f32[16,64,256]{2,1,0:T(8,128)} %bitcast.42, f32[16,64,256]{2,1,0:T(8,128)} %copy-done.2, f32[8,16,8,256]{3,2,1,0:T(8,128)S(1)} %bitcast.25), custom_call_target="tpu_custom_call" | custom-call | tf_op jit(solution)/shard_map/advance_forward/pallas_call | solution.py:508
  97.1 2.9 %advance_adjoint.1 = (f32[16,64,256]{2,1,0:T(8,128)S(1)}, f32[16,64,256]{2,1,0:T(8,128)S(1)}) custom-call(s32[102]{0:T(128)S(1)} %concatenate.12.ints, f32[16,64,256]{2,1,0:T(8,128)} %bitcast.37, f32[16,64,256]{2,1,0:T(8,128)} %bitcast.44, f32[16,64,256]{2,1,0:T(8,128)} %copy-done.4, f32[8,16,8,256]{3,2,1,0:T(8,128)S(1)} %bitcast.26), custom_call_target="tpu_custom_call" | custom-call | tf_op jit(solution)/shard_map/advance_adjoint/pallas_call | solution.py:508
  100.1 2.8 %forward.3 = (f32[16,64,256]{2,1,0:T(8,128)S(1)}, f32[16,64,256]{2,1,0:T(8,128)S(1)}, f32[16,64,256]{2,1,0:T(8,128)S(1)}, f32[4,64,256]{2,1,0:T(8,128)S(1)}, f32[4,64,256]{2,1,0:T(8,128)S(1)}) custom-call(s32[102]{0:T(128)S(1)} %concatenate.12.ints, f32[132]{0:T(256)S(1)} %pad_maximum_fusion.2.floats, f32[16,64,256]{2,1,0:T(8,128)S(1)} %get-tuple-element.62.u, ...), custom_call_target="tpu_custom_call" | custom-call | tf_op jit(solution)/shard_map/forward/pallas_call | solution.py:33
  102.9 3.6 %collective-permute-start.13 = (f32[4,64,256]{2,1,0:T(8,128)S(1)}, f32[4,64,256]{2,1,0:T(8,128)S(1)}, u32[]{:S(2)}, u32[]{:S(2)}) collective-permute-start(f32[4,64,256]{2,1,0:T(8,128)S(1)} %get-tuple-element.69), channel_id=1, source_target_pairs={{1,2},{3,4},{5,6},{7,8},{9,10},{11,12},{13,14},{15,16},{17,18},{19... | collective-permute-start | bytes 786440 | tf_op jit(solution)/shard_map/ppermute | solution.py:530
  109.4 5.0 %collective-permute-start.7 = (f32[4,64,256]{2,1,0:T(8,128)S(1)}, f32[4,64,256]{2,1,0:T(8,128)S(1)}, u32[]{:S(2)}, u32[]{:S(2)}) collective-permute-start(f32[4,64,256]{2,1,0:T(8,128)S(1)} %get-tuple-element.56), channel_id=1, source_target_pairs={{1,2},{3,4},{5,6},{7,8},{9,10},{11,12},{13,14},{15,16},{17,18},{19... | collective-permute-start | bytes 786440 | tf_op jit(solution)/shard_map/ppermute | solution.py:530
  114.4 2.8 %forward.4 = (f32[16,64,256]{2,1,0:T(8,128)S(1)}, f32[16,64,256]{2,1,0:T(8,128)S(1)}, f32[16,64,256]{2,1,0:T(8,128)S(1)}, f32[4,64,256]{2,1,0:T(8,128)S(1)}, f32[4,64,256]{2,1,0:T(8,128)S(1)}) custom-call(s32[102]{0:T(128)S(1)} %concatenate.12.ints, f32[132]{0:T(256)S(1)} %pad_maximum_fusion.2.floats, f32[16,64,256]{2,1,0:T(8,128)S(1)} %get-tuple-element.66.u, ...), custom_call_target="tpu_custom_call" | custom-call | tf_op jit(solution)/shard_map/forward/pallas_call | solution.py:33
  117.3 4.1 %collective-permute-start.15 = (f32[4,64,256]{2,1,0:T(8,128)S(1)}, f32[4,64,256]{2,1,0:T(8,128)S(1)}, u32[]{:S(2)}, u32[]{:S(2)}) collective-permute-start(f32[4,64,256]{2,1,0:T(8,128)S(1)} %get-tuple-element.73), channel_id=1, source_target_pairs={{1,2},{3,4},{5,6},{7,8},{9,10},{11,12},{13,14},{15,16},{17,18},{19... | collective-permute-start | bytes 786440 | tf_op jit(solution)/shard_map/ppermute | solution.py:530
  124.3 5.5 %collective-permute-start.9 = (f32[4,64,256]{2,1,0:T(8,128)S(1)}, f32[4,64,256]{2,1,0:T(8,128)S(1)}, u32[]{:S(2)}, u32[]{:S(2)}) collective-permute-start(f32[4,64,256]{2,1,0:T(8,128)S(1)} %get-tuple-element.60), channel_id=1, source_target_pairs={{1,2},{3,4},{5,6},{7,8},{9,10},{11,12},{13,14},{15,16},{17,18},{19... | collective-permute-start | bytes 786440 | tf_op jit(solution)/shard_map/ppermute | solution.py:530
  133.2 2.8 %collective-permute-done.9.far = f32[4,64,256]{2,1,0:T(8,128)S(1)} collective-permute-done((f32[4,64,256]{2,1,0:T(8,128)S(1)}, f32[4,64,256]{2,1,0:T(8,128)S(1)}, u32[]{:S(2)}, u32[]{:S(2)}) %collective-permute-start.9) | collective-permute-done | bytes 262176 | tf_op jit(solution)/shard_map/ppermute | solution.py:530
  136.0 3.0 %adjoint.5 = f32[8,16,8,256]{3,2,1,0:T(8,128)S(1)} custom-call(s32[102]{0:T(128)S(1)} %concatenate.12.ints, f32[132]{0:T(256)S(1)} %pad_maximum_fusion.2.floats, f32[16,64,256]{2,1,0:T(8,128)S(1)} %get-tuple-element.57.refs_4_.w, f32[16,64,256]{2,1,0:T(8,128)S(1)} %get-tuple-element.58.vw, f32[8,16,8,256]{3,2,1,0:T(8,128)S(1)} %bitcast.32, ...), custom_call_target="tpu_custom_call" | custom-call | tf_op jit(solution)/shard_map/adjoint/pallas_call | solution.py:33
  139.0 23.6 %all_to_all.21.got = f32[32,4,8,256]{3,2,1,0:T(8,128)S(1)} all-to-all(f32[32,4,8,256]{3,2,1,0:T(8,128)S(1)} %bitcast.39), channel_id=1, replica_groups=mesh['shot'=8,'zz'=8,'quad'=4] {'shot','quad'}, dimensions={0} | all-to-all | bytes 2097152 | tf_op jit(solution)/shard_map/all_to_all | solution.py:400
  162.6 3.2 %scatter.1 = (f32[32,4,8,256]{3,2,1,0:T(8,128)}, f32[2,4,8,256]{3,2,1,0:T(8,128)S(1)}, f32[2,4,8,256]{3,2,1,0:T(8,128)S(1)}) custom-call(s32[8]{0:T(128)S(1)} %all-reduce.table, s32[3]{0:T(128)S(1)} %pad_add_fusion.spot, f32[32,4,8,256]{3,2,1,0:T(8,128)S(1)} %all_to_all.21.got), custom_call_target="tpu_custom_call" | custom-call | tf_op jit(solution)/shard_map/scatter/pallas_call | solution.py:462
  165.8 8.1 %all-to-all-start.3 = ((f32[32,4,8,256]{3,2,1,0:T(8,128)}), f32[32,4,8,256]{3,2,1,0:T(8,128)S(1)}, u32[]{:S(2)}, u32[]{:S(2)}) async-start(f32[32,4,8,256]{3,2,1,0:T(8,128)} %get-tuple-element.76), calls=%async_computation.3 | async-start | bytes 2097152 | tf_op jit(solution)/shard_map/all_to_all | solution.py:400
  175.2 2.9 %collective-permute-start.17 = (f32[2,4,8,256]{3,2,1,0:T(8,128)S(1)}, f32[2,4,8,256]{3,2,1,0:T(8,128)S(1)}, u32[]{:S(2)}, u32[]{:S(2)}) collective-permute-start(f32[2,4,8,256]{3,2,1,0:T(8,128)S(1)} %relay.3), channel_id=1, source_target_pairs={{0,2},{1,3},{2,0},{3,1},{4,6},{5,7},{6,4},{7,5},{8,10},{9,11},{10,... | collective-permute-start | bytes 196616 | tf_op jit(solution)/shard_map/ppermute | solution.py:404
  180.2 21.7 %all-to-all-done.3.came = f32[32,4,8,256]{3,2,1,0:T(8,128)S(1)} async-done(((f32[32,4,8,256]{3,2,1,0:T(8,128)}), f32[32,4,8,256]{3,2,1,0:T(8,128)S(1)}, u32[]{:S(2)}, u32[]{:S(2)}) %all-to-all-start.3) | async-done | bytes 1048608 | tf_op jit(solution)/shard_map/all_to_all | solution.py:400
  (70 shorter events, 27.3 us)
Async XLA Ops:
  4.1 40.8 %all-to-all-start = ((f32[32,4,8,256]{3,2,1,0:T(8,128)}), f32[32,4,8,256]{3,2,1,0:T(8,128)S(1)}, u32[]{:S(2)}, u32[]{:S(2)}) async-start(f32[32,4,8,256]{3,2,1,0:T(8,128)} %bitcast.40), calls=%async_computation | async-start | bytes 2097152 | tf_op jit(solution)/shard_map/all_to_all | solution.py:400
  16.9 17.9 %copy-start.7 = (s32[1,32,3]{1,0,2:T(1,128)S(1)}, s32[1,32,3]{1,0,2:T(1,128)}, u32[]{:S(2)}) copy-start(s32[1,32,3]{1,0,2:T(1,128)} %param.15) | copy-start | bytes 1156
  16.9 18.8 %copy-start.6 = (f32[1,4,32]{2,1,0:T(4,128)S(1)}, f32[1,4,32]{2,1,0:T(4,128)}, u32[]{:S(2)}) copy-start(f32[1,4,32]{2,1,0:T(4,128)} %param.16) | copy-start | bytes 1540
  16.9 18.8 %copy-start.8 = (s32[1,3]{1,0:T(1,128)S(1)}, s32[1,3]{1,0:T(1,128)}, u32[]{:S(2)}) copy-start(s32[1,3]{1,0:T(1,128)} %param.13) | copy-start | bytes 40
  16.9 21.0 %copy-start.9 = (f32[1,4]{1,0:T(1,128)S(1)}, f32[1,4]{1,0:T(1,128)}, u32[]{:S(2)}) copy-start(f32[1,4]{1,0:T(1,128)} %param.14) | copy-start | bytes 52
  18.1 19.8 %collective-permute-start.2 = (f32[8,64,256]{2,1,0:T(8,128)}, f32[8,64,256]{2,1,0:T(8,128)}, u32[]{:S(2)}, u32[]{:S(2)}) collective-permute-start(f32[8,64,256]{2,1,0:T(8,128)} %get-tuple-element.80), channel_id=1, source_target_pairs={{0,1},{1,0},{2,3},{3,2},{4,5},{5,4},{6,7},{7,6},{8,9},{9,8},{10,11... | collective-permute-start | bytes 1572872 | tf_op jit(solution)/shard_map/ppermute | solution.py:529
  18.4 19.6 %collective-permute-start.3 = (f32[8,64,256]{2,1,0:T(8,128)}, f32[8,64,256]{2,1,0:T(8,128)}, u32[]{:S(2)}, u32[]{:S(2)}) collective-permute-start(f32[8,64,256]{2,1,0:T(8,128)} %get-tuple-element.79), channel_id=1, source_target_pairs={{1,2},{3,4},{5,6},{7,8},{9,10},{11,12},{13,14},{15,16},{17,18},{19... | collective-permute-start | bytes 1572872 | tf_op jit(solution)/shard_map/ppermute | solution.py:530
  23.3 12.6 %collective-permute-start = (f32[2,4,8,256]{3,2,1,0:T(8,128)S(1)}, f32[2,4,8,256]{3,2,1,0:T(8,128)S(1)}, u32[]{:S(2)}, u32[]{:S(2)}) collective-permute-start(f32[2,4,8,256]{3,2,1,0:T(8,128)S(1)} %get-tuple-element.44), channel_id=1, source_target_pairs={{0,1},{1,0},{2,3},{3,2},{4,5},{5,4},{6,7},{7,6},{8,9},{9,8},{10,11... | collective-permute-start | bytes 196616 | tf_op jit(solution)/shard_map/ppermute | solution.py:404
  35.8 9.0 %collective-permute-start.1 = (f32[2,4,8,256]{3,2,1,0:T(8,128)S(1)}, f32[2,4,8,256]{3,2,1,0:T(8,128)S(1)}, u32[]{:S(2)}, u32[]{:S(2)}) collective-permute-start(f32[2,4,8,256]{3,2,1,0:T(8,128)S(1)} %relay.2), channel_id=1, source_target_pairs={{0,2},{1,3},{2,0},{3,1},{4,6},{5,7},{6,4},{7,5},{8,10},{9,11},{10,... | collective-permute-start | bytes 196616 | tf_op jit(solution)/shard_map/ppermute | solution.py:404
  83.4 16.7 %collective-permute-start.10 = (f32[4,64,256]{2,1,0:T(8,128)S(1)}, f32[4,64,256]{2,1,0:T(8,128)S(1)}, u32[]{:S(2)}, u32[]{:S(2)}) collective-permute-start(f32[4,64,256]{2,1,0:T(8,128)S(1)} %get-tuple-element.64), channel_id=1, source_target_pairs={{0,1},{1,0},{2,3},{3,2},{4,5},{5,4},{6,7},{7,6},{8,9},{9,8},{10,11... | collective-permute-start | bytes 786440 | tf_op jit(solution)/shard_map/ppermute | solution.py:529
  83.9 16.2 %collective-permute-start.11 = (f32[4,64,256]{2,1,0:T(8,128)S(1)}, f32[4,64,256]{2,1,0:T(8,128)S(1)}, u32[]{:S(2)}, u32[]{:S(2)}) collective-permute-start(f32[4,64,256]{2,1,0:T(8,128)S(1)} %get-tuple-element.65), channel_id=1, source_target_pairs={{1,2},{3,4},{5,6},{7,8},{9,10},{11,12},{13,14},{15,16},{17,18},{19... | collective-permute-start | bytes 786440 | tf_op jit(solution)/shard_map/ppermute | solution.py:530
  89.2 17.3 %collective-permute-start.4 = (f32[4,64,256]{2,1,0:T(8,128)S(1)}, f32[4,64,256]{2,1,0:T(8,128)S(1)}, u32[]{:S(2)}, u32[]{:S(2)}) collective-permute-start(f32[4,64,256]{2,1,0:T(8,128)S(1)} %get-tuple-element.51), channel_id=1, source_target_pairs={{0,1},{1,0},{2,3},{3,2},{4,5},{5,4},{6,7},{7,6},{8,9},{9,8},{10,11... | collective-permute-start | bytes 786440 | tf_op jit(solution)/shard_map/ppermute | solution.py:529
  89.3 17.2 %collective-permute-start.5 = (f32[4,64,256]{2,1,0:T(8,128)S(1)}, f32[4,64,256]{2,1,0:T(8,128)S(1)}, u32[]{:S(2)}, u32[]{:S(2)}) collective-permute-start(f32[4,64,256]{2,1,0:T(8,128)S(1)} %get-tuple-element.52), channel_id=1, source_target_pairs={{1,2},{3,4},{5,6},{7,8},{9,10},{11,12},{13,14},{15,16},{17,18},{19... | collective-permute-start | bytes 786440 | tf_op jit(solution)/shard_map/ppermute | solution.py:530
  102.8 11.6 %collective-permute-start.12 = (f32[4,64,256]{2,1,0:T(8,128)S(1)}, f32[4,64,256]{2,1,0:T(8,128)S(1)}, u32[]{:S(2)}, u32[]{:S(2)}) collective-permute-start(f32[4,64,256]{2,1,0:T(8,128)S(1)} %get-tuple-element.68), channel_id=1, source_target_pairs={{0,1},{1,0},{2,3},{3,2},{4,5},{5,4},{6,7},{7,6},{8,9},{9,8},{10,11... | collective-permute-start | bytes 786440 | tf_op jit(solution)/shard_map/ppermute | solution.py:529
  102.9 11.5 %collective-permute-start.13 = (f32[4,64,256]{2,1,0:T(8,128)S(1)}, f32[4,64,256]{2,1,0:T(8,128)S(1)}, u32[]{:S(2)}, u32[]{:S(2)}) collective-permute-start(f32[4,64,256]{2,1,0:T(8,128)S(1)} %get-tuple-element.69), channel_id=1, source_target_pairs={{1,2},{3,4},{5,6},{7,8},{9,10},{11,12},{13,14},{15,16},{17,18},{19... | collective-permute-start | bytes 786440 | tf_op jit(solution)/shard_map/ppermute | solution.py:530
  109.3 12.1 %collective-permute-start.6 = (f32[4,64,256]{2,1,0:T(8,128)S(1)}, f32[4,64,256]{2,1,0:T(8,128)S(1)}, u32[]{:S(2)}, u32[]{:S(2)}) collective-permute-start(f32[4,64,256]{2,1,0:T(8,128)S(1)} %get-tuple-element.55), channel_id=1, source_target_pairs={{0,1},{1,0},{2,3},{3,2},{4,5},{5,4},{6,7},{7,6},{8,9},{9,8},{10,11... | collective-permute-start | bytes 786440 | tf_op jit(solution)/shard_map/ppermute | solution.py:529
  109.4 12.0 %collective-permute-start.7 = (f32[4,64,256]{2,1,0:T(8,128)S(1)}, f32[4,64,256]{2,1,0:T(8,128)S(1)}, u32[]{:S(2)}, u32[]{:S(2)}) collective-permute-start(f32[4,64,256]{2,1,0:T(8,128)S(1)} %get-tuple-element.56), channel_id=1, source_target_pairs={{1,2},{3,4},{5,6},{7,8},{9,10},{11,12},{13,14},{15,16},{17,18},{19... | collective-permute-start | bytes 786440 | tf_op jit(solution)/shard_map/ppermute | solution.py:530
  117.2 12.7 %collective-permute-start.14 = (f32[4,64,256]{2,1,0:T(8,128)S(1)}, f32[4,64,256]{2,1,0:T(8,128)S(1)}, u32[]{:S(2)}, u32[]{:S(2)}) collective-permute-start(f32[4,64,256]{2,1,0:T(8,128)S(1)} %get-tuple-element.72), channel_id=1, source_target_pairs={{0,1},{1,0},{2,3},{3,2},{4,5},{5,4},{6,7},{7,6},{8,9},{9,8},{10,11... | collective-permute-start | bytes 786440 | tf_op jit(solution)/shard_map/ppermute | solution.py:529
  117.3 12.6 %collective-permute-start.15 = (f32[4,64,256]{2,1,0:T(8,128)S(1)}, f32[4,64,256]{2,1,0:T(8,128)S(1)}, u32[]{:S(2)}, u32[]{:S(2)}) collective-permute-start(f32[4,64,256]{2,1,0:T(8,128)S(1)} %get-tuple-element.73), channel_id=1, source_target_pairs={{1,2},{3,4},{5,6},{7,8},{9,10},{11,12},{13,14},{15,16},{17,18},{19... | collective-permute-start | bytes 786440 | tf_op jit(solution)/shard_map/ppermute | solution.py:530
  124.2 8.9 %collective-permute-start.8 = (f32[4,64,256]{2,1,0:T(8,128)S(1)}, f32[4,64,256]{2,1,0:T(8,128)S(1)}, u32[]{:S(2)}, u32[]{:S(2)}) collective-permute-start(f32[4,64,256]{2,1,0:T(8,128)S(1)} %get-tuple-element.59), channel_id=1, source_target_pairs={{0,1},{1,0},{2,3},{3,2},{4,5},{5,4},{6,7},{7,6},{8,9},{9,8},{10,11... | collective-permute-start | bytes 786440 | tf_op jit(solution)/shard_map/ppermute | solution.py:529
  124.3 11.7 %collective-permute-start.9 = (f32[4,64,256]{2,1,0:T(8,128)S(1)}, f32[4,64,256]{2,1,0:T(8,128)S(1)}, u32[]{:S(2)}, u32[]{:S(2)}) collective-permute-start(f32[4,64,256]{2,1,0:T(8,128)S(1)} %get-tuple-element.60), channel_id=1, source_target_pairs={{1,2},{3,4},{5,6},{7,8},{9,10},{11,12},{13,14},{15,16},{17,18},{19... | collective-permute-start | bytes 786440 | tf_op jit(solution)/shard_map/ppermute | solution.py:530
  165.8 36.1 %all-to-all-start.3 = ((f32[32,4,8,256]{3,2,1,0:T(8,128)}), f32[32,4,8,256]{3,2,1,0:T(8,128)S(1)}, u32[]{:S(2)}, u32[]{:S(2)}) async-start(f32[32,4,8,256]{3,2,1,0:T(8,128)} %get-tuple-element.76), calls=%async_computation.3 | async-start | bytes 2097152 | tf_op jit(solution)/shard_map/all_to_all | solution.py:400
  173.9 1.3 collective-permute-start.16
  175.2 5.0 %collective-permute-start.17 = (f32[2,4,8,256]{3,2,1,0:T(8,128)S(1)}, f32[2,4,8,256]{3,2,1,0:T(8,128)S(1)}, u32[]{:S(2)}, u32[]{:S(2)}) collective-permute-start(f32[2,4,8,256]{3,2,1,0:T(8,128)S(1)} %relay.3), channel_id=1, source_target_pairs={{0,2},{1,3},{2,0},{3,1},{4,6},{5,7},{6,4},{7,5},{8,10},{9,11},{10,... | collective-permute-start | bytes 196616 | tf_op jit(solution)/shard_map/ppermute | solution.py:404
  (7 other events, 47.3 us)

commit v5 on v4

--- a/solution.py
+++ b/solution.py
@@ -6,6 +6,7 @@
 from jax.experimental import pallas as pl
 from jax.experimental.pallas import tpu as pltpu
 from jax.sharding import Mesh, PartitionSpec as P
+
 
 COEF = (-205.0 / 72.0, 1.6, -0.2, 8.0 / 315.0, -1.0 / 560.0)
 QUAD = 4
@@ -20,14 +21,25 @@
 
 
 def all_first(first):
-    return lax.all_gather(first, "shot", tiled=True)
+    shots = lax.axis_size("shot")
+    me = lax.axis_index("shot")
+    known = jnp.where(jnp.arange(shots, dtype=jnp.int32) == me, first, 0)
+    step = 1
+    while step < shots:
+        known = known + lax.ppermute(known, "shot", [(i, i ^ step) for i in range(shots)])
+        step *= 2
+    return known
 
 
 def f32(*shape):
     return jax.ShapeDtypeStruct(shape, jnp.float32)
 
 
-def local_kernel(body, name, scalars, arrays, outs, scratch=()):
+def hbm32(*shape):
+    return pltpu.HBM(shape, jnp.float32)
+
+
+def local_kernel(body, scalars, arrays, outs, scratch=()):
     vmem = pl.BlockSpec(memory_space=pltpu.VMEM)
     smem = pl.BlockSpec(memory_space=pltpu.SMEM)
     return pl.pallas_call(
@@ -37,7 +49,6 @@
         out_specs=[vmem] * len(outs),
         scratch_shapes=list(scratch),
         compiler_params=pltpu.CompilerParams(vmem_limit_bytes=VMEM_LIMIT),
-        name=name,
     )(*scalars, *arrays)
 
 
@@ -137,23 +148,29 @@
     return jnp.where(ints[COUNT] > n, 1.0, 0.0).astype(jnp.float32)
 
 
-def first_kernel(steps, receivers, ints, floats, u, w, inner, outer, d, e, pad_u, pad_w):
-    prepare(u, pad_u, d)
-    prepare(w, pad_w, e)
-    add_source(d, ints, floats, 0)
-    add_receivers(e, ints, floats, steps, receivers, steps - 1)
-    live_u = switch_on(ints, 0)
-    live_w = switch_on(ints, steps - 1)
+def first_kernel(steps, receivers, ints, floats, u, w, near, far, d, e, along_u, along_w, pad, sems):
     even = ints[EVEN] == 1
-
-    def work(i, y0, h, lanes):
-        rows = pl.ds(y0, SUB)
-        for x, _, total in laplacian(pad_u, d, even, inner, outer, y0, h):
-            d[x, rows, lanes] = live_u * total
-        for x, _, total in laplacian(pad_w, e, even, inner, outer, y0, h, REACH):
-            e[x, rows, lanes] = live_w * total
-
-    each_block(u, work)
+    copies = []
+    for k, (field, along, out) in enumerate(((u, along_u, d), (w, along_w, e))):
+        prepare(field, pad, along)
+        if k == 0:
+            add_source(along, ints, floats, 0)
+            live = switch_on(ints, 0)
+        else:
+            add_receivers(along, ints, floats, steps, receivers, steps - 1)
+            live = switch_on(ints, steps - 1)
+
+        def work(i, y0, h, lanes):
+            rows = pl.ds(y0, SUB)
+            for x, _, total in laplacian(pad, along, even, near, far, y0, h, k * REACH):
+                along[x, rows, lanes] = live * total
+
+        each_block(field, work)
+        copy = pltpu.make_async_copy(along, out, sems.at[k])
+        copy.start()
+        copies.append(copy)
+    for copy in copies:
+        copy.wait()
 
 
 def edge_out(even, field, inner, outer):
@@ -171,7 +188,7 @@
 
 
 def edges_kernel(n, ints, now, back, drive, speed, inner, outer, held, sems):
-    xs, ys, nz = now.shape
+    xs, ys, _ = now.shape
     live = switch_on(ints, n)
     even = ints[EVEN] == 1
     starts = (0, xs - REACH)
@@ -210,7 +227,7 @@
         outer[...] = held[0, 1]
 
 
-def advance_kernel(n, ints, now, back, drive, speed, new, gain):
+def opening(ints, n, now, back, drive, speed, new, gain):
     live = switch_on(ints, n)
 
     def work(i, y0, h, lanes):
@@ -224,11 +241,15 @@
     each_block(now, work)
 
 
-def forward_kernel(n, last, ints, floats, u, vu, p, near, far, drive, *rest):
-    if last:
-        pad, along = rest
+def forward_kernel(n, last, ints, floats, *refs):
+    if n == 1:
+        u0, back, drive0, p, near, far, drive, new, gain, inner, outer, pad, along = refs
+        opening(ints, 0, u0, back, drive0, p, new, gain)
+        u, vu = new, gain
+    elif last:
+        u, vu, p, near, far, drive, pad, along = refs
     else:
-        new, gain, inner, outer, pad, along = rest
+        u, vu, p, near, far, drive, new, gain, inner, outer, pad, along = refs
     prepare(u, pad, along)
     add_source(along, ints, floats, n)
     live = switch_on(ints, n)
@@ -250,11 +271,15 @@
         edge_out(even, new, inner, outer)
 
 
-def adjoint_kernel(steps, receivers, n, last, ints, floats, w, vw, p, near, far, *rest):
-    if last:
-        partial, drive, image, pad, along = rest
+def adjoint_kernel(steps, receivers, n, last, ints, floats, *refs):
+    if n == steps - 2:
+        w0, back, push, p, near, far, w, new, gain, inner, outer, pad, along = refs
+        opening(ints, steps - 1, w0, back, push, p, w, gain)
+        vw = gain
+    elif last:
+        w, vw, p, near, far, partial, drive, image, pad, along = refs
     else:
-        new, gain, inner, outer, pad, along = rest
+        w, vw, p, near, far, new, gain, inner, outer, pad, along = refs
     prepare(w, pad, along)
     add_receivers(along, ints, floats, steps, receivers, n)
     live = switch_on(ints, n)
@@ -290,7 +315,7 @@
     each_block(out, work)
 
 
-def split_kernel(spot, courant, parts, swap, keep, slab_in, sems):
+def split_kernel(spot, courant, u, w, parts, inner, outer, swap, keep, slab_in, sems):
     zs = parts.shape[0]
     _, tile_x, slab, _ = slab_in.shape
     planes = tile_x // QUAD
@@ -298,13 +323,26 @@
     rows = pl.ds(pl.multiple_of(me_shot * slab, SUB), slab)
     load = pltpu.make_async_copy(courant.at[:, :, rows, :], slab_in, sems.at[zs])
     load.start()
+    copies = []
+    first = jnp.where(me_q % 2 == 0, tile_x - REACH, 0)
+    for k, field in enumerate((u, w)):
+        for side, out in enumerate((inner, outer)):
+            x0 = first if side == 0 else tile_x - REACH - first
+            copies.append(
+                pltpu.make_async_copy(
+                    field.at[pl.ds(x0, REACH)],
+                    out.at[pl.ds(k * REACH, REACH)],
+                    sems.at[zs + 1 + 2 * k + side],
+                )
+            )
+    for copy in copies:
+        copy.start()
     load.wait()
-    copies = []
     for z in range(zs):
         row = jnp.where(z <= me_z, 0, 1)
-        copies.append(pltpu.make_async_copy(slab_in.at[row], parts.at[z], sems.at[z]))
-    for copy in copies:
+        copy = pltpu.make_async_copy(slab_in.at[row], parts.at[z], sems.at[z])
         copy.start()
+        copies.append(copy)
     for k, turn in enumerate((0, 2)):
         keep[k] = slab_in[1, pl.ds((me_q ^ turn) * planes, planes)]
         swap[k] = slab_in[1, pl.ds((me_q ^ turn ^ 1) * planes, planes)]
@@ -317,40 +355,49 @@
     out[1] = swapped[1]
 
 
-def gather_kernel(zs, table, spot, line, keep, swapped, far, sent, held, sems):
-    shots = sent.shape[0] // QUAD
+def gather_kernel(zs, table, spot, line, keep, swapped, far, sent, sems):
+    slots = sent.shape[0]
     me_z, me_q = spot[1], spot[2]
-    copies = []
-    for s in range(shots):
-
-        def one(j, carry):
-            tile = table[s] + j
-            place = ((me_z + tile // QUAD) % zs) * QUAD + tile % QUAD
-            turn = me_q ^ (tile % QUAD)
-
-            @pl.when(tile < zs * QUAD)
+
+    def one(slot, carry):
+        tile = table[slot // QUAD] + slot % QUAD
+        place = ((me_z + tile // QUAD) % zs) * QUAD + tile % QUAD
+        turn = me_q ^ (tile % QUAD)
+
+        def send(source):
+            pltpu.make_async_copy(source, sent.at[slot], sems.at[slot]).start()
+
+        @pl.when(tile < zs * QUAD)
+        def _():
+            send(line.at[place])
+
+        @pl.when(tile >= zs * QUAD)
+        def _():
+            @pl.when(turn == 0)
             def _():
-                held[s, j] = line[place]
-
-            @pl.when(tile >= zs * QUAD)
+                send(keep.at[0])
+
+            @pl.when(turn == 1)
             def _():
-                near = jnp.where(turn == 0, keep[0], swapped[0])
-                other = jnp.where(turn == 2, far[0], far[1])
-                held[s, j] = jnp.where(turn < 2, near, other)
-
-            return carry
-
-        lax.fori_loop(0, QUAD, one, 0)
-        copy = pltpu.make_async_copy(held.at[s], sent.at[pl.ds(s * QUAD, QUAD)], sems.at[s])
-        copy.start()
-        copies.append(copy)
-    for copy in copies:
-        copy.wait()
+                send(swapped.at[0])
+
+            @pl.when(turn > 1)
+            def _():
+                send(far.at[turn - 2])
+
+        return carry
+
+    lax.fori_loop(0, slots, one, 0)
+
+    def done(slot, carry):
+        pltpu.make_async_copy(line.at[0], sent.at[slot], sems.at[slot]).wait()
+        return carry
+
+    lax.fori_loop(0, slots, done, 0)
 
 
 def scatter_kernel(zs, table, spot, got, line, keep, swap, held, sems):
     me_z, me_q = spot[1], spot[2]
-    planes = held.shape[1]
     held[...] = jnp.zeros_like(held)
     keep[...] = jnp.zeros_like(keep)
     swap[...] = jnp.zeros_like(swap)
@@ -406,48 +453,45 @@
 
 def quad_relay(keep, swap):
     swapped = swap_quads(swap, 1)
-    (far,) = local_kernel(relay_kernel, "relay", [], [keep, swapped], [f32(*keep.shape)])
+    (far,) = local_kernel(relay_kernel, [], [keep, swapped], [f32(*keep.shape)])
     return keep, swapped, swap_quads(far, 2)
 
 
-def model_line(courant, spot):
+def open_moves(courant, u, w, spot):
     rows, tile_x, ny, nz = courant.shape
     zs = lax.axis_size("zz")
     slab = ny // lax.axis_size("shot")
     planes = tile_x // QUAD
     hbm = pl.BlockSpec(memory_space=pltpu.HBM)
     vmem = pl.BlockSpec(memory_space=pltpu.VMEM)
-    parts, swap, keep = pl.pallas_call(
+    parts, inner, outer, swap, keep = pl.pallas_call(
         split_kernel,
-        out_shape=[f32(zs, tile_x, slab, nz)] + [f32(2, planes, slab, nz)] * 2,
-        in_specs=[pl.BlockSpec(memory_space=pltpu.SMEM), hbm],
-        out_specs=[hbm, vmem, vmem],
+        out_shape=[hbm32(zs, tile_x, slab, nz)]
+        + [hbm32(2 * REACH, ny, nz)] * 2
+        + [f32(2, planes, slab, nz)] * 2,
+        in_specs=[pl.BlockSpec(memory_space=pltpu.SMEM), hbm, hbm, hbm],
+        out_specs=[hbm, hbm, hbm, vmem, vmem],
         scratch_shapes=[
             pltpu.VMEM((rows, tile_x, slab, nz), jnp.float32),
-            pltpu.SemaphoreType.DMA((zs + 1,)),
+            pltpu.SemaphoreType.DMA((zs + 5,)),
         ],
         compiler_params=pltpu.CompilerParams(vmem_limit_bytes=VMEM_LIMIT),
         name="split",
-    )(spot, in_hbm(courant))
-    line = exchange(parts.reshape(zs * QUAD, planes, slab, nz), MP)
-    return line, quad_relay(keep, swap)
+    )(spot, in_hbm(courant), in_hbm(u), in_hbm(w))
+    return parts.reshape(zs * QUAD, planes, slab, nz), inner, outer, keep, swap
 
 
 def model_parts(line, extras, table, spot):
-    shots = lax.axis_size("shot")
+    slots = lax.axis_size("shot") * QUAD
     smem = pl.BlockSpec(memory_space=pltpu.SMEM)
-    vmem = pl.BlockSpec(memory_space=pltpu.VMEM)
-    shape = line.shape[1:]
+    anywhere = pl.BlockSpec(memory_space=pl.ANY)
     return pl.pallas_call(
         functools.partial(gather_kernel, lax.axis_size("zz")),
-        out_shape=f32(shots * QUAD, *shape),
-        in_specs=[smem, smem] + [vmem] * 4,
+        out_shape=hbm32(slots, *line.shape[1:]),
+        in_specs=[smem, smem] + [anywhere] * 4,
         out_specs=pl.BlockSpec(memory_space=pltpu.HBM),
-        scratch_shapes=[
-            pltpu.VMEM((shots, QUAD, *shape), jnp.float32),
-            pltpu.SemaphoreType.DMA((shots,)),
-        ],
-        compiler_params=pltpu.CompilerParams(vmem_limit_bytes=VMEM_LIMIT),
+        scratch_shapes=[pltpu.SemaphoreType.DMA((slots,))],
+        compiler_params=pltpu.CompilerParams(vmem_limit_bytes=1 << 20),
         name="gather",
     )(table, spot, line, *extras)
 
@@ -461,7 +505,7 @@
     vmem = pl.BlockSpec(memory_space=pltpu.VMEM)
     line, keep, swap = pl.pallas_call(
         functools.partial(scatter_kernel, zs),
-        out_shape=[f32(zs * QUAD, planes, slab, nz)] + [f32(2, planes, slab, nz)] * 2,
+        out_shape=[hbm32(zs * QUAD, planes, slab, nz)] + [f32(2, planes, slab, nz)] * 2,
         in_specs=[smem, smem, vmem],
         out_specs=[pl.BlockSpec(memory_space=pltpu.HBM), vmem, vmem],
         scratch_shapes=[
@@ -475,7 +519,6 @@
     extras = quad_relay(keep, swap)
     (out,) = local_kernel(
         functools.partial(finish_kernel, zs),
-        "finish",
         [spot],
         [came, *extras],
         [f32(2, tile_x, slab, nz)],
@@ -483,7 +526,7 @@
     return out
 
 
-def edges(n, name, ints, now, back, drive, speed):
+def edges(n, ints, now, back, drive, speed):
     _, ny, nz = now.shape
     hbm = pl.BlockSpec(memory_space=pltpu.HBM)
     vmem = pl.BlockSpec(memory_space=pltpu.VMEM)
@@ -497,28 +540,6 @@
             pltpu.SemaphoreType.DMA((3, 2)),
         ],
         compiler_params=pltpu.CompilerParams(vmem_limit_bytes=VMEM_LIMIT),
-        name=name,
-    )(ints, in_hbm(now), in_hbm(back), in_hbm(drive), speed)
-
-
-def advance(n, name, ints, now, back, drive, speed):
-    tile_x, ny, nz = now.shape
-    rows = 2 * SUB
-    block = pl.BlockSpec((tile_x, rows, nz), lambda i: (0, i, 0))
-    return pl.pallas_call(
-        functools.partial(advance_kernel, n),
-        grid=(ny // rows,),
-        out_shape=[f32(tile_x, ny, nz)] * 2,
-        in_specs=[
-            pl.BlockSpec(memory_space=pltpu.SMEM),
-            block,
-            block,
-            block,
-            pl.BlockSpec((2, tile_x, SUB, nz), lambda i: (i, 0, 0, 0)),
-        ],
-        out_specs=[block, block],
-        compiler_params=pltpu.CompilerParams(vmem_limit_bytes=VMEM_LIMIT),
-        name=name,
     )(ints, in_hbm(now), in_hbm(back), in_hbm(drive), speed)
 
 
@@ -531,7 +552,7 @@
     )
 
 
-def body(
+def window(
     courant,
     aperture_first,
     source_pos,
@@ -549,8 +570,12 @@
     receivers = receiver_pos.shape[1]
     spot = [lax.axis_index(name) for name in ("shot", "zz", "quad")]
     spot = jnp.stack(spot).astype(jnp.int32)
-    line, extras = model_line(courant, spot)
-    table = all_first(aperture_first)
+    u, w = forward_now[0], adjoint_now[0]
+    parts, inner, outer, keep, swap = open_moves(courant, u, w, spot)
+    sides = halos(inner, outer)
+    line = exchange(parts, MP)
+    extras = quad_relay(keep, swap)
+    table = all_first(aperture_first[0])
     me_index = lax.axis_index(MP)
     even = me_index % 2 == 0
     base = (me_index * tile_x).reshape(1).astype(jnp.int32)
@@ -564,42 +589,40 @@
         ]
     )
     floats = jnp.concatenate([wavelet[0], residual[0].reshape(-1)])
-    u, w = forward_now[0], adjoint_now[0]
     field = f32(tile_x, ny, nz)
     edge = f32(REACH, ny, nz)
     padded = pltpu.VMEM((nz // LANES, tile_x, ny + 2 * SUB, LANES), jnp.float32)
     along = pltpu.VMEM((tile_x, ny, nz), jnp.float32)
     scalars = [ints, floats]
-    low = jnp.concatenate([u[:REACH], w[:REACH]])
-    high = jnp.concatenate([u[tile_x - REACH :], w[tile_x - REACH :]])
-    sides = halos(jnp.where(even, high, low), jnp.where(even, low, high))
     drives = []
-    drive, push = local_kernel(
+    hbm = pl.BlockSpec(memory_space=pltpu.HBM)
+    vmem = pl.BlockSpec(memory_space=pltpu.VMEM)
+    smem = pl.BlockSpec(memory_space=pltpu.SMEM)
+    drive, push = pl.pallas_call(
         functools.partial(first_kernel, steps, receivers),
-        "first",
-        scalars,
-        [u, w, *sides],
-        [field, field],
-        [padded, padded],
-    )
+        out_shape=[hbm32(tile_x, ny, nz)] * 2,
+        in_specs=[smem, smem] + [vmem] * 4,
+        out_specs=[hbm, hbm],
+        scratch_shapes=[along, along, padded, pltpu.SemaphoreType.DMA((2,))],
+        compiler_params=pltpu.CompilerParams(vmem_limit_bytes=VMEM_LIMIT),
+        name="first",
+    )(*scalars, u, w, *sides)
     sent = model_parts(line, extras, table, spot)
     sent, drive, push = lax.optimization_barrier((sent, drive, push))
     owned = exchange(sent, PLANE).reshape(-1, tile_x, SUB, nz)
     drives.append(drive)
     before_u = (0, ints, u, forward_prev[0], drive, owned)
     before_w = (steps - 1, ints, w, adjoint_prev[0], push, owned)
-    u_sides = halos(*edges(before_u[0], "edges_forward", *before_u[1:]))
-    w_sides = halos(*edges(before_w[0], "edges_adjoint", *before_w[1:]))
-    u, vu = advance(before_u[0], "advance_forward", *before_u[1:])
-    w, vw = advance(before_w[0], "advance_adjoint", *before_w[1:])
-    backs = [w]
+    u_sides = halos(*edges(before_u[0], *before_u[1:]))
+    w_sides = halos(*edges(before_w[0], *before_w[1:]))
+    backs = []
     for n in range(1, steps):
         last = n == steps - 1
+        state = [u, forward_prev[0], drive] if n == 1 else [u, vu]
         drive, *moved = local_kernel(
             functools.partial(forward_kernel, n, last),
-            "forward",
             scalars,
-            [u, vu, owned, *u_sides],
+            [*state, owned, *u_sides],
             [field] if last else [field, field, field, edge, edge],
             [padded, along],
         )
@@ -613,21 +636,24 @@
             for k in range(steps - 1):
                 pairs += [backs[k], drives[steps - 1 - k]]
             (partial,) = local_kernel(
-                functools.partial(products_kernel, steps - 1), "products", [], pairs, [field]
+                functools.partial(products_kernel, steps - 1), [], pairs, [field]
             )
             extra_in = [partial, drives[0]]
+        state = [w, adjoint_prev[0], push] if n == 1 else [w, vw]
+        outs = [field, field, edge, edge]
+        if n == 1:
+            outs = [field] + outs
         moved = local_kernel(
             functools.partial(adjoint_kernel, steps, receivers, steps - 1 - n, last),
-            "adjoint",
             scalars,
-            [w, vw, owned, *w_sides, *extra_in],
-            [f32(ny // SUB, tile_x, SUB, nz)] if last else [field, field, edge, edge],
+            [*state, owned, *w_sides, *extra_in],
+            [f32(ny // SUB, tile_x, SUB, nz)] if last else outs,
             [padded, along],
         )
         if not last:
-            w, vw, inner, outer = moved
+            *opened, w, vw, inner, outer = moved
             w_sides = halos(inner, outer)
-            backs.append(w)
+            backs += [*opened, w]
     return return_image(moved[0], table, spot)
 
 
@@ -635,7 +661,7 @@
     shots, mp = mesh.devices.shape
     fine = Mesh(mesh.devices.reshape(shots, mp // QUAD, QUAD), ("shot", "zz", "quad"))
     return jax.shard_map(
-        body,
+        window,
         mesh=fine,
         in_specs=(
             P(None, MP, None, None),

time: 204 us -> 231 us (1.13)
  Pallas kernels: 42.9 us -> 71.3 us
  blocking collectives: 66.4 us -> 58 us
  waiting for transfers between devices: 27.7 us -> 35.3 us
  starting transfers between devices: 58.5 us -> 63.3 us
  local copies, waits for them, and re-layouts: 4.77 us -> 0.42 us
    pallas_call x4 -> x3, Pallas kernels: 12 us -> 44.3 us  [the longest x1 33.5 us: open_moves(): pl.pallas_call(split_kernel, out_shape=[hbm32(zs, tile_x, slab, nz)] + [h...]
    unnamed x1 -> x0, blocking collectives: 9.42 us -> none
    ppermute x0 -> x3, waiting for transfers between devices: none -> 7.45 us  [all_first(): lax.ppermute(known, 'shot', [(i, i ^ step) for i in range(shots)])]
    ppermute x0 -> x3, starting transfers between devices: none -> 4.44 us  [all_first(): lax.ppermute(known, 'shot', [(i, i ^ step) for i in range(shots)])]
    unnamed x26 -> x25, local copies, waits for them, and re-layouts: 4.42 us -> 0.16 us
    pallas_call x11 -> x10, Pallas kernels: 23.7 us -> 20 us  [local_kernel(): pl.pallas_call(body, out_shape=outs, in_specs=[smem] * len(scalars) + [vm...]
  transfers between devices with their start and end apart: 20 -> 23, of which waited for: 4 -> 8; matrix products, arithmetic and copies ran while one was open for 1% -> 0% of each run, Pallas kernels for 13% -> 11%
where the time goes in v5:
time: 231 us; the launch traced here: 230 us
  Pallas kernels  71.3 us (31%)
  starting transfers between devices  63.3 us (27%)
  blocking collectives  58 us (25%)
  waiting for transfers between devices  35.3 us (15%)
    all_to_all x2, blocking collectives, exchange(): return lax.all_to_all(parts, axes, split_axis=0, concat_axis=0, tiled=True)  58 us
    pallas_call x1, Pallas kernels, open_moves(): pl.pallas_call(split_kernel, out_shape=[hbm32(zs, tile_x, slab, nz)] + [h...  33.5 us
    ppermute x7, starting transfers between devices, halos(): lax.ppermute(outer, MP, across + [(j, i) for i, j in across])  30.6 us
    all_to_all x2, waiting for transfers between devices, exchange(): return lax.all_to_all(parts, axes, split_axis=0, concat_axis=0, tiled=True)  21.9 us
    all_to_all x2, starting transfers between devices, exchange(): return lax.all_to_all(parts, axes, split_axis=0, concat_axis=0, tiled=True)  21.9 us
    pallas_call x10, Pallas kernels, local_kernel(): pl.pallas_call(body, out_shape=outs, in_specs=[smem] * len(scalars) + [vm...  20 us
    pallas_call x1, Pallas kernels, window(): pl.pallas_call(functools.partial(first_kernel, steps, receivers), out_sha...  7.57 us
    ppermute x3, waiting for transfers between devices, all_first(): lax.ppermute(known, 'shot', [(i, i ^ step) for i in range(shots)])  7.45 us
  transfers between devices with their start and end apart: 23, of which 8 were waited for; matrix products, arithmetic and copies ran while one was open for 0% of the time, Pallas kernels for 11%

profile of v5, /device:TPU:1, one launch (start us, length us, event | category | flops | bytes accessed | tf_op | source)
XLA Modules:
  0.0 230.2 jit_solution(17276276270227366311)
XLA Ops:
  0.1 33.5 %split.1 = (f32[8,16,8,256]{3,2,1,0:T(8,128)}, f32[8,64,256]{2,1,0:T(8,128)}, f32[8,64,256]{2,1,0:T(8,128)}, f32[2,4,8,256]{3,2,1,0:T(8,128)S(1)}, f32[2,4,8,256]{3,2,1,0:T(8,128)S(1)}) custom-call(s32[3]{0:T(128)S(1)} %pad_add_fusion.spot, f32[2,16,64,256]{3,2,1,0:T(8,128)} %courant.1, f32[16,64,256]{2,1,0:T(8,128)} %bitcast.26, f32[16,64,256]{2,1,0:T(8,128)} %bitcast.30), custom_call_target="tpu_custom_call" | custom-call | tf_op jit(solution)/shard_map/split/pallas_call | solution.py:467
  33.7 12.9 %all-to-all-start = ((f32[32,4,8,256]{3,2,1,0:T(8,128)}), f32[32,4,8,256]{3,2,1,0:T(8,128)S(1)}, u32[]{:S(2)}, u32[]{:S(2)}) async-start(f32[32,4,8,256]{3,2,1,0:T(8,128)} %bitcast.39), calls=%async_computation | async-start | bytes 2097152 | tf_op jit(solution)/shard_map/all_to_all | solution.py:447
  46.9 4.9 %collective-permute-start.6 = (f32[8,64,256]{2,1,0:T(8,128)}, f32[8,64,256]{2,1,0:T(8,128)}, u32[]{:S(2)}, u32[]{:S(2)}) collective-permute-start(f32[8,64,256]{2,1,0:T(8,128)} %get-tuple-element.45), channel_id=1, source_target_pairs={{1,2},{3,4},{5,6},{7,8},{9,10},{11,12},{13,14},{15,16},{17,18},{19... | collective-permute-start | bytes 1572872 | tf_op jit(solution)/shard_map/ppermute | solution.py:551
  55.3 2.7 %collective-permute-start.1 = (s32[8]{0:T(128)S(1)}, s32[8]{0:T(128)S(1)}, u32[]{:S(2)}, u32[]{:S(2)}) collective-permute-start(s32[8]{0:T(128)S(1)} %fusion), channel_id=1, source_target_pairs={{0,64},{32,96},{64,0},{96,32},{128,192},{160,224},{192,128},{224,1... | collective-permute-start | bytes 104 | tf_op jit(solution)/shard_map/ppermute | solution.py:29
  59.9 7.0 %collective-permute-done.2 = s32[8]{0:T(128)S(1)} collective-permute-done((s32[8]{0:T(128)S(1)}, s32[8]{0:T(128)S(1)}, u32[]{:S(2)}, u32[]{:S(2)}) %collective-permute-start.2) | collective-permute-done | bytes 64 | tf_op jit(solution)/shard_map/ppermute | solution.py:29
  66.9 7.6 %first.1 = (f32[16,64,256]{2,1,0:T(8,128)}, f32[16,64,256]{2,1,0:T(8,128)}) custom-call(s32[102]{0:T(128)S(1)} %concatenate.6.ints, f32[132]{0:T(256)S(1)} %pad_maximum_fusion.floats, f32[16,64,256]{2,1,0:T(8,128)S(1)} %bitcast.28, f32[16,64,256]{2,1,0:T(8,128)S(1)} %bitcast.32, f32[8,64,256]{2,1,0:T(8,128)} %collective-permute-done.5.near, ...), custom_call_target="tpu_custom_call" | custom-call | tf_op jit(solution)/shard_map/first/pallas_call | solution.py:601
  77.1 34.3 %all_to_all.20 = f32[32,4,8,256]{3,2,1,0:T(8,128)S(1)} all-to-all(f32[32,4,8,256]{3,2,1,0:T(8,128)} %gather.1), channel_id=1, replica_groups=mesh['shot'=8,'zz'=8,'quad'=4] {'shot','quad'}, dimensions={0} | all-to-all | bytes 2097152 | tf_op jit(solution)/shard_map/all_to_all | solution.py:447
  114.0 3.2 %collective-permute-start.14 = (f32[4,64,256]{2,1,0:T(8,128)S(1)}, f32[4,64,256]{2,1,0:T(8,128)S(1)}, u32[]{:S(2)}, u32[]{:S(2)}) collective-permute-start(f32[4,64,256]{2,1,0:T(8,128)S(1)} %get-tuple-element.63), channel_id=1, source_target_pairs={{1,2},{3,4},{5,6},{7,8},{9,10},{11,12},{13,14},{15,16},{17,18},{19... | collective-permute-start | bytes 786440 | tf_op jit(solution)/shard_map/ppermute | solution.py:551
  119.8 5.0 %collective-permute-start.8 = (f32[4,64,256]{2,1,0:T(8,128)S(1)}, f32[4,64,256]{2,1,0:T(8,128)S(1)}, u32[]{:S(2)}, u32[]{:S(2)}) collective-permute-start(f32[4,64,256]{2,1,0:T(8,128)S(1)} %get-tuple-element.51), channel_id=1, source_target_pairs={{1,2},{3,4},{5,6},{7,8},{9,10},{11,12},{13,14},{15,16},{17,18},{19... | collective-permute-start | bytes 786440 | tf_op jit(solution)/shard_map/ppermute | solution.py:551
  124.9 3.4 %shard_map.114 = (f32[16,64,256]{2,1,0:T(8,128)S(1)}, f32[16,64,256]{2,1,0:T(8,128)S(1)}, f32[16,64,256]{2,1,0:T(8,128)S(1)}, f32[4,64,256]{2,1,0:T(8,128)S(1)}, f32[4,64,256]{2,1,0:T(8,128)S(1)}) custom-call(s32[102]{0:T(128)S(1)} %concatenate.6.ints, f32[132]{0:T(256)S(1)} %pad_maximum_fusion.floats, f32[16,64,256]{2,1,0:T(8,128)S(1)} %bitcast.29, ...), custom_call_target="tpu_custom_call" | custom-call | tf_op jit(solution)/shard_map/pallas_call | solution.py:45
  128.3 4.3 %collective-permute-start.16 = (f32[4,64,256]{2,1,0:T(8,128)S(1)}, f32[4,64,256]{2,1,0:T(8,128)S(1)}, u32[]{:S(2)}, u32[]{:S(2)}) collective-permute-start(f32[4,64,256]{2,1,0:T(8,128)S(1)} %get-tuple-element.67), channel_id=1, source_target_pairs={{1,2},{3,4},{5,6},{7,8},{9,10},{11,12},{13,14},{15,16},{17,18},{19... | collective-permute-start | bytes 786440 | tf_op jit(solution)/shard_map/ppermute | solution.py:551
  132.7 3.5 %shard_map.111 = (f32[16,64,256]{2,1,0:T(8,128)S(1)}, f32[16,64,256]{2,1,0:T(8,128)S(1)}, f32[16,64,256]{2,1,0:T(8,128)S(1)}, f32[4,64,256]{2,1,0:T(8,128)S(1)}, f32[4,64,256]{2,1,0:T(8,128)S(1)}) custom-call(s32[102]{0:T(128)S(1)} %concatenate.6.ints, f32[132]{0:T(256)S(1)} %pad_maximum_fusion.floats, f32[16,64,256]{2,1,0:T(8,128)S(1)} %bitcast.33, ...), custom_call_target="tpu_custom_call" | custom-call | tf_op jit(solution)/shard_map/pallas_call | solution.py:45
  136.2 4.1 %collective-permute-start.10 = (f32[4,64,256]{2,1,0:T(8,128)S(1)}, f32[4,64,256]{2,1,0:T(8,128)S(1)}, u32[]{:S(2)}, u32[]{:S(2)}) collective-permute-start(f32[4,64,256]{2,1,0:T(8,128)S(1)} %get-tuple-element.55), channel_id=1, source_target_pairs={{1,2},{3,4},{5,6},{7,8},{9,10},{11,12},{13,14},{15,16},{17,18},{19... | collective-permute-start | bytes 786440 | tf_op jit(solution)/shard_map/ppermute | solution.py:551
  140.5 2.8 %shard_map.115 = (f32[16,64,256]{2,1,0:T(8,128)S(1)}, f32[16,64,256]{2,1,0:T(8,128)S(1)}, f32[16,64,256]{2,1,0:T(8,128)S(1)}, f32[4,64,256]{2,1,0:T(8,128)S(1)}, f32[4,64,256]{2,1,0:T(8,128)S(1)}) custom-call(s32[102]{0:T(128)S(1)} %concatenate.6.ints, f32[132]{0:T(256)S(1)} %pad_maximum_fusion.floats, f32[16,64,256]{2,1,0:T(8,128)S(1)} %get-tuple-element.64.refs_0_, ...), custom_call_target="tpu_custom_call" | custom-call | tf_op jit(solution)/shard_map/pallas_call | solution.py:45
  143.9 3.8 %collective-permute-start.18 = (f32[4,64,256]{2,1,0:T(8,128)S(1)}, f32[4,64,256]{2,1,0:T(8,128)S(1)}, u32[]{:S(2)}, u32[]{:S(2)}) collective-permute-start(f32[4,64,256]{2,1,0:T(8,128)S(1)} %get-tuple-element.71), channel_id=1, source_target_pairs={{1,2},{3,4},{5,6},{7,8},{9,10},{11,12},{13,14},{15,16},{17,18},{19... | collective-permute-start | bytes 786440 | tf_op jit(solution)/shard_map/ppermute | solution.py:551
  147.7 2.8 %shard_map.112 = (f32[16,64,256]{2,1,0:T(8,128)S(1)}, f32[16,64,256]{2,1,0:T(8,128)S(1)}, f32[4,64,256]{2,1,0:T(8,128)S(1)}, f32[4,64,256]{2,1,0:T(8,128)S(1)}) custom-call(s32[102]{0:T(128)S(1)} %concatenate.6.ints, f32[132]{0:T(256)S(1)} %pad_maximum_fusion.floats, f32[16,64,256]{2,1,0:T(8,128)S(1)} %get-tuple-element.52.refs_0_.refs_2_, ...), custom_call_target="tpu_custom_call" | custom-call | tf_op jit(solution)/shard_map/pallas_call | solution.py:45
  150.6 5.2 %collective-permute-start.12 = (f32[4,64,256]{2,1,0:T(8,128)S(1)}, f32[4,64,256]{2,1,0:T(8,128)S(1)}, u32[]{:S(2)}, u32[]{:S(2)}) collective-permute-start(f32[4,64,256]{2,1,0:T(8,128)S(1)} %get-tuple-element.59), channel_id=1, source_target_pairs={{1,2},{3,4},{5,6},{7,8},{9,10},{11,12},{13,14},{15,16},{17,18},{19... | collective-permute-start | bytes 786440 | tf_op jit(solution)/shard_map/ppermute | solution.py:551
  159.1 2.8 %collective-permute-done.12.refs_4_ = f32[4,64,256]{2,1,0:T(8,128)S(1)} collective-permute-done((f32[4,64,256]{2,1,0:T(8,128)S(1)}, f32[4,64,256]{2,1,0:T(8,128)S(1)}, u32[]{:S(2)}, u32[]{:S(2)}) %collective-permute-start.12) | collective-permute-done | bytes 262176 | tf_op jit(solution)/shard_map/ppermute | solution.py:551
  161.9 3.0 %shard_map.118 = f32[8,16,8,256]{3,2,1,0:T(8,128)S(1)} custom-call(s32[102]{0:T(128)S(1)} %concatenate.6.ints, f32[132]{0:T(256)S(1)} %pad_maximum_fusion.floats, f32[16,64,256]{2,1,0:T(8,128)S(1)} %get-tuple-element.56.refs_4_.refs_0_, f32[16,64,256]{2,1,0:T(8,128)S(1)} %get-tuple-element.57.refs_1_, f32[8,16,8,256]{3,2,1,0:T(8,128)S(1)} %bitcast.25, ...), custom_call_target="tpu_custom_call" | custom-call | tf_op jit(solution)/shard_map/pallas_call | solution.py:45
  164.9 23.7 %all_to_all.21.got = f32[32,4,8,256]{3,2,1,0:T(8,128)S(1)} all-to-all(f32[32,4,8,256]{3,2,1,0:T(8,128)S(1)} %bitcast.38), channel_id=1, replica_groups=mesh['shot'=8,'zz'=8,'quad'=4] {'shot','quad'}, dimensions={0} | all-to-all | bytes 2097152 | tf_op jit(solution)/shard_map/all_to_all | solution.py:447
  188.6 3.2 %scatter.1 = (f32[32,4,8,256]{3,2,1,0:T(8,128)}, f32[2,4,8,256]{3,2,1,0:T(8,128)S(1)}, f32[2,4,8,256]{3,2,1,0:T(8,128)S(1)}) custom-call(s32[8]{0:T(128)S(1)} %add.18.table, s32[3]{0:T(128)S(1)} %pad_add_fusion.spot, f32[32,4,8,256]{3,2,1,0:T(8,128)S(1)} %all_to_all.21.got), custom_call_target="tpu_custom_call" | custom-call | tf_op jit(solution)/shard_map/scatter/pallas_call | solution.py:506
  191.8 9.0 %all-to-all-start.3 = ((f32[32,4,8,256]{3,2,1,0:T(8,128)}), f32[32,4,8,256]{3,2,1,0:T(8,128)S(1)}, u32[]{:S(2)}, u32[]{:S(2)}) async-start(f32[32,4,8,256]{3,2,1,0:T(8,128)} %get-tuple-element.74), calls=%async_computation.3 | async-start | bytes 2097152 | tf_op jit(solution)/shard_map/all_to_all | solution.py:447
  202.1 2.9 %collective-permute-start.20 = (f32[2,4,8,256]{3,2,1,0:T(8,128)S(1)}, f32[2,4,8,256]{3,2,1,0:T(8,128)S(1)}, u32[]{:S(2)}, u32[]{:S(2)}) collective-permute-start(f32[2,4,8,256]{3,2,1,0:T(8,128)S(1)} %shard_map.119), channel_id=1, source_target_pairs={{0,2},{1,3},{2,0},{3,1},{4,6},{5,7},{6,4},{7,5},{8,10},{9,11},{10,... | collective-permute-start | bytes 196616 | tf_op jit(solution)/shard_map/ppermute | solution.py:451
  207.1 21.7 %all-to-all-done.3.came = f32[32,4,8,256]{3,2,1,0:T(8,128)S(1)} async-done(((f32[32,4,8,256]{3,2,1,0:T(8,128)}), f32[32,4,8,256]{3,2,1,0:T(8,128)S(1)}, u32[]{:S(2)}, u32[]{:S(2)}) %all-to-all-start.3) | async-done | bytes 1048608 | tf_op jit(solution)/shard_map/all_to_all | solution.py:447
  (74 shorter events, 21.1 us)
Async XLA Ops:
  33.7 33.2 %copy-start = (f32[1,16,64,256]{3,2,1,0:T(8,128)S(1)}, f32[1,16,64,256]{3,2,1,0:T(8,128)}, u32[]{:S(2)}) copy-start(f32[1,16,64,256]{3,2,1,0:T(8,128)} %param.19) | copy-start | bytes 3145732
  33.7 41.0 %all-to-all-start = ((f32[32,4,8,256]{3,2,1,0:T(8,128)}), f32[32,4,8,256]{3,2,1,0:T(8,128)S(1)}, u32[]{:S(2)}, u32[]{:S(2)}) async-start(f32[32,4,8,256]{3,2,1,0:T(8,128)} %bitcast.39), calls=%async_computation | async-start | bytes 2097152 | tf_op jit(solution)/shard_map/all_to_all | solution.py:447
  46.6 20.3 %collective-permute-start.5 = (f32[8,64,256]{2,1,0:T(8,128)}, f32[8,64,256]{2,1,0:T(8,128)}, u32[]{:S(2)}, u32[]{:S(2)}) collective-permute-start(f32[8,64,256]{2,1,0:T(8,128)} %get-tuple-element.44), channel_id=1, source_target_pairs={{0,1},{1,0},{2,3},{3,2},{4,5},{5,4},{6,7},{7,6},{8,9},{9,8},{10,11... | collective-permute-start | bytes 1572872 | tf_op jit(solution)/shard_map/ppermute | solution.py:550
  46.9 20.0 %collective-permute-start.6 = (f32[8,64,256]{2,1,0:T(8,128)}, f32[8,64,256]{2,1,0:T(8,128)}, u32[]{:S(2)}, u32[]{:S(2)}) collective-permute-start(f32[8,64,256]{2,1,0:T(8,128)} %get-tuple-element.45), channel_id=1, source_target_pairs={{1,2},{3,4},{5,6},{7,8},{9,10},{11,12},{13,14},{15,16},{17,18},{19... | collective-permute-start | bytes 1572872 | tf_op jit(solution)/shard_map/ppermute | solution.py:551
  52.5 2.8 %collective-permute-start = (s32[8]{0:T(128)S(1)}, s32[8]{0:T(128)S(1)}, u32[]{:S(2)}, u32[]{:S(2)}) collective-permute-start(s32[8]{0:T(128)S(1)} %compare_select_fusion), channel_id=1, source_target_pairs={{0,32},{32,0},{64,96},{96,64},{128,160},{160,128},{192,224},{224,1... | collective-permute-start | bytes 104 | tf_op jit(solution)/shard_map/ppermute | solution.py:29
  53.8 4.3 %collective-permute-start.3 = (f32[2,4,8,256]{3,2,1,0:T(8,128)S(1)}, f32[2,4,8,256]{3,2,1,0:T(8,128)S(1)}, u32[]{:S(2)}, u32[]{:S(2)}) collective-permute-start(f32[2,4,8,256]{3,2,1,0:T(8,128)S(1)} %get-tuple-element.43), channel_id=1, source_target_pairs={{0,1},{1,0},{2,3},{3,2},{4,5},{5,4},{6,7},{7,6},{8,9},{9,8},{10,11... | collective-permute-start | bytes 196616 | tf_op jit(solution)/shard_map/ppermute | solution.py:451
  55.3 4.2 %collective-permute-start.1 = (s32[8]{0:T(128)S(1)}, s32[8]{0:T(128)S(1)}, u32[]{:S(2)}, u32[]{:S(2)}) collective-permute-start(s32[8]{0:T(128)S(1)} %fusion), channel_id=1, source_target_pairs={{0,64},{32,96},{64,0},{96,32},{128,192},{160,224},{192,128},{224,1... | collective-permute-start | bytes 104 | tf_op jit(solution)/shard_map/ppermute | solution.py:29
  58.1 16.5 %collective-permute-start.4 = (f32[2,4,8,256]{3,2,1,0:T(8,128)S(1)}, f32[2,4,8,256]{3,2,1,0:T(8,128)S(1)}, u32[]{:S(2)}, u32[]{:S(2)}) collective-permute-start(f32[2,4,8,256]{3,2,1,0:T(8,128)S(1)} %shard_map.109), channel_id=1, source_target_pairs={{0,2},{1,3},{2,0},{3,1},{4,6},{5,7},{6,4},{7,5},{8,10},{9,11},{10,... | collective-permute-start | bytes 196616 | tf_op jit(solution)/shard_map/ppermute | solution.py:451
  59.5 7.4 %collective-permute-start.2 = (s32[8]{0:T(128)S(1)}, s32[8]{0:T(128)S(1)}, u32[]{:S(2)}, u32[]{:S(2)}) collective-permute-start(s32[8]{0:T(128)S(1)} %fusion.1), channel_id=1, source_target_pairs={{0,128},{32,160},{64,192},{96,224},{128,0},{160,32},{192,64},{224,... | collective-permute-start | bytes 104 | tf_op jit(solution)/shard_map/ppermute | solution.py:29
  113.5 11.4 %collective-permute-start.13 = (f32[4,64,256]{2,1,0:T(8,128)S(1)}, f32[4,64,256]{2,1,0:T(8,128)S(1)}, u32[]{:S(2)}, u32[]{:S(2)}) collective-permute-start(f32[4,64,256]{2,1,0:T(8,128)S(1)} %get-tuple-element.62), channel_id=1, source_target_pairs={{0,1},{1,0},{2,3},{3,2},{4,5},{5,4},{6,7},{7,6},{8,9},{9,8},{10,11... | collective-permute-start | bytes 786440 | tf_op jit(solution)/shard_map/ppermute | solution.py:550
  114.0 10.9 %collective-permute-start.14 = (f32[4,64,256]{2,1,0:T(8,128)S(1)}, f32[4,64,256]{2,1,0:T(8,128)S(1)}, u32[]{:S(2)}, u32[]{:S(2)}) collective-permute-start(f32[4,64,256]{2,1,0:T(8,128)S(1)} %get-tuple-element.63), channel_id=1, source_target_pairs={{1,2},{3,4},{5,6},{7,8},{9,10},{11,12},{13,14},{15,16},{17,18},{19... | collective-permute-start | bytes 786440 | tf_op jit(solution)/shard_map/ppermute | solution.py:551
  119.6 13.0 %collective-permute-start.7 = (f32[4,64,256]{2,1,0:T(8,128)S(1)}, f32[4,64,256]{2,1,0:T(8,128)S(1)}, u32[]{:S(2)}, u32[]{:S(2)}) collective-permute-start(f32[4,64,256]{2,1,0:T(8,128)S(1)} %get-tuple-element.50), channel_id=1, source_target_pairs={{0,1},{1,0},{2,3},{3,2},{4,5},{5,4},{6,7},{7,6},{8,9},{9,8},{10,11... | collective-permute-start | bytes 786440 | tf_op jit(solution)/shard_map/ppermute | solution.py:550
  119.8 12.9 %collective-permute-start.8 = (f32[4,64,256]{2,1,0:T(8,128)S(1)}, f32[4,64,256]{2,1,0:T(8,128)S(1)}, u32[]{:S(2)}, u32[]{:S(2)}) collective-permute-start(f32[4,64,256]{2,1,0:T(8,128)S(1)} %get-tuple-element.51), channel_id=1, source_target_pairs={{1,2},{3,4},{5,6},{7,8},{9,10},{11,12},{13,14},{15,16},{17,18},{19... | collective-permute-start | bytes 786440 | tf_op jit(solution)/shard_map/ppermute | solution.py:551
  128.2 12.2 %collective-permute-start.15 = (f32[4,64,256]{2,1,0:T(8,128)S(1)}, f32[4,64,256]{2,1,0:T(8,128)S(1)}, u32[]{:S(2)}, u32[]{:S(2)}) collective-permute-start(f32[4,64,256]{2,1,0:T(8,128)S(1)} %get-tuple-element.66), channel_id=1, source_target_pairs={{0,1},{1,0},{2,3},{3,2},{4,5},{5,4},{6,7},{7,6},{8,9},{9,8},{10,11... | collective-permute-start | bytes 786440 | tf_op jit(solution)/shard_map/ppermute | solution.py:550
  128.3 12.1 %collective-permute-start.16 = (f32[4,64,256]{2,1,0:T(8,128)S(1)}, f32[4,64,256]{2,1,0:T(8,128)S(1)}, u32[]{:S(2)}, u32[]{:S(2)}) collective-permute-start(f32[4,64,256]{2,1,0:T(8,128)S(1)} %get-tuple-element.67), channel_id=1, source_target_pairs={{1,2},{3,4},{5,6},{7,8},{9,10},{11,12},{13,14},{15,16},{17,18},{19... | collective-permute-start | bytes 786440 | tf_op jit(solution)/shard_map/ppermute | solution.py:551
  136.2 11.5 %collective-permute-start.10 = (f32[4,64,256]{2,1,0:T(8,128)S(1)}, f32[4,64,256]{2,1,0:T(8,128)S(1)}, u32[]{:S(2)}, u32[]{:S(2)}) collective-permute-start(f32[4,64,256]{2,1,0:T(8,128)S(1)} %get-tuple-element.55), channel_id=1, source_target_pairs={{1,2},{3,4},{5,6},{7,8},{9,10},{11,12},{13,14},{15,16},{17,18},{19... | collective-permute-start | bytes 786440 | tf_op jit(solution)/shard_map/ppermute | solution.py:551
  140.4 7.3 %collective-permute-start.9 = (f32[4,64,256]{2,1,0:T(8,128)S(1)}, f32[4,64,256]{2,1,0:T(8,128)S(1)}, u32[]{:S(2)}, u32[]{:S(2)}) collective-permute-start(f32[4,64,256]{2,1,0:T(8,128)S(1)} %get-tuple-element.54), channel_id=1, source_target_pairs={{0,1},{1,0},{2,3},{3,2},{4,5},{5,4},{6,7},{7,6},{8,9},{9,8},{10,11... | collective-permute-start | bytes 786440 | tf_op jit(solution)/shard_map/ppermute | solution.py:550
  143.3 12.5 %collective-permute-start.17 = (f32[4,64,256]{2,1,0:T(8,128)S(1)}, f32[4,64,256]{2,1,0:T(8,128)S(1)}, u32[]{:S(2)}, u32[]{:S(2)}) collective-permute-start(f32[4,64,256]{2,1,0:T(8,128)S(1)} %get-tuple-element.70), channel_id=1, source_target_pairs={{0,1},{1,0},{2,3},{3,2},{4,5},{5,4},{6,7},{7,6},{8,9},{9,8},{10,11... | collective-permute-start | bytes 786440 | tf_op jit(solution)/shard_map/ppermute | solution.py:550
  143.9 11.9 %collective-permute-start.18 = (f32[4,64,256]{2,1,0:T(8,128)S(1)}, f32[4,64,256]{2,1,0:T(8,128)S(1)}, u32[]{:S(2)}, u32[]{:S(2)}) collective-permute-start(f32[4,64,256]{2,1,0:T(8,128)S(1)} %get-tuple-element.71), channel_id=1, source_target_pairs={{1,2},{3,4},{5,6},{7,8},{9,10},{11,12},{13,14},{15,16},{17,18},{19... | collective-permute-start | bytes 786440 | tf_op jit(solution)/shard_map/ppermute | solution.py:551
  150.5 8.6 %collective-permute-start.11 = (f32[4,64,256]{2,1,0:T(8,128)S(1)}, f32[4,64,256]{2,1,0:T(8,128)S(1)}, u32[]{:S(2)}, u32[]{:S(2)}) collective-permute-start(f32[4,64,256]{2,1,0:T(8,128)S(1)} %get-tuple-element.58), channel_id=1, source_target_pairs={{0,1},{1,0},{2,3},{3,2},{4,5},{5,4},{6,7},{7,6},{8,9},{9,8},{10,11... | collective-permute-start | bytes 786440 | tf_op jit(solution)/shard_map/ppermute | solution.py:550
  150.6 11.3 %collective-permute-start.12 = (f32[4,64,256]{2,1,0:T(8,128)S(1)}, f32[4,64,256]{2,1,0:T(8,128)S(1)}, u32[]{:S(2)}, u32[]{:S(2)}) collective-permute-start(f32[4,64,256]{2,1,0:T(8,128)S(1)} %get-tuple-element.59), channel_id=1, source_target_pairs={{1,2},{3,4},{5,6},{7,8},{9,10},{11,12},{13,14},{15,16},{17,18},{19... | collective-permute-start | bytes 786440 | tf_op jit(solution)/shard_map/ppermute | solution.py:551
  191.8 37.0 %all-to-all-start.3 = ((f32[32,4,8,256]{3,2,1,0:T(8,128)}), f32[32,4,8,256]{3,2,1,0:T(8,128)S(1)}, u32[]{:S(2)}, u32[]{:S(2)}) async-start(f32[32,4,8,256]{3,2,1,0:T(8,128)} %get-tuple-element.74), calls=%async_computation.3 | async-start | bytes 2097152 | tf_op jit(solution)/shard_map/all_to_all | solution.py:447
  200.7 1.3 collective-permute-start.19
  202.1 5.0 %collective-permute-start.20 = (f32[2,4,8,256]{3,2,1,0:T(8,128)S(1)}, f32[2,4,8,256]{3,2,1,0:T(8,128)S(1)}, u32[]{:S(2)}, u32[]{:S(2)}) collective-permute-start(f32[2,4,8,256]{3,2,1,0:T(8,128)S(1)} %shard_map.119), channel_id=1, source_target_pairs={{0,2},{1,3},{2,0},{3,1},{4,6},{5,7},{6,4},{7,5},{8,10},{9,11},{10,... | collective-permute-start | bytes 196616 | tf_op jit(solution)/shard_map/ppermute | solution.py:451
  (11 other events, 178.5 us)

commit v6 on v5

--- a/solution.py
+++ b/solution.py
@@ -39,7 +39,7 @@
     return pltpu.HBM(shape, jnp.float32)
 
 
-def local_kernel(body, scalars, arrays, outs, scratch=()):
+def local_kernel(body, scalars, arrays, outs, scratch=(), aliases=None):
     vmem = pl.BlockSpec(memory_space=pltpu.VMEM)
     smem = pl.BlockSpec(memory_space=pltpu.SMEM)
     return pl.pallas_call(
@@ -48,6 +48,7 @@
         in_specs=[smem] * len(scalars) + [vmem] * len(arrays),
         out_specs=[vmem] * len(outs),
         scratch_shapes=list(scratch),
+        input_output_aliases=aliases or {},
         compiler_params=pltpu.CompilerParams(vmem_limit_bytes=VMEM_LIMIT),
     )(*scalars, *arrays)
 
@@ -115,19 +116,24 @@
     xs = along_z.shape[0]
     rows = pl.ds(y0, SUB)
     lanes = slice(h * LANES, (h + 1) * LANES)
-    near = [inner[plane + j, rows, lanes] for j in range(REACH)]
-    far = [outer[plane + j, rows, lanes] for j in range(REACH)]
-    column = [jnp.where(even, far[j], near[j]) for j in range(REACH)]
-    column += [padded[h, x, pl.ds(y0 + SUB, SUB), :] for x in range(xs)]
-    column += [jnp.where(even, near[j], far[j]) for j in range(REACH)]
+    if inner is None:
+        before = after = [None] * REACH
+    else:
+        near = [inner[plane + j, rows, lanes] for j in range(REACH)]
+        far = [outer[plane + j, rows, lanes] for j in range(REACH)]
+        before = [jnp.where(even, far[j], near[j]) for j in range(REACH)]
+        after = [jnp.where(even, near[j], far[j]) for j in range(REACH)]
+    column = before + [padded[h, x, pl.ds(y0 + SUB, SUB), :] for x in range(xs)] + after
     for x in range(xs):
         total = along_z[x, rows, lanes]
         for k in range(1, REACH + 1):
-            pair = column[x + REACH + k] + column[x + REACH - k]
-            pair = pair + (
+            pair = (
                 padded[h, x, pl.ds(y0 + SUB + k, SUB), :]
                 + padded[h, x, pl.ds(y0 + SUB - k, SUB), :]
             )
+            for other in (column[x + REACH + k], column[x + REACH - k]):
+                if other is not None:
+                    pair = pair + other
             total = total + COEF[k] * pair
         yield x, column[x + REACH], total
 
@@ -187,44 +193,50 @@
         outer[...] = field[xs - REACH :]
 
 
-def edges_kernel(n, ints, now, back, drive, speed, inner, outer, held, sems):
-    xs, ys, _ = now.shape
-    live = switch_on(ints, n)
+def edges_kernel(steps, ints, *refs):
+    fields, speed = (refs[0:3], refs[3:6]), refs[6]
+    outs, held, sems = (refs[7:9], refs[9:11]), refs[11], refs[12]
+    xs, ys, _ = refs[0].shape
     even = ints[EVEN] == 1
     starts = (0, xs - REACH)
-    copies = []
-    for k, source in enumerate((now, back, drive)):
-        for side, x0 in enumerate(starts):
-            copies.append(
-                pltpu.make_async_copy(
-                    source.at[pl.ds(x0, REACH)], held.at[k, side], sems.at[k, side]
-                )
-            )
+    copies = [
+        pltpu.make_async_copy(
+            source.at[pl.ds(x0, REACH)], held.at[f, k, side], sems.at[f, k, side]
+        )
+        for f in range(2)
+        for k, source in enumerate(fields[f])
+        for side, x0 in enumerate(starts)
+    ]
     for copy in copies:
         copy.start()
-    for copy in copies:
-        copy.wait()
-
-    def step(i, carry):
-        rows = pl.ds(pl.multiple_of(i * SUB, SUB), SUB)
-        for side, x0 in enumerate(starts):
-            for j in range(REACH):
-                here = held[0, side, j, rows, :]
-                more = (here - held[1, side, j, rows, :]) + speed[i, x0 + j] * held[2, side, j, rows, :]
-                held[0, side, j, rows, :] = here + live * more
-        return carry
-
-    lax.fori_loop(0, ys // SUB, step, 0)
-
-    @pl.when(even)
-    def _():
-        inner[...] = held[0, 1]
-        outer[...] = held[0, 0]
-
-    @pl.when(jnp.logical_not(even))
-    def _():
-        inner[...] = held[0, 0]
-        outer[...] = held[0, 1]
+    for f in range(2):
+        live = switch_on(ints, 0 if f == 0 else steps - 1)
+        for copy in copies[6 * f : 6 * f + 6]:
+            copy.wait()
+
+        def step(i, carry):
+            rows = pl.ds(pl.multiple_of(i * SUB, SUB), SUB)
+            for side, x0 in enumerate(starts):
+                for j in range(REACH):
+                    here = held[f, 0, side, j, rows, :]
+                    more = (here - held[f, 1, side, j, rows, :]) + speed[i, x0 + j] * held[
+                        f, 2, side, j, rows, :
+                    ]
+                    held[f, 0, side, j, rows, :] = here + live * more
+            return carry
+
+        lax.fori_loop(0, ys // SUB, step, 0)
+        inner, outer = outs[f]
+
+        @pl.when(even)
+        def _():
+            inner[...] = held[f, 0, 1]
+            outer[...] = held[f, 0, 0]
+
+        @pl.when(jnp.logical_not(even))
+        def _():
+            inner[...] = held[f, 0, 0]
+            outer[...] = held[f, 0, 1]
 
 
 def opening(ints, n, now, back, drive, speed, new, gain):
@@ -271,13 +283,11 @@
         edge_out(even, new, inner, outer)
 
 
-def adjoint_kernel(steps, receivers, n, last, ints, floats, *refs):
+def adjoint_kernel(steps, receivers, n, ints, floats, *refs):
     if n == steps - 2:
         w0, back, push, p, near, far, w, new, gain, inner, outer, pad, along = refs
         opening(ints, steps - 1, w0, back, push, p, w, gain)
         vw = gain
-    elif last:
-        w, vw, p, near, far, partial, drive, image, pad, along = refs
     else:
         w, vw, p, near, far, new, gain, inner, outer, pad, along = refs
     prepare(w, pad, along)
@@ -289,16 +299,57 @@
         rows = pl.ds(y0, SUB)
         for x, here, total in laplacian(pad, along, even, near, far, y0, h):
             more = vw[x, rows, lanes] + (live * p[i, x, :, lanes]) * total
+            gain[x, rows, lanes] = more
+            new[x, rows, lanes] = here + live * more
+
+    each_block(w, work)
+    edge_out(even, new, inner, outer)
+
+
+def last_inner_kernel(steps, receivers, ints, floats, w, vw, p, partial, drive, image, open_sum, pad, along):
+    xs = w.shape[0]
+    prepare(w, pad, along)
+    add_receivers(along, ints, floats, steps, receivers, 0)
+    live = switch_on(ints, 0)
+
+    def work(i, y0, h, lanes):
+        rows = pl.ds(y0, SUB)
+        for x, here, total in laplacian(pad, along, None, None, None, y0, h):
+            if x < REACH or x >= xs - REACH:
+                open_sum[x if x < REACH else x + 2 * REACH - xs, rows, lanes] = total
+                continue
+            more = vw[x, rows, lanes] + (live * p[i, x, :, lanes]) * total
             here = here + live * more
-            if last:
-                image[i, x, :, lanes] = partial[x, rows, lanes] + here * drive[x, rows, lanes]
-                continue
-            gain[x, rows, lanes] = more
-            new[x, rows, lanes] = here
+            image[i, x, :, lanes] = partial[x, rows, lanes] + here * drive[x, rows, lanes]
 
     each_block(w, work)
-    if not last:
-        edge_out(even, new, inner, outer)
+
+
+def last_outer_kernel(ints, w, vw, p, partial, drive, open_sum, near, far, inside, image):
+    del inside
+    xs = w.shape[0]
+    live = switch_on(ints, 0)
+    even = ints[EVEN] == 1
+
+    def work(i, y0, h, lanes):
+        rows = pl.ds(y0, SUB)
+        a = [near[j, rows, lanes] for j in range(REACH)]
+        b = [far[j, rows, lanes] for j in range(REACH)]
+        before = [jnp.where(even, b[j], a[j]) for j in range(REACH)]
+        after = [jnp.where(even, a[j], b[j]) for j in range(REACH)]
+        for side in range(2 * REACH):
+            x = side if side < REACH else side + xs - 2 * REACH
+            total = open_sum[side, rows, lanes]
+            for k in range(1, REACH + 1):
+                if x - k < 0:
+                    total = total + COEF[k] * before[REACH + x - k]
+                if x + k >= xs:
+                    total = total + COEF[k] * after[x + k - xs]
+            more = vw[x, rows, lanes] + (live * p[i, x, :, lanes]) * total
+            here = w[x, rows, lanes] + live * more
+            image[i, x, :, lanes] = partial[x, rows, lanes] + here * drive[x, rows, lanes]
+
+    each_block(w, work)
 
 
 def products_kernel(pairs, *refs):
@@ -315,39 +366,43 @@
     each_block(out, work)
 
 
-def split_kernel(spot, courant, u, w, parts, inner, outer, swap, keep, slab_in, sems):
+def split_kernel(spot, courant, u, w, parts, inner, outer, swap, keep, slab_in, sides, sems):
     zs = parts.shape[0]
     _, tile_x, slab, _ = slab_in.shape
     planes = tile_x // QUAD
     me_shot, me_z, me_q = spot[0], spot[1], spot[2]
     rows = pl.ds(pl.multiple_of(me_shot * slab, SUB), slab)
-    load = pltpu.make_async_copy(courant.at[:, :, rows, :], slab_in, sems.at[zs])
-    load.start()
-    copies = []
     first = jnp.where(me_q % 2 == 0, tile_x - REACH, 0)
-    for k, field in enumerate((u, w)):
-        for side, out in enumerate((inner, outer)):
-            x0 = first if side == 0 else tile_x - REACH - first
-            copies.append(
+    loads = []
+    for side in range(2):
+        x0 = first if side == 0 else tile_x - REACH - first
+        for k, field in enumerate((u, w)):
+            loads.append(
                 pltpu.make_async_copy(
                     field.at[pl.ds(x0, REACH)],
-                    out.at[pl.ds(k * REACH, REACH)],
-                    sems.at[zs + 1 + 2 * k + side],
+                    sides.at[side, pl.ds(k * REACH, REACH)],
+                    sems.at[2 * side + k],
                 )
             )
-    for copy in copies:
-        copy.start()
-    load.wait()
+    loads.append(pltpu.make_async_copy(courant.at[:, :, rows, :], slab_in, sems.at[4]))
+    for load in loads:
+        load.start()
+    stores = []
+    for side, out in enumerate((inner, outer)):
+        loads[2 * side].wait()
+        loads[2 * side + 1].wait()
+        stores.append(pltpu.make_async_copy(sides.at[side], out, sems.at[5 + side]))
+        stores[-1].start()
+    loads[4].wait()
     for z in range(zs):
         row = jnp.where(z <= me_z, 0, 1)
-        copy = pltpu.make_async_copy(slab_in.at[row], parts.at[z], sems.at[z])
-        copy.start()
-        copies.append(copy)
+        stores.append(pltpu.make_async_copy(slab_in.at[row], parts.at[z], sems.at[7 + z]))
+        stores[-1].start()
     for k, turn in enumerate((0, 2)):
         keep[k] = slab_in[1, pl.ds((me_q ^ turn) * planes, planes)]
         swap[k] = slab_in[1, pl.ds((me_q ^ turn ^ 1) * planes, planes)]
-    for copy in copies:
-        copy.wait()
+    for store in stores:
+        store.wait()
 
 
 def relay_kernel(keep, swapped, out):
@@ -399,32 +454,27 @@
 def scatter_kernel(zs, table, spot, got, line, keep, swap, held, sems):
     me_z, me_q = spot[1], spot[2]
     held[...] = jnp.zeros_like(held)
-    keep[...] = jnp.zeros_like(keep)
-    swap[...] = jnp.zeros_like(swap)
-
-    def one(slot, carry):
-        tile = table[slot // QUAD] + slot % QUAD
-        place = ((me_z + tile // QUAD) % zs) * QUAD + tile % QUAD
-        turn = me_q ^ (tile % QUAD)
-
-        @pl.when(tile < zs * QUAD)
-        def _():
-            held[place] = held[place] + got[slot]
-
-        @pl.when((tile >= zs * QUAD) & (turn % 2 == 0))
-        def _():
-            keep[turn // 2] = keep[turn // 2] + got[slot]
-
-        @pl.when((tile >= zs * QUAD) & (turn % 2 == 1))
-        def _():
-            swap[turn // 2] = swap[turn // 2] + got[slot]
-
+
+    def one(s, carry):
+        place = pl.ds(table[s], QUAD)
+        held[place] = held[place] + got[pl.ds(s * QUAD, QUAD)]
         return carry
 
-    lax.fori_loop(0, got.shape[0], one, 0)
-    copy = pltpu.make_async_copy(held, line, sems.at[0])
-    copy.start()
-    copy.wait()
+    lax.fori_loop(0, got.shape[0] // QUAD, one, 0)
+    copies = []
+    for j in range(zs):
+        to = ((me_z + j) % zs) * QUAD
+        copies.append(
+            pltpu.make_async_copy(
+                held.at[pl.ds(j * QUAD, QUAD)], line.at[pl.ds(to, QUAD)], sems.at[j]
+            )
+        )
+        copies[-1].start()
+    for k, turn in enumerate((0, 2)):
+        keep[k] = held[zs * QUAD + (me_q ^ turn)]
+        swap[k] = held[zs * QUAD + (me_q ^ turn ^ 1)]
+    for copy in copies:
+        copy.wait()
 
 
 def finish_kernel(zs, spot, came, keep, swapped, far, out):
@@ -473,7 +523,8 @@
         out_specs=[hbm, hbm, hbm, vmem, vmem],
         scratch_shapes=[
             pltpu.VMEM((rows, tile_x, slab, nz), jnp.float32),
-            pltpu.SemaphoreType.DMA((zs + 5,)),
+            pltpu.VMEM((2, 2 * REACH, ny, nz), jnp.float32),
+            pltpu.SemaphoreType.DMA((zs + 7,)),
         ],
         compiler_params=pltpu.CompilerParams(vmem_limit_bytes=VMEM_LIMIT),
         name="split",
@@ -509,8 +560,8 @@
         in_specs=[smem, smem, vmem],
         out_specs=[pl.BlockSpec(memory_space=pltpu.HBM), vmem, vmem],
         scratch_shapes=[
-            pltpu.VMEM((zs * QUAD, planes, slab, nz), jnp.float32),
-            pltpu.SemaphoreType.DMA((1,)),
+            pltpu.VMEM(((zs + 1) * QUAD, planes, slab, nz), jnp.float32),
+            pltpu.SemaphoreType.DMA((zs,)),
         ],
         compiler_params=pltpu.CompilerParams(vmem_limit_bytes=VMEM_LIMIT),
         name="scatter",
@@ -518,29 +569,27 @@
     came = exchange(line, MP)
     extras = quad_relay(keep, swap)
     (out,) = local_kernel(
-        functools.partial(finish_kernel, zs),
-        [spot],
-        [came, *extras],
-        [f32(2, tile_x, slab, nz)],
+        functools.partial(finish_kernel, zs), [spot], [came, *extras], [f32(2, tile_x, slab, nz)]
     )
     return out
 
 
-def edges(n, ints, now, back, drive, speed):
-    _, ny, nz = now.shape
+def edges(steps, ints, forward, adjoint, speed):
+    _, ny, nz = forward[0].shape
     hbm = pl.BlockSpec(memory_space=pltpu.HBM)
     vmem = pl.BlockSpec(memory_space=pltpu.VMEM)
     return pl.pallas_call(
-        functools.partial(edges_kernel, n),
-        out_shape=[f32(REACH, ny, nz)] * 2,
-        in_specs=[pl.BlockSpec(memory_space=pltpu.SMEM), hbm, hbm, hbm, vmem],
-        out_specs=[vmem, vmem],
+        functools.partial(edges_kernel, steps),
+        out_shape=[f32(REACH, ny, nz)] * 4,
+        in_specs=[pl.BlockSpec(memory_space=pltpu.SMEM)] + [hbm] * 6 + [vmem],
+        out_specs=[vmem] * 4,
         scratch_shapes=[
-            pltpu.VMEM((3, 2, REACH, ny, nz), jnp.float32),
-            pltpu.SemaphoreType.DMA((3, 2)),
+            pltpu.VMEM((2, 3, 2, REACH, ny, nz), jnp.float32),
+            pltpu.SemaphoreType.DMA((2, 3, 2)),
         ],
         compiler_params=pltpu.CompilerParams(vmem_limit_bytes=VMEM_LIMIT),
-    )(ints, in_hbm(now), in_hbm(back), in_hbm(drive), speed)
+        name="edges",
+    )(ints, *map(in_hbm, forward), *map(in_hbm, adjoint), speed)
 
 
 def halos(inner, outer):
@@ -611,10 +660,11 @@
     sent, drive, push = lax.optimization_barrier((sent, drive, push))
     owned = exchange(sent, PLANE).reshape(-1, tile_x, SUB, nz)
     drives.append(drive)
-    before_u = (0, ints, u, forward_prev[0], drive, owned)
-    before_w = (steps - 1, ints, w, adjoint_prev[0], push, owned)
-    u_sides = halos(*edges(before_u[0], *before_u[1:]))
-    w_sides = halos(*edges(before_w[0], *before_w[1:]))
+    openings = edges(
+        steps, ints, (u, forward_prev[0], drive), (w, adjoint_prev[0], push), owned
+    )
+    u_sides = halos(*openings[:2])
+    w_sides = halos(*openings[2:])
     backs = []
     for n in range(1, steps):
         last = n == steps - 1
@@ -630,31 +680,38 @@
         if not last:
             u, vu, inner, outer = moved
             u_sides = halos(inner, outer)
-        extra_in = []
         if last:
-            pairs = []
-            for k in range(steps - 1):
-                pairs += [backs[k], drives[steps - 1 - k]]
-            (partial,) = local_kernel(
-                functools.partial(products_kernel, steps - 1), [], pairs, [field]
-            )
-            extra_in = [partial, drives[0]]
+            break
         state = [w, adjoint_prev[0], push] if n == 1 else [w, vw]
         outs = [field, field, edge, edge]
         if n == 1:
             outs = [field] + outs
-        moved = local_kernel(
-            functools.partial(adjoint_kernel, steps, receivers, steps - 1 - n, last),
+        *opened, w, vw, inner, outer = local_kernel(
+            functools.partial(adjoint_kernel, steps, receivers, steps - 1 - n),
             scalars,
-            [*state, owned, *w_sides, *extra_in],
-            [f32(ny // SUB, tile_x, SUB, nz)] if last else outs,
+            [*state, owned, *w_sides],
+            outs,
             [padded, along],
         )
-        if not last:
-            *opened, w, vw, inner, outer = moved
-            w_sides = halos(inner, outer)
-            backs += [*opened, w]
-    return return_image(moved[0], table, spot)
+        w_sides = halos(inner, outer)
+        backs += [*opened, w]
+    pairs = []
+    for k in range(steps - 1):
+        pairs += [backs[k], drives[steps - 1 - k]]
+    (partial,) = local_kernel(functools.partial(products_kernel, steps - 1), [], pairs, [field])
+    state = [w, vw, owned, partial, drives[0]]
+    whole = f32(ny // SUB, tile_x, SUB, nz)
+    image, open_sum = local_kernel(
+        functools.partial(last_inner_kernel, steps, receivers),
+        scalars,
+        state,
+        [whole, f32(2 * REACH, ny, nz)],
+        [padded, along],
+    )
+    (image,) = local_kernel(
+        last_outer_kernel, [ints], [*state, open_sum, *w_sides, image], [whole], aliases={9: 0}
+    )
+    return return_image(image, table, spot)
 
 
 def solution(mesh):

time: 231 us -> 200 us (0.87)
  Pallas kernels: 71.3 us -> 38.4 us
  starting transfers between devices: 63.3 us -> 67.1 us
    pallas_call x1, Pallas kernels: 33.5 us -> 3.03 us  [open_moves(): pl.pallas_call(split_kernel, out_shape=[hbm32(zs, tile_x, slab, nz)] + [h...]
    ppermute x7, starting transfers between devices: 30.6 us -> 35 us  [halos(): lax.ppermute(outer, MP, across + [(j, i) for i, j in across])]
    pallas_call x10 -> x11, Pallas kernels: 20 us -> 20.6 us  [local_kernel(): pl.pallas_call(body, out_shape=outs, in_specs=[smem] * len(scalars) + [vm...]
  transfers between devices with their start and end apart: 23 -> 23, of which waited for: 8 -> 9; matrix products, arithmetic and copies ran while one was open for 0% -> 0% of each run, Pallas kernels for 11% -> 13%
where the time goes in v6:
time: 200 us; the launch traced here: 199 us
  starting transfers between devices  67.1 us (34%)
  blocking collectives  58 us (29%)
  Pallas kernels  38.4 us (19%)
  waiting for transfers between devices  33.5 us (17%)
    all_to_all x2, blocking collectives, exchange(): return lax.all_to_all(parts, axes, split_axis=0, concat_axis=0, tiled=True)  58 us
    ppermute x7, starting transfers between devices, halos(): lax.ppermute(outer, MP, across + [(j, i) for i, j in across])  35 us
    all_to_all x2, waiting for transfers between devices, exchange(): return lax.all_to_all(parts, axes, split_axis=0, concat_axis=0, tiled=True)  21.8 us
    all_to_all x2, starting transfers between devices, exchange(): return lax.all_to_all(parts, axes, split_axis=0, concat_axis=0, tiled=True)  21.3 us
    pallas_call x11, Pallas kernels, local_kernel(): pl.pallas_call(body, out_shape=outs, in_specs=[smem] * len(scalars) + [vm...  20.6 us
    pallas_call x1, Pallas kernels, window(): pl.pallas_call(functools.partial(first_kernel, steps, receivers), out_sha...  7.6 us
    ppermute x3, waiting for transfers between devices, all_first(): lax.ppermute(known, 'shot', [(i, i ^ step) for i in range(shots)])  7.45 us
    ppermute x4, starting transfers between devices, swap_quads(): return lax.ppermute(value, 'quad', [(q, q ^ turn) for q in range(QUAD)])  4.6 us
  transfers between devices with their start and end apart: 23, of which 9 were waited for; matrix products, arithmetic and copies ran while one was open for 0% of the time, Pallas kernels for 13%

profile of v6, /device:TPU:1, one launch (start us, length us, event | category | flops | bytes accessed | tf_op | source)
XLA Modules:
  0.0 199.3 jit_solution(17593272243241770651)
XLA Ops:
  0.1 3.0 %split.1 = (f32[8,16,8,256]{3,2,1,0:T(8,128)}, f32[8,64,256]{2,1,0:T(8,128)}, f32[8,64,256]{2,1,0:T(8,128)}, f32[2,4,8,256]{3,2,1,0:T(8,128)S(1)}, f32[2,4,8,256]{3,2,1,0:T(8,128)S(1)}) custom-call(s32[3]{0:T(128)S(1)} %pad_add_fusion.spot, f32[2,16,64,256]{3,2,1,0:T(8,128)} %courant.1, f32[16,64,256]{2,1,0:T(8,128)} %bitcast.26, f32[16,64,256]{2,1,0:T(8,128)} %bitcast.30), custom_call_target="tpu_custom_call" | custom-call | tf_op jit(solution)/shard_map/split/pallas_call | solution.py:517
  3.2 12.9 %all-to-all-start = ((f32[32,4,8,256]{3,2,1,0:T(8,128)}), f32[32,4,8,256]{3,2,1,0:T(8,128)S(1)}, u32[]{:S(2)}, u32[]{:S(2)}) async-start(f32[32,4,8,256]{3,2,1,0:T(8,128)} %bitcast.39), calls=%async_computation | async-start | bytes 2097152 | tf_op jit(solution)/shard_map/all_to_all | solution.py:497
  16.4 4.9 %collective-permute-start.6 = (f32[8,64,256]{2,1,0:T(8,128)}, f32[8,64,256]{2,1,0:T(8,128)}, u32[]{:S(2)}, u32[]{:S(2)}) collective-permute-start(f32[8,64,256]{2,1,0:T(8,128)} %get-tuple-element.47), channel_id=1, source_target_pairs={{1,2},{3,4},{5,6},{7,8},{9,10},{11,12},{13,14},{15,16},{17,18},{19... | collective-permute-start | bytes 1572872 | tf_op jit(solution)/shard_map/ppermute | solution.py:600
  24.8 2.7 %collective-permute-start.1 = (s32[8]{0:T(128)S(1)}, s32[8]{0:T(128)S(1)}, u32[]{:S(2)}, u32[]{:S(2)}) collective-permute-start(s32[8]{0:T(128)S(1)} %fusion), channel_id=1, source_target_pairs={{0,64},{32,96},{64,0},{96,32},{128,192},{160,224},{192,128},{224,1... | collective-permute-start | bytes 104 | tf_op jit(solution)/shard_map/ppermute | solution.py:29
  29.4 7.0 %collective-permute-done.2 = s32[8]{0:T(128)S(1)} collective-permute-done((s32[8]{0:T(128)S(1)}, s32[8]{0:T(128)S(1)}, u32[]{:S(2)}, u32[]{:S(2)}) %collective-permute-start.2) | collective-permute-done | bytes 64 | tf_op jit(solution)/shard_map/ppermute | solution.py:29
  36.4 7.6 %first.1 = (f32[16,64,256]{2,1,0:T(8,128)}, f32[16,64,256]{2,1,0:T(8,128)}) custom-call(s32[102]{0:T(128)S(1)} %concatenate.6.ints, f32[132]{0:T(256)S(1)} %pad_maximum_fusion.floats, f32[16,64,256]{2,1,0:T(8,128)S(1)} %bitcast.28, f32[16,64,256]{2,1,0:T(8,128)S(1)} %bitcast.32, f32[8,64,256]{2,1,0:T(8,128)} %collective-permute-done.5.near, ...), custom_call_target="tpu_custom_call" | custom-call | tf_op jit(solution)/shard_map/first/pallas_call | solution.py:650
  44.2 2.4 %gather.1 = f32[32,4,8,256]{3,2,1,0:T(8,128)} custom-call(s32[8]{0:T(128)S(1)} %add.18.table, s32[3]{0:T(128)S(1)} %pad_add_fusion.spot, f32[32,4,8,256]{3,2,1,0:T(8,128)S(1)} %all-to-all-done.line, f32[2,4,8,256]{3,2,1,0:T(8,128)S(1)} %get-tuple-element.44.keep, f32[2,4,8,256]{3,2,1,0:T(8,128)S(1)} %collective-permute-done.3.swapped, ...), custom_call_target="tpu_custom_call" | custom-call | tf_op jit(solution)/shard_map/gather/pallas_call | solution.py:539
  46.6 34.3 %all_to_all.20 = f32[32,4,8,256]{3,2,1,0:T(8,128)S(1)} all-to-all(f32[32,4,8,256]{3,2,1,0:T(8,128)} %gather.1), channel_id=1, replica_groups=mesh['shot'=8,'zz'=8,'quad'=4] {'shot','quad'}, dimensions={0} | all-to-all | bytes 2097152 | tf_op jit(solution)/shard_map/all_to_all | solution.py:497
  80.8 2.9 %edges.1 = (f32[4,64,256]{2,1,0:T(8,128)S(1)}, f32[4,64,256]{2,1,0:T(8,128)S(1)}, f32[4,64,256]{2,1,0:T(8,128)S(1)}, f32[4,64,256]{2,1,0:T(8,128)S(1)}) custom-call(s32[102]{0:T(128)S(1)} %concatenate.6.ints, f32[16,64,256]{2,1,0:T(8,128)} %bitcast.27, f32[16,64,256]{2,1,0:T(8,128)} %bitcast.35, f32[16,64,256]{2,1,0:T(8,128)} %get-tuple-element.52.refs_2_.drive, ...), custom_call_target="tpu_custom_call" | custom-call | tf_op jit(solution)/shard_map/edges/pallas_call | solution.py:581
  84.3 3.2 %collective-permute-start.12 = (f32[4,64,256]{2,1,0:T(8,128)S(1)}, f32[4,64,256]{2,1,0:T(8,128)S(1)}, u32[]{:S(2)}, u32[]{:S(2)}) collective-permute-start(f32[4,64,256]{2,1,0:T(8,128)S(1)} %get-tuple-element.63), channel_id=1, source_target_pairs={{1,2},{3,4},{5,6},{7,8},{9,10},{11,12},{13,14},{15,16},{17,18},{19... | collective-permute-start | bytes 786440 | tf_op jit(solution)/shard_map/ppermute | solution.py:600
  87.6 5.0 %collective-permute-start.8 = (f32[4,64,256]{2,1,0:T(8,128)S(1)}, f32[4,64,256]{2,1,0:T(8,128)S(1)}, u32[]{:S(2)}, u32[]{:S(2)}) collective-permute-start(f32[4,64,256]{2,1,0:T(8,128)S(1)} %get-tuple-element.54), channel_id=1, source_target_pairs={{1,2},{3,4},{5,6},{7,8},{9,10},{11,12},{13,14},{15,16},{17,18},{19... | collective-permute-start | bytes 786440 | tf_op jit(solution)/shard_map/ppermute | solution.py:600
  93.6 3.3 %shard_map.112 = (f32[16,64,256]{2,1,0:T(8,128)S(1)}, f32[16,64,256]{2,1,0:T(8,128)S(1)}, f32[16,64,256]{2,1,0:T(8,128)S(1)}, f32[4,64,256]{2,1,0:T(8,128)S(1)}, f32[4,64,256]{2,1,0:T(8,128)S(1)}) custom-call(s32[102]{0:T(128)S(1)} %concatenate.6.ints, f32[132]{0:T(256)S(1)} %pad_maximum_fusion.floats, f32[16,64,256]{2,1,0:T(8,128)S(1)} %bitcast.29, ...), custom_call_target="tpu_custom_call" | custom-call | tf_op jit(solution)/shard_map/pallas_call | solution.py:45
  97.0 5.9 %collective-permute-start.14 = (f32[4,64,256]{2,1,0:T(8,128)S(1)}, f32[4,64,256]{2,1,0:T(8,128)S(1)}, u32[]{:S(2)}, u32[]{:S(2)}) collective-permute-start(f32[4,64,256]{2,1,0:T(8,128)S(1)} %get-tuple-element.67), channel_id=1, source_target_pairs={{1,2},{3,4},{5,6},{7,8},{9,10},{11,12},{13,14},{15,16},{17,18},{19... | collective-permute-start | bytes 786440 | tf_op jit(solution)/shard_map/ppermute | solution.py:600
  103.0 3.5 %shard_map.110 = (f32[16,64,256]{2,1,0:T(8,128)S(1)}, f32[16,64,256]{2,1,0:T(8,128)S(1)}, f32[16,64,256]{2,1,0:T(8,128)S(1)}, f32[4,64,256]{2,1,0:T(8,128)S(1)}, f32[4,64,256]{2,1,0:T(8,128)S(1)}) custom-call(s32[102]{0:T(128)S(1)} %concatenate.6.ints, f32[132]{0:T(256)S(1)} %pad_maximum_fusion.floats, f32[16,64,256]{2,1,0:T(8,128)S(1)} %bitcast.33, ...), custom_call_target="tpu_custom_call" | custom-call | tf_op jit(solution)/shard_map/pallas_call | solution.py:45
  108.8 2.8 %shard_map.113 = (f32[16,64,256]{2,1,0:T(8,128)S(1)}, f32[16,64,256]{2,1,0:T(8,128)S(1)}, f32[16,64,256]{2,1,0:T(8,128)S(1)}, f32[4,64,256]{2,1,0:T(8,128)S(1)}, f32[4,64,256]{2,1,0:T(8,128)S(1)}) custom-call(s32[102]{0:T(128)S(1)} %concatenate.6.ints, f32[132]{0:T(256)S(1)} %pad_maximum_fusion.floats, f32[16,64,256]{2,1,0:T(8,128)S(1)} %get-tuple-element.64.refs_0_, ...), custom_call_target="tpu_custom_call" | custom-call | tf_op jit(solution)/shard_map/pallas_call | solution.py:45
  112.1 7.3 %collective-permute-start.16 = (f32[4,64,256]{2,1,0:T(8,128)S(1)}, f32[4,64,256]{2,1,0:T(8,128)S(1)}, u32[]{:S(2)}, u32[]{:S(2)}) collective-permute-start(f32[4,64,256]{2,1,0:T(8,128)S(1)} %get-tuple-element.71), channel_id=1, source_target_pairs={{1,2},{3,4},{5,6},{7,8},{9,10},{11,12},{13,14},{15,16},{17,18},{19... | collective-permute-start | bytes 786440 | tf_op jit(solution)/shard_map/ppermute | solution.py:600
  119.5 2.8 %shard_map.111 = (f32[16,64,256]{2,1,0:T(8,128)S(1)}, f32[16,64,256]{2,1,0:T(8,128)S(1)}, f32[4,64,256]{2,1,0:T(8,128)S(1)}, f32[4,64,256]{2,1,0:T(8,128)S(1)}) custom-call(s32[102]{0:T(128)S(1)} %concatenate.6.ints, f32[132]{0:T(256)S(1)} %pad_maximum_fusion.floats, f32[16,64,256]{2,1,0:T(8,128)S(1)} %get-tuple-element.55.refs_0_.refs_2_, ...), custom_call_target="tpu_custom_call" | custom-call | tf_op jit(solution)/shard_map/pallas_call | solution.py:45
  122.4 6.5 %collective-permute-start.18 = (f32[4,64,256]{2,1,0:T(8,128)S(1)}, f32[4,64,256]{2,1,0:T(8,128)S(1)}, u32[]{:S(2)}, u32[]{:S(2)}) collective-permute-start(f32[4,64,256]{2,1,0:T(8,128)S(1)} %get-tuple-element.76), channel_id=1, source_target_pairs={{1,2},{3,4},{5,6},{7,8},{9,10},{11,12},{13,14},{15,16},{17,18},{19... | collective-permute-start | bytes 786440 | tf_op jit(solution)/shard_map/ppermute | solution.py:600
  128.9 2.5 %shard_map.114.refs_1_ = f32[16,64,256]{2,1,0:T(8,128)S(1)} custom-call(s32[102]{0:T(128)S(1)} %concatenate.6.ints, f32[132]{0:T(256)S(1)} %pad_maximum_fusion.floats, f32[16,64,256]{2,1,0:T(8,128)S(1)} %get-tuple-element.68.refs_0_, f32[16,64,256]{2,1,0:T(8,128)S(1)} %get-tuple-element.69.refs_1_, f32[8,16,8,256]{3,2,1,0:T(8,128)S(1)} %bitcast.23, ...), custom_call_target="tpu_custom_call" | custom-call | tf_op jit(solution)/shard_map/pallas_call | solution.py:45
  132.2 2.6 %shard_map.116 = (f32[8,16,8,256]{3,2,1,0:T(8,128)S(1)}, f32[8,64,256]{2,1,0:T(8,128)S(1)}) custom-call(s32[102]{0:T(128)S(1)} %concatenate.6.ints, f32[132]{0:T(256)S(1)} %pad_maximum_fusion.floats, f32[16,64,256]{2,1,0:T(8,128)S(1)} %get-tuple-element.59.refs_4_.w, f32[16,64,256]{2,1,0:T(8,128)S(1)} %get-tuple-element.60.vw, ...), custom_call_target="tpu_custom_call" | custom-call | tf_op jit(solution)/shard_map/pallas_call | solution.py:45
  136.0 23.7 %all_to_all.21.got = f32[32,4,8,256]{3,2,1,0:T(8,128)S(1)} all-to-all(f32[32,4,8,256]{3,2,1,0:T(8,128)S(1)} %bitcast.34), channel_id=1, replica_groups=mesh['shot'=8,'zz'=8,'quad'=4] {'shot','quad'}, dimensions={0} | all-to-all | bytes 2097152 | tf_op jit(solution)/shard_map/all_to_all | solution.py:497
  161.5 8.4 %all-to-all-start.3 = ((f32[32,4,8,256]{3,2,1,0:T(8,128)}), f32[32,4,8,256]{3,2,1,0:T(8,128)S(1)}, u32[]{:S(2)}, u32[]{:S(2)}) async-start(f32[32,4,8,256]{3,2,1,0:T(8,128)} %get-tuple-element.78), calls=%async_computation.3 | async-start | bytes 2097152 | tf_op jit(solution)/shard_map/all_to_all | solution.py:497
  171.2 2.9 %collective-permute-start.20 = (f32[2,4,8,256]{3,2,1,0:T(8,128)S(1)}, f32[2,4,8,256]{3,2,1,0:T(8,128)S(1)}, u32[]{:S(2)}, u32[]{:S(2)}) collective-permute-start(f32[2,4,8,256]{3,2,1,0:T(8,128)S(1)} %shard_map.118), channel_id=1, source_target_pairs={{0,2},{1,3},{2,0},{3,1},{4,6},{5,7},{6,4},{7,5},{8,10},{9,11},{10,... | collective-permute-start | bytes 196616 | tf_op jit(solution)/shard_map/ppermute | solution.py:501
  176.2 21.7 %all-to-all-done.3.came = f32[32,4,8,256]{3,2,1,0:T(8,128)S(1)} async-done(((f32[32,4,8,256]{3,2,1,0:T(8,128)}), f32[32,4,8,256]{3,2,1,0:T(8,128)S(1)}, u32[]{:S(2)}, u32[]{:S(2)}) %all-to-all-start.3) | async-done | bytes 1048608 | tf_op jit(solution)/shard_map/all_to_all | solution.py:497
  (74 shorter events, 17.6 us)
Async XLA Ops:
  3.2 33.2 %copy-start = (f32[1,16,64,256]{3,2,1,0:T(8,128)S(1)}, f32[1,16,64,256]{3,2,1,0:T(8,128)}, u32[]{:S(2)}) copy-start(f32[1,16,64,256]{3,2,1,0:T(8,128)} %param.19) | copy-start | bytes 3145732
  3.2 41.0 %all-to-all-start = ((f32[32,4,8,256]{3,2,1,0:T(8,128)}), f32[32,4,8,256]{3,2,1,0:T(8,128)S(1)}, u32[]{:S(2)}, u32[]{:S(2)}) async-start(f32[32,4,8,256]{3,2,1,0:T(8,128)} %bitcast.39), calls=%async_computation | async-start | bytes 2097152 | tf_op jit(solution)/shard_map/all_to_all | solution.py:497
  16.1 20.3 %collective-permute-start.5 = (f32[8,64,256]{2,1,0:T(8,128)}, f32[8,64,256]{2,1,0:T(8,128)}, u32[]{:S(2)}, u32[]{:S(2)}) collective-permute-start(f32[8,64,256]{2,1,0:T(8,128)} %get-tuple-element.46), channel_id=1, source_target_pairs={{0,1},{1,0},{2,3},{3,2},{4,5},{5,4},{6,7},{7,6},{8,9},{9,8},{10,11... | collective-permute-start | bytes 1572872 | tf_op jit(solution)/shard_map/ppermute | solution.py:599
  16.4 20.0 %collective-permute-start.6 = (f32[8,64,256]{2,1,0:T(8,128)}, f32[8,64,256]{2,1,0:T(8,128)}, u32[]{:S(2)}, u32[]{:S(2)}) collective-permute-start(f32[8,64,256]{2,1,0:T(8,128)} %get-tuple-element.47), channel_id=1, source_target_pairs={{1,2},{3,4},{5,6},{7,8},{9,10},{11,12},{13,14},{15,16},{17,18},{19... | collective-permute-start | bytes 1572872 | tf_op jit(solution)/shard_map/ppermute | solution.py:600
  22.0 2.8 %collective-permute-start = (s32[8]{0:T(128)S(1)}, s32[8]{0:T(128)S(1)}, u32[]{:S(2)}, u32[]{:S(2)}) collective-permute-start(s32[8]{0:T(128)S(1)} %compare_select_fusion), channel_id=1, source_target_pairs={{0,32},{32,0},{64,96},{96,64},{128,160},{160,128},{192,224},{224,1... | collective-permute-start | bytes 104 | tf_op jit(solution)/shard_map/ppermute | solution.py:29
  23.3 4.3 %collective-permute-start.3 = (f32[2,4,8,256]{3,2,1,0:T(8,128)S(1)}, f32[2,4,8,256]{3,2,1,0:T(8,128)S(1)}, u32[]{:S(2)}, u32[]{:S(2)}) collective-permute-start(f32[2,4,8,256]{3,2,1,0:T(8,128)S(1)} %get-tuple-element.45), channel_id=1, source_target_pairs={{0,1},{1,0},{2,3},{3,2},{4,5},{5,4},{6,7},{7,6},{8,9},{9,8},{10,11... | collective-permute-start | bytes 196616 | tf_op jit(solution)/shard_map/ppermute | solution.py:501
  24.8 4.2 %collective-permute-start.1 = (s32[8]{0:T(128)S(1)}, s32[8]{0:T(128)S(1)}, u32[]{:S(2)}, u32[]{:S(2)}) collective-permute-start(s32[8]{0:T(128)S(1)} %fusion), channel_id=1, source_target_pairs={{0,64},{32,96},{64,0},{96,32},{128,192},{160,224},{192,128},{224,1... | collective-permute-start | bytes 104 | tf_op jit(solution)/shard_map/ppermute | solution.py:29
  27.6 16.5 %collective-permute-start.4 = (f32[2,4,8,256]{3,2,1,0:T(8,128)S(1)}, f32[2,4,8,256]{3,2,1,0:T(8,128)S(1)}, u32[]{:S(2)}, u32[]{:S(2)}) collective-permute-start(f32[2,4,8,256]{3,2,1,0:T(8,128)S(1)} %shard_map.109), channel_id=1, source_target_pairs={{0,2},{1,3},{2,0},{3,1},{4,6},{5,7},{6,4},{7,5},{8,10},{9,11},{10,... | collective-permute-start | bytes 196616 | tf_op jit(solution)/shard_map/ppermute | solution.py:501
  29.0 7.4 %collective-permute-start.2 = (s32[8]{0:T(128)S(1)}, s32[8]{0:T(128)S(1)}, u32[]{:S(2)}, u32[]{:S(2)}) collective-permute-start(s32[8]{0:T(128)S(1)} %fusion.1), channel_id=1, source_target_pairs={{0,128},{32,160},{64,192},{96,224},{128,0},{160,32},{192,64},{224,... | collective-permute-start | bytes 104 | tf_op jit(solution)/shard_map/ppermute | solution.py:29
  83.8 8.9 %collective-permute-start.11 = (f32[4,64,256]{2,1,0:T(8,128)S(1)}, f32[4,64,256]{2,1,0:T(8,128)S(1)}, u32[]{:S(2)}, u32[]{:S(2)}) collective-permute-start(f32[4,64,256]{2,1,0:T(8,128)S(1)} %get-tuple-element.62), channel_id=1, source_target_pairs={{0,1},{1,0},{2,3},{3,2},{4,5},{5,4},{6,7},{7,6},{8,9},{9,8},{10,11... | collective-permute-start | bytes 786440 | tf_op jit(solution)/shard_map/ppermute | solution.py:599
  84.3 9.3 %collective-permute-start.12 = (f32[4,64,256]{2,1,0:T(8,128)S(1)}, f32[4,64,256]{2,1,0:T(8,128)S(1)}, u32[]{:S(2)}, u32[]{:S(2)}) collective-permute-start(f32[4,64,256]{2,1,0:T(8,128)S(1)} %get-tuple-element.63), channel_id=1, source_target_pairs={{1,2},{3,4},{5,6},{7,8},{9,10},{11,12},{13,14},{15,16},{17,18},{19... | collective-permute-start | bytes 786440 | tf_op jit(solution)/shard_map/ppermute | solution.py:600
  87.5 15.5 %collective-permute-start.7 = (f32[4,64,256]{2,1,0:T(8,128)S(1)}, f32[4,64,256]{2,1,0:T(8,128)S(1)}, u32[]{:S(2)}, u32[]{:S(2)}) collective-permute-start(f32[4,64,256]{2,1,0:T(8,128)S(1)} %get-tuple-element.53), channel_id=1, source_target_pairs={{0,1},{1,0},{2,3},{3,2},{4,5},{5,4},{6,7},{7,6},{8,9},{9,8},{10,11... | collective-permute-start | bytes 786440 | tf_op jit(solution)/shard_map/ppermute | solution.py:599
  87.6 15.3 %collective-permute-start.8 = (f32[4,64,256]{2,1,0:T(8,128)S(1)}, f32[4,64,256]{2,1,0:T(8,128)S(1)}, u32[]{:S(2)}, u32[]{:S(2)}) collective-permute-start(f32[4,64,256]{2,1,0:T(8,128)S(1)} %get-tuple-element.54), channel_id=1, source_target_pairs={{1,2},{3,4},{5,6},{7,8},{9,10},{11,12},{13,14},{15,16},{17,18},{19... | collective-permute-start | bytes 786440 | tf_op jit(solution)/shard_map/ppermute | solution.py:600
  96.9 11.8 %collective-permute-start.13 = (f32[4,64,256]{2,1,0:T(8,128)S(1)}, f32[4,64,256]{2,1,0:T(8,128)S(1)}, u32[]{:S(2)}, u32[]{:S(2)}) collective-permute-start(f32[4,64,256]{2,1,0:T(8,128)S(1)} %get-tuple-element.66), channel_id=1, source_target_pairs={{0,1},{1,0},{2,3},{3,2},{4,5},{5,4},{6,7},{7,6},{8,9},{9,8},{10,11... | collective-permute-start | bytes 786440 | tf_op jit(solution)/shard_map/ppermute | solution.py:599
  97.0 11.7 %collective-permute-start.14 = (f32[4,64,256]{2,1,0:T(8,128)S(1)}, f32[4,64,256]{2,1,0:T(8,128)S(1)}, u32[]{:S(2)}, u32[]{:S(2)}) collective-permute-start(f32[4,64,256]{2,1,0:T(8,128)S(1)} %get-tuple-element.67), channel_id=1, source_target_pairs={{1,2},{3,4},{5,6},{7,8},{9,10},{11,12},{13,14},{15,16},{17,18},{19... | collective-permute-start | bytes 786440 | tf_op jit(solution)/shard_map/ppermute | solution.py:600
  106.5 13.0 %collective-permute-start.10 = (f32[4,64,256]{2,1,0:T(8,128)S(1)}, f32[4,64,256]{2,1,0:T(8,128)S(1)}, u32[]{:S(2)}, u32[]{:S(2)}) collective-permute-start(f32[4,64,256]{2,1,0:T(8,128)S(1)} %get-tuple-element.58), channel_id=1, source_target_pairs={{1,2},{3,4},{5,6},{7,8},{9,10},{11,12},{13,14},{15,16},{17,18},{19... | collective-permute-start | bytes 786440 | tf_op jit(solution)/shard_map/ppermute | solution.py:600
  108.7 10.8 %collective-permute-start.9 = (f32[4,64,256]{2,1,0:T(8,128)S(1)}, f32[4,64,256]{2,1,0:T(8,128)S(1)}, u32[]{:S(2)}, u32[]{:S(2)}) collective-permute-start(f32[4,64,256]{2,1,0:T(8,128)S(1)} %get-tuple-element.57), channel_id=1, source_target_pairs={{0,1},{1,0},{2,3},{3,2},{4,5},{5,4},{6,7},{7,6},{8,9},{9,8},{10,11... | collective-permute-start | bytes 786440 | tf_op jit(solution)/shard_map/ppermute | solution.py:599
  111.6 17.3 %collective-permute-start.15 = (f32[4,64,256]{2,1,0:T(8,128)S(1)}, f32[4,64,256]{2,1,0:T(8,128)S(1)}, u32[]{:S(2)}, u32[]{:S(2)}) collective-permute-start(f32[4,64,256]{2,1,0:T(8,128)S(1)} %get-tuple-element.70), channel_id=1, source_target_pairs={{0,1},{1,0},{2,3},{3,2},{4,5},{5,4},{6,7},{7,6},{8,9},{9,8},{10,11... | collective-permute-start | bytes 786440 | tf_op jit(solution)/shard_map/ppermute | solution.py:599
  112.1 16.8 %collective-permute-start.16 = (f32[4,64,256]{2,1,0:T(8,128)S(1)}, f32[4,64,256]{2,1,0:T(8,128)S(1)}, u32[]{:S(2)}, u32[]{:S(2)}) collective-permute-start(f32[4,64,256]{2,1,0:T(8,128)S(1)} %get-tuple-element.71), channel_id=1, source_target_pairs={{1,2},{3,4},{5,6},{7,8},{9,10},{11,12},{13,14},{15,16},{17,18},{19... | collective-permute-start | bytes 786440 | tf_op jit(solution)/shard_map/ppermute | solution.py:600
  122.3 12.5 %collective-permute-start.17 = (f32[4,64,256]{2,1,0:T(8,128)S(1)}, f32[4,64,256]{2,1,0:T(8,128)S(1)}, u32[]{:S(2)}, u32[]{:S(2)}) collective-permute-start(f32[4,64,256]{2,1,0:T(8,128)S(1)} %get-tuple-element.75), channel_id=1, source_target_pairs={{0,1},{1,0},{2,3},{3,2},{4,5},{5,4},{6,7},{7,6},{8,9},{9,8},{10,11... | collective-permute-start | bytes 786440 | tf_op jit(solution)/shard_map/ppermute | solution.py:599
  122.4 12.6 %collective-permute-start.18 = (f32[4,64,256]{2,1,0:T(8,128)S(1)}, f32[4,64,256]{2,1,0:T(8,128)S(1)}, u32[]{:S(2)}, u32[]{:S(2)}) collective-permute-start(f32[4,64,256]{2,1,0:T(8,128)S(1)} %get-tuple-element.76), channel_id=1, source_target_pairs={{1,2},{3,4},{5,6},{7,8},{9,10},{11,12},{13,14},{15,16},{17,18},{19... | collective-permute-start | bytes 786440 | tf_op jit(solution)/shard_map/ppermute | solution.py:600
  161.5 36.5 %all-to-all-start.3 = ((f32[32,4,8,256]{3,2,1,0:T(8,128)}), f32[32,4,8,256]{3,2,1,0:T(8,128)S(1)}, u32[]{:S(2)}, u32[]{:S(2)}) async-start(f32[32,4,8,256]{3,2,1,0:T(8,128)} %get-tuple-element.78), calls=%async_computation.3 | async-start | bytes 2097152 | tf_op jit(solution)/shard_map/all_to_all | solution.py:497
  169.9 1.3 collective-permute-start.19
  171.2 5.0 %collective-permute-start.20 = (f32[2,4,8,256]{3,2,1,0:T(8,128)S(1)}, f32[2,4,8,256]{3,2,1,0:T(8,128)S(1)}, u32[]{:S(2)}, u32[]{:S(2)}) collective-permute-start(f32[2,4,8,256]{3,2,1,0:T(8,128)S(1)} %shard_map.118), channel_id=1, source_target_pairs={{0,2},{1,3},{2,0},{3,1},{4,6},{5,7},{6,4},{7,5},{8,10},{9,11},{10,... | collective-permute-start | bytes 196616 | tf_op jit(solution)/shard_map/ppermute | solution.py:501
  (11 other events, 201.1 us)

commit v7 on v6

--- a/solution.py
+++ b/solution.py
@@ -9,6 +9,8 @@
 
 
 COEF = (-205.0 / 72.0, 1.6, -0.2, 8.0 / 315.0, -1.0 / 560.0)
+WHOLE = (8064.0, -1008.0, 128.0, -9.0)
+SCALE = 5040.0
 QUAD = 4
 MP = ("zz", "quad")
 PLANE = ("shot", "quad")
@@ -61,20 +63,28 @@
     rows = lax.broadcasted_iota(jnp.int32, (nz, nz), 0)
     cols = lax.broadcasted_iota(jnp.int32, (nz, nz), 1)
     apart = jnp.abs(rows - cols)
-    band = jnp.where(apart == 0, 3.0 * COEF[0], 0.0)
+    band = jnp.zeros((nz, nz), jnp.float32)
     for k in range(1, REACH + 1):
-        band = jnp.where(apart == k, COEF[k], band)
-    return band
+        band = jnp.where(apart == k, WHOLE[k - 1], band)
+    return band.astype(jnp.bfloat16)
 
 
 def prepare(field, padded, along_z):
     xs, ys, nz = field.shape
-    along_z[...] = jnp.dot(
-        field[...].reshape(xs * ys, nz),
-        band_matrix(nz),
-        precision=lax.Precision.HIGHEST,
-        preferred_element_type=jnp.float32,
-    ).reshape(xs, ys, nz)
+    band = band_matrix(nz)
+
+    def times_band(part):
+        return jnp.dot(part, band, preferred_element_type=jnp.float32)
+
+    for x in range(0, xs, REACH):
+        value = field[x : x + REACH].reshape(REACH * ys, nz)
+        high = value.astype(jnp.bfloat16)
+        rest = value - high.astype(jnp.float32)
+        middle = rest.astype(jnp.bfloat16)
+        low = (rest - middle.astype(jnp.float32)).astype(jnp.bfloat16)
+        total = (times_band(low) + times_band(middle)) + times_band(high)
+        total = total * (1.0 / SCALE) + (3.0 * COEF[0]) * value
+        along_z[x : x + REACH] = total.reshape(REACH, ys, nz)
     edge = jnp.zeros((xs, SUB, LANES), jnp.float32)
     for h in range(nz // LANES):
         padded[h, :, 0:SUB, :] = edge
@@ -92,21 +102,33 @@
         target[place] = target[place] + jnp.where(cells == z, amount, 0.0)
 
 
-def add_source(target, ints, floats, n):
-    x = ints[SOURCE] - ints[BASE]
-    add_point(target, x, ints[SOURCE + 1], ints[SOURCE + 2], floats[n])
-
-
-def add_receivers(target, ints, floats, steps, receivers, n):
+def whole(scalars, at):
+    return scalars[at].astype(jnp.int32)
+
+
+def is_even(scalars):
+    return scalars[EVEN] > 0.5
+
+
+def add_source(target, receivers, scalars, n):
+    x = whole(scalars, SOURCE) - whole(scalars, BASE)
+    amount = scalars[RECEIVERS + 3 * receivers + n]
+    add_point(target, x, whole(scalars, SOURCE + 1), whole(scalars, SOURCE + 2), amount)
+
+
+def add_receivers(target, scalars, steps, receivers, n):
     xs = target.shape[0]
-    away = ints[SOURCE] - ints[BASE]
+    base = whole(scalars, BASE)
+    away = whole(scalars, SOURCE) - base
+    amounts = RECEIVERS + 3 * receivers + steps + n * receivers
 
     @pl.when((away + NEAR >= 0) & (away - NEAR < xs))
     def _():
         def one(j, carry):
             at = RECEIVERS + 3 * j
-            amount = floats[steps + n * receivers + j]
-            add_point(target, ints[at] - ints[BASE], ints[at + 1], ints[at + 2], amount)
+            x = whole(scalars, at) - base
+            y, z = whole(scalars, at + 1), whole(scalars, at + 2)
+            add_point(target, x, y, z, scalars[amounts + j])
             return carry
 
         lax.fori_loop(0, receivers, one, 0)
@@ -150,21 +172,21 @@
     lax.fori_loop(0, ys // SUB, step, 0)
 
 
-def switch_on(ints, n):
-    return jnp.where(ints[COUNT] > n, 1.0, 0.0).astype(jnp.float32)
-
-
-def first_kernel(steps, receivers, ints, floats, u, w, near, far, d, e, along_u, along_w, pad, sems):
-    even = ints[EVEN] == 1
+def switch_on(scalars, n):
+    return jnp.where(scalars[COUNT] > n + 0.5, 1.0, 0.0).astype(jnp.float32)
+
+
+def first_kernel(steps, receivers, scalars, u, w, near, far, d, e, along_u, along_w, pad, sems):
+    even = is_even(scalars)
     copies = []
     for k, (field, along, out) in enumerate(((u, along_u, d), (w, along_w, e))):
         prepare(field, pad, along)
         if k == 0:
-            add_source(along, ints, floats, 0)
-            live = switch_on(ints, 0)
+            add_source(along, receivers, scalars, 0)
+            live = switch_on(scalars, 0)
         else:
-            add_receivers(along, ints, floats, steps, receivers, steps - 1)
-            live = switch_on(ints, steps - 1)
+            add_receivers(along, scalars, steps, receivers, steps - 1)
+            live = switch_on(scalars, steps - 1)
 
         def work(i, y0, h, lanes):
             rows = pl.ds(y0, SUB)
@@ -193,11 +215,11 @@
         outer[...] = field[xs - REACH :]
 
 
-def edges_kernel(steps, ints, *refs):
+def edges_kernel(steps, scalars, *refs):
     fields, speed = (refs[0:3], refs[3:6]), refs[6]
     outs, held, sems = (refs[7:9], refs[9:11]), refs[11], refs[12]
     xs, ys, _ = refs[0].shape
-    even = ints[EVEN] == 1
+    even = is_even(scalars)
     starts = (0, xs - REACH)
     copies = [
         pltpu.make_async_copy(
@@ -210,7 +232,7 @@
     for copy in copies:
         copy.start()
     for f in range(2):
-        live = switch_on(ints, 0 if f == 0 else steps - 1)
+        live = switch_on(scalars, 0 if f == 0 else steps - 1)
         for copy in copies[6 * f : 6 * f + 6]:
             copy.wait()
 
@@ -239,8 +261,8 @@
             outer[...] = held[f, 0, 1]
 
 
-def opening(ints, n, now, back, drive, speed, new, gain):
-    live = switch_on(ints, n)
+def opening(scalars, n, now, back, drive, speed, new, gain):
+    live = switch_on(scalars, n)
 
     def work(i, y0, h, lanes):
         rows = pl.ds(y0, SUB)
@@ -253,19 +275,19 @@
     each_block(now, work)
 
 
-def forward_kernel(n, last, ints, floats, *refs):
+def forward_kernel(receivers, n, last, scalars, *refs):
     if n == 1:
         u0, back, drive0, p, near, far, drive, new, gain, inner, outer, pad, along = refs
-        opening(ints, 0, u0, back, drive0, p, new, gain)
+        opening(scalars, 0, u0, back, drive0, p, new, gain)
         u, vu = new, gain
     elif last:
         u, vu, p, near, far, drive, pad, along = refs
     else:
         u, vu, p, near, far, drive, new, gain, inner, outer, pad, along = refs
     prepare(u, pad, along)
-    add_source(along, ints, floats, n)
-    live = switch_on(ints, n)
-    even = ints[EVEN] == 1
+    add_source(along, receivers, scalars, n)
+    live = switch_on(scalars, n)
+    even = is_even(scalars)
 
     def work(i, y0, h, lanes):
         rows = pl.ds(y0, SUB)
@@ -283,17 +305,17 @@
         edge_out(even, new, inner, outer)
 
 
-def adjoint_kernel(steps, receivers, n, ints, floats, *refs):
+def adjoint_kernel(steps, receivers, n, scalars, *refs):
     if n == steps - 2:
         w0, back, push, p, near, far, w, new, gain, inner, outer, pad, along = refs
-        opening(ints, steps - 1, w0, back, push, p, w, gain)
+        opening(scalars, steps - 1, w0, back, push, p, w, gain)
         vw = gain
     else:
         w, vw, p, near, far, new, gain, inner, outer, pad, along = refs
     prepare(w, pad, along)
-    add_receivers(along, ints, floats, steps, receivers, n)
-    live = switch_on(ints, n)
-    even = ints[EVEN] == 1
+    add_receivers(along, scalars, steps, receivers, n)
+    live = switch_on(scalars, n)
+    even = is_even(scalars)
 
     def work(i, y0, h, lanes):
         rows = pl.ds(y0, SUB)
@@ -306,11 +328,11 @@
     edge_out(even, new, inner, outer)
 
 
-def last_inner_kernel(steps, receivers, ints, floats, w, vw, p, partial, drive, image, open_sum, pad, along):
+def last_inner_kernel(steps, receivers, scalars, w, vw, p, partial, drive, image, open_sum, pad, along):
     xs = w.shape[0]
     prepare(w, pad, along)
-    add_receivers(along, ints, floats, steps, receivers, 0)
-    live = switch_on(ints, 0)
+    add_receivers(along, scalars, steps, receivers, 0)
+    live = switch_on(scalars, 0)
 
     def work(i, y0, h, lanes):
         rows = pl.ds(y0, SUB)
@@ -325,11 +347,11 @@
     each_block(w, work)
 
 
-def last_outer_kernel(ints, w, vw, p, partial, drive, open_sum, near, far, inside, image):
+def last_outer_kernel(scalars, w, vw, p, partial, drive, open_sum, near, far, inside, image):
     del inside
     xs = w.shape[0]
-    live = switch_on(ints, 0)
-    even = ints[EVEN] == 1
+    live = switch_on(scalars, 0)
+    even = is_even(scalars)
 
     def work(i, y0, h, lanes):
         rows = pl.ds(y0, SUB)
@@ -410,9 +432,9 @@
     out[1] = swapped[1]
 
 
-def gather_kernel(zs, table, spot, line, keep, swapped, far, sent, sems):
+def gather_kernel(zs, table, line, keep, swapped, far, sent, sems):
     slots = sent.shape[0]
-    me_z, me_q = spot[1], spot[2]
+    me_z, me_q = table[table.shape[0] - 2], table[table.shape[0] - 1]
 
     def one(slot, carry):
         tile = table[slot // QUAD] + slot % QUAD
@@ -451,8 +473,8 @@
     lax.fori_loop(0, slots, done, 0)
 
 
-def scatter_kernel(zs, table, spot, got, line, keep, swap, held, sems):
-    me_z, me_q = spot[1], spot[2]
+def scatter_kernel(zs, table, got, line, keep, swap, held, sems):
+    me_z, me_q = table[table.shape[0] - 2], table[table.shape[0] - 1]
     held[...] = jnp.zeros_like(held)
 
     def one(s, carry):
@@ -477,9 +499,9 @@
         copy.wait()
 
 
-def finish_kernel(zs, spot, came, keep, swapped, far, out):
+def finish_kernel(zs, table, came, keep, swapped, far, out):
     planes = came.shape[1]
-    me_z, me_q = spot[1], spot[2]
+    me_z, me_q = table[table.shape[0] - 2], table[table.shape[0] - 1]
     extras = (keep[0], swapped[0], far[0], far[1])
     for turn in range(QUAD):
         q = me_q ^ turn
@@ -532,22 +554,22 @@
     return parts.reshape(zs * QUAD, planes, slab, nz), inner, outer, keep, swap
 
 
-def model_parts(line, extras, table, spot):
+def model_parts(line, extras, table):
     slots = lax.axis_size("shot") * QUAD
     smem = pl.BlockSpec(memory_space=pltpu.SMEM)
     anywhere = pl.BlockSpec(memory_space=pl.ANY)
     return pl.pallas_call(
         functools.partial(gather_kernel, lax.axis_size("zz")),
         out_shape=hbm32(slots, *line.shape[1:]),
-        in_specs=[smem, smem] + [anywhere] * 4,
+        in_specs=[smem] + [anywhere] * 4,
         out_specs=pl.BlockSpec(memory_space=pltpu.HBM),
         scratch_shapes=[pltpu.SemaphoreType.DMA((slots,))],
         compiler_params=pltpu.CompilerParams(vmem_limit_bytes=1 << 20),
         name="gather",
-    )(table, spot, line, *extras)
-
-
-def return_image(image, table, spot):
+    )(table, line, *extras)
+
+
+def return_image(image, table):
     shots, tile_x, slab, nz = image.shape
     zs = lax.axis_size("zz")
     planes = tile_x // QUAD
@@ -557,7 +579,7 @@
     line, keep, swap = pl.pallas_call(
         functools.partial(scatter_kernel, zs),
         out_shape=[hbm32(zs * QUAD, planes, slab, nz)] + [f32(2, planes, slab, nz)] * 2,
-        in_specs=[smem, smem, vmem],
+        in_specs=[smem, vmem],
         out_specs=[pl.BlockSpec(memory_space=pltpu.HBM), vmem, vmem],
         scratch_shapes=[
             pltpu.VMEM(((zs + 1) * QUAD, planes, slab, nz), jnp.float32),
@@ -565,16 +587,16 @@
         ],
         compiler_params=pltpu.CompilerParams(vmem_limit_bytes=VMEM_LIMIT),
         name="scatter",
-    )(table, spot, got)
+    )(table, got)
     came = exchange(line, MP)
     extras = quad_relay(keep, swap)
     (out,) = local_kernel(
-        functools.partial(finish_kernel, zs), [spot], [came, *extras], [f32(2, tile_x, slab, nz)]
+        functools.partial(finish_kernel, zs), [table], [came, *extras], [f32(2, tile_x, slab, nz)]
     )
     return out
 
 
-def edges(steps, ints, forward, adjoint, speed):
+def edges(steps, scalars, forward, adjoint, speed):
     _, ny, nz = forward[0].shape
     hbm = pl.BlockSpec(memory_space=pltpu.HBM)
     vmem = pl.BlockSpec(memory_space=pltpu.VMEM)
@@ -589,7 +611,7 @@
         ],
         compiler_params=pltpu.CompilerParams(vmem_limit_bytes=VMEM_LIMIT),
         name="edges",
-    )(ints, *map(in_hbm, forward), *map(in_hbm, adjoint), speed)
+    )(scalars, *map(in_hbm, forward), *map(in_hbm, adjoint), speed)
 
 
 def halos(inner, outer):
@@ -624,25 +646,25 @@
     sides = halos(inner, outer)
     line = exchange(parts, MP)
     extras = quad_relay(keep, swap)
-    table = all_first(aperture_first[0])
+    table = jnp.concatenate([all_first(aperture_first[0]), spot])
     me_index = lax.axis_index(MP)
     even = me_index % 2 == 0
     base = (me_index * tile_x).reshape(1).astype(jnp.int32)
-    ints = jnp.concatenate(
+    scalars = jnp.concatenate(
         [
-            step_count,
-            base,
-            even.reshape(1).astype(jnp.int32),
-            source_pos[0],
-            receiver_pos[0].reshape(-1),
+            step_count.astype(jnp.float32),
+            base.astype(jnp.float32),
+            even.reshape(1).astype(jnp.float32),
+            source_pos[0].astype(jnp.float32),
+            receiver_pos[0].reshape(-1).astype(jnp.float32),
+            wavelet[0],
+            residual[0].reshape(-1),
         ]
     )
-    floats = jnp.concatenate([wavelet[0], residual[0].reshape(-1)])
     field = f32(tile_x, ny, nz)
     edge = f32(REACH, ny, nz)
     padded = pltpu.VMEM((nz // LANES, tile_x, ny + 2 * SUB, LANES), jnp.float32)
     along = pltpu.VMEM((tile_x, ny, nz), jnp.float32)
-    scalars = [ints, floats]
     drives = []
     hbm = pl.BlockSpec(memory_space=pltpu.HBM)
     vmem = pl.BlockSpec(memory_space=pltpu.VMEM)
@@ -650,18 +672,18 @@
     drive, push = pl.pallas_call(
         functools.partial(first_kernel, steps, receivers),
         out_shape=[hbm32(tile_x, ny, nz)] * 2,
-        in_specs=[smem, smem] + [vmem] * 4,
+        in_specs=[smem] + [vmem] * 4,
         out_specs=[hbm, hbm],
         scratch_shapes=[along, along, padded, pltpu.SemaphoreType.DMA((2,))],
         compiler_params=pltpu.CompilerParams(vmem_limit_bytes=VMEM_LIMIT),
         name="first",
-    )(*scalars, u, w, *sides)
-    sent = model_parts(line, extras, table, spot)
+    )(scalars, u, w, *sides)
+    sent = model_parts(line, extras, table)
     sent, drive, push = lax.optimization_barrier((sent, drive, push))
     owned = exchange(sent, PLANE).reshape(-1, tile_x, SUB, nz)
     drives.append(drive)
     openings = edges(
-        steps, ints, (u, forward_prev[0], drive), (w, adjoint_prev[0], push), owned
+        steps, scalars, (u, forward_prev[0], drive), (w, adjoint_prev[0], push), owned
     )
     u_sides = halos(*openings[:2])
     w_sides = halos(*openings[2:])
@@ -670,8 +692,8 @@
         last = n == steps - 1
         state = [u, forward_prev[0], drive] if n == 1 else [u, vu]
         drive, *moved = local_kernel(
-            functools.partial(forward_kernel, n, last),
-            scalars,
+            functools.partial(forward_kernel, receivers, n, last),
+            [scalars],
             [*state, owned, *u_sides],
             [field] if last else [field, field, field, edge, edge],
             [padded, along],
@@ -688,7 +710,7 @@
             outs = [field] + outs
         *opened, w, vw, inner, outer = local_kernel(
             functools.partial(adjoint_kernel, steps, receivers, steps - 1 - n),
-            scalars,
+            [scalars],
             [*state, owned, *w_sides],
             outs,
             [padded, along],
@@ -703,15 +725,15 @@
     whole = f32(ny // SUB, tile_x, SUB, nz)
     image, open_sum = local_kernel(
         functools.partial(last_inner_kernel, steps, receivers),
-        scalars,
+        [scalars],
         state,
         [whole, f32(2 * REACH, ny, nz)],
         [padded, along],
     )
     (image,) = local_kernel(
-        last_outer_kernel, [ints], [*state, open_sum, *w_sides, image], [whole], aliases={9: 0}
+        last_outer_kernel, [scalars], [*state, open_sum, *w_sides, image], [whole], aliases={9: 0}
     )
-    return return_image(image, table, spot)
+    return return_image(image, table)
 
 
 def solution(mesh):

time: 200 us -> 197 us (0.985)
  Pallas kernels: 38.4 us -> 34 us
  waiting for transfers between devices: 33.5 us -> 37.7 us
  blocking collectives: 58 us -> 55.8 us
    all_to_all x2, waiting for transfers between devices: 21.8 us -> 24.4 us  [exchange(): return lax.all_to_all(parts, axes, split_axis=0, concat_axis=0, tiled=True)]
    pallas_call x11, Pallas kernels: 20.6 us -> 18.4 us  [local_kernel(): pl.pallas_call(body, out_shape=outs, in_specs=[smem] * len(scalars) + [vm...]
    pallas_call x1, Pallas kernels: 7.6 us -> 5.44 us  [window(): pl.pallas_call(functools.partial(first_kernel, steps, receivers), out_sha...]
    all_to_all x2, blocking collectives: 58 us -> 55.8 us  [exchange(): return lax.all_to_all(parts, axes, split_axis=0, concat_axis=0, tiled=True)]
    ppermute x4, waiting for transfers between devices: 3.12 us -> 5.13 us  [swap_quads(): return lax.ppermute(value, 'quad', [(q, q ^ turn) for q in range(QUAD)])]
  transfers between devices with their start and end apart: 23 -> 23, of which waited for: 9 -> 10; matrix products, arithmetic and copies ran while one was open for 0% -> 0% of each run, Pallas kernels for 13% -> 11%
where the time goes in v7:
time: 197 us; the launch traced here: 196 us
  starting transfers between devices  66.4 us (34%)
  blocking collectives  55.8 us (28%)
  waiting for transfers between devices  37.7 us (19%)
  Pallas kernels  34 us (17%)
    all_to_all x2, blocking collectives, exchange(): return lax.all_to_all(parts, axes, split_axis=0, concat_axis=0, tiled=True)  55.8 us
    ppermute x7, starting transfers between devices, halos(): lax.ppermute(outer, MP, across + [(j, i) for i, j in across])  35.4 us
    all_to_all x2, waiting for transfers between devices, exchange(): return lax.all_to_all(parts, axes, split_axis=0, concat_axis=0, tiled=True)  24.4 us
    all_to_all x2, starting transfers between devices, exchange(): return lax.all_to_all(parts, axes, split_axis=0, concat_axis=0, tiled=True)  21.3 us
    pallas_call x11, Pallas kernels, local_kernel(): pl.pallas_call(body, out_shape=outs, in_specs=[smem] * len(scalars) + [vm...  18.4 us
    ppermute x3, waiting for transfers between devices, all_first(): lax.ppermute(known, 'shot', [(i, i ^ step) for i in range(shots)])  6.3 us
    pallas_call x1, Pallas kernels, window(): pl.pallas_call(functools.partial(first_kernel, steps, receivers), out_sha...  5.44 us
    ppermute x4, waiting for transfers between devices, swap_quads(): return lax.ppermute(value, 'quad', [(q, q ^ turn) for q in range(QUAD)])  5.13 us
  transfers between devices with their start and end apart: 23, of which 10 were waited for; matrix products, arithmetic and copies ran while one was open for 0% of the time, Pallas kernels for 11%

profile of v7, /device:TPU:1, one launch (start us, length us, event | category | flops | bytes accessed | tf_op | source)
XLA Modules:
  0.0 196.2 jit_solution(15773483858607613145)
XLA Ops:
  0.1 3.0 %split.1 = (f32[8,16,8,256]{3,2,1,0:T(8,128)}, f32[8,64,256]{2,1,0:T(8,128)}, f32[8,64,256]{2,1,0:T(8,128)}, f32[2,4,8,256]{3,2,1,0:T(8,128)S(1)}, f32[2,4,8,256]{3,2,1,0:T(8,128)S(1)}) custom-call(s32[3]{0:T(128)S(1)} %pad_add_fusion.1.spot, f32[2,16,64,256]{3,2,1,0:T(8,128)} %courant.1, f32[16,64,256]{2,1,0:T(8,128)} %bitcast.27, f32[16,64,256]{2,1,0:T(8,128)} %bitcast.31), custom_call_target="tpu_custom_call" | custom-call | tf_op jit(solution)/shard_map/split/pallas_call | solution.py:539
  3.2 12.9 %all-to-all-start = ((f32[32,4,8,256]{3,2,1,0:T(8,128)}), f32[32,4,8,256]{3,2,1,0:T(8,128)S(1)}, u32[]{:S(2)}, u32[]{:S(2)}) async-start(f32[32,4,8,256]{3,2,1,0:T(8,128)} %bitcast.40), calls=%async_computation | async-start | bytes 2097152 | tf_op jit(solution)/shard_map/all_to_all | solution.py:519
  16.4 4.9 %collective-permute-start.6 = (f32[8,64,256]{2,1,0:T(8,128)}, f32[8,64,256]{2,1,0:T(8,128)}, u32[]{:S(2)}, u32[]{:S(2)}) collective-permute-start(f32[8,64,256]{2,1,0:T(8,128)} %get-tuple-element.47), channel_id=1, source_target_pairs={{1,2},{3,4},{5,6},{7,8},{9,10},{11,12},{13,14},{15,16},{17,18},{19... | collective-permute-start | bytes 1572872 | tf_op jit(solution)/shard_map/ppermute | solution.py:622
  24.8 2.7 %collective-permute-start.1 = (s32[8]{0:T(128)S(1)}, s32[8]{0:T(128)S(1)}, u32[]{:S(2)}, u32[]{:S(2)}) collective-permute-start(s32[8]{0:T(128)S(1)} %fusion), channel_id=1, source_target_pairs={{0,64},{32,96},{64,0},{96,32},{128,192},{160,224},{192,128},{224,1... | collective-permute-start | bytes 104 | tf_op jit(solution)/shard_map/ppermute | solution.py:31
  29.4 4.4 %collective-permute-done.2 = s32[8]{0:T(128)S(1)} collective-permute-done((s32[8]{0:T(128)S(1)}, s32[8]{0:T(128)S(1)}, u32[]{:S(2)}, u32[]{:S(2)}) %collective-permute-start.2) | collective-permute-done | bytes 64 | tf_op jit(solution)/shard_map/ppermute | solution.py:31
  34.0 5.4 %first.1 = (f32[16,64,256]{2,1,0:T(8,128)}, f32[16,64,256]{2,1,0:T(8,128)}) custom-call(f32[234]{0:T(256)S(1)} %concatenate.8.scalars, f32[16,64,256]{2,1,0:T(8,128)S(1)} %bitcast.29, f32[16,64,256]{2,1,0:T(8,128)S(1)} %bitcast.33, f32[8,64,256]{2,1,0:T(8,128)} %collective-permute-done.5.near, f32[8,64,256]{2,1,0:T(8,128)} %collective-permute-done.6.far), custom_call_target="tpu_custom_call" | custom-call | tf_op jit(solution)/shard_map/first/pallas_call | solution.py:672
  41.5 2.7 %all-to-all-done.line = f32[32,4,8,256]{3,2,1,0:T(8,128)S(1)} async-done(((f32[32,4,8,256]{3,2,1,0:T(8,128)}), f32[32,4,8,256]{3,2,1,0:T(8,128)S(1)}, u32[]{:S(2)}, u32[]{:S(2)}) %all-to-all-start) | async-done | bytes 1048608 | tf_op jit(solution)/shard_map/all_to_all | solution.py:519
  44.2 2.4 %gather.1 = f32[32,4,8,256]{3,2,1,0:T(8,128)} custom-call(s32[11]{0:T(128)S(1)} %pad_add_fusion.table, f32[32,4,8,256]{3,2,1,0:T(8,128)S(1)} %all-to-all-done.line, f32[2,4,8,256]{3,2,1,0:T(8,128)S(1)} %get-tuple-element.44.keep, f32[2,4,8,256]{3,2,1,0:T(8,128)S(1)} %collective-permute-done.3.swapped, f32[2,4,8,256]{3,2,1,0:T(8,128)S(1)} %collective-permute-done.4.far), custom_call_target="tpu_custom_call" | custom-call | tf_op jit(solution)/shard_map/gather/pallas_call | solution.py:561
  46.5 32.1 %all_to_all.20 = f32[32,4,8,256]{3,2,1,0:T(8,128)S(1)} all-to-all(f32[32,4,8,256]{3,2,1,0:T(8,128)} %gather.1), channel_id=1, replica_groups=mesh['shot'=8,'zz'=8,'quad'=4] {'shot','quad'}, dimensions={0} | all-to-all | bytes 2097152 | tf_op jit(solution)/shard_map/all_to_all | solution.py:519
  78.7 2.9 %edges.1 = (f32[4,64,256]{2,1,0:T(8,128)S(1)}, f32[4,64,256]{2,1,0:T(8,128)S(1)}, f32[4,64,256]{2,1,0:T(8,128)S(1)}, f32[4,64,256]{2,1,0:T(8,128)S(1)}) custom-call(f32[234]{0:T(256)S(1)} %concatenate.8.scalars, f32[16,64,256]{2,1,0:T(8,128)} %bitcast.28, f32[16,64,256]{2,1,0:T(8,128)} %bitcast.36, f32[16,64,256]{2,1,0:T(8,128)} %get-tuple-element.52.refs_2_.drive, ...), custom_call_target="tpu_custom_call" | custom-call | tf_op jit(solution)/shard_map/edges/pallas_call | solution.py:603
  82.1 3.2 %collective-permute-start.12 = (f32[4,64,256]{2,1,0:T(8,128)S(1)}, f32[4,64,256]{2,1,0:T(8,128)S(1)}, u32[]{:S(2)}, u32[]{:S(2)}) collective-permute-start(f32[4,64,256]{2,1,0:T(8,128)S(1)} %get-tuple-element.63), channel_id=1, source_target_pairs={{1,2},{3,4},{5,6},{7,8},{9,10},{11,12},{13,14},{15,16},{17,18},{19... | collective-permute-start | bytes 786440 | tf_op jit(solution)/shard_map/ppermute | solution.py:622
  85.5 5.0 %collective-permute-start.8 = (f32[4,64,256]{2,1,0:T(8,128)S(1)}, f32[4,64,256]{2,1,0:T(8,128)S(1)}, u32[]{:S(2)}, u32[]{:S(2)}) collective-permute-start(f32[4,64,256]{2,1,0:T(8,128)S(1)} %get-tuple-element.54), channel_id=1, source_target_pairs={{1,2},{3,4},{5,6},{7,8},{9,10},{11,12},{13,14},{15,16},{17,18},{19... | collective-permute-start | bytes 786440 | tf_op jit(solution)/shard_map/ppermute | solution.py:622
  91.4 3.0 %shard_map.112 = (f32[16,64,256]{2,1,0:T(8,128)S(1)}, f32[16,64,256]{2,1,0:T(8,128)S(1)}, f32[16,64,256]{2,1,0:T(8,128)S(1)}, f32[4,64,256]{2,1,0:T(8,128)S(1)}, f32[4,64,256]{2,1,0:T(8,128)S(1)}) custom-call(f32[234]{0:T(256)S(1)} %concatenate.8.scalars, f32[16,64,256]{2,1,0:T(8,128)S(1)} %bitcast.30, f32[16,64,256]{2,1,0:T(8,128)S(1)} %bitcast.37, ...), custom_call_target="tpu_custom_call" | custom-call | tf_op jit(solution)/shard_map/pallas_call | solution.py:47
  94.5 5.9 %collective-permute-start.14 = (f32[4,64,256]{2,1,0:T(8,128)S(1)}, f32[4,64,256]{2,1,0:T(8,128)S(1)}, u32[]{:S(2)}, u32[]{:S(2)}) collective-permute-start(f32[4,64,256]{2,1,0:T(8,128)S(1)} %get-tuple-element.67), channel_id=1, source_target_pairs={{1,2},{3,4},{5,6},{7,8},{9,10},{11,12},{13,14},{15,16},{17,18},{19... | collective-permute-start | bytes 786440 | tf_op jit(solution)/shard_map/ppermute | solution.py:622
  100.5 3.0 %shard_map.110 = (f32[16,64,256]{2,1,0:T(8,128)S(1)}, f32[16,64,256]{2,1,0:T(8,128)S(1)}, f32[16,64,256]{2,1,0:T(8,128)S(1)}, f32[4,64,256]{2,1,0:T(8,128)S(1)}, f32[4,64,256]{2,1,0:T(8,128)S(1)}) custom-call(f32[234]{0:T(256)S(1)} %concatenate.8.scalars, f32[16,64,256]{2,1,0:T(8,128)S(1)} %bitcast.34, f32[16,64,256]{2,1,0:T(8,128)S(1)} %bitcast.39, ...), custom_call_target="tpu_custom_call" | custom-call | tf_op jit(solution)/shard_map/pallas_call | solution.py:47
  103.5 2.5 %collective-permute-start.10 = (f32[4,64,256]{2,1,0:T(8,128)S(1)}, f32[4,64,256]{2,1,0:T(8,128)S(1)}, u32[]{:S(2)}, u32[]{:S(2)}) collective-permute-start(f32[4,64,256]{2,1,0:T(8,128)S(1)} %get-tuple-element.58), channel_id=1, source_target_pairs={{1,2},{3,4},{5,6},{7,8},{9,10},{11,12},{13,14},{15,16},{17,18},{19... | collective-permute-start | bytes 786440 | tf_op jit(solution)/shard_map/ppermute | solution.py:622
  106.1 2.4 %shard_map.113 = (f32[16,64,256]{2,1,0:T(8,128)S(1)}, f32[16,64,256]{2,1,0:T(8,128)S(1)}, f32[16,64,256]{2,1,0:T(8,128)S(1)}, f32[4,64,256]{2,1,0:T(8,128)S(1)}, f32[4,64,256]{2,1,0:T(8,128)S(1)}) custom-call(f32[234]{0:T(256)S(1)} %concatenate.8.scalars, f32[16,64,256]{2,1,0:T(8,128)S(1)} %get-tuple-element.64.refs_0_, ...), custom_call_target="tpu_custom_call" | custom-call | tf_op jit(solution)/shard_map/pallas_call | solution.py:47
  109.3 7.0 %collective-permute-start.16 = (f32[4,64,256]{2,1,0:T(8,128)S(1)}, f32[4,64,256]{2,1,0:T(8,128)S(1)}, u32[]{:S(2)}, u32[]{:S(2)}) collective-permute-start(f32[4,64,256]{2,1,0:T(8,128)S(1)} %get-tuple-element.71), channel_id=1, source_target_pairs={{1,2},{3,4},{5,6},{7,8},{9,10},{11,12},{13,14},{15,16},{17,18},{19... | collective-permute-start | bytes 786440 | tf_op jit(solution)/shard_map/ppermute | solution.py:622
  116.3 2.4 %shard_map.111 = (f32[16,64,256]{2,1,0:T(8,128)S(1)}, f32[16,64,256]{2,1,0:T(8,128)S(1)}, f32[4,64,256]{2,1,0:T(8,128)S(1)}, f32[4,64,256]{2,1,0:T(8,128)S(1)}) custom-call(f32[234]{0:T(256)S(1)} %concatenate.8.scalars, f32[16,64,256]{2,1,0:T(8,128)S(1)} %get-tuple-element.55.refs_0_.refs_2_, f32[16,64,256]{2,1,0:T(8,128)S(1)} %get-tuple-element.56.refs_1_, ...), custom_call_target="tpu_custom_call" | custom-call | tf_op jit(solution)/shard_map/pallas_call | solution.py:47
  118.9 6.9 %collective-permute-start.18 = (f32[4,64,256]{2,1,0:T(8,128)S(1)}, f32[4,64,256]{2,1,0:T(8,128)S(1)}, u32[]{:S(2)}, u32[]{:S(2)}) collective-permute-start(f32[4,64,256]{2,1,0:T(8,128)S(1)} %get-tuple-element.76), channel_id=1, source_target_pairs={{1,2},{3,4},{5,6},{7,8},{9,10},{11,12},{13,14},{15,16},{17,18},{19... | collective-permute-start | bytes 786440 | tf_op jit(solution)/shard_map/ppermute | solution.py:622
  132.8 23.7 %all_to_all.21.got = f32[32,4,8,256]{3,2,1,0:T(8,128)S(1)} all-to-all(f32[32,4,8,256]{3,2,1,0:T(8,128)S(1)} %bitcast.35), channel_id=1, replica_groups=mesh['shot'=8,'zz'=8,'quad'=4] {'shot','quad'}, dimensions={0} | all-to-all | bytes 2097152 | tf_op jit(solution)/shard_map/all_to_all | solution.py:519
  158.4 8.4 %all-to-all-start.3 = ((f32[32,4,8,256]{3,2,1,0:T(8,128)}), f32[32,4,8,256]{3,2,1,0:T(8,128)S(1)}, u32[]{:S(2)}, u32[]{:S(2)}) async-start(f32[32,4,8,256]{3,2,1,0:T(8,128)} %get-tuple-element.78), calls=%async_computation.3 | async-start | bytes 2097152 | tf_op jit(solution)/shard_map/all_to_all | solution.py:519
  168.1 2.9 %collective-permute-start.20 = (f32[2,4,8,256]{3,2,1,0:T(8,128)S(1)}, f32[2,4,8,256]{3,2,1,0:T(8,128)S(1)}, u32[]{:S(2)}, u32[]{:S(2)}) collective-permute-start(f32[2,4,8,256]{3,2,1,0:T(8,128)S(1)} %shard_map.118), channel_id=1, source_target_pairs={{0,2},{1,3},{2,0},{3,1},{4,6},{5,7},{6,4},{7,5},{8,10},{9,11},{10,... | collective-permute-start | bytes 196616 | tf_op jit(solution)/shard_map/ppermute | solution.py:523
  173.1 21.7 %all-to-all-done.3.came = f32[32,4,8,256]{3,2,1,0:T(8,128)S(1)} async-done(((f32[32,4,8,256]{3,2,1,0:T(8,128)}), f32[32,4,8,256]{3,2,1,0:T(8,128)S(1)}, u32[]{:S(2)}, u32[]{:S(2)}) %all-to-all-start.3) | async-done | bytes 1048608 | tf_op jit(solution)/shard_map/all_to_all | solution.py:519
  (76 shorter events, 22.9 us)
Async XLA Ops:
  3.2 30.8 %copy-start = (f32[1,16,64,256]{3,2,1,0:T(8,128)S(1)}, f32[1,16,64,256]{3,2,1,0:T(8,128)}, u32[]{:S(2)}) copy-start(f32[1,16,64,256]{3,2,1,0:T(8,128)} %param.19) | copy-start | bytes 3145732
  3.2 41.0 %all-to-all-start = ((f32[32,4,8,256]{3,2,1,0:T(8,128)}), f32[32,4,8,256]{3,2,1,0:T(8,128)S(1)}, u32[]{:S(2)}, u32[]{:S(2)}) async-start(f32[32,4,8,256]{3,2,1,0:T(8,128)} %bitcast.40), calls=%async_computation | async-start | bytes 2097152 | tf_op jit(solution)/shard_map/all_to_all | solution.py:519
  16.1 17.9 %collective-permute-start.5 = (f32[8,64,256]{2,1,0:T(8,128)}, f32[8,64,256]{2,1,0:T(8,128)}, u32[]{:S(2)}, u32[]{:S(2)}) collective-permute-start(f32[8,64,256]{2,1,0:T(8,128)} %get-tuple-element.46), channel_id=1, source_target_pairs={{0,1},{1,0},{2,3},{3,2},{4,5},{5,4},{6,7},{7,6},{8,9},{9,8},{10,11... | collective-permute-start | bytes 1572872 | tf_op jit(solution)/shard_map/ppermute | solution.py:621
  16.4 17.6 %collective-permute-start.6 = (f32[8,64,256]{2,1,0:T(8,128)}, f32[8,64,256]{2,1,0:T(8,128)}, u32[]{:S(2)}, u32[]{:S(2)}) collective-permute-start(f32[8,64,256]{2,1,0:T(8,128)} %get-tuple-element.47), channel_id=1, source_target_pairs={{1,2},{3,4},{5,6},{7,8},{9,10},{11,12},{13,14},{15,16},{17,18},{19... | collective-permute-start | bytes 1572872 | tf_op jit(solution)/shard_map/ppermute | solution.py:622
  22.0 2.8 %collective-permute-start = (s32[8]{0:T(128)S(1)}, s32[8]{0:T(128)S(1)}, u32[]{:S(2)}, u32[]{:S(2)}) collective-permute-start(s32[8]{0:T(128)S(1)} %compare_select_fusion), channel_id=1, source_target_pairs={{0,32},{32,0},{64,96},{96,64},{128,160},{160,128},{192,224},{224,1... | collective-permute-start | bytes 104 | tf_op jit(solution)/shard_map/ppermute | solution.py:31
  23.3 10.5 %collective-permute-start.3 = (f32[2,4,8,256]{3,2,1,0:T(8,128)S(1)}, f32[2,4,8,256]{3,2,1,0:T(8,128)S(1)}, u32[]{:S(2)}, u32[]{:S(2)}) collective-permute-start(f32[2,4,8,256]{3,2,1,0:T(8,128)S(1)} %get-tuple-element.45), channel_id=1, source_target_pairs={{0,1},{1,0},{2,3},{3,2},{4,5},{5,4},{6,7},{7,6},{8,9},{9,8},{10,11... | collective-permute-start | bytes 196616 | tf_op jit(solution)/shard_map/ppermute | solution.py:523
  24.8 4.2 %collective-permute-start.1 = (s32[8]{0:T(128)S(1)}, s32[8]{0:T(128)S(1)}, u32[]{:S(2)}, u32[]{:S(2)}) collective-permute-start(s32[8]{0:T(128)S(1)} %fusion), channel_id=1, source_target_pairs={{0,64},{32,96},{64,0},{96,32},{128,192},{160,224},{192,128},{224,1... | collective-permute-start | bytes 104 | tf_op jit(solution)/shard_map/ppermute | solution.py:31
  29.0 4.8 %collective-permute-start.2 = (s32[8]{0:T(128)S(1)}, s32[8]{0:T(128)S(1)}, u32[]{:S(2)}, u32[]{:S(2)}) collective-permute-start(s32[8]{0:T(128)S(1)} %fusion.1), channel_id=1, source_target_pairs={{0,128},{32,160},{64,192},{96,224},{128,0},{160,32},{192,64},{224,... | collective-permute-start | bytes 104 | tf_op jit(solution)/shard_map/ppermute | solution.py:31
  33.8 7.7 %collective-permute-start.4 = (f32[2,4,8,256]{3,2,1,0:T(8,128)S(1)}, f32[2,4,8,256]{3,2,1,0:T(8,128)S(1)}, u32[]{:S(2)}, u32[]{:S(2)}) collective-permute-start(f32[2,4,8,256]{3,2,1,0:T(8,128)S(1)} %shard_map.109), channel_id=1, source_target_pairs={{0,2},{1,3},{2,0},{3,1},{4,6},{5,7},{6,4},{7,5},{8,10},{9,11},{10,... | collective-permute-start | bytes 196616 | tf_op jit(solution)/shard_map/ppermute | solution.py:523
  81.6 8.9 %collective-permute-start.11 = (f32[4,64,256]{2,1,0:T(8,128)S(1)}, f32[4,64,256]{2,1,0:T(8,128)S(1)}, u32[]{:S(2)}, u32[]{:S(2)}) collective-permute-start(f32[4,64,256]{2,1,0:T(8,128)S(1)} %get-tuple-element.62), channel_id=1, source_target_pairs={{0,1},{1,0},{2,3},{3,2},{4,5},{5,4},{6,7},{7,6},{8,9},{9,8},{10,11... | collective-permute-start | bytes 786440 | tf_op jit(solution)/shard_map/ppermute | solution.py:621
  82.1 9.3 %collective-permute-start.12 = (f32[4,64,256]{2,1,0:T(8,128)S(1)}, f32[4,64,256]{2,1,0:T(8,128)S(1)}, u32[]{:S(2)}, u32[]{:S(2)}) collective-permute-start(f32[4,64,256]{2,1,0:T(8,128)S(1)} %get-tuple-element.63), channel_id=1, source_target_pairs={{1,2},{3,4},{5,6},{7,8},{9,10},{11,12},{13,14},{15,16},{17,18},{19... | collective-permute-start | bytes 786440 | tf_op jit(solution)/shard_map/ppermute | solution.py:622
  85.3 15.1 %collective-permute-start.7 = (f32[4,64,256]{2,1,0:T(8,128)S(1)}, f32[4,64,256]{2,1,0:T(8,128)S(1)}, u32[]{:S(2)}, u32[]{:S(2)}) collective-permute-start(f32[4,64,256]{2,1,0:T(8,128)S(1)} %get-tuple-element.53), channel_id=1, source_target_pairs={{0,1},{1,0},{2,3},{3,2},{4,5},{5,4},{6,7},{7,6},{8,9},{9,8},{10,11... | collective-permute-start | bytes 786440 | tf_op jit(solution)/shard_map/ppermute | solution.py:621
  85.5 15.0 %collective-permute-start.8 = (f32[4,64,256]{2,1,0:T(8,128)S(1)}, f32[4,64,256]{2,1,0:T(8,128)S(1)}, u32[]{:S(2)}, u32[]{:S(2)}) collective-permute-start(f32[4,64,256]{2,1,0:T(8,128)S(1)} %get-tuple-element.54), channel_id=1, source_target_pairs={{1,2},{3,4},{5,6},{7,8},{9,10},{11,12},{13,14},{15,16},{17,18},{19... | collective-permute-start | bytes 786440 | tf_op jit(solution)/shard_map/ppermute | solution.py:622
  94.4 11.6 %collective-permute-start.13 = (f32[4,64,256]{2,1,0:T(8,128)S(1)}, f32[4,64,256]{2,1,0:T(8,128)S(1)}, u32[]{:S(2)}, u32[]{:S(2)}) collective-permute-start(f32[4,64,256]{2,1,0:T(8,128)S(1)} %get-tuple-element.66), channel_id=1, source_target_pairs={{0,1},{1,0},{2,3},{3,2},{4,5},{5,4},{6,7},{7,6},{8,9},{9,8},{10,11... | collective-permute-start | bytes 786440 | tf_op jit(solution)/shard_map/ppermute | solution.py:621
  94.5 11.6 %collective-permute-start.14 = (f32[4,64,256]{2,1,0:T(8,128)S(1)}, f32[4,64,256]{2,1,0:T(8,128)S(1)}, u32[]{:S(2)}, u32[]{:S(2)}) collective-permute-start(f32[4,64,256]{2,1,0:T(8,128)S(1)} %get-tuple-element.67), channel_id=1, source_target_pairs={{1,2},{3,4},{5,6},{7,8},{9,10},{11,12},{13,14},{15,16},{17,18},{19... | collective-permute-start | bytes 786440 | tf_op jit(solution)/shard_map/ppermute | solution.py:622
  103.5 12.8 %collective-permute-start.10 = (f32[4,64,256]{2,1,0:T(8,128)S(1)}, f32[4,64,256]{2,1,0:T(8,128)S(1)}, u32[]{:S(2)}, u32[]{:S(2)}) collective-permute-start(f32[4,64,256]{2,1,0:T(8,128)S(1)} %get-tuple-element.58), channel_id=1, source_target_pairs={{1,2},{3,4},{5,6},{7,8},{9,10},{11,12},{13,14},{15,16},{17,18},{19... | collective-permute-start | bytes 786440 | tf_op jit(solution)/shard_map/ppermute | solution.py:622
  106.0 10.3 %collective-permute-start.9 = (f32[4,64,256]{2,1,0:T(8,128)S(1)}, f32[4,64,256]{2,1,0:T(8,128)S(1)}, u32[]{:S(2)}, u32[]{:S(2)}) collective-permute-start(f32[4,64,256]{2,1,0:T(8,128)S(1)} %get-tuple-element.57), channel_id=1, source_target_pairs={{0,1},{1,0},{2,3},{3,2},{4,5},{5,4},{6,7},{7,6},{8,9},{9,8},{10,11... | collective-permute-start | bytes 786440 | tf_op jit(solution)/shard_map/ppermute | solution.py:621
  108.5 17.2 %collective-permute-start.15 = (f32[4,64,256]{2,1,0:T(8,128)S(1)}, f32[4,64,256]{2,1,0:T(8,128)S(1)}, u32[]{:S(2)}, u32[]{:S(2)}) collective-permute-start(f32[4,64,256]{2,1,0:T(8,128)S(1)} %get-tuple-element.70), channel_id=1, source_target_pairs={{0,1},{1,0},{2,3},{3,2},{4,5},{5,4},{6,7},{7,6},{8,9},{9,8},{10,11... | collective-permute-start | bytes 786440 | tf_op jit(solution)/shard_map/ppermute | solution.py:621
  109.3 16.4 %collective-permute-start.16 = (f32[4,64,256]{2,1,0:T(8,128)S(1)}, f32[4,64,256]{2,1,0:T(8,128)S(1)}, u32[]{:S(2)}, u32[]{:S(2)}) collective-permute-start(f32[4,64,256]{2,1,0:T(8,128)S(1)} %get-tuple-element.71), channel_id=1, source_target_pairs={{1,2},{3,4},{5,6},{7,8},{9,10},{11,12},{13,14},{15,16},{17,18},{19... | collective-permute-start | bytes 786440 | tf_op jit(solution)/shard_map/ppermute | solution.py:622
  118.8 12.2 %collective-permute-start.17 = (f32[4,64,256]{2,1,0:T(8,128)S(1)}, f32[4,64,256]{2,1,0:T(8,128)S(1)}, u32[]{:S(2)}, u32[]{:S(2)}) collective-permute-start(f32[4,64,256]{2,1,0:T(8,128)S(1)} %get-tuple-element.75), channel_id=1, source_target_pairs={{0,1},{1,0},{2,3},{3,2},{4,5},{5,4},{6,7},{7,6},{8,9},{9,8},{10,11... | collective-permute-start | bytes 786440 | tf_op jit(solution)/shard_map/ppermute | solution.py:621
  118.9 13.0 %collective-permute-start.18 = (f32[4,64,256]{2,1,0:T(8,128)S(1)}, f32[4,64,256]{2,1,0:T(8,128)S(1)}, u32[]{:S(2)}, u32[]{:S(2)}) collective-permute-start(f32[4,64,256]{2,1,0:T(8,128)S(1)} %get-tuple-element.76), channel_id=1, source_target_pairs={{1,2},{3,4},{5,6},{7,8},{9,10},{11,12},{13,14},{15,16},{17,18},{19... | collective-permute-start | bytes 786440 | tf_op jit(solution)/shard_map/ppermute | solution.py:622
  158.4 36.5 %all-to-all-start.3 = ((f32[32,4,8,256]{3,2,1,0:T(8,128)}), f32[32,4,8,256]{3,2,1,0:T(8,128)S(1)}, u32[]{:S(2)}, u32[]{:S(2)}) async-start(f32[32,4,8,256]{3,2,1,0:T(8,128)} %get-tuple-element.78), calls=%async_computation.3 | async-start | bytes 2097152 | tf_op jit(solution)/shard_map/all_to_all | solution.py:519
  166.8 1.3 collective-permute-start.19
  168.1 5.0 %collective-permute-start.20 = (f32[2,4,8,256]{3,2,1,0:T(8,128)S(1)}, f32[2,4,8,256]{3,2,1,0:T(8,128)S(1)}, u32[]{:S(2)}, u32[]{:S(2)}) collective-permute-start(f32[2,4,8,256]{3,2,1,0:T(8,128)S(1)} %shard_map.118), channel_id=1, source_target_pairs={{0,2},{1,3},{2,0},{3,1},{4,6},{5,7},{6,4},{7,5},{8,10},{9,11},{10,... | collective-permute-start | bytes 196616 | tf_op jit(solution)/shard_map/ppermute | solution.py:523
  (11 other events, 197.6 us)

commit v8 on v7

--- a/solution.py
+++ b/solution.py
@@ -112,23 +112,24 @@
 
 def add_source(target, receivers, scalars, n):
     x = whole(scalars, SOURCE) - whole(scalars, BASE)
-    amount = scalars[RECEIVERS + 3 * receivers + n]
+    amount = scalars[RECEIVERS + receivers + n]
     add_point(target, x, whole(scalars, SOURCE + 1), whole(scalars, SOURCE + 2), amount)
 
 
 def add_receivers(target, scalars, steps, receivers, n):
-    xs = target.shape[0]
+    xs, ys, nz = target.shape
     base = whole(scalars, BASE)
     away = whole(scalars, SOURCE) - base
-    amounts = RECEIVERS + 3 * receivers + steps + n * receivers
+    amounts = RECEIVERS + receivers + steps + n * receivers
+    z_bits = nz.bit_length() - 1
+    x_bits = z_bits + ys.bit_length() - 1
 
     @pl.when((away + NEAR >= 0) & (away - NEAR < xs))
     def _():
         def one(j, carry):
-            at = RECEIVERS + 3 * j
-            x = whole(scalars, at) - base
-            y, z = whole(scalars, at + 1), whole(scalars, at + 2)
-            add_point(target, x, y, z, scalars[amounts + j])
+            cell = whole(scalars, RECEIVERS + j)
+            x, y = (cell >> x_bits) - base, (cell >> z_bits) & (ys - 1)
+            add_point(target, x, y, cell & (nz - 1), scalars[amounts + j])
             return carry
 
         lax.fori_loop(0, receivers, one, 0)
@@ -215,50 +216,43 @@
         outer[...] = field[xs - REACH :]
 
 
-def edges_kernel(steps, scalars, *refs):
-    fields, speed = (refs[0:3], refs[3:6]), refs[6]
-    outs, held, sems = (refs[7:9], refs[9:11]), refs[11], refs[12]
-    xs, ys, _ = refs[0].shape
+def edges_kernel(n, scalars, now, back, drive, speed, inner, outer, held, sems):
+    xs, ys, _ = now.shape
     even = is_even(scalars)
+    live = switch_on(scalars, n)
     starts = (0, xs - REACH)
     copies = [
-        pltpu.make_async_copy(
-            source.at[pl.ds(x0, REACH)], held.at[f, k, side], sems.at[f, k, side]
-        )
-        for f in range(2)
-        for k, source in enumerate(fields[f])
+        pltpu.make_async_copy(source.at[pl.ds(x0, REACH)], held.at[k, side], sems.at[k, side])
         for side, x0 in enumerate(starts)
+        for k, source in enumerate((now, back, drive))
     ]
     for copy in copies:
         copy.start()
-    for f in range(2):
-        live = switch_on(scalars, 0 if f == 0 else steps - 1)
-        for copy in copies[6 * f : 6 * f + 6]:
+    for side, x0 in enumerate(starts):
+        for copy in copies[3 * side : 3 * side + 3]:
             copy.wait()
-
-        def step(i, carry):
-            rows = pl.ds(pl.multiple_of(i * SUB, SUB), SUB)
-            for side, x0 in enumerate(starts):
+        ahead = even if side == 1 else jnp.logical_not(even)
+
+        def update(out):
+            def step(i, carry):
+                rows = pl.ds(pl.multiple_of(i * SUB, SUB), SUB)
                 for j in range(REACH):
-                    here = held[f, 0, side, j, rows, :]
-                    more = (here - held[f, 1, side, j, rows, :]) + speed[i, x0 + j] * held[
-                        f, 2, side, j, rows, :
+                    here = held[0, side, j, rows, :]
+                    more = (here - held[1, side, j, rows, :]) + speed[i, x0 + j] * held[
+                        2, side, j, rows, :
                     ]
-                    held[f, 0, side, j, rows, :] = here + live * more
-            return carry
-
-        lax.fori_loop(0, ys // SUB, step, 0)
-        inner, outer = outs[f]
-
-        @pl.when(even)
+                    out[j, rows, :] = here + live * more
+                return carry
+
+            lax.fori_loop(0, ys // SUB, step, 0)
+
+        @pl.when(ahead)
         def _():
-            inner[...] = held[f, 0, 1]
-            outer[...] = held[f, 0, 0]
-
-        @pl.when(jnp.logical_not(even))
+            update(inner)
+
+        @pl.when(jnp.logical_not(ahead))
         def _():
-            inner[...] = held[f, 0, 0]
-            outer[...] = held[f, 0, 1]
+            update(outer)
 
 
 def opening(scalars, n, now, back, drive, speed, new, gain):
@@ -596,31 +590,29 @@
     return out
 
 
-def edges(steps, scalars, forward, adjoint, speed):
-    _, ny, nz = forward[0].shape
+def edges(n, scalars, now, back, drive, speed):
+    _, ny, nz = now.shape
     hbm = pl.BlockSpec(memory_space=pltpu.HBM)
     vmem = pl.BlockSpec(memory_space=pltpu.VMEM)
     return pl.pallas_call(
-        functools.partial(edges_kernel, steps),
-        out_shape=[f32(REACH, ny, nz)] * 4,
-        in_specs=[pl.BlockSpec(memory_space=pltpu.SMEM)] + [hbm] * 6 + [vmem],
-        out_specs=[vmem] * 4,
+        functools.partial(edges_kernel, n),
+        out_shape=[f32(REACH, ny, nz)] * 2,
+        in_specs=[pl.BlockSpec(memory_space=pltpu.SMEM), hbm, hbm, hbm, vmem],
+        out_specs=[vmem] * 2,
         scratch_shapes=[
-            pltpu.VMEM((2, 3, 2, REACH, ny, nz), jnp.float32),
-            pltpu.SemaphoreType.DMA((2, 3, 2)),
+            pltpu.VMEM((3, 2, REACH, ny, nz), jnp.float32),
+            pltpu.SemaphoreType.DMA((3, 2)),
         ],
         compiler_params=pltpu.CompilerParams(vmem_limit_bytes=VMEM_LIMIT),
-        name="edges",
-    )(scalars, *map(in_hbm, forward), *map(in_hbm, adjoint), speed)
+    )(scalars, in_hbm(now), in_hbm(back), in_hbm(drive), speed)
 
 
 def halos(inner, outer):
     count = lax.axis_size(MP)
-    across = [(i, i + 1) for i in range(1, count - 1, 2)]
-    return (
-        lax.ppermute(inner, MP, [(i, i ^ 1) for i in range(count)]),
-        lax.ppermute(outer, MP, across + [(j, i) for i, j in across]),
-    )
+    pairs = [(i, i + 1) for i in range(1, count - 1, 2)]
+    far = lax.ppermute(outer, MP, pairs + [(j, i) for i, j in pairs])
+    near = lax.ppermute(inner, MP, [(i, i ^ 1) for i in range(count)])
+    return near, far
 
 
 def window(
@@ -650,13 +642,15 @@
     me_index = lax.axis_index(MP)
     even = me_index % 2 == 0
     base = (me_index * tile_x).reshape(1).astype(jnp.int32)
+    spots = receiver_pos[0]
+    cells = (spots[:, 0] * ny + spots[:, 1]) * nz + spots[:, 2]
     scalars = jnp.concatenate(
         [
             step_count.astype(jnp.float32),
             base.astype(jnp.float32),
             even.reshape(1).astype(jnp.float32),
             source_pos[0].astype(jnp.float32),
-            receiver_pos[0].reshape(-1).astype(jnp.float32),
+            cells.astype(jnp.float32),
             wavelet[0],
             residual[0].reshape(-1),
         ]
@@ -682,11 +676,8 @@
     sent, drive, push = lax.optimization_barrier((sent, drive, push))
     owned = exchange(sent, PLANE).reshape(-1, tile_x, SUB, nz)
     drives.append(drive)
-    openings = edges(
-        steps, scalars, (u, forward_prev[0], drive), (w, adjoint_prev[0], push), owned
-    )
-    u_sides = halos(*openings[:2])
-    w_sides = halos(*openings[2:])
+    u_sides = halos(*edges(0, scalars, u, forward_prev[0], drive, owned))
+    w_sides = halos(*edges(steps - 1, scalars, w, adjoint_prev[0], push, owned))
     backs = []
     for n in range(1, steps):
         last = n == steps - 1

time: 197 us -> 194 us (0.985)
  starting transfers between devices: 66.4 us -> 62 us
    ppermute x14, starting transfers between devices: 37.3 us -> 33 us  [the longest x7 31.1 us: halos(): far = lax.ppermute(outer, MP, pairs + [(j, i) for i, j in pairs])]
    pallas_call x1 -> x2, Pallas kernels: 2.94 us -> 4.39 us  [edges(): pl.pallas_call(functools.partial(edges_kernel, n), out_shape=[f32(REACH,...]
  transfers between devices with their start and end apart: 23 -> 23, of which waited for: 10 -> 9; matrix products, arithmetic and copies ran while one was open for 0% -> 0% of each run, Pallas kernels for 11% -> 12%
where the time goes in v8:
time: 194 us; the launch traced here: 193 us
  starting transfers between devices  62 us (32%)
  blocking collectives  56.1 us (29%)
  waiting for transfers between devices  37 us (19%)
  Pallas kernels  35.5 us (18%)
    all_to_all x2, blocking collectives, exchange(): return lax.all_to_all(parts, axes, split_axis=0, concat_axis=0, tiled=True)  56.1 us
    ppermute x7, starting transfers between devices, halos(): far = lax.ppermute(outer, MP, pairs + [(j, i) for i, j in pairs])  31.1 us
    all_to_all x2, waiting for transfers between devices, exchange(): return lax.all_to_all(parts, axes, split_axis=0, concat_axis=0, tiled=True)  24.3 us
    all_to_all x2, starting transfers between devices, exchange(): return lax.all_to_all(parts, axes, split_axis=0, concat_axis=0, tiled=True)  21.2 us
    pallas_call x11, Pallas kernels, local_kernel(): pl.pallas_call(body, out_shape=outs, in_specs=[smem] * len(scalars) + [vm...  18.4 us
    ppermute x3, waiting for transfers between devices, all_first(): lax.ppermute(known, 'shot', [(i, i ^ step) for i in range(shots)])  6.49 us
    pallas_call x1, Pallas kernels, window(): pl.pallas_call(functools.partial(first_kernel, steps, receivers), out_sha...  5.43 us
    ppermute x4, waiting for transfers between devices, swap_quads(): return lax.ppermute(value, 'quad', [(q, q ^ turn) for q in range(QUAD)])  5.23 us
  transfers between devices with their start and end apart: 23, of which 9 were waited for; matrix products, arithmetic and copies ran while one was open for 0% of the time, Pallas kernels for 12%

profile of v8, /device:TPU:1, one launch (start us, length us, event | category | flops | bytes accessed | tf_op | source)
XLA Modules:
  0.0 192.8 jit_solution(17117329169739566203)
XLA Ops:
  0.1 3.1 %split.1 = (f32[8,16,8,256]{3,2,1,0:T(8,128)}, f32[8,64,256]{2,1,0:T(8,128)}, f32[8,64,256]{2,1,0:T(8,128)}, f32[2,4,8,256]{3,2,1,0:T(8,128)S(1)}, f32[2,4,8,256]{3,2,1,0:T(8,128)S(1)}) custom-call(s32[3]{0:T(128)S(1)} %pad_add_fusion.1.spot, f32[2,16,64,256]{3,2,1,0:T(8,128)} %courant.1, f32[16,64,256]{2,1,0:T(8,128)} %bitcast.33, f32[16,64,256]{2,1,0:T(8,128)} %bitcast.37), custom_call_target="tpu_custom_call" | custom-call | tf_op jit(solution)/shard_map/split/pallas_call | solution.py:533
  3.2 12.9 %all-to-all-start = ((f32[32,4,8,256]{3,2,1,0:T(8,128)}), f32[32,4,8,256]{3,2,1,0:T(8,128)S(1)}, u32[]{:S(2)}, u32[]{:S(2)}) async-start(f32[32,4,8,256]{3,2,1,0:T(8,128)} %bitcast.46), calls=%async_computation | async-start | bytes 2097152 | tf_op jit(solution)/shard_map/all_to_all | solution.py:513
  16.4 4.9 %collective-permute-start.6 = (f32[8,64,256]{2,1,0:T(8,128)}, f32[8,64,256]{2,1,0:T(8,128)}, u32[]{:S(2)}, u32[]{:S(2)}) collective-permute-start(f32[8,64,256]{2,1,0:T(8,128)} %get-tuple-element.47), channel_id=1, source_target_pairs={{1,2},{3,4},{5,6},{7,8},{9,10},{11,12},{13,14},{15,16},{17,18},{19... | collective-permute-start | bytes 1572872 | tf_op jit(solution)/shard_map/ppermute | solution.py:613
  24.8 2.7 %collective-permute-start.1 = (s32[8]{0:T(128)S(1)}, s32[8]{0:T(128)S(1)}, u32[]{:S(2)}, u32[]{:S(2)}) collective-permute-start(s32[8]{0:T(128)S(1)} %fusion), channel_id=1, source_target_pairs={{0,64},{32,96},{64,0},{96,32},{128,192},{160,224},{192,128},{224,1... | collective-permute-start | bytes 104 | tf_op jit(solution)/shard_map/ppermute | solution.py:31
  29.4 4.4 %collective-permute-done.2 = s32[8]{0:T(128)S(1)} collective-permute-done((s32[8]{0:T(128)S(1)}, s32[8]{0:T(128)S(1)}, u32[]{:S(2)}, u32[]{:S(2)}) %collective-permute-start.2) | collective-permute-done | bytes 64 | tf_op jit(solution)/shard_map/ppermute | solution.py:31
  34.0 5.4 %first.1 = (f32[16,64,256]{2,1,0:T(8,128)}, f32[16,64,256]{2,1,0:T(8,128)}) custom-call(f32[170]{0:T(256)S(1)} %concatenate.8.scalars, f32[16,64,256]{2,1,0:T(8,128)S(1)} %bitcast.35, f32[16,64,256]{2,1,0:T(8,128)S(1)} %bitcast.39, f32[8,64,256]{2,1,0:T(8,128)} %collective-permute-done.5.near, f32[8,64,256]{2,1,0:T(8,128)} %collective-permute-done.6.far), custom_call_target="tpu_custom_call" | custom-call | tf_op jit(solution)/shard_map/first/pallas_call | solution.py:666
  41.6 2.6 %all-to-all-done.line = f32[32,4,8,256]{3,2,1,0:T(8,128)S(1)} async-done(((f32[32,4,8,256]{3,2,1,0:T(8,128)}), f32[32,4,8,256]{3,2,1,0:T(8,128)S(1)}, u32[]{:S(2)}, u32[]{:S(2)}) %all-to-all-start) | async-done | bytes 1048608 | tf_op jit(solution)/shard_map/all_to_all | solution.py:513
  44.2 2.4 %gather.1 = f32[32,4,8,256]{3,2,1,0:T(8,128)} custom-call(s32[11]{0:T(128)S(1)} %pad_add_fusion.table, f32[32,4,8,256]{3,2,1,0:T(8,128)S(1)} %all-to-all-done.line, f32[2,4,8,256]{3,2,1,0:T(8,128)S(1)} %get-tuple-element.44.keep, f32[2,4,8,256]{3,2,1,0:T(8,128)S(1)} %collective-permute-done.3.swapped, f32[2,4,8,256]{3,2,1,0:T(8,128)S(1)} %collective-permute-done.4.far), custom_call_target="tpu_custom_call" | custom-call | tf_op jit(solution)/shard_map/gather/pallas_call | solution.py:555
  46.6 32.1 %all_to_all.20 = f32[32,4,8,256]{3,2,1,0:T(8,128)S(1)} all-to-all(f32[32,4,8,256]{3,2,1,0:T(8,128)} %gather.1), channel_id=1, replica_groups=mesh['shot'=8,'zz'=8,'quad'=4] {'shot','quad'}, dimensions={0} | all-to-all | bytes 2097152 | tf_op jit(solution)/shard_map/all_to_all | solution.py:513
  81.3 3.2 %collective-permute-start.12 = (f32[4,64,256]{2,1,0:T(8,128)S(1)}, f32[4,64,256]{2,1,0:T(8,128)S(1)}, u32[]{:S(2)}, u32[]{:S(2)}) collective-permute-start(f32[4,64,256]{2,1,0:T(8,128)S(1)} %get-tuple-element.63), channel_id=1, source_target_pairs={{1,2},{3,4},{5,6},{7,8},{9,10},{11,12},{13,14},{15,16},{17,18},{19... | collective-permute-start | bytes 786440 | tf_op jit(solution)/shard_map/ppermute | solution.py:613
  84.5 2.3 %shard_map.110 = (f32[4,64,256]{2,1,0:T(8,128)S(1)}, f32[4,64,256]{2,1,0:T(8,128)S(1)}) custom-call(f32[170]{0:T(256)S(1)} %concatenate.8.scalars, f32[16,64,256]{2,1,0:T(8,128)} %bitcast.38, f32[16,64,256]{2,1,0:T(8,128)} %bitcast.43, f32[16,64,256]{2,1,0:T(8,128)} %get-tuple-element.50.drive.refs_2_, f32[8,16,8,256]{3,2,1,0:T(8,128)S(1)} %bitcast.25), custom_call_target="tpu_custom_call" | custom-call | tf_op jit(solution)/shard_map/pallas_call | solution.py:597
  87.0 5.0 %collective-permute-start.8 = (f32[4,64,256]{2,1,0:T(8,128)S(1)}, f32[4,64,256]{2,1,0:T(8,128)S(1)}, u32[]{:S(2)}, u32[]{:S(2)}) collective-permute-start(f32[4,64,256]{2,1,0:T(8,128)S(1)} %get-tuple-element.53), channel_id=1, source_target_pairs={{1,2},{3,4},{5,6},{7,8},{9,10},{11,12},{13,14},{15,16},{17,18},{19... | collective-permute-start | bytes 786440 | tf_op jit(solution)/shard_map/ppermute | solution.py:613
  92.1 3.0 %shard_map.114 = (f32[16,64,256]{2,1,0:T(8,128)S(1)}, f32[16,64,256]{2,1,0:T(8,128)S(1)}, f32[16,64,256]{2,1,0:T(8,128)S(1)}, f32[4,64,256]{2,1,0:T(8,128)S(1)}, f32[4,64,256]{2,1,0:T(8,128)S(1)}) custom-call(f32[170]{0:T(256)S(1)} %concatenate.8.scalars, f32[16,64,256]{2,1,0:T(8,128)S(1)} %bitcast.36, f32[16,64,256]{2,1,0:T(8,128)S(1)} %bitcast.42, ...), custom_call_target="tpu_custom_call" | custom-call | tf_op jit(solution)/shard_map/pallas_call | solution.py:47
  95.2 4.4 %collective-permute-start.14 = (f32[4,64,256]{2,1,0:T(8,128)S(1)}, f32[4,64,256]{2,1,0:T(8,128)S(1)}, u32[]{:S(2)}, u32[]{:S(2)}) collective-permute-start(f32[4,64,256]{2,1,0:T(8,128)S(1)} %get-tuple-element.67), channel_id=1, source_target_pairs={{1,2},{3,4},{5,6},{7,8},{9,10},{11,12},{13,14},{15,16},{17,18},{19... | collective-permute-start | bytes 786440 | tf_op jit(solution)/shard_map/ppermute | solution.py:613
  99.6 3.0 %shard_map.111 = (f32[16,64,256]{2,1,0:T(8,128)S(1)}, f32[16,64,256]{2,1,0:T(8,128)S(1)}, f32[16,64,256]{2,1,0:T(8,128)S(1)}, f32[4,64,256]{2,1,0:T(8,128)S(1)}, f32[4,64,256]{2,1,0:T(8,128)S(1)}) custom-call(f32[170]{0:T(256)S(1)} %concatenate.8.scalars, f32[16,64,256]{2,1,0:T(8,128)S(1)} %bitcast.40, f32[16,64,256]{2,1,0:T(8,128)S(1)} %bitcast.44, ...), custom_call_target="tpu_custom_call" | custom-call | tf_op jit(solution)/shard_map/pallas_call | solution.py:47
  102.6 4.4 %collective-permute-start.10 = (f32[4,64,256]{2,1,0:T(8,128)S(1)}, f32[4,64,256]{2,1,0:T(8,128)S(1)}, u32[]{:S(2)}, u32[]{:S(2)}) collective-permute-start(f32[4,64,256]{2,1,0:T(8,128)S(1)} %get-tuple-element.57), channel_id=1, source_target_pairs={{1,2},{3,4},{5,6},{7,8},{9,10},{11,12},{13,14},{15,16},{17,18},{19... | collective-permute-start | bytes 786440 | tf_op jit(solution)/shard_map/ppermute | solution.py:613
  107.2 2.4 %shard_map.115 = (f32[16,64,256]{2,1,0:T(8,128)S(1)}, f32[16,64,256]{2,1,0:T(8,128)S(1)}, f32[16,64,256]{2,1,0:T(8,128)S(1)}, f32[4,64,256]{2,1,0:T(8,128)S(1)}, f32[4,64,256]{2,1,0:T(8,128)S(1)}) custom-call(f32[170]{0:T(256)S(1)} %concatenate.8.scalars, f32[16,64,256]{2,1,0:T(8,128)S(1)} %get-tuple-element.64.refs_0_, ...), custom_call_target="tpu_custom_call" | custom-call | tf_op jit(solution)/shard_map/pallas_call | solution.py:47
  110.4 3.9 %collective-permute-start.16 = (f32[4,64,256]{2,1,0:T(8,128)S(1)}, f32[4,64,256]{2,1,0:T(8,128)S(1)}, u32[]{:S(2)}, u32[]{:S(2)}) collective-permute-start(f32[4,64,256]{2,1,0:T(8,128)S(1)} %get-tuple-element.71), channel_id=1, source_target_pairs={{1,2},{3,4},{5,6},{7,8},{9,10},{11,12},{13,14},{15,16},{17,18},{19... | collective-permute-start | bytes 786440 | tf_op jit(solution)/shard_map/ppermute | solution.py:613
  114.3 2.4 %shard_map.112 = (f32[16,64,256]{2,1,0:T(8,128)S(1)}, f32[16,64,256]{2,1,0:T(8,128)S(1)}, f32[4,64,256]{2,1,0:T(8,128)S(1)}, f32[4,64,256]{2,1,0:T(8,128)S(1)}) custom-call(f32[170]{0:T(256)S(1)} %concatenate.8.scalars, f32[16,64,256]{2,1,0:T(8,128)S(1)} %get-tuple-element.54.refs_0_.refs_2_, f32[16,64,256]{2,1,0:T(8,128)S(1)} %get-tuple-element.55.refs_1_, ...), custom_call_target="tpu_custom_call" | custom-call | tf_op jit(solution)/shard_map/pallas_call | solution.py:47
  116.9 5.2 %collective-permute-start.18 = (f32[4,64,256]{2,1,0:T(8,128)S(1)}, f32[4,64,256]{2,1,0:T(8,128)S(1)}, u32[]{:S(2)}, u32[]{:S(2)}) collective-permute-start(f32[4,64,256]{2,1,0:T(8,128)S(1)} %get-tuple-element.76), channel_id=1, source_target_pairs={{1,2},{3,4},{5,6},{7,8},{9,10},{11,12},{13,14},{15,16},{17,18},{19... | collective-permute-start | bytes 786440 | tf_op jit(solution)/shard_map/ppermute | solution.py:613
  129.1 24.0 %all_to_all.21.got = f32[32,4,8,256]{3,2,1,0:T(8,128)S(1)} all-to-all(f32[32,4,8,256]{3,2,1,0:T(8,128)S(1)} %bitcast.45), channel_id=1, replica_groups=mesh['shot'=8,'zz'=8,'quad'=4] {'shot','quad'}, dimensions={0} | all-to-all | bytes 2097152 | tf_op jit(solution)/shard_map/all_to_all | solution.py:513
  155.0 8.4 %all-to-all-start.3 = ((f32[32,4,8,256]{3,2,1,0:T(8,128)}), f32[32,4,8,256]{3,2,1,0:T(8,128)S(1)}, u32[]{:S(2)}, u32[]{:S(2)}) async-start(f32[32,4,8,256]{3,2,1,0:T(8,128)} %get-tuple-element.78), calls=%async_computation.3 | async-start | bytes 2097152 | tf_op jit(solution)/shard_map/all_to_all | solution.py:513
  164.7 2.9 %collective-permute-start.20 = (f32[2,4,8,256]{3,2,1,0:T(8,128)S(1)}, f32[2,4,8,256]{3,2,1,0:T(8,128)S(1)}, u32[]{:S(2)}, u32[]{:S(2)}) collective-permute-start(f32[2,4,8,256]{3,2,1,0:T(8,128)S(1)} %shard_map.120), channel_id=1, source_target_pairs={{0,2},{1,3},{2,0},{3,1},{4,6},{5,7},{6,4},{7,5},{8,10},{9,11},{10,... | collective-permute-start | bytes 196616 | tf_op jit(solution)/shard_map/ppermute | solution.py:517
  169.7 21.7 %all-to-all-done.3.came = f32[32,4,8,256]{3,2,1,0:T(8,128)S(1)} async-done(((f32[32,4,8,256]{3,2,1,0:T(8,128)}), f32[32,4,8,256]{3,2,1,0:T(8,128)S(1)}, u32[]{:S(2)}, u32[]{:S(2)}) %all-to-all-start.3) | async-done | bytes 1048608 | tf_op jit(solution)/shard_map/all_to_all | solution.py:513
  (76 shorter events, 24.2 us)
Async XLA Ops:
  3.2 30.8 %copy-start = (f32[1,16,64,256]{3,2,1,0:T(8,128)S(1)}, f32[1,16,64,256]{3,2,1,0:T(8,128)}, u32[]{:S(2)}) copy-start(f32[1,16,64,256]{3,2,1,0:T(8,128)} %param.19) | copy-start | bytes 3145732
  3.2 41.0 %all-to-all-start = ((f32[32,4,8,256]{3,2,1,0:T(8,128)}), f32[32,4,8,256]{3,2,1,0:T(8,128)S(1)}, u32[]{:S(2)}, u32[]{:S(2)}) async-start(f32[32,4,8,256]{3,2,1,0:T(8,128)} %bitcast.46), calls=%async_computation | async-start | bytes 2097152 | tf_op jit(solution)/shard_map/all_to_all | solution.py:513
  16.1 17.9 %collective-permute-start.5 = (f32[8,64,256]{2,1,0:T(8,128)}, f32[8,64,256]{2,1,0:T(8,128)}, u32[]{:S(2)}, u32[]{:S(2)}) collective-permute-start(f32[8,64,256]{2,1,0:T(8,128)} %get-tuple-element.46), channel_id=1, source_target_pairs={{0,1},{1,0},{2,3},{3,2},{4,5},{5,4},{6,7},{7,6},{8,9},{9,8},{10,11... | collective-permute-start | bytes 1572872 | tf_op jit(solution)/shard_map/ppermute | solution.py:614
  16.4 17.6 %collective-permute-start.6 = (f32[8,64,256]{2,1,0:T(8,128)}, f32[8,64,256]{2,1,0:T(8,128)}, u32[]{:S(2)}, u32[]{:S(2)}) collective-permute-start(f32[8,64,256]{2,1,0:T(8,128)} %get-tuple-element.47), channel_id=1, source_target_pairs={{1,2},{3,4},{5,6},{7,8},{9,10},{11,12},{13,14},{15,16},{17,18},{19... | collective-permute-start | bytes 1572872 | tf_op jit(solution)/shard_map/ppermute | solution.py:613
  22.0 2.8 %collective-permute-start = (s32[8]{0:T(128)S(1)}, s32[8]{0:T(128)S(1)}, u32[]{:S(2)}, u32[]{:S(2)}) collective-permute-start(s32[8]{0:T(128)S(1)} %compare_select_fusion), channel_id=1, source_target_pairs={{0,32},{32,0},{64,96},{96,64},{128,160},{160,128},{192,224},{224,1... | collective-permute-start | bytes 104 | tf_op jit(solution)/shard_map/ppermute | solution.py:31
  23.3 10.5 %collective-permute-start.3 = (f32[2,4,8,256]{3,2,1,0:T(8,128)S(1)}, f32[2,4,8,256]{3,2,1,0:T(8,128)S(1)}, u32[]{:S(2)}, u32[]{:S(2)}) collective-permute-start(f32[2,4,8,256]{3,2,1,0:T(8,128)S(1)} %get-tuple-element.45), channel_id=1, source_target_pairs={{0,1},{1,0},{2,3},{3,2},{4,5},{5,4},{6,7},{7,6},{8,9},{9,8},{10,11... | collective-permute-start | bytes 196616 | tf_op jit(solution)/shard_map/ppermute | solution.py:517
  24.8 4.2 %collective-permute-start.1 = (s32[8]{0:T(128)S(1)}, s32[8]{0:T(128)S(1)}, u32[]{:S(2)}, u32[]{:S(2)}) collective-permute-start(s32[8]{0:T(128)S(1)} %fusion), channel_id=1, source_target_pairs={{0,64},{32,96},{64,0},{96,32},{128,192},{160,224},{192,128},{224,1... | collective-permute-start | bytes 104 | tf_op jit(solution)/shard_map/ppermute | solution.py:31
  29.0 4.8 %collective-permute-start.2 = (s32[8]{0:T(128)S(1)}, s32[8]{0:T(128)S(1)}, u32[]{:S(2)}, u32[]{:S(2)}) collective-permute-start(s32[8]{0:T(128)S(1)} %fusion.1), channel_id=1, source_target_pairs={{0,128},{32,160},{64,192},{96,224},{128,0},{160,32},{192,64},{224,... | collective-permute-start | bytes 104 | tf_op jit(solution)/shard_map/ppermute | solution.py:31
  33.8 7.8 %collective-permute-start.4 = (f32[2,4,8,256]{3,2,1,0:T(8,128)S(1)}, f32[2,4,8,256]{3,2,1,0:T(8,128)S(1)}, u32[]{:S(2)}, u32[]{:S(2)}) collective-permute-start(f32[2,4,8,256]{3,2,1,0:T(8,128)S(1)} %shard_map.109), channel_id=1, source_target_pairs={{0,2},{1,3},{2,0},{3,1},{4,6},{5,7},{6,4},{7,5},{8,10},{9,11},{10,... | collective-permute-start | bytes 196616 | tf_op jit(solution)/shard_map/ppermute | solution.py:517
  80.8 11.3 %collective-permute-start.11 = (f32[4,64,256]{2,1,0:T(8,128)S(1)}, f32[4,64,256]{2,1,0:T(8,128)S(1)}, u32[]{:S(2)}, u32[]{:S(2)}) collective-permute-start(f32[4,64,256]{2,1,0:T(8,128)S(1)} %get-tuple-element.62), channel_id=1, source_target_pairs={{0,1},{1,0},{2,3},{3,2},{4,5},{5,4},{6,7},{7,6},{8,9},{9,8},{10,11... | collective-permute-start | bytes 786440 | tf_op jit(solution)/shard_map/ppermute | solution.py:614
  81.3 10.8 %collective-permute-start.12 = (f32[4,64,256]{2,1,0:T(8,128)S(1)}, f32[4,64,256]{2,1,0:T(8,128)S(1)}, u32[]{:S(2)}, u32[]{:S(2)}) collective-permute-start(f32[4,64,256]{2,1,0:T(8,128)S(1)} %get-tuple-element.63), channel_id=1, source_target_pairs={{1,2},{3,4},{5,6},{7,8},{9,10},{11,12},{13,14},{15,16},{17,18},{19... | collective-permute-start | bytes 786440 | tf_op jit(solution)/shard_map/ppermute | solution.py:613
  86.8 12.7 %collective-permute-start.7 = (f32[4,64,256]{2,1,0:T(8,128)S(1)}, f32[4,64,256]{2,1,0:T(8,128)S(1)}, u32[]{:S(2)}, u32[]{:S(2)}) collective-permute-start(f32[4,64,256]{2,1,0:T(8,128)S(1)} %get-tuple-element.52), channel_id=1, source_target_pairs={{0,1},{1,0},{2,3},{3,2},{4,5},{5,4},{6,7},{7,6},{8,9},{9,8},{10,11... | collective-permute-start | bytes 786440 | tf_op jit(solution)/shard_map/ppermute | solution.py:614
  87.0 12.6 %collective-permute-start.8 = (f32[4,64,256]{2,1,0:T(8,128)S(1)}, f32[4,64,256]{2,1,0:T(8,128)S(1)}, u32[]{:S(2)}, u32[]{:S(2)}) collective-permute-start(f32[4,64,256]{2,1,0:T(8,128)S(1)} %get-tuple-element.53), channel_id=1, source_target_pairs={{1,2},{3,4},{5,6},{7,8},{9,10},{11,12},{13,14},{15,16},{17,18},{19... | collective-permute-start | bytes 786440 | tf_op jit(solution)/shard_map/ppermute | solution.py:613
  95.1 12.1 %collective-permute-start.13 = (f32[4,64,256]{2,1,0:T(8,128)S(1)}, f32[4,64,256]{2,1,0:T(8,128)S(1)}, u32[]{:S(2)}, u32[]{:S(2)}) collective-permute-start(f32[4,64,256]{2,1,0:T(8,128)S(1)} %get-tuple-element.66), channel_id=1, source_target_pairs={{0,1},{1,0},{2,3},{3,2},{4,5},{5,4},{6,7},{7,6},{8,9},{9,8},{10,11... | collective-permute-start | bytes 786440 | tf_op jit(solution)/shard_map/ppermute | solution.py:614
  95.2 12.0 %collective-permute-start.14 = (f32[4,64,256]{2,1,0:T(8,128)S(1)}, f32[4,64,256]{2,1,0:T(8,128)S(1)}, u32[]{:S(2)}, u32[]{:S(2)}) collective-permute-start(f32[4,64,256]{2,1,0:T(8,128)S(1)} %get-tuple-element.67), channel_id=1, source_target_pairs={{1,2},{3,4},{5,6},{7,8},{9,10},{11,12},{13,14},{15,16},{17,18},{19... | collective-permute-start | bytes 786440 | tf_op jit(solution)/shard_map/ppermute | solution.py:613
  102.6 11.7 %collective-permute-start.10 = (f32[4,64,256]{2,1,0:T(8,128)S(1)}, f32[4,64,256]{2,1,0:T(8,128)S(1)}, u32[]{:S(2)}, u32[]{:S(2)}) collective-permute-start(f32[4,64,256]{2,1,0:T(8,128)S(1)} %get-tuple-element.57), channel_id=1, source_target_pairs={{1,2},{3,4},{5,6},{7,8},{9,10},{11,12},{13,14},{15,16},{17,18},{19... | collective-permute-start | bytes 786440 | tf_op jit(solution)/shard_map/ppermute | solution.py:613
  107.1 7.3 %collective-permute-start.9 = (f32[4,64,256]{2,1,0:T(8,128)S(1)}, f32[4,64,256]{2,1,0:T(8,128)S(1)}, u32[]{:S(2)}, u32[]{:S(2)}) collective-permute-start(f32[4,64,256]{2,1,0:T(8,128)S(1)} %get-tuple-element.56), channel_id=1, source_target_pairs={{0,1},{1,0},{2,3},{3,2},{4,5},{5,4},{6,7},{7,6},{8,9},{9,8},{10,11... | collective-permute-start | bytes 786440 | tf_op jit(solution)/shard_map/ppermute | solution.py:614
  109.6 12.4 %collective-permute-start.15 = (f32[4,64,256]{2,1,0:T(8,128)S(1)}, f32[4,64,256]{2,1,0:T(8,128)S(1)}, u32[]{:S(2)}, u32[]{:S(2)}) collective-permute-start(f32[4,64,256]{2,1,0:T(8,128)S(1)} %get-tuple-element.70), channel_id=1, source_target_pairs={{0,1},{1,0},{2,3},{3,2},{4,5},{5,4},{6,7},{7,6},{8,9},{9,8},{10,11... | collective-permute-start | bytes 786440 | tf_op jit(solution)/shard_map/ppermute | solution.py:614
  110.4 11.7 %collective-permute-start.16 = (f32[4,64,256]{2,1,0:T(8,128)S(1)}, f32[4,64,256]{2,1,0:T(8,128)S(1)}, u32[]{:S(2)}, u32[]{:S(2)}) collective-permute-start(f32[4,64,256]{2,1,0:T(8,128)S(1)} %get-tuple-element.71), channel_id=1, source_target_pairs={{1,2},{3,4},{5,6},{7,8},{9,10},{11,12},{13,14},{15,16},{17,18},{19... | collective-permute-start | bytes 786440 | tf_op jit(solution)/shard_map/ppermute | solution.py:613
  116.8 10.5 %collective-permute-start.17 = (f32[4,64,256]{2,1,0:T(8,128)S(1)}, f32[4,64,256]{2,1,0:T(8,128)S(1)}, u32[]{:S(2)}, u32[]{:S(2)}) collective-permute-start(f32[4,64,256]{2,1,0:T(8,128)S(1)} %get-tuple-element.75), channel_id=1, source_target_pairs={{0,1},{1,0},{2,3},{3,2},{4,5},{5,4},{6,7},{7,6},{8,9},{9,8},{10,11... | collective-permute-start | bytes 786440 | tf_op jit(solution)/shard_map/ppermute | solution.py:614
  116.9 11.3 %collective-permute-start.18 = (f32[4,64,256]{2,1,0:T(8,128)S(1)}, f32[4,64,256]{2,1,0:T(8,128)S(1)}, u32[]{:S(2)}, u32[]{:S(2)}) collective-permute-start(f32[4,64,256]{2,1,0:T(8,128)S(1)} %get-tuple-element.76), channel_id=1, source_target_pairs={{1,2},{3,4},{5,6},{7,8},{9,10},{11,12},{13,14},{15,16},{17,18},{19... | collective-permute-start | bytes 786440 | tf_op jit(solution)/shard_map/ppermute | solution.py:613
  155.0 36.4 %all-to-all-start.3 = ((f32[32,4,8,256]{3,2,1,0:T(8,128)}), f32[32,4,8,256]{3,2,1,0:T(8,128)S(1)}, u32[]{:S(2)}, u32[]{:S(2)}) async-start(f32[32,4,8,256]{3,2,1,0:T(8,128)} %get-tuple-element.78), calls=%async_computation.3 | async-start | bytes 2097152 | tf_op jit(solution)/shard_map/all_to_all | solution.py:513
  163.4 1.3 collective-permute-start.19
  164.7 5.0 %collective-permute-start.20 = (f32[2,4,8,256]{3,2,1,0:T(8,128)S(1)}, f32[2,4,8,256]{3,2,1,0:T(8,128)S(1)}, u32[]{:S(2)}, u32[]{:S(2)}) collective-permute-start(f32[2,4,8,256]{3,2,1,0:T(8,128)S(1)} %shard_map.120), channel_id=1, source_target_pairs={{0,2},{1,3},{2,0},{3,1},{4,6},{5,7},{6,4},{7,5},{8,10},{9,11},{10,... | collective-permute-start | bytes 196616 | tf_op jit(solution)/shard_map/ppermute | solution.py:517
  (11 other events, 174.4 us)

commit v9 on v8

--- a/solution.py
+++ b/solution.py
@@ -427,44 +427,57 @@
 
 
 def gather_kernel(zs, table, line, keep, swapped, far, sent, sems):
-    slots = sent.shape[0]
+    shots = sent.shape[0] // QUAD
+    tiles = zs * QUAD
     me_z, me_q = table[table.shape[0] - 2], table[table.shape[0] - 1]
 
-    def one(slot, carry):
-        tile = table[slot // QUAD] + slot % QUAD
-        place = ((me_z + tile // QUAD) % zs) * QUAD + tile % QUAD
-        turn = me_q ^ (tile % QUAD)
-
-        def send(source):
-            pltpu.make_async_copy(source, sent.at[slot], sems.at[slot]).start()
-
-        @pl.when(tile < zs * QUAD)
+    def one(s, carry):
+        first = table[s]
+        start = (me_z * QUAD + first) % tiles
+        together = (first + QUAD <= tiles) & (start + QUAD <= tiles)
+
+        @pl.when(together)
         def _():
-            send(line.at[place])
-
-        @pl.when(tile >= zs * QUAD)
+            pltpu.make_async_copy(
+                line.at[pl.ds(start, QUAD)], sent.at[pl.ds(s * QUAD, QUAD)], sems.at[s]
+            ).start()
+
+        @pl.when(jnp.logical_not(together))
         def _():
-            @pl.when(turn == 0)
-            def _():
-                send(keep.at[0])
-
-            @pl.when(turn == 1)
-            def _():
-                send(swapped.at[0])
-
-            @pl.when(turn > 1)
-            def _():
-                send(far.at[turn - 2])
+            for k in range(QUAD):
+                tile = first + k
+                turn = me_q ^ (tile % QUAD)
+
+                def send(source):
+                    pltpu.make_async_copy(source, sent.at[s * QUAD + k], sems.at[s]).start()
+
+                @pl.when(tile < tiles)
+                def _():
+                    send(line.at[(start + k) % tiles])
+
+                @pl.when((tile >= tiles) & (turn == 0))
+                def _():
+                    send(keep.at[0])
+
+                @pl.when((tile >= tiles) & (turn == 1))
+                def _():
+                    send(swapped.at[0])
+
+                @pl.when((tile >= tiles) & (turn > 1))
+                def _():
+                    send(far.at[turn - 2])
 
         return carry
 
-    lax.fori_loop(0, slots, one, 0)
-
-    def done(slot, carry):
-        pltpu.make_async_copy(line.at[0], sent.at[slot], sems.at[slot]).wait()
+    lax.fori_loop(0, shots, one, 0)
+
+    def done(s, carry):
+        pltpu.make_async_copy(
+            line.at[pl.ds(0, QUAD)], sent.at[pl.ds(s * QUAD, QUAD)], sems.at[s]
+        ).wait()
         return carry
 
-    lax.fori_loop(0, slots, done, 0)
+    lax.fori_loop(0, shots, done, 0)
 
 
 def scatter_kernel(zs, table, got, line, keep, swap, held, sems):
@@ -557,7 +570,7 @@
         out_shape=hbm32(slots, *line.shape[1:]),
         in_specs=[smem] + [anywhere] * 4,
         out_specs=pl.BlockSpec(memory_space=pltpu.HBM),
-        scratch_shapes=[pltpu.SemaphoreType.DMA((slots,))],
+        scratch_shapes=[pltpu.SemaphoreType.DMA((slots // QUAD,))],
         compiler_params=pltpu.CompilerParams(vmem_limit_bytes=1 << 20),
         name="gather",
     )(table, line, *extras)

time: 194 us -> 193 us (level)
  no operation moved by 1% of the time
where the time goes in v9:
time: 193 us; the launch traced here: 192 us
  starting transfers between devices  62 us (32%)
  blocking collectives  56.1 us (29%)
  waiting for transfers between devices  37 us (19%)
  Pallas kernels  34.8 us (18%)
    all_to_all x2, blocking collectives, exchange(): return lax.all_to_all(parts, axes, split_axis=0, concat_axis=0, tiled=True)  56.1 us
    ppermute x7, starting transfers between devices, halos(): far = lax.ppermute(outer, MP, pairs + [(j, i) for i, j in pairs])  31.1 us
    all_to_all x2, waiting for transfers between devices, exchange(): return lax.all_to_all(parts, axes, split_axis=0, concat_axis=0, tiled=True)  24.3 us
    all_to_all x2, starting transfers between devices, exchange(): return lax.all_to_all(parts, axes, split_axis=0, concat_axis=0, tiled=True)  21.2 us
    pallas_call x11, Pallas kernels, local_kernel(): pl.pallas_call(body, out_shape=outs, in_specs=[smem] * len(scalars) + [vm...  18.4 us
    ppermute x3, waiting for transfers between devices, all_first(): lax.ppermute(known, 'shot', [(i, i ^ step) for i in range(shots)])  6.49 us
    pallas_call x1, Pallas kernels, window(): pl.pallas_call(functools.partial(first_kernel, steps, receivers), out_sha...  5.43 us
    ppermute x4, waiting for transfers between devices, swap_quads(): return lax.ppermute(value, 'quad', [(q, q ^ turn) for q in range(QUAD)])  5.23 us
  transfers between devices with their start and end apart: 23, of which 9 were waited for; matrix products, arithmetic and copies ran while one was open for 0% of the time, Pallas kernels for 12%

profile of v9, /device:TPU:1, one launch (start us, length us, event | category | flops | bytes accessed | tf_op | source)
XLA Modules:
  0.0 192.1 jit_solution(2553490476603517566)
XLA Ops:
  0.1 3.1 %split.1 = (f32[8,16,8,256]{3,2,1,0:T(8,128)}, f32[8,64,256]{2,1,0:T(8,128)}, f32[8,64,256]{2,1,0:T(8,128)}, f32[2,4,8,256]{3,2,1,0:T(8,128)S(1)}, f32[2,4,8,256]{3,2,1,0:T(8,128)S(1)}) custom-call(s32[3]{0:T(128)S(1)} %pad_add_fusion.1.spot, f32[2,16,64,256]{3,2,1,0:T(8,128)} %courant.1, f32[16,64,256]{2,1,0:T(8,128)} %bitcast.33, f32[16,64,256]{2,1,0:T(8,128)} %bitcast.37), custom_call_target="tpu_custom_call" | custom-call | tf_op jit(solution)/shard_map/split/pallas_call | solution.py:546
  3.2 12.9 %all-to-all-start = ((f32[32,4,8,256]{3,2,1,0:T(8,128)}), f32[32,4,8,256]{3,2,1,0:T(8,128)S(1)}, u32[]{:S(2)}, u32[]{:S(2)}) async-start(f32[32,4,8,256]{3,2,1,0:T(8,128)} %bitcast.46), calls=%async_computation | async-start | bytes 2097152 | tf_op jit(solution)/shard_map/all_to_all | solution.py:526
  16.4 4.9 %collective-permute-start.6 = (f32[8,64,256]{2,1,0:T(8,128)}, f32[8,64,256]{2,1,0:T(8,128)}, u32[]{:S(2)}, u32[]{:S(2)}) collective-permute-start(f32[8,64,256]{2,1,0:T(8,128)} %get-tuple-element.47), channel_id=1, source_target_pairs={{1,2},{3,4},{5,6},{7,8},{9,10},{11,12},{13,14},{15,16},{17,18},{19... | collective-permute-start | bytes 1572872 | tf_op jit(solution)/shard_map/ppermute | solution.py:626
  24.8 2.7 %collective-permute-start.1 = (s32[8]{0:T(128)S(1)}, s32[8]{0:T(128)S(1)}, u32[]{:S(2)}, u32[]{:S(2)}) collective-permute-start(s32[8]{0:T(128)S(1)} %fusion), channel_id=1, source_target_pairs={{0,64},{32,96},{64,0},{96,32},{128,192},{160,224},{192,128},{224,1... | collective-permute-start | bytes 104 | tf_op jit(solution)/shard_map/ppermute | solution.py:31
  29.4 4.4 %collective-permute-done.2 = s32[8]{0:T(128)S(1)} collective-permute-done((s32[8]{0:T(128)S(1)}, s32[8]{0:T(128)S(1)}, u32[]{:S(2)}, u32[]{:S(2)}) %collective-permute-start.2) | collective-permute-done | bytes 64 | tf_op jit(solution)/shard_map/ppermute | solution.py:31
  34.0 5.4 %first.1 = (f32[16,64,256]{2,1,0:T(8,128)}, f32[16,64,256]{2,1,0:T(8,128)}) custom-call(f32[170]{0:T(256)S(1)} %concatenate.8.scalars, f32[16,64,256]{2,1,0:T(8,128)S(1)} %bitcast.35, f32[16,64,256]{2,1,0:T(8,128)S(1)} %bitcast.39, f32[8,64,256]{2,1,0:T(8,128)} %collective-permute-done.5.near, f32[8,64,256]{2,1,0:T(8,128)} %collective-permute-done.6.far), custom_call_target="tpu_custom_call" | custom-call | tf_op jit(solution)/shard_map/first/pallas_call | solution.py:679
  41.6 2.6 %all-to-all-done.line = f32[32,4,8,256]{3,2,1,0:T(8,128)S(1)} async-done(((f32[32,4,8,256]{3,2,1,0:T(8,128)}), f32[32,4,8,256]{3,2,1,0:T(8,128)S(1)}, u32[]{:S(2)}, u32[]{:S(2)}) %all-to-all-start) | async-done | bytes 1048608 | tf_op jit(solution)/shard_map/all_to_all | solution.py:526
  45.8 32.1 %all_to_all.20 = f32[32,4,8,256]{3,2,1,0:T(8,128)S(1)} all-to-all(f32[32,4,8,256]{3,2,1,0:T(8,128)} %gather.1), channel_id=1, replica_groups=mesh['shot'=8,'zz'=8,'quad'=4] {'shot','quad'}, dimensions={0} | all-to-all | bytes 2097152 | tf_op jit(solution)/shard_map/all_to_all | solution.py:526
  80.5 3.2 %collective-permute-start.12 = (f32[4,64,256]{2,1,0:T(8,128)S(1)}, f32[4,64,256]{2,1,0:T(8,128)S(1)}, u32[]{:S(2)}, u32[]{:S(2)}) collective-permute-start(f32[4,64,256]{2,1,0:T(8,128)S(1)} %get-tuple-element.63), channel_id=1, source_target_pairs={{1,2},{3,4},{5,6},{7,8},{9,10},{11,12},{13,14},{15,16},{17,18},{19... | collective-permute-start | bytes 786440 | tf_op jit(solution)/shard_map/ppermute | solution.py:626
  83.8 2.3 %shard_map.110 = (f32[4,64,256]{2,1,0:T(8,128)S(1)}, f32[4,64,256]{2,1,0:T(8,128)S(1)}) custom-call(f32[170]{0:T(256)S(1)} %concatenate.8.scalars, f32[16,64,256]{2,1,0:T(8,128)} %bitcast.38, f32[16,64,256]{2,1,0:T(8,128)} %bitcast.43, f32[16,64,256]{2,1,0:T(8,128)} %get-tuple-element.50.drive.refs_2_, f32[8,16,8,256]{3,2,1,0:T(8,128)S(1)} %bitcast.25), custom_call_target="tpu_custom_call" | custom-call | tf_op jit(solution)/shard_map/pallas_call | solution.py:610
  86.2 5.0 %collective-permute-start.8 = (f32[4,64,256]{2,1,0:T(8,128)S(1)}, f32[4,64,256]{2,1,0:T(8,128)S(1)}, u32[]{:S(2)}, u32[]{:S(2)}) collective-permute-start(f32[4,64,256]{2,1,0:T(8,128)S(1)} %get-tuple-element.53), channel_id=1, source_target_pairs={{1,2},{3,4},{5,6},{7,8},{9,10},{11,12},{13,14},{15,16},{17,18},{19... | collective-permute-start | bytes 786440 | tf_op jit(solution)/shard_map/ppermute | solution.py:626
  91.3 3.0 %shard_map.114 = (f32[16,64,256]{2,1,0:T(8,128)S(1)}, f32[16,64,256]{2,1,0:T(8,128)S(1)}, f32[16,64,256]{2,1,0:T(8,128)S(1)}, f32[4,64,256]{2,1,0:T(8,128)S(1)}, f32[4,64,256]{2,1,0:T(8,128)S(1)}) custom-call(f32[170]{0:T(256)S(1)} %concatenate.8.scalars, f32[16,64,256]{2,1,0:T(8,128)S(1)} %bitcast.36, f32[16,64,256]{2,1,0:T(8,128)S(1)} %bitcast.42, ...), custom_call_target="tpu_custom_call" | custom-call | tf_op jit(solution)/shard_map/pallas_call | solution.py:47
  94.4 4.4 %collective-permute-start.14 = (f32[4,64,256]{2,1,0:T(8,128)S(1)}, f32[4,64,256]{2,1,0:T(8,128)S(1)}, u32[]{:S(2)}, u32[]{:S(2)}) collective-permute-start(f32[4,64,256]{2,1,0:T(8,128)S(1)} %get-tuple-element.67), channel_id=1, source_target_pairs={{1,2},{3,4},{5,6},{7,8},{9,10},{11,12},{13,14},{15,16},{17,18},{19... | collective-permute-start | bytes 786440 | tf_op jit(solution)/shard_map/ppermute | solution.py:626
  98.9 3.0 %shard_map.111 = (f32[16,64,256]{2,1,0:T(8,128)S(1)}, f32[16,64,256]{2,1,0:T(8,128)S(1)}, f32[16,64,256]{2,1,0:T(8,128)S(1)}, f32[4,64,256]{2,1,0:T(8,128)S(1)}, f32[4,64,256]{2,1,0:T(8,128)S(1)}) custom-call(f32[170]{0:T(256)S(1)} %concatenate.8.scalars, f32[16,64,256]{2,1,0:T(8,128)S(1)} %bitcast.40, f32[16,64,256]{2,1,0:T(8,128)S(1)} %bitcast.44, ...), custom_call_target="tpu_custom_call" | custom-call | tf_op jit(solution)/shard_map/pallas_call | solution.py:47
  101.9 4.4 %collective-permute-start.10 = (f32[4,64,256]{2,1,0:T(8,128)S(1)}, f32[4,64,256]{2,1,0:T(8,128)S(1)}, u32[]{:S(2)}, u32[]{:S(2)}) collective-permute-start(f32[4,64,256]{2,1,0:T(8,128)S(1)} %get-tuple-element.57), channel_id=1, source_target_pairs={{1,2},{3,4},{5,6},{7,8},{9,10},{11,12},{13,14},{15,16},{17,18},{19... | collective-permute-start | bytes 786440 | tf_op jit(solution)/shard_map/ppermute | solution.py:626
  106.4 2.4 %shard_map.115 = (f32[16,64,256]{2,1,0:T(8,128)S(1)}, f32[16,64,256]{2,1,0:T(8,128)S(1)}, f32[16,64,256]{2,1,0:T(8,128)S(1)}, f32[4,64,256]{2,1,0:T(8,128)S(1)}, f32[4,64,256]{2,1,0:T(8,128)S(1)}) custom-call(f32[170]{0:T(256)S(1)} %concatenate.8.scalars, f32[16,64,256]{2,1,0:T(8,128)S(1)} %get-tuple-element.64.refs_0_, ...), custom_call_target="tpu_custom_call" | custom-call | tf_op jit(solution)/shard_map/pallas_call | solution.py:47
  109.6 3.9 %collective-permute-start.16 = (f32[4,64,256]{2,1,0:T(8,128)S(1)}, f32[4,64,256]{2,1,0:T(8,128)S(1)}, u32[]{:S(2)}, u32[]{:S(2)}) collective-permute-start(f32[4,64,256]{2,1,0:T(8,128)S(1)} %get-tuple-element.71), channel_id=1, source_target_pairs={{1,2},{3,4},{5,6},{7,8},{9,10},{11,12},{13,14},{15,16},{17,18},{19... | collective-permute-start | bytes 786440 | tf_op jit(solution)/shard_map/ppermute | solution.py:626
  113.6 2.4 %shard_map.112 = (f32[16,64,256]{2,1,0:T(8,128)S(1)}, f32[16,64,256]{2,1,0:T(8,128)S(1)}, f32[4,64,256]{2,1,0:T(8,128)S(1)}, f32[4,64,256]{2,1,0:T(8,128)S(1)}) custom-call(f32[170]{0:T(256)S(1)} %concatenate.8.scalars, f32[16,64,256]{2,1,0:T(8,128)S(1)} %get-tuple-element.54.refs_0_.refs_2_, f32[16,64,256]{2,1,0:T(8,128)S(1)} %get-tuple-element.55.refs_1_, ...), custom_call_target="tpu_custom_call" | custom-call | tf_op jit(solution)/shard_map/pallas_call | solution.py:47
  116.1 5.2 %collective-permute-start.18 = (f32[4,64,256]{2,1,0:T(8,128)S(1)}, f32[4,64,256]{2,1,0:T(8,128)S(1)}, u32[]{:S(2)}, u32[]{:S(2)}) collective-permute-start(f32[4,64,256]{2,1,0:T(8,128)S(1)} %get-tuple-element.76), channel_id=1, source_target_pairs={{1,2},{3,4},{5,6},{7,8},{9,10},{11,12},{13,14},{15,16},{17,18},{19... | collective-permute-start | bytes 786440 | tf_op jit(solution)/shard_map/ppermute | solution.py:626
  124.3 2.3 %shard_map.118 = (f32[8,16,8,256]{3,2,1,0:T(8,128)S(1)}, f32[8,64,256]{2,1,0:T(8,128)S(1)}) custom-call(f32[170]{0:T(256)S(1)} %concatenate.8.scalars, f32[16,64,256]{2,1,0:T(8,128)S(1)} %get-tuple-element.58.refs_4_.w, f32[16,64,256]{2,1,0:T(8,128)S(1)} %get-tuple-element.59.vw, f32[8,16,8,256]{3,2,1,0:T(8,128)S(1)} %bitcast.31, ...), custom_call_target="tpu_custom_call" | custom-call | tf_op jit(solution)/shard_map/pallas_call | solution.py:47
  128.4 24.0 %all_to_all.21.got = f32[32,4,8,256]{3,2,1,0:T(8,128)S(1)} all-to-all(f32[32,4,8,256]{3,2,1,0:T(8,128)S(1)} %bitcast.45), channel_id=1, replica_groups=mesh['shot'=8,'zz'=8,'quad'=4] {'shot','quad'}, dimensions={0} | all-to-all | bytes 2097152 | tf_op jit(solution)/shard_map/all_to_all | solution.py:526
  154.2 8.4 %all-to-all-start.3 = ((f32[32,4,8,256]{3,2,1,0:T(8,128)}), f32[32,4,8,256]{3,2,1,0:T(8,128)S(1)}, u32[]{:S(2)}, u32[]{:S(2)}) async-start(f32[32,4,8,256]{3,2,1,0:T(8,128)} %get-tuple-element.78), calls=%async_computation.3 | async-start | bytes 2097152 | tf_op jit(solution)/shard_map/all_to_all | solution.py:526
  164.0 2.9 %collective-permute-start.20 = (f32[2,4,8,256]{3,2,1,0:T(8,128)S(1)}, f32[2,4,8,256]{3,2,1,0:T(8,128)S(1)}, u32[]{:S(2)}, u32[]{:S(2)}) collective-permute-start(f32[2,4,8,256]{3,2,1,0:T(8,128)S(1)} %shard_map.120), channel_id=1, source_target_pairs={{0,2},{1,3},{2,0},{3,1},{4,6},{5,7},{6,4},{7,5},{8,10},{9,11},{10,... | collective-permute-start | bytes 196616 | tf_op jit(solution)/shard_map/ppermute | solution.py:530
  169.0 21.7 %all-to-all-done.3.came = f32[32,4,8,256]{3,2,1,0:T(8,128)S(1)} async-done(((f32[32,4,8,256]{3,2,1,0:T(8,128)}), f32[32,4,8,256]{3,2,1,0:T(8,128)S(1)}, u32[]{:S(2)}, u32[]{:S(2)}) %all-to-all-start.3) | async-done | bytes 1048608 | tf_op jit(solution)/shard_map/all_to_all | solution.py:526
  (76 shorter events, 23.6 us)
Async XLA Ops:
  3.2 30.8 %copy-start = (f32[1,16,64,256]{3,2,1,0:T(8,128)S(1)}, f32[1,16,64,256]{3,2,1,0:T(8,128)}, u32[]{:S(2)}) copy-start(f32[1,16,64,256]{3,2,1,0:T(8,128)} %param.19) | copy-start | bytes 3145732
  3.2 41.0 %all-to-all-start = ((f32[32,4,8,256]{3,2,1,0:T(8,128)}), f32[32,4,8,256]{3,2,1,0:T(8,128)S(1)}, u32[]{:S(2)}, u32[]{:S(2)}) async-start(f32[32,4,8,256]{3,2,1,0:T(8,128)} %bitcast.46), calls=%async_computation | async-start | bytes 2097152 | tf_op jit(solution)/shard_map/all_to_all | solution.py:526
  16.1 17.9 %collective-permute-start.5 = (f32[8,64,256]{2,1,0:T(8,128)}, f32[8,64,256]{2,1,0:T(8,128)}, u32[]{:S(2)}, u32[]{:S(2)}) collective-permute-start(f32[8,64,256]{2,1,0:T(8,128)} %get-tuple-element.46), channel_id=1, source_target_pairs={{0,1},{1,0},{2,3},{3,2},{4,5},{5,4},{6,7},{7,6},{8,9},{9,8},{10,11... | collective-permute-start | bytes 1572872 | tf_op jit(solution)/shard_map/ppermute | solution.py:627
  16.4 17.6 %collective-permute-start.6 = (f32[8,64,256]{2,1,0:T(8,128)}, f32[8,64,256]{2,1,0:T(8,128)}, u32[]{:S(2)}, u32[]{:S(2)}) collective-permute-start(f32[8,64,256]{2,1,0:T(8,128)} %get-tuple-element.47), channel_id=1, source_target_pairs={{1,2},{3,4},{5,6},{7,8},{9,10},{11,12},{13,14},{15,16},{17,18},{19... | collective-permute-start | bytes 1572872 | tf_op jit(solution)/shard_map/ppermute | solution.py:626
  22.0 2.8 %collective-permute-start = (s32[8]{0:T(128)S(1)}, s32[8]{0:T(128)S(1)}, u32[]{:S(2)}, u32[]{:S(2)}) collective-permute-start(s32[8]{0:T(128)S(1)} %compare_select_fusion), channel_id=1, source_target_pairs={{0,32},{32,0},{64,96},{96,64},{128,160},{160,128},{192,224},{224,1... | collective-permute-start | bytes 104 | tf_op jit(solution)/shard_map/ppermute | solution.py:31
  23.3 10.5 %collective-permute-start.3 = (f32[2,4,8,256]{3,2,1,0:T(8,128)S(1)}, f32[2,4,8,256]{3,2,1,0:T(8,128)S(1)}, u32[]{:S(2)}, u32[]{:S(2)}) collective-permute-start(f32[2,4,8,256]{3,2,1,0:T(8,128)S(1)} %get-tuple-element.45), channel_id=1, source_target_pairs={{0,1},{1,0},{2,3},{3,2},{4,5},{5,4},{6,7},{7,6},{8,9},{9,8},{10,11... | collective-permute-start | bytes 196616 | tf_op jit(solution)/shard_map/ppermute | solution.py:530
  24.8 4.2 %collective-permute-start.1 = (s32[8]{0:T(128)S(1)}, s32[8]{0:T(128)S(1)}, u32[]{:S(2)}, u32[]{:S(2)}) collective-permute-start(s32[8]{0:T(128)S(1)} %fusion), channel_id=1, source_target_pairs={{0,64},{32,96},{64,0},{96,32},{128,192},{160,224},{192,128},{224,1... | collective-permute-start | bytes 104 | tf_op jit(solution)/shard_map/ppermute | solution.py:31
  29.0 4.8 %collective-permute-start.2 = (s32[8]{0:T(128)S(1)}, s32[8]{0:T(128)S(1)}, u32[]{:S(2)}, u32[]{:S(2)}) collective-permute-start(s32[8]{0:T(128)S(1)} %fusion.1), channel_id=1, source_target_pairs={{0,128},{32,160},{64,192},{96,224},{128,0},{160,32},{192,64},{224,... | collective-permute-start | bytes 104 | tf_op jit(solution)/shard_map/ppermute | solution.py:31
  33.8 7.8 %collective-permute-start.4 = (f32[2,4,8,256]{3,2,1,0:T(8,128)S(1)}, f32[2,4,8,256]{3,2,1,0:T(8,128)S(1)}, u32[]{:S(2)}, u32[]{:S(2)}) collective-permute-start(f32[2,4,8,256]{3,2,1,0:T(8,128)S(1)} %shard_map.109), channel_id=1, source_target_pairs={{0,2},{1,3},{2,0},{3,1},{4,6},{5,7},{6,4},{7,5},{8,10},{9,11},{10,... | collective-permute-start | bytes 196616 | tf_op jit(solution)/shard_map/ppermute | solution.py:530
  80.0 11.3 %collective-permute-start.11 = (f32[4,64,256]{2,1,0:T(8,128)S(1)}, f32[4,64,256]{2,1,0:T(8,128)S(1)}, u32[]{:S(2)}, u32[]{:S(2)}) collective-permute-start(f32[4,64,256]{2,1,0:T(8,128)S(1)} %get-tuple-element.62), channel_id=1, source_target_pairs={{0,1},{1,0},{2,3},{3,2},{4,5},{5,4},{6,7},{7,6},{8,9},{9,8},{10,11... | collective-permute-start | bytes 786440 | tf_op jit(solution)/shard_map/ppermute | solution.py:627
  80.5 10.8 %collective-permute-start.12 = (f32[4,64,256]{2,1,0:T(8,128)S(1)}, f32[4,64,256]{2,1,0:T(8,128)S(1)}, u32[]{:S(2)}, u32[]{:S(2)}) collective-permute-start(f32[4,64,256]{2,1,0:T(8,128)S(1)} %get-tuple-element.63), channel_id=1, source_target_pairs={{1,2},{3,4},{5,6},{7,8},{9,10},{11,12},{13,14},{15,16},{17,18},{19... | collective-permute-start | bytes 786440 | tf_op jit(solution)/shard_map/ppermute | solution.py:626
  86.1 12.7 %collective-permute-start.7 = (f32[4,64,256]{2,1,0:T(8,128)S(1)}, f32[4,64,256]{2,1,0:T(8,128)S(1)}, u32[]{:S(2)}, u32[]{:S(2)}) collective-permute-start(f32[4,64,256]{2,1,0:T(8,128)S(1)} %get-tuple-element.52), channel_id=1, source_target_pairs={{0,1},{1,0},{2,3},{3,2},{4,5},{5,4},{6,7},{7,6},{8,9},{9,8},{10,11... | collective-permute-start | bytes 786440 | tf_op jit(solution)/shard_map/ppermute | solution.py:627
  86.2 12.6 %collective-permute-start.8 = (f32[4,64,256]{2,1,0:T(8,128)S(1)}, f32[4,64,256]{2,1,0:T(8,128)S(1)}, u32[]{:S(2)}, u32[]{:S(2)}) collective-permute-start(f32[4,64,256]{2,1,0:T(8,128)S(1)} %get-tuple-element.53), channel_id=1, source_target_pairs={{1,2},{3,4},{5,6},{7,8},{9,10},{11,12},{13,14},{15,16},{17,18},{19... | collective-permute-start | bytes 786440 | tf_op jit(solution)/shard_map/ppermute | solution.py:626
  94.3 12.1 %collective-permute-start.13 = (f32[4,64,256]{2,1,0:T(8,128)S(1)}, f32[4,64,256]{2,1,0:T(8,128)S(1)}, u32[]{:S(2)}, u32[]{:S(2)}) collective-permute-start(f32[4,64,256]{2,1,0:T(8,128)S(1)} %get-tuple-element.66), channel_id=1, source_target_pairs={{0,1},{1,0},{2,3},{3,2},{4,5},{5,4},{6,7},{7,6},{8,9},{9,8},{10,11... | collective-permute-start | bytes 786440 | tf_op jit(solution)/shard_map/ppermute | solution.py:627
  94.4 12.0 %collective-permute-start.14 = (f32[4,64,256]{2,1,0:T(8,128)S(1)}, f32[4,64,256]{2,1,0:T(8,128)S(1)}, u32[]{:S(2)}, u32[]{:S(2)}) collective-permute-start(f32[4,64,256]{2,1,0:T(8,128)S(1)} %get-tuple-element.67), channel_id=1, source_target_pairs={{1,2},{3,4},{5,6},{7,8},{9,10},{11,12},{13,14},{15,16},{17,18},{19... | collective-permute-start | bytes 786440 | tf_op jit(solution)/shard_map/ppermute | solution.py:626
  101.9 11.7 %collective-permute-start.10 = (f32[4,64,256]{2,1,0:T(8,128)S(1)}, f32[4,64,256]{2,1,0:T(8,128)S(1)}, u32[]{:S(2)}, u32[]{:S(2)}) collective-permute-start(f32[4,64,256]{2,1,0:T(8,128)S(1)} %get-tuple-element.57), channel_id=1, source_target_pairs={{1,2},{3,4},{5,6},{7,8},{9,10},{11,12},{13,14},{15,16},{17,18},{19... | collective-permute-start | bytes 786440 | tf_op jit(solution)/shard_map/ppermute | solution.py:626
  106.3 7.3 %collective-permute-start.9 = (f32[4,64,256]{2,1,0:T(8,128)S(1)}, f32[4,64,256]{2,1,0:T(8,128)S(1)}, u32[]{:S(2)}, u32[]{:S(2)}) collective-permute-start(f32[4,64,256]{2,1,0:T(8,128)S(1)} %get-tuple-element.56), channel_id=1, source_target_pairs={{0,1},{1,0},{2,3},{3,2},{4,5},{5,4},{6,7},{7,6},{8,9},{9,8},{10,11... | collective-permute-start | bytes 786440 | tf_op jit(solution)/shard_map/ppermute | solution.py:627
  108.9 12.4 %collective-permute-start.15 = (f32[4,64,256]{2,1,0:T(8,128)S(1)}, f32[4,64,256]{2,1,0:T(8,128)S(1)}, u32[]{:S(2)}, u32[]{:S(2)}) collective-permute-start(f32[4,64,256]{2,1,0:T(8,128)S(1)} %get-tuple-element.70), channel_id=1, source_target_pairs={{0,1},{1,0},{2,3},{3,2},{4,5},{5,4},{6,7},{7,6},{8,9},{9,8},{10,11... | collective-permute-start | bytes 786440 | tf_op jit(solution)/shard_map/ppermute | solution.py:627
  109.6 11.7 %collective-permute-start.16 = (f32[4,64,256]{2,1,0:T(8,128)S(1)}, f32[4,64,256]{2,1,0:T(8,128)S(1)}, u32[]{:S(2)}, u32[]{:S(2)}) collective-permute-start(f32[4,64,256]{2,1,0:T(8,128)S(1)} %get-tuple-element.71), channel_id=1, source_target_pairs={{1,2},{3,4},{5,6},{7,8},{9,10},{11,12},{13,14},{15,16},{17,18},{19... | collective-permute-start | bytes 786440 | tf_op jit(solution)/shard_map/ppermute | solution.py:626
  116.0 10.5 %collective-permute-start.17 = (f32[4,64,256]{2,1,0:T(8,128)S(1)}, f32[4,64,256]{2,1,0:T(8,128)S(1)}, u32[]{:S(2)}, u32[]{:S(2)}) collective-permute-start(f32[4,64,256]{2,1,0:T(8,128)S(1)} %get-tuple-element.75), channel_id=1, source_target_pairs={{0,1},{1,0},{2,3},{3,2},{4,5},{5,4},{6,7},{7,6},{8,9},{9,8},{10,11... | collective-permute-start | bytes 786440 | tf_op jit(solution)/shard_map/ppermute | solution.py:627
  116.1 11.3 %collective-permute-start.18 = (f32[4,64,256]{2,1,0:T(8,128)S(1)}, f32[4,64,256]{2,1,0:T(8,128)S(1)}, u32[]{:S(2)}, u32[]{:S(2)}) collective-permute-start(f32[4,64,256]{2,1,0:T(8,128)S(1)} %get-tuple-element.76), channel_id=1, source_target_pairs={{1,2},{3,4},{5,6},{7,8},{9,10},{11,12},{13,14},{15,16},{17,18},{19... | collective-permute-start | bytes 786440 | tf_op jit(solution)/shard_map/ppermute | solution.py:626
  154.2 36.4 %all-to-all-start.3 = ((f32[32,4,8,256]{3,2,1,0:T(8,128)}), f32[32,4,8,256]{3,2,1,0:T(8,128)S(1)}, u32[]{:S(2)}, u32[]{:S(2)}) async-start(f32[32,4,8,256]{3,2,1,0:T(8,128)} %get-tuple-element.78), calls=%async_computation.3 | async-start | bytes 2097152 | tf_op jit(solution)/shard_map/all_to_all | solution.py:526
  162.6 1.3 collective-permute-start.19
  164.0 5.0 %collective-permute-start.20 = (f32[2,4,8,256]{3,2,1,0:T(8,128)S(1)}, f32[2,4,8,256]{3,2,1,0:T(8,128)S(1)}, u32[]{:S(2)}, u32[]{:S(2)}) collective-permute-start(f32[2,4,8,256]{3,2,1,0:T(8,128)S(1)} %shard_map.120), channel_id=1, source_target_pairs={{0,2},{1,3},{2,0},{3,1},{4,6},{5,7},{6,4},{7,5},{8,10},{9,11},{10,... | collective-permute-start | bytes 196616 | tf_op jit(solution)/shard_map/ppermute | solution.py:530
  (11 other events, 174.4 us)

commit v10 on v9

--- a/solution.py
+++ b/solution.py
@@ -389,6 +389,8 @@
     me_shot, me_z, me_q = spot[0], spot[1], spot[2]
     rows = pl.ds(pl.multiple_of(me_shot * slab, SUB), slab)
     first = jnp.where(me_q % 2 == 0, tile_x - REACH, 0)
+    load = pltpu.make_async_copy(courant.at[:, :, rows, :], slab_in, sems.at[4])
+    load.start()
     loads = []
     for side in range(2):
         x0 = first if side == 0 else tile_x - REACH - first
@@ -400,19 +402,17 @@
                     sems.at[2 * side + k],
                 )
             )
-    loads.append(pltpu.make_async_copy(courant.at[:, :, rows, :], slab_in, sems.at[4]))
-    for load in loads:
-        load.start()
+            loads[-1].start()
+    load.wait()
     stores = []
+    for z in range(zs):
+        row = jnp.where(z <= me_z, 0, 1)
+        stores.append(pltpu.make_async_copy(slab_in.at[row], parts.at[z], sems.at[7 + z]))
+        stores[-1].start()
     for side, out in enumerate((inner, outer)):
         loads[2 * side].wait()
         loads[2 * side + 1].wait()
         stores.append(pltpu.make_async_copy(sides.at[side], out, sems.at[5 + side]))
-        stores[-1].start()
-    loads[4].wait()
-    for z in range(zs):
-        row = jnp.where(z <= me_z, 0, 1)
-        stores.append(pltpu.make_async_copy(slab_in.at[row], parts.at[z], sems.at[7 + z]))
         stores[-1].start()
     for k, turn in enumerate((0, 2)):
         keep[k] = slab_in[1, pl.ds((me_q ^ turn) * planes, planes)]

time: 193 us -> 193 us (level)
  no operation moved by 1% of the time
where the time goes in v10:
time: 193 us; the launch traced here: 192 us
  starting transfers between devices  62 us (32%)
  blocking collectives  56.1 us (29%)
  waiting for transfers between devices  37 us (19%)
  Pallas kernels  34.7 us (18%)
    all_to_all x2, blocking collectives, exchange(): return lax.all_to_all(parts, axes, split_axis=0, concat_axis=0, tiled=True)  56.1 us
    ppermute x7, starting transfers between devices, halos(): far = lax.ppermute(outer, MP, pairs + [(j, i) for i, j in pairs])  31.1 us
    all_to_all x2, waiting for transfers between devices, exchange(): return lax.all_to_all(parts, axes, split_axis=0, concat_axis=0, tiled=True)  24.3 us
    all_to_all x2, starting transfers between devices, exchange(): return lax.all_to_all(parts, axes, split_axis=0, concat_axis=0, tiled=True)  21.2 us
    pallas_call x11, Pallas kernels, local_kernel(): pl.pallas_call(body, out_shape=outs, in_specs=[smem] * len(scalars) + [vm...  18.4 us
    ppermute x3, waiting for transfers between devices, all_first(): lax.ppermute(known, 'shot', [(i, i ^ step) for i in range(shots)])  6.49 us
    pallas_call x1, Pallas kernels, window(): pl.pallas_call(functools.partial(first_kernel, steps, receivers), out_sha...  5.43 us
    ppermute x4, waiting for transfers between devices, swap_quads(): return lax.ppermute(value, 'quad', [(q, q ^ turn) for q in range(QUAD)])  5.23 us
  transfers between devices with their start and end apart: 23, of which 9 were waited for; matrix products, arithmetic and copies ran while one was open for 0% of the time, Pallas kernels for 12%

profile of v10, /device:TPU:1, one launch (start us, length us, event | category | flops | bytes accessed | tf_op | source)
XLA Modules:
  0.0 192.0 jit_solution(14580977409201358044)
XLA Ops:
  0.1 3.0 %split.1 = (f32[8,16,8,256]{3,2,1,0:T(8,128)}, f32[8,64,256]{2,1,0:T(8,128)}, f32[8,64,256]{2,1,0:T(8,128)}, f32[2,4,8,256]{3,2,1,0:T(8,128)S(1)}, f32[2,4,8,256]{3,2,1,0:T(8,128)S(1)}) custom-call(s32[3]{0:T(128)S(1)} %pad_add_fusion.1.spot, f32[2,16,64,256]{3,2,1,0:T(8,128)} %courant.1, f32[16,64,256]{2,1,0:T(8,128)} %bitcast.33, f32[16,64,256]{2,1,0:T(8,128)} %bitcast.37), custom_call_target="tpu_custom_call" | custom-call | tf_op jit(solution)/shard_map/split/pallas_call | solution.py:546
  3.1 12.9 %all-to-all-start = ((f32[32,4,8,256]{3,2,1,0:T(8,128)}), f32[32,4,8,256]{3,2,1,0:T(8,128)S(1)}, u32[]{:S(2)}, u32[]{:S(2)}) async-start(f32[32,4,8,256]{3,2,1,0:T(8,128)} %bitcast.46), calls=%async_computation | async-start | bytes 2097152 | tf_op jit(solution)/shard_map/all_to_all | solution.py:526
  16.3 4.9 %collective-permute-start.6 = (f32[8,64,256]{2,1,0:T(8,128)}, f32[8,64,256]{2,1,0:T(8,128)}, u32[]{:S(2)}, u32[]{:S(2)}) collective-permute-start(f32[8,64,256]{2,1,0:T(8,128)} %get-tuple-element.47), channel_id=1, source_target_pairs={{1,2},{3,4},{5,6},{7,8},{9,10},{11,12},{13,14},{15,16},{17,18},{19... | collective-permute-start | bytes 1572872 | tf_op jit(solution)/shard_map/ppermute | solution.py:626
  24.7 2.7 %collective-permute-start.1 = (s32[8]{0:T(128)S(1)}, s32[8]{0:T(128)S(1)}, u32[]{:S(2)}, u32[]{:S(2)}) collective-permute-start(s32[8]{0:T(128)S(1)} %fusion), channel_id=1, source_target_pairs={{0,64},{32,96},{64,0},{96,32},{128,192},{160,224},{192,128},{224,1... | collective-permute-start | bytes 104 | tf_op jit(solution)/shard_map/ppermute | solution.py:31
  29.4 4.4 %collective-permute-done.2 = s32[8]{0:T(128)S(1)} collective-permute-done((s32[8]{0:T(128)S(1)}, s32[8]{0:T(128)S(1)}, u32[]{:S(2)}, u32[]{:S(2)}) %collective-permute-start.2) | collective-permute-done | bytes 64 | tf_op jit(solution)/shard_map/ppermute | solution.py:31
  33.9 5.4 %first.1 = (f32[16,64,256]{2,1,0:T(8,128)}, f32[16,64,256]{2,1,0:T(8,128)}) custom-call(f32[170]{0:T(256)S(1)} %concatenate.8.scalars, f32[16,64,256]{2,1,0:T(8,128)S(1)} %bitcast.35, f32[16,64,256]{2,1,0:T(8,128)S(1)} %bitcast.39, f32[8,64,256]{2,1,0:T(8,128)} %collective-permute-done.5.near, f32[8,64,256]{2,1,0:T(8,128)} %collective-permute-done.6.far), custom_call_target="tpu_custom_call" | custom-call | tf_op jit(solution)/shard_map/first/pallas_call | solution.py:679
  41.5 2.6 %all-to-all-done.line = f32[32,4,8,256]{3,2,1,0:T(8,128)S(1)} async-done(((f32[32,4,8,256]{3,2,1,0:T(8,128)}), f32[32,4,8,256]{3,2,1,0:T(8,128)S(1)}, u32[]{:S(2)}, u32[]{:S(2)}) %all-to-all-start) | async-done | bytes 1048608 | tf_op jit(solution)/shard_map/all_to_all | solution.py:526
  45.8 32.1 %all_to_all.20 = f32[32,4,8,256]{3,2,1,0:T(8,128)S(1)} all-to-all(f32[32,4,8,256]{3,2,1,0:T(8,128)} %gather.1), channel_id=1, replica_groups=mesh['shot'=8,'zz'=8,'quad'=4] {'shot','quad'}, dimensions={0} | all-to-all | bytes 2097152 | tf_op jit(solution)/shard_map/all_to_all | solution.py:526
  80.4 3.2 %collective-permute-start.12 = (f32[4,64,256]{2,1,0:T(8,128)S(1)}, f32[4,64,256]{2,1,0:T(8,128)S(1)}, u32[]{:S(2)}, u32[]{:S(2)}) collective-permute-start(f32[4,64,256]{2,1,0:T(8,128)S(1)} %get-tuple-element.63), channel_id=1, source_target_pairs={{1,2},{3,4},{5,6},{7,8},{9,10},{11,12},{13,14},{15,16},{17,18},{19... | collective-permute-start | bytes 786440 | tf_op jit(solution)/shard_map/ppermute | solution.py:626
  83.7 2.3 %shard_map.110 = (f32[4,64,256]{2,1,0:T(8,128)S(1)}, f32[4,64,256]{2,1,0:T(8,128)S(1)}) custom-call(f32[170]{0:T(256)S(1)} %concatenate.8.scalars, f32[16,64,256]{2,1,0:T(8,128)} %bitcast.38, f32[16,64,256]{2,1,0:T(8,128)} %bitcast.43, f32[16,64,256]{2,1,0:T(8,128)} %get-tuple-element.50.drive.refs_2_, f32[8,16,8,256]{3,2,1,0:T(8,128)S(1)} %bitcast.25), custom_call_target="tpu_custom_call" | custom-call | tf_op jit(solution)/shard_map/pallas_call | solution.py:610
  86.2 5.0 %collective-permute-start.8 = (f32[4,64,256]{2,1,0:T(8,128)S(1)}, f32[4,64,256]{2,1,0:T(8,128)S(1)}, u32[]{:S(2)}, u32[]{:S(2)}) collective-permute-start(f32[4,64,256]{2,1,0:T(8,128)S(1)} %get-tuple-element.53), channel_id=1, source_target_pairs={{1,2},{3,4},{5,6},{7,8},{9,10},{11,12},{13,14},{15,16},{17,18},{19... | collective-permute-start | bytes 786440 | tf_op jit(solution)/shard_map/ppermute | solution.py:626
  91.3 3.0 %shard_map.114 = (f32[16,64,256]{2,1,0:T(8,128)S(1)}, f32[16,64,256]{2,1,0:T(8,128)S(1)}, f32[16,64,256]{2,1,0:T(8,128)S(1)}, f32[4,64,256]{2,1,0:T(8,128)S(1)}, f32[4,64,256]{2,1,0:T(8,128)S(1)}) custom-call(f32[170]{0:T(256)S(1)} %concatenate.8.scalars, f32[16,64,256]{2,1,0:T(8,128)S(1)} %bitcast.36, f32[16,64,256]{2,1,0:T(8,128)S(1)} %bitcast.42, ...), custom_call_target="tpu_custom_call" | custom-call | tf_op jit(solution)/shard_map/pallas_call | solution.py:47
  94.4 4.4 %collective-permute-start.14 = (f32[4,64,256]{2,1,0:T(8,128)S(1)}, f32[4,64,256]{2,1,0:T(8,128)S(1)}, u32[]{:S(2)}, u32[]{:S(2)}) collective-permute-start(f32[4,64,256]{2,1,0:T(8,128)S(1)} %get-tuple-element.67), channel_id=1, source_target_pairs={{1,2},{3,4},{5,6},{7,8},{9,10},{11,12},{13,14},{15,16},{17,18},{19... | collective-permute-start | bytes 786440 | tf_op jit(solution)/shard_map/ppermute | solution.py:626
  98.8 3.0 %shard_map.111 = (f32[16,64,256]{2,1,0:T(8,128)S(1)}, f32[16,64,256]{2,1,0:T(8,128)S(1)}, f32[16,64,256]{2,1,0:T(8,128)S(1)}, f32[4,64,256]{2,1,0:T(8,128)S(1)}, f32[4,64,256]{2,1,0:T(8,128)S(1)}) custom-call(f32[170]{0:T(256)S(1)} %concatenate.8.scalars, f32[16,64,256]{2,1,0:T(8,128)S(1)} %bitcast.40, f32[16,64,256]{2,1,0:T(8,128)S(1)} %bitcast.44, ...), custom_call_target="tpu_custom_call" | custom-call | tf_op jit(solution)/shard_map/pallas_call | solution.py:47
  101.8 4.4 %collective-permute-start.10 = (f32[4,64,256]{2,1,0:T(8,128)S(1)}, f32[4,64,256]{2,1,0:T(8,128)S(1)}, u32[]{:S(2)}, u32[]{:S(2)}) collective-permute-start(f32[4,64,256]{2,1,0:T(8,128)S(1)} %get-tuple-element.57), channel_id=1, source_target_pairs={{1,2},{3,4},{5,6},{7,8},{9,10},{11,12},{13,14},{15,16},{17,18},{19... | collective-permute-start | bytes 786440 | tf_op jit(solution)/shard_map/ppermute | solution.py:626
  106.4 2.4 %shard_map.115 = (f32[16,64,256]{2,1,0:T(8,128)S(1)}, f32[16,64,256]{2,1,0:T(8,128)S(1)}, f32[16,64,256]{2,1,0:T(8,128)S(1)}, f32[4,64,256]{2,1,0:T(8,128)S(1)}, f32[4,64,256]{2,1,0:T(8,128)S(1)}) custom-call(f32[170]{0:T(256)S(1)} %concatenate.8.scalars, f32[16,64,256]{2,1,0:T(8,128)S(1)} %get-tuple-element.64.refs_0_, ...), custom_call_target="tpu_custom_call" | custom-call | tf_op jit(solution)/shard_map/pallas_call | solution.py:47
  109.6 3.9 %collective-permute-start.16 = (f32[4,64,256]{2,1,0:T(8,128)S(1)}, f32[4,64,256]{2,1,0:T(8,128)S(1)}, u32[]{:S(2)}, u32[]{:S(2)}) collective-permute-start(f32[4,64,256]{2,1,0:T(8,128)S(1)} %get-tuple-element.71), channel_id=1, source_target_pairs={{1,2},{3,4},{5,6},{7,8},{9,10},{11,12},{13,14},{15,16},{17,18},{19... | collective-permute-start | bytes 786440 | tf_op jit(solution)/shard_map/ppermute | solution.py:626
  113.5 2.4 %shard_map.112 = (f32[16,64,256]{2,1,0:T(8,128)S(1)}, f32[16,64,256]{2,1,0:T(8,128)S(1)}, f32[4,64,256]{2,1,0:T(8,128)S(1)}, f32[4,64,256]{2,1,0:T(8,128)S(1)}) custom-call(f32[170]{0:T(256)S(1)} %concatenate.8.scalars, f32[16,64,256]{2,1,0:T(8,128)S(1)} %get-tuple-element.54.refs_0_.refs_2_, f32[16,64,256]{2,1,0:T(8,128)S(1)} %get-tuple-element.55.refs_1_, ...), custom_call_target="tpu_custom_call" | custom-call | tf_op jit(solution)/shard_map/pallas_call | solution.py:47
  116.0 5.2 %collective-permute-start.18 = (f32[4,64,256]{2,1,0:T(8,128)S(1)}, f32[4,64,256]{2,1,0:T(8,128)S(1)}, u32[]{:S(2)}, u32[]{:S(2)}) collective-permute-start(f32[4,64,256]{2,1,0:T(8,128)S(1)} %get-tuple-element.76), channel_id=1, source_target_pairs={{1,2},{3,4},{5,6},{7,8},{9,10},{11,12},{13,14},{15,16},{17,18},{19... | collective-permute-start | bytes 786440 | tf_op jit(solution)/shard_map/ppermute | solution.py:626
  124.2 2.3 %shard_map.118 = (f32[8,16,8,256]{3,2,1,0:T(8,128)S(1)}, f32[8,64,256]{2,1,0:T(8,128)S(1)}) custom-call(f32[170]{0:T(256)S(1)} %concatenate.8.scalars, f32[16,64,256]{2,1,0:T(8,128)S(1)} %get-tuple-element.58.refs_4_.w, f32[16,64,256]{2,1,0:T(8,128)S(1)} %get-tuple-element.59.vw, f32[8,16,8,256]{3,2,1,0:T(8,128)S(1)} %bitcast.31, ...), custom_call_target="tpu_custom_call" | custom-call | tf_op jit(solution)/shard_map/pallas_call | solution.py:47
  128.3 24.0 %all_to_all.21.got = f32[32,4,8,256]{3,2,1,0:T(8,128)S(1)} all-to-all(f32[32,4,8,256]{3,2,1,0:T(8,128)S(1)} %bitcast.45), channel_id=1, replica_groups=mesh['shot'=8,'zz'=8,'quad'=4] {'shot','quad'}, dimensions={0} | all-to-all | bytes 2097152 | tf_op jit(solution)/shard_map/all_to_all | solution.py:526
  154.2 8.4 %all-to-all-start.3 = ((f32[32,4,8,256]{3,2,1,0:T(8,128)}), f32[32,4,8,256]{3,2,1,0:T(8,128)S(1)}, u32[]{:S(2)}, u32[]{:S(2)}) async-start(f32[32,4,8,256]{3,2,1,0:T(8,128)} %get-tuple-element.78), calls=%async_computation.3 | async-start | bytes 2097152 | tf_op jit(solution)/shard_map/all_to_all | solution.py:526
  163.9 2.9 %collective-permute-start.20 = (f32[2,4,8,256]{3,2,1,0:T(8,128)S(1)}, f32[2,4,8,256]{3,2,1,0:T(8,128)S(1)}, u32[]{:S(2)}, u32[]{:S(2)}) collective-permute-start(f32[2,4,8,256]{3,2,1,0:T(8,128)S(1)} %shard_map.120), channel_id=1, source_target_pairs={{0,2},{1,3},{2,0},{3,1},{4,6},{5,7},{6,4},{7,5},{8,10},{9,11},{10,... | collective-permute-start | bytes 196616 | tf_op jit(solution)/shard_map/ppermute | solution.py:530
  168.9 21.7 %all-to-all-done.3.came = f32[32,4,8,256]{3,2,1,0:T(8,128)S(1)} async-done(((f32[32,4,8,256]{3,2,1,0:T(8,128)}), f32[32,4,8,256]{3,2,1,0:T(8,128)S(1)}, u32[]{:S(2)}, u32[]{:S(2)}) %all-to-all-start.3) | async-done | bytes 1048608 | tf_op jit(solution)/shard_map/all_to_all | solution.py:526
  (76 shorter events, 23.5 us)
Async XLA Ops:
  3.1 30.8 %copy-start = (f32[1,16,64,256]{3,2,1,0:T(8,128)S(1)}, f32[1,16,64,256]{3,2,1,0:T(8,128)}, u32[]{:S(2)}) copy-start(f32[1,16,64,256]{3,2,1,0:T(8,128)} %param.19) | copy-start | bytes 3145732
  3.1 41.0 %all-to-all-start = ((f32[32,4,8,256]{3,2,1,0:T(8,128)}), f32[32,4,8,256]{3,2,1,0:T(8,128)S(1)}, u32[]{:S(2)}, u32[]{:S(2)}) async-start(f32[32,4,8,256]{3,2,1,0:T(8,128)} %bitcast.46), calls=%async_computation | async-start | bytes 2097152 | tf_op jit(solution)/shard_map/all_to_all | solution.py:526
  16.0 17.9 %collective-permute-start.5 = (f32[8,64,256]{2,1,0:T(8,128)}, f32[8,64,256]{2,1,0:T(8,128)}, u32[]{:S(2)}, u32[]{:S(2)}) collective-permute-start(f32[8,64,256]{2,1,0:T(8,128)} %get-tuple-element.46), channel_id=1, source_target_pairs={{0,1},{1,0},{2,3},{3,2},{4,5},{5,4},{6,7},{7,6},{8,9},{9,8},{10,11... | collective-permute-start | bytes 1572872 | tf_op jit(solution)/shard_map/ppermute | solution.py:627
  16.3 17.6 %collective-permute-start.6 = (f32[8,64,256]{2,1,0:T(8,128)}, f32[8,64,256]{2,1,0:T(8,128)}, u32[]{:S(2)}, u32[]{:S(2)}) collective-permute-start(f32[8,64,256]{2,1,0:T(8,128)} %get-tuple-element.47), channel_id=1, source_target_pairs={{1,2},{3,4},{5,6},{7,8},{9,10},{11,12},{13,14},{15,16},{17,18},{19... | collective-permute-start | bytes 1572872 | tf_op jit(solution)/shard_map/ppermute | solution.py:626
  21.9 2.8 %collective-permute-start = (s32[8]{0:T(128)S(1)}, s32[8]{0:T(128)S(1)}, u32[]{:S(2)}, u32[]{:S(2)}) collective-permute-start(s32[8]{0:T(128)S(1)} %compare_select_fusion), channel_id=1, source_target_pairs={{0,32},{32,0},{64,96},{96,64},{128,160},{160,128},{192,224},{224,1... | collective-permute-start | bytes 104 | tf_op jit(solution)/shard_map/ppermute | solution.py:31
  23.2 10.5 %collective-permute-start.3 = (f32[2,4,8,256]{3,2,1,0:T(8,128)S(1)}, f32[2,4,8,256]{3,2,1,0:T(8,128)S(1)}, u32[]{:S(2)}, u32[]{:S(2)}) collective-permute-start(f32[2,4,8,256]{3,2,1,0:T(8,128)S(1)} %get-tuple-element.45), channel_id=1, source_target_pairs={{0,1},{1,0},{2,3},{3,2},{4,5},{5,4},{6,7},{7,6},{8,9},{9,8},{10,11... | collective-permute-start | bytes 196616 | tf_op jit(solution)/shard_map/ppermute | solution.py:530
  24.7 4.2 %collective-permute-start.1 = (s32[8]{0:T(128)S(1)}, s32[8]{0:T(128)S(1)}, u32[]{:S(2)}, u32[]{:S(2)}) collective-permute-start(s32[8]{0:T(128)S(1)} %fusion), channel_id=1, source_target_pairs={{0,64},{32,96},{64,0},{96,32},{128,192},{160,224},{192,128},{224,1... | collective-permute-start | bytes 104 | tf_op jit(solution)/shard_map/ppermute | solution.py:31
  29.0 4.8 %collective-permute-start.2 = (s32[8]{0:T(128)S(1)}, s32[8]{0:T(128)S(1)}, u32[]{:S(2)}, u32[]{:S(2)}) collective-permute-start(s32[8]{0:T(128)S(1)} %fusion.1), channel_id=1, source_target_pairs={{0,128},{32,160},{64,192},{96,224},{128,0},{160,32},{192,64},{224,... | collective-permute-start | bytes 104 | tf_op jit(solution)/shard_map/ppermute | solution.py:31
  33.7 7.8 %collective-permute-start.4 = (f32[2,4,8,256]{3,2,1,0:T(8,128)S(1)}, f32[2,4,8,256]{3,2,1,0:T(8,128)S(1)}, u32[]{:S(2)}, u32[]{:S(2)}) collective-permute-start(f32[2,4,8,256]{3,2,1,0:T(8,128)S(1)} %shard_map.109), channel_id=1, source_target_pairs={{0,2},{1,3},{2,0},{3,1},{4,6},{5,7},{6,4},{7,5},{8,10},{9,11},{10,... | collective-permute-start | bytes 196616 | tf_op jit(solution)/shard_map/ppermute | solution.py:530
  79.9 11.3 %collective-permute-start.11 = (f32[4,64,256]{2,1,0:T(8,128)S(1)}, f32[4,64,256]{2,1,0:T(8,128)S(1)}, u32[]{:S(2)}, u32[]{:S(2)}) collective-permute-start(f32[4,64,256]{2,1,0:T(8,128)S(1)} %get-tuple-element.62), channel_id=1, source_target_pairs={{0,1},{1,0},{2,3},{3,2},{4,5},{5,4},{6,7},{7,6},{8,9},{9,8},{10,11... | collective-permute-start | bytes 786440 | tf_op jit(solution)/shard_map/ppermute | solution.py:627
  80.4 10.8 %collective-permute-start.12 = (f32[4,64,256]{2,1,0:T(8,128)S(1)}, f32[4,64,256]{2,1,0:T(8,128)S(1)}, u32[]{:S(2)}, u32[]{:S(2)}) collective-permute-start(f32[4,64,256]{2,1,0:T(8,128)S(1)} %get-tuple-element.63), channel_id=1, source_target_pairs={{1,2},{3,4},{5,6},{7,8},{9,10},{11,12},{13,14},{15,16},{17,18},{19... | collective-permute-start | bytes 786440 | tf_op jit(solution)/shard_map/ppermute | solution.py:626
  86.0 12.7 %collective-permute-start.7 = (f32[4,64,256]{2,1,0:T(8,128)S(1)}, f32[4,64,256]{2,1,0:T(8,128)S(1)}, u32[]{:S(2)}, u32[]{:S(2)}) collective-permute-start(f32[4,64,256]{2,1,0:T(8,128)S(1)} %get-tuple-element.52), channel_id=1, source_target_pairs={{0,1},{1,0},{2,3},{3,2},{4,5},{5,4},{6,7},{7,6},{8,9},{9,8},{10,11... | collective-permute-start | bytes 786440 | tf_op jit(solution)/shard_map/ppermute | solution.py:627
  86.2 12.6 %collective-permute-start.8 = (f32[4,64,256]{2,1,0:T(8,128)S(1)}, f32[4,64,256]{2,1,0:T(8,128)S(1)}, u32[]{:S(2)}, u32[]{:S(2)}) collective-permute-start(f32[4,64,256]{2,1,0:T(8,128)S(1)} %get-tuple-element.53), channel_id=1, source_target_pairs={{1,2},{3,4},{5,6},{7,8},{9,10},{11,12},{13,14},{15,16},{17,18},{19... | collective-permute-start | bytes 786440 | tf_op jit(solution)/shard_map/ppermute | solution.py:626
  94.3 12.1 %collective-permute-start.13 = (f32[4,64,256]{2,1,0:T(8,128)S(1)}, f32[4,64,256]{2,1,0:T(8,128)S(1)}, u32[]{:S(2)}, u32[]{:S(2)}) collective-permute-start(f32[4,64,256]{2,1,0:T(8,128)S(1)} %get-tuple-element.66), channel_id=1, source_target_pairs={{0,1},{1,0},{2,3},{3,2},{4,5},{5,4},{6,7},{7,6},{8,9},{9,8},{10,11... | collective-permute-start | bytes 786440 | tf_op jit(solution)/shard_map/ppermute | solution.py:627
  94.4 12.0 %collective-permute-start.14 = (f32[4,64,256]{2,1,0:T(8,128)S(1)}, f32[4,64,256]{2,1,0:T(8,128)S(1)}, u32[]{:S(2)}, u32[]{:S(2)}) collective-permute-start(f32[4,64,256]{2,1,0:T(8,128)S(1)} %get-tuple-element.67), channel_id=1, source_target_pairs={{1,2},{3,4},{5,6},{7,8},{9,10},{11,12},{13,14},{15,16},{17,18},{19... | collective-permute-start | bytes 786440 | tf_op jit(solution)/shard_map/ppermute | solution.py:626
  101.8 11.7 %collective-permute-start.10 = (f32[4,64,256]{2,1,0:T(8,128)S(1)}, f32[4,64,256]{2,1,0:T(8,128)S(1)}, u32[]{:S(2)}, u32[]{:S(2)}) collective-permute-start(f32[4,64,256]{2,1,0:T(8,128)S(1)} %get-tuple-element.57), channel_id=1, source_target_pairs={{1,2},{3,4},{5,6},{7,8},{9,10},{11,12},{13,14},{15,16},{17,18},{19... | collective-permute-start | bytes 786440 | tf_op jit(solution)/shard_map/ppermute | solution.py:626
  106.2 7.3 %collective-permute-start.9 = (f32[4,64,256]{2,1,0:T(8,128)S(1)}, f32[4,64,256]{2,1,0:T(8,128)S(1)}, u32[]{:S(2)}, u32[]{:S(2)}) collective-permute-start(f32[4,64,256]{2,1,0:T(8,128)S(1)} %get-tuple-element.56), channel_id=1, source_target_pairs={{0,1},{1,0},{2,3},{3,2},{4,5},{5,4},{6,7},{7,6},{8,9},{9,8},{10,11... | collective-permute-start | bytes 786440 | tf_op jit(solution)/shard_map/ppermute | solution.py:627
  108.8 12.4 %collective-permute-start.15 = (f32[4,64,256]{2,1,0:T(8,128)S(1)}, f32[4,64,256]{2,1,0:T(8,128)S(1)}, u32[]{:S(2)}, u32[]{:S(2)}) collective-permute-start(f32[4,64,256]{2,1,0:T(8,128)S(1)} %get-tuple-element.70), channel_id=1, source_target_pairs={{0,1},{1,0},{2,3},{3,2},{4,5},{5,4},{6,7},{7,6},{8,9},{9,8},{10,11... | collective-permute-start | bytes 786440 | tf_op jit(solution)/shard_map/ppermute | solution.py:627
  109.6 11.7 %collective-permute-start.16 = (f32[4,64,256]{2,1,0:T(8,128)S(1)}, f32[4,64,256]{2,1,0:T(8,128)S(1)}, u32[]{:S(2)}, u32[]{:S(2)}) collective-permute-start(f32[4,64,256]{2,1,0:T(8,128)S(1)} %get-tuple-element.71), channel_id=1, source_target_pairs={{1,2},{3,4},{5,6},{7,8},{9,10},{11,12},{13,14},{15,16},{17,18},{19... | collective-permute-start | bytes 786440 | tf_op jit(solution)/shard_map/ppermute | solution.py:626
  115.9 10.5 %collective-permute-start.17 = (f32[4,64,256]{2,1,0:T(8,128)S(1)}, f32[4,64,256]{2,1,0:T(8,128)S(1)}, u32[]{:S(2)}, u32[]{:S(2)}) collective-permute-start(f32[4,64,256]{2,1,0:T(8,128)S(1)} %get-tuple-element.75), channel_id=1, source_target_pairs={{0,1},{1,0},{2,3},{3,2},{4,5},{5,4},{6,7},{7,6},{8,9},{9,8},{10,11... | collective-permute-start | bytes 786440 | tf_op jit(solution)/shard_map/ppermute | solution.py:627
  116.0 11.3 %collective-permute-start.18 = (f32[4,64,256]{2,1,0:T(8,128)S(1)}, f32[4,64,256]{2,1,0:T(8,128)S(1)}, u32[]{:S(2)}, u32[]{:S(2)}) collective-permute-start(f32[4,64,256]{2,1,0:T(8,128)S(1)} %get-tuple-element.76), channel_id=1, source_target_pairs={{1,2},{3,4},{5,6},{7,8},{9,10},{11,12},{13,14},{15,16},{17,18},{19... | collective-permute-start | bytes 786440 | tf_op jit(solution)/shard_map/ppermute | solution.py:626
  154.2 36.4 %all-to-all-start.3 = ((f32[32,4,8,256]{3,2,1,0:T(8,128)}), f32[32,4,8,256]{3,2,1,0:T(8,128)S(1)}, u32[]{:S(2)}, u32[]{:S(2)}) async-start(f32[32,4,8,256]{3,2,1,0:T(8,128)} %get-tuple-element.78), calls=%async_computation.3 | async-start | bytes 2097152 | tf_op jit(solution)/shard_map/all_to_all | solution.py:526
  162.5 1.3 collective-permute-start.19
  163.9 5.0 %collective-permute-start.20 = (f32[2,4,8,256]{3,2,1,0:T(8,128)S(1)}, f32[2,4,8,256]{3,2,1,0:T(8,128)S(1)}, u32[]{:S(2)}, u32[]{:S(2)}) collective-permute-start(f32[2,4,8,256]{3,2,1,0:T(8,128)S(1)} %shard_map.120), channel_id=1, source_target_pairs={{0,2},{1,3},{2,0},{3,1},{4,6},{5,7},{6,4},{7,5},{8,10},{9,11},{10,... | collective-permute-start | bytes 196616 | tf_op jit(solution)/shard_map/ppermute | solution.py:530
  (11 other events, 174.4 us)
